TPU v7x, 32 devices: a whole 2x2x4 slice. The times are simulated.
32 devices in a mesh: dp: 8 (over z, core), tensor: 4 (over y, x).
Axes of the slice: x: 2, y: 2, z: 4, core: 2. Of those that a mesh axis runs over, the one named last changes fastest.
Arguments:
- block_input: float32 [16384, 768], P(('dp', 'tensor')), may hold values from -6 to 6
- segment_ids: int32 [8, 2048], P('dp'), may hold values from 0 to 3, never falling along the last dimension, each value on 1 to 1024 neighbouring positions
- norm_gain: float32 [768], replicated, may hold values from 0.5 to 1.5
- gate_proj: bfloat16 [768, 1536], P('dp', 'tensor'), may hold values from -0.21875 to 0.21875
- value_proj: bfloat16 [768, 1536], P('dp', 'tensor'), may hold values from -0.21875 to 0.21875
- shared_proj: bfloat16 [768, 256], P('dp'), may hold values from -0.21875 to 0.21875
- step_proj: bfloat16 [768, 24], P('dp', 'tensor'), may hold values from -0.21875 to 0.21875
- conv_value_weight: float32 [4, 1536], P(None, 'tensor'), may hold values from -2 to 2
- conv_value_bias: float32 [1536], P('tensor'), may hold values from -0.5 to 0.5
- conv_shared_weight: float32 [4, 256], replicated, may hold values from -2 to 2
- conv_shared_bias: float32 [256], replicated, may hold values from -0.5 to 0.5
- step_bias: float32 [24], P('tensor'), may hold values from -5 to -2
- decay_log: float32 [24], P('tensor'), may hold values from -2 to 2
- skip_weight: float32 [24], P('tensor'), may hold values from 0.5 to 1.5
- gate_gain: float32 [1536], P('tensor'), may hold values from 0.5 to 1.5
- output_proj: bfloat16 [1536, 768], P('tensor', 'dp'), may hold values from -0.15625 to 0.15625
- out_cotangent: bfloat16 [16384, 768], P(('dp', 'tensor')), may hold values from -6 to 6
Outputs:
- block_output: float32 [16384, 768], P(('dp', 'tensor'))
- input_grad: float32 [16384, 768], P(('dp', 'tensor'))
- norm_gain_grad: float32 [768], replicated
- gate_proj_grad: float32 [768, 1536], P('dp', 'tensor')
- value_proj_grad: float32 [768, 1536], P('dp', 'tensor')
- shared_proj_grad: float32 [768, 256], P('dp')
- step_proj_grad: float32 [768, 24], P('dp', 'tensor')
- conv_value_weight_grad: float32 [4, 1536], P(None, 'tensor')
- conv_value_bias_grad: float32 [1536], P('tensor')
- conv_shared_weight_grad: float32 [4, 256], replicated
- conv_shared_bias_grad: float32 [256], replicated
- step_bias_grad: float32 [24], P('tensor')
- decay_log_grad: float32 [24], P('tensor')
- skip_weight_grad: float32 [24], P('tensor')
- gate_gain_grad: float32 [1536], P('tensor')
- output_proj_grad: float32 [1536, 768], P('tensor', 'dp')
Inputs may be any that keep to these rules, and one draw needn't show every extreme that they name: `segment_ids`: along each sequence the segment numbers never fall and every number from 0 to 3 occurs; a document holds at most 1024 tokens, and one document of each sequence holds exactly that many.
All inputs are finite; a program needn't handle non-finite values.
Results may differ from a plain program's by a relative error of at most 0.019.
Values may be sent and summed in bfloat16 or wider, within the bound.
No kernel may reach another device: no remote copies, remote signals or barrier semaphores. Data moves between devices by JAX's collectives and lax.ppermute only.
A program may use at most 192 MiB of HBM per device.

v0:
```python
import functools
import math

import jax
import jax.numpy as jnp
from jax import lax
from jax.experimental import pallas as pl
from jax.experimental.pallas import tpu as pltpu
from jax.sharding import PartitionSpec as P


BLOCK = 256
LANES = 128
EPS = 1e-05
LOG2E = math.log2(math.e)
FAR = -1e30
F32 = jnp.float32
BF16 = jnp.bfloat16

MM = (((1,), (0,)), ((), ()))
MT = (((1,), (1,)), ((), ()))
TM = (((0,), (0,)), ((), ()))


def dot(a, b, dims=MM):
    return lax.dot_general(a, b, dims, preferred_element_type=F32)


def dot_split(exact, values, dims=MM):
    high = values.astype(BF16)
    low = (values - high.astype(F32)).astype(BF16)
    return dot(exact, high, dims) + dot(exact, low, dims)


def split_dot(values, exact, dims=MM):
    high = values.astype(BF16)
    low = (values - high.astype(F32)).astype(BF16)
    return dot(high, exact, dims) + dot(low, exact, dims)


def up(n, to=LANES):
    return -(-n // to) * to


def softplus(v):
    return jnp.maximum(v, 0.0) + jnp.log1p(jnp.exp(-jnp.abs(v)))


def sigmoid(v):
    return 1.0 / (1.0 + jnp.exp(-v))


def colsum(v):
    return jnp.sum(v.reshape(v.shape[0] // 8, 8, v.shape[1]), axis=0)


def spread(cols, pair, hd):
    per = LANES // hd
    lane = lax.broadcasted_iota(jnp.int32, (cols.shape[0], LANES), 1)
    out = jnp.broadcast_to(cols[:, pair * per : pair * per + 1], lane.shape)
    for j in range(1, per):
        col = cols[:, pair * per + j : pair * per + j + 1]
        out = jnp.where(lane >= j * hd, jnp.broadcast_to(col, lane.shape), out)
    return out


def columns_of(rows):
    pad = jnp.zeros((LANES - rows.shape[0], rows.shape[1]), F32)
    return jnp.concatenate([rows, pad], axis=0).T


class Dims:
    def __init__(self, n_dp, n_t, length, width, inner, hd, state, part_rows, chunk_rows):
        self.length, self.width, self.state, self.hd = length, width, state, hd
        self.n_dp, self.n_t, self.n_hi = n_dp, n_t, n_dp // 2
        self.ip = up(inner)
        self.vs = self.ip + 2 * state
        self.np = self.ip + self.vs + LANES
        self.wc = self.np + self.ip
        self.blocks = length // BLOCK
        self.part_rows, self.chunk_rows = part_rows, chunk_rows
        self.pairs = self.ip // LANES
        self.per = LANES // hd
        self.halves = 2 if n_t == 4 and chunk_rows == 2 * BLOCK else 1
        self.piece_rows = chunk_rows // self.halves
        self.pieces = n_t * self.halves
        self.at_n = n_dp
        self.at_c = self.at_n + self.pieces
        self.at_keep = self.at_c + n_t
        self.at_rel = self.at_keep + self.blocks
        self.at_group = self.at_rel + self.blocks
        self.at_slot = self.at_group + self.blocks
        self.at_hi = self.at_slot + self.blocks
        self.at_core = self.at_hi + self.n_hi


def load_parts(refs, target, sems, scalars, first, rows):
    return [
        pltpu.make_async_copy(
            ref, target.at[pl.ds(pl.multiple_of(scalars[first + k], rows), rows), :], sems.at[k]
        )
        for k, ref in enumerate(refs)
    ]


def decay_parts(raw, hp_ref, cols, tri):
    delta = softplus(raw + hp_ref[0:1, :])
    logs = dot_split(tri, delta * (hp_ref[1:2, :] * LOG2E))
    enter = jnp.exp2(logs) * cols[:, 7:8]
    ending = jnp.exp2(logs[BLOCK - 1 :, :] - logs) * cols[:, 8:9]
    return delta, logs, enter, ending


def norm_kernel(steps, x_ref, gain_ref, *outs):
    x = x_ref[...]
    root = lax.rsqrt(jnp.mean(x * x, axis=1, keepdims=True) + EPS)
    normed = (x * root * gain_ref[...]).astype(BF16)
    for k, out in enumerate(outs):

        @pl.when(pl.program_id(0) // steps == k)
        def _():
            out[...] = normed


def pack_kernel(dm, gate_ref, value_ref, shared_ref, step_ref, outp_ref, out_ref):
    out_ref[...] = jnp.zeros_like(out_ref)
    inner, heads, r = gate_ref.shape[1], step_ref.shape[0], step_ref.shape[1]
    row = lax.broadcasted_iota(jnp.int32, (r, r), 0)
    col = lax.broadcasted_iota(jnp.int32, (r, r), 1)
    eye = jnp.where(row == col, 1.0, 0.0).astype(BF16)
    out_ref[:, :inner] = gate_ref[...]
    out_ref[:, dm.ip : dm.ip + inner] = value_ref[...]
    out_ref[:, 2 * dm.ip : dm.ip + dm.vs] = shared_ref[...]
    out_ref[:, dm.ip + dm.vs : dm.ip + dm.vs + heads] = dot(eye, step_ref[...], MT).astype(BF16)
    out_ref[:, dm.np : dm.np + inner] = outp_ref[...]


def forward_kernel(dm, scalars, *refs):
    q, ip, vs, st, hd = BLOCK, dm.ip, dm.vs, dm.state, dm.hd
    w_parts = refs[: dm.n_dp]
    n_parts = refs[dm.n_dp : dm.n_dp + dm.pieces]
    rest = refs[dm.n_dp + dm.pieces :]
    rows_ref, conv_ref, hp_ref, lane_ref = rest[:4]
    (g_out, v_out, cv_out, ys_out, st_out, h_out, sum_out, nt_out, sg_out, w_out) = rest[4:14]
    (w_v, nm_v, h_ref, vbuf, tri_ref, bias_ref, w_sem, n_sem, o_sem) = rest[14:]
    i = pl.program_id(0)
    at = pl.ds(pl.multiple_of(i * q, q), q)
    save = pltpu.make_async_copy(w_v, w_out, o_sem)

    @pl.when(i == 0)
    def _():
        copies = load_parts(w_parts, w_v, w_sem, scalars, 0, dm.part_rows)
        copies += load_parts(n_parts, nm_v, n_sem, scalars, dm.at_n, dm.piece_rows)
        for copy in copies:
            copy.start()
        h_ref[...] = jnp.zeros_like(h_ref)
        vbuf[...] = jnp.zeros_like(vbuf)
        r = lax.broadcasted_iota(jnp.int32, (q, q), 0)
        c = lax.broadcasted_iota(jnp.int32, (q, q), 1)
        tri_ref[...] = jnp.where(r >= c, 1.0, 0.0).astype(BF16)
        for copy in copies:
            copy.wait()
        save.start()

    rows = rows_ref[...]
    cols = columns_of(rows)
    normed = nm_v[at, :]
    nt_out[...] = normed
    projected = dot(normed, w_v[:, : dm.np])
    g_out[...] = projected[:, :ip]
    vbuf[0:8, :] = vbuf[q : q + 8, :]
    vbuf[8 : 8 + q, :] = projected[:, ip : ip + vs]
    v_out[...] = projected[:, ip : ip + vs]
    raw = projected[:, ip + vs :]
    st_out[...] = raw

    acts = []
    for c in range(vs // LANES):
        g = slice(c * LANES, (c + 1) * LANES)
        acc = conv_ref[4:5, g] + conv_ref[3:4, g] * vbuf[8 : 8 + q, g]
        for lag in range(1, 4):
            acc = acc + conv_ref[3 - lag : 4 - lag, g] * (
                vbuf[8 - lag : 8 - lag + q, g] * cols[:, lag : lag + 1]
            )
        cv_out[:, g] = acc
        acts.append(acc * sigmoid(acc))
    in_map = jnp.concatenate(acts[dm.pairs : dm.pairs + st // LANES], axis=1).astype(BF16)
    out_map = jnp.concatenate(acts[dm.pairs + st // LANES :], axis=1).astype(BF16)

    delta, logs, enter, ending = decay_parts(raw, hp_ref, cols, tri_ref[...])
    logs_t = logs.T
    r = lax.broadcasted_iota(jnp.int32, (q, q), 0)
    c = lax.broadcasted_iota(jnp.int32, (q, q), 1)
    bias_ref[...] = jnp.where((r >= c) & (cols[:, 0:1] == rows[0:1, :]), 0.0, FAR)
    scores = dot(out_map, in_map, MT)
    keep = scalars[dm.at_keep + i].astype(F32)
    total = jnp.exp2(logs[q - 1 :, :]) * keep
    lane = lax.broadcasted_iota(jnp.int32, (q, LANES), 1)
    h_out[...] = h_ref[...]
    in_map_t = in_map.T
    squares = jnp.zeros((q, LANES), F32)
    for p in range(dm.pairs):
        g = slice(p * LANES, (p + 1) * LANES)
        x = acts[p]
        u = x * spread(delta, p, hd)
        ub = u.astype(BF16)
        y = None
        for j in range(dm.per):
            h = p * dm.per + j
            decay = jnp.exp2(logs[:, h : h + 1] - logs_t[h : h + 1, :] + bias_ref[...])
            part = dot((decay * scores).astype(BF16), ub)
            y = part if y is None else jnp.where(lane >= j * hd, part, y)
        held = h_ref[:, g]
        y = y + dot(out_map, held.astype(BF16)) * spread(enter, p, hd)
        wu = (u * spread(ending, p, hd)).astype(BF16)
        h_ref[:, g] = held * spread(total, p, hd) + dot(in_map_t, wu)
        ys_out[:, g] = y
        gate = g_out[:, g]
        gated = (y + lane_ref[0:1, g] * x) * (gate * sigmoid(gate))
        sg_out[:, g] = (gated * lane_ref[1:2, g]).astype(BF16)
        squares = squares + gated * gated
    sum_out[...] = jnp.sum(squares.T, axis=0, keepdims=True)

    @pl.when(i == dm.blocks - 1)
    def _():
        save.wait()


def cotangent_kernel(dm, scalars, *refs):
    q = BLOCK
    c_parts = refs[: dm.n_t]
    w_ref, sg_ref, sq_ref = refs[dm.n_t : dm.n_t + 3]
    sc_out, sum_out, ct_out = refs[dm.n_t + 3 : dm.n_t + 6]
    ct_v, c_sem = refs[dm.n_t + 6 :]
    i = pl.program_id(0)

    @pl.when(i == 0)
    def _():
        copies = load_parts(c_parts, ct_v, c_sem, scalars, dm.at_c, dm.chunk_rows)
        for copy in copies:
            copy.start()
        for copy in copies:
            copy.wait()

    cot = ct_v[pl.ds(pl.multiple_of(i * q, q), q), :]
    ct_out[...] = cot
    sc = dot(cot, w_ref[...])
    sc_out[...] = sc.astype(BF16)
    prod = sc * sg_ref[...].astype(F32)
    dots = prod[:, :LANES]
    for p in range(1, dm.pairs):
        dots = dots + prod[:, p * LANES : (p + 1) * LANES]
    sum_out[0:1, :] = sq_ref[...]
    sum_out[1:2, :] = jnp.sum(dots.T, axis=0, keepdims=True)


def branch_kernel(dm, scalars, w_ref, sg_ref, *refs):
    outs, (buf, sem) = refs[: dm.n_t], refs[dm.n_t :]
    i = pl.program_id(0)
    slot = lax.rem(i, 2)
    per = dm.chunk_rows // BLOCK

    def copy(k, at, row):
        return pltpu.make_async_copy(buf.at[at], outs[k].at[row], sem.at[at])

    @pl.when(i >= 2)
    def _():
        copy(0, slot, 0).wait()

    buf[slot] = dot(sg_ref[...], w_ref[...], MT).astype(BF16)
    for k in range(dm.n_t):

        @pl.when(scalars[dm.at_rel + i] == k)
        def _():
            copy(k, slot, lax.rem(i, per)).start()

    @pl.when(i == dm.blocks - 1)
    def _():
        copy(0, 1 - slot, 0).wait()
        copy(0, slot, 0).wait()


def gate_kernel(dm, scalars, *refs):
    q, ip, r = BLOCK, dm.ip, dm.part_rows
    (w_ref, rk_ref, lane_ref, g_in, cv_in, ys_in, sc_in, nm_in, ct_in) = refs[:9]
    dg_out, dy_out, lane_out, rows_out, own_out = refs[9:14]
    z_outs = refs[14 : 13 + dm.n_hi]
    acc, both = refs[13 + dm.n_hi :]
    i = pl.program_id(0)

    @pl.when(i == 0)
    def _():
        lane_out[...] = jnp.zeros_like(lane_out)
        acc[...] = jnp.zeros_like(acc)

    pad = jnp.zeros((LANES - 2, q), F32)
    cols = jnp.concatenate([rk_ref[...], pad], axis=0).T
    root, pull = cols[:, 0:1], cols[:, 1:2]
    for p in range(dm.pairs):
        g = slice(p * LANES, (p + 1) * LANES)
        gate, sc, ys, cv = g_in[:, g], sc_in[:, g].astype(F32), ys_in[:, g], cv_in[:, g]
        x = cv * sigmoid(cv)
        sig = sigmoid(gate)
        z = gate * sig
        y = ys + lane_ref[0:1, g] * x
        gated = y * z
        cot = root * (lane_ref[1:2, g] * sc) - pull * gated
        lane_out[0:8, g] += colsum(sc * gated * root)
        dy = cot * z
        dy_out[:, g] = dy
        dg_out[:, g] = (cot * y * (sig + z * (1.0 - sig))).astype(BF16)
        lane_out[8:16, g] += colsum(dy * x)
        both[:, g] = (gated * lane_ref[1:2, g] * root).astype(BF16)
    acc[:, :ip] += dot(nm_in[...], dg_out[...], TM)
    acc[:, ip:] += dot(ct_in[...], both[...], TM)

    @pl.when(i == dm.blocks - 1)
    def _():
        prod = acc[:, :LANES] * w_ref[:, :LANES].astype(F32)
        for p in range(1, dm.pairs):
            g = slice(p * LANES, (p + 1) * LANES)
            prod = prod + acc[:, g] * w_ref[:, g].astype(F32)
        rows_out[...] = gain_rows(prod)
        hi = scalars[dm.at_hi]
        own_out[...] = acc[pl.ds(pl.multiple_of(hi * 2 * r, 8), 2 * r), :]
        for k, z_out in enumerate(z_outs):
            at = pl.multiple_of(scalars[dm.at_hi + k + 1] * 2 * r, 8)
            z_out[...] = acc[pl.ds(at, 2 * r), :].astype(BF16)


def backward_kernel(dm, scalars, *refs):
    q, ip, vs, st, hd = BLOCK, dm.ip, dm.vs, dm.state, dm.hd
    groups = dm.group_sizes
    w_ref, rows_ref, conv_ref, hp_ref, lane_ref = refs[:5]
    dg_in, dy_in, v_in, cv_in, ys_in, st_in, h_in = refs[5:12]
    pj_out, tap_out, head_out = refs[12:15]
    nc_outs = refs[15 : 15 + len(groups)]
    (w_v, dh_ref, dbuf, tri_ref, bias_ref, ds_ref, u_s, dx_s, act_s, t1_s, t2_s, nc_buf, w_sem, nc_sem) = refs[
        15 + len(groups) :
    ]
    i = pl.program_id(0)
    blk = dm.blocks - 1 - i
    load = pltpu.make_async_copy(w_ref, w_v, w_sem)

    def send(k, at, row):
        return pltpu.make_async_copy(nc_buf.at[at], nc_outs[k].at[row], nc_sem.at[at])

    @pl.when(i == 0)
    def _():
        load.start()
        dh_ref[...] = jnp.zeros_like(dh_ref)
        dbuf[...] = jnp.zeros_like(dbuf)
        tap_out[...] = jnp.zeros_like(tap_out)
        head_out[...] = jnp.zeros_like(head_out)
        r = lax.broadcasted_iota(jnp.int32, (q, q), 0)
        c = lax.broadcasted_iota(jnp.int32, (q, q), 1)
        tri_ref[...] = jnp.where(r >= c, 1.0, 0.0).astype(BF16)

    rows = rows_ref[...]
    cols = columns_of(rows)
    raw = st_in[...]
    tri = tri_ref[...]
    delta, logs, enter, ending = decay_parts(raw, hp_ref, cols, tri)
    logs_t = logs.T
    lane = lax.broadcasted_iota(jnp.int32, (q, LANES), 1)

    acts, slopes = [], []
    for c in range(vs // LANES):
        g = slice(c * LANES, (c + 1) * LANES)
        cv = cv_in[:, g]
        sig = sigmoid(cv)
        act = cv * sig
        acts.append(act)
        slopes.append(sig + act * (1.0 - sig))
    in_map = jnp.concatenate(acts[dm.pairs : dm.pairs + st // LANES], axis=1).astype(BF16)
    out_map = jnp.concatenate(acts[dm.pairs + st // LANES :], axis=1).astype(BF16)

    for p in range(dm.pairs):
        g = slice(p * LANES, (p + 1) * LANES)
        u_s[:, g] = acts[p] * spread(delta, p, hd)

    r = lax.broadcasted_iota(jnp.int32, (q, q), 0)
    c = lax.broadcasted_iota(jnp.int32, (q, q), 1)
    bias_ref[...] = jnp.where((r <= c) & (cols[:, 0:1] == rows[0:1, :]), 0.0, FAR)
    scores = dot(in_map, out_map, MT)
    dh_b = dh_ref[...].astype(BF16)
    h_b = h_in[...].astype(BF16)
    out_map_t = out_map.T
    keep = scalars[dm.at_keep + blk].astype(F32)
    total = jnp.exp2(logs[q - 1 :, :]) * keep
    d_in = jnp.zeros((q, st), F32)
    d_out = jnp.zeros((q, st), F32)
    for p in range(dm.pairs):
        g = slice(p * LANES, (p + 1) * LANES)
        u, dy = u_s[:, g], dy_in[:, g]
        ub, dyb = u.astype(BF16), dy.astype(BF16)
        du = None
        for j in range(dm.per):
            h = p * dm.per + j
            mine = (lane >= j * hd) & (lane < (j + 1) * hd)
            decay = jnp.exp2(logs_t[h : h + 1, :] - logs[:, h : h + 1] + bias_ref[...])
            part = dot((decay * scores).astype(BF16), dyb)
            du = part if du is None else jnp.where(lane >= j * hd, part, du)
            dm_t = dot(jnp.where(mine, u, 0.0).astype(BF16), dyb, MT)
            if p == 0 and j == 0:
                ds_ref[...] = dm_t * decay
            else:
                ds_ref[...] += dm_t * decay
        end_e = spread(ending, p, hd)
        late = end_e * dot(in_map, dh_b[:, g])
        du = du + late
        wu = (u * end_e).astype(BF16)
        edy = (dy * spread(enter, p, hd)).astype(BF16)
        d_in = d_in + dot(wu, dh_b[:, g], MT)
        d_out = d_out + dot(edy, h_b[:, g], MT)
        u32 = ub.astype(F32)
        t1_s[:, g] = dyb.astype(F32) * ys_in[:, g] - u32 * du
        t2_s[:, g] = du * acts[p]
        kept = dh_ref[:, g] * spread(total, p, hd)
        act_s[:, g] = colsum(u32 * late) + colsum(h_in[:, g] * kept)
        dh_ref[:, g] = kept + dot(out_map_t, edy)
        dx_s[:, g] = (spread(delta, p, hd) * du + lane_ref[0:1, g] * dy) * slopes[p]
    ds_b = ds_ref[...].astype(BF16)
    d_in = d_in + dot(ds_b, out_map)
    d_out = d_out + dot(ds_b, in_map, TM)

    hr = lax.broadcasted_iota(jnp.int32, (ip, LANES), 0)
    hc = lax.broadcasted_iota(jnp.int32, (ip, LANES), 1)
    pick = jnp.where(hr // hd == hc, 1.0, 0.0).astype(BF16)
    d_log = split_dot(t1_s[...], pick)
    last = split_dot(jnp.sum(act_s[...], axis=0, keepdims=True), pick)
    row = lax.broadcasted_iota(jnp.int32, (q, LANES), 0)
    d_log = d_log + jnp.where(row == q - 1, last, 0.0)
    d_step = dot_split(tri, d_log, TM)
    head_out[8:16, :] += colsum(d_step * delta)
    d_delta = hp_ref[1:2, :] * d_step + split_dot(t2_s[...], pick)
    d_raw = d_delta * sigmoid(raw + hp_ref[0:1, :])
    head_out[0:8, :] += colsum(d_raw)
    pj_out[:, vs:] = d_raw.astype(BF16)

    dbuf[q : q + 8, :] = dbuf[0:8, :]
    for c in range(vs // LANES):
        g = slice(c * LANES, (c + 1) * LANES)
        if c < dm.pairs:
            dbuf[0:q, g] = dx_s[:, g]
        else:
            k = (c - dm.pairs) * LANES
            source = d_in[:, k : k + LANES] if k < st else d_out[:, k - st : k - st + LANES]
            dbuf[0:q, g] = source * slopes[c]
    for c in range(vs // LANES):
        g = slice(c * LANES, (c + 1) * LANES)
        v = v_in[:, g]
        shifted = dbuf[0:q, g]
        tap_out[32:40, g] += colsum(shifted)
        tap_out[24:32, g] += colsum(shifted * v)
        dv = conv_ref[3:4, g] * shifted
        for lag in range(1, 4):
            shifted = dbuf[lag : lag + q, g] * cols[:, 3 + lag : 4 + lag]
            tap_out[24 - 8 * lag : 32 - 8 * lag, g] += colsum(shifted * v)
            dv = dv + conv_ref[3 - lag : 4 - lag, g] * shifted
        pj_out[:, g] = dv.astype(BF16)

    @pl.when(i == 0)
    def _():
        load.wait()

    slot = lax.rem(i, 2)

    @pl.when(i >= 2)
    def _():
        send(0, slot, 0).wait()

    nc = dot(dg_in[...], w_v[:, :ip], MT) + dot(pj_out[...], w_v[:, ip : dm.np], MT)
    nc_buf[slot] = nc.astype(BF16)
    for k in range(len(groups)):

        @pl.when(scalars[dm.at_group + blk] == k)
        def _():
            send(k, slot, scalars[dm.at_slot + blk]).start()

    @pl.when(i == dm.blocks - 1)
    def _():
        send(0, 1 - slot, 0).wait()
        send(0, slot, 0).wait()


def joined_kernel(dm, scalars, nm_ref, pj_ref, w_ref, taps_ref, lanes_ref, heads_ref, rows_ref, *refs):
    mine_out, theirs_out, small_out, acc = refs
    n = pl.program_id(0)
    r = dm.part_rows

    @pl.when(n == 0)
    def _():
        acc[...] = jnp.zeros_like(acc)

    acc[...] += dot(nm_ref[...], pj_ref[...], TM)

    @pl.when(n == pl.num_programs(0) - 1)
    def _():
        core = scalars[dm.at_core]
        for h in range(dm.n_hi):
            at = pl.multiple_of((2 * h + core) * r, 8)
            mine_out[h] = acc[pl.ds(at, r), :]
            at = pl.multiple_of((2 * h + 1 - core) * r, 8)
            theirs_out[h] = acc[pl.ds(at, r), :].astype(BF16)
        small_out[...] = jnp.zeros_like(small_out)
        row = 0

        def put(v):
            nonlocal row
            for c in range(v.shape[1] // LANES):
                small_out[row : row + 1, :] = jnp.sum(
                    v[:, c * LANES : (c + 1) * LANES], axis=0, keepdims=True
                )
                row += 1

        for k in range(5):
            put(taps_ref[8 * k : 8 * k + 8, : dm.ip])
        for k in range(2):
            put(lanes_ref[8 * k : 8 * k + 8, :])
        for k in range(2):
            put(heads_ref[8 * k : 8 * k + 8, :])
        row = dm.local_rows
        for k in range(5):
            put(taps_ref[8 * k : 8 * k + 8, dm.ip :])
        prod = acc[:, :LANES] * w_ref[:, dm.ip : dm.ip + LANES].astype(F32)
        for p in range(1, (dm.vs + LANES) // LANES):
            g = slice(p * LANES, (p + 1) * LANES)
            o = slice(dm.ip + p * LANES, dm.ip + (p + 1) * LANES)
            prod = prod + acc[:, g] * w_ref[:, o].astype(F32)
        put(gain_rows(prod) + rows_ref[...])


def gain_rows(acc):
    high = acc.astype(BF16)
    rest = acc - high.astype(F32)
    mid = rest.astype(BF16)
    low = (rest - mid.astype(F32)).astype(BF16)
    one = jnp.ones((8, LANES), BF16)
    return (dot(one, high, MT) + dot(one, mid, MT) + dot(one, low, MT)) * 0.125


def pair_kernel(scalars, mine_ref, theirs_ref, own_out, *outs):
    k = pl.program_id(0)
    both = mine_ref[...] + theirs_ref[...].astype(F32)

    @pl.when(k == 0)
    def _():
        own_out[...] = both

    for j, out in enumerate(outs):

        @pl.when(k == j + 1)
        def _():
            out[...] = both.astype(BF16)


def early_kernel(dm, scalars, own_ref, *refs):
    parts, (mine_out, theirs_out, total) = refs[: dm.n_hi - 1], refs[dm.n_hi - 1 :]
    r = dm.part_rows
    both = own_ref[...]
    for part in parts:
        both = both + part[...].astype(F32)
    total[...] = both
    core = scalars[dm.at_core]
    mine_out[...] = total[pl.ds(pl.multiple_of(core * r, 8), r), :]
    theirs_out[...] = total[pl.ds(pl.multiple_of((1 - core) * r, 8), r), :].astype(BF16)


def grads_kernel(dm, own_ref, mine_ref, theirs_ref, *refs):
    parts, outs = refs[: dm.n_hi - 1], refs[dm.n_hi - 1 :]
    gate_out, value_out, step_out, outp_out, shared_out = outs
    total = own_ref[...]
    for part in parts:
        total = total + part[...].astype(F32)
    early = mine_ref[...] + theirs_ref[...].astype(F32)
    inner, heads = gate_out.shape[1], step_out.shape[1]
    gate_out[...] = early[:, :inner]
    outp_out[...] = early[:, dm.ip : dm.ip + inner]
    value_out[...] = total[:, :inner]
    shared_out[...] = total[:, dm.ip : dm.vs]
    step_out[...] = total[:, dm.vs : dm.vs + heads]


def input_kernel(sets, steps, x_ref, cot_ref, gain_ref, *refs):
    out = refs[-1]
    x = x_ref[...]
    root = lax.rsqrt(jnp.mean(x * x, axis=1, keepdims=True) + EPS)
    first = 0
    for k, count in enumerate(sets):
        parts = refs[first : first + count]
        first += count

        @pl.when(pl.program_id(0) // steps == k)
        def _():
            nc = parts[0][...].astype(F32)
            for part in parts[1:]:
                nc = nc + part[...].astype(F32)
            hat = nc * gain_ref[...]
            mean = jnp.mean(hat * x, axis=1, keepdims=True)
            out[...] = cot_ref[...].astype(F32) + root * hat - x * (root * root * root * mean)


def shift_hi(n, k):
    return [(i, ((i // 2 + k) % (n // 2)) * 2 + i % 2) for i in range(n)]


def swap(n, k):
    return [(i, i ^ k) for i in range(n)]


def all_sum(v, axis, n):
    k = 1
    while k < n:
        v = v + lax.ppermute(v, axis, swap(n, k))
        k *= 2
    return v


def pad_cols(v, to):
    return jnp.pad(v, ((0, 0), (0, to - v.shape[1])))


def pad_vec(v, to):
    return jnp.pad(v, (0, to - v.shape[0]))


def body(
    n_dp,
    n_t,
    block_input,
    segment_ids,
    norm_gain,
    gate_proj,
    value_proj,
    shared_proj,
    step_proj,
    conv_value_weight,
    conv_value_bias,
    conv_shared_weight,
    conv_shared_bias,
    step_bias,
    decay_log,
    skip_weight,
    gate_gain,
    output_proj,
    out_cotangent,
):
    q = BLOCK
    chunk_rows, width = block_input.shape
    length = segment_ids.shape[1]
    inner, heads = gate_proj.shape[1], step_proj.shape[1]
    part_rows = gate_proj.shape[0]
    state = shared_proj.shape[1] // 2
    hd = inner // heads
    dm = Dims(n_dp, n_t, length, width, inner, hd, state, part_rows, chunk_rows)
    ip, vs, nb, n_hi = dm.ip, dm.vs, dm.blocks, dm.n_hi
    dm.local_rows = up(7 * dm.pairs + 2, 8)
    dm.small_rows = up(dm.local_rows + 10 * state // LANES + width // LANES, 8)
    me_t = lax.axis_index("tensor")
    me_dp = lax.axis_index("dp")
    hi, core = me_dp // 2, me_dp % 2

    def across(v, k):
        return lax.ppermute(v, "tensor", swap(n_t, k))

    def along(v, k):
        return lax.ppermute(v, "dp", shift_hi(n_dp, k))

    def partner(v):
        return lax.ppermute(v, "dp", swap(n_dp, 1))

    def vmem(shape, dtype):
        return pltpu.VMEM(shape, dtype)

    limit = 60 * 1024 * 1024
    params = pltpu.CompilerParams(dimension_semantics=("arbitrary",), vmem_limit_bytes=limit)
    hbm = pl.BlockSpec(memory_space=pl.ANY)

    def out(*shape, dtype=F32):
        return jax.ShapeDtypeStruct(shape, dtype)

    gain = norm_gain.reshape(1, width)
    part = min(LANES, dm.piece_rows)
    steps = dm.piece_rows // part

    def turn(k, rows=part):
        return pl.BlockSpec(
            (rows, width), lambda i: (jnp.clip(i - k * steps, 0, steps - 1), 0)
        )

    normed = pl.pallas_call(
        functools.partial(norm_kernel, steps),
        out_shape=[out(dm.piece_rows, width, dtype=BF16)] * dm.halves,
        grid=(dm.halves * steps,),
        in_specs=[
            pl.BlockSpec((part, width), lambda i: (i, 0)),
            pl.BlockSpec((1, width), lambda i: (0, 0)),
        ],
        out_specs=[turn(k) for k in range(dm.halves)],
        compiler_params=params,
        name="normalize",
    )(block_input, gain)
    if dm.halves == 2:
        a, b = normed
        xa, yb = across(a, 1), across(b, 2)
        ya, xb = across(a, 2), across(b, 1)
        n_list = [a, b, xa, xb, ya, yb, across(xa, 2), across(yb, 1)]
        n_rows = jnp.concatenate(
            [(me_t ^ k) * chunk_rows + jnp.arange(2) * dm.piece_rows for k in range(4)]
        )
    else:
        n_list = [normed[0]] + [across(normed[0], k) for k in range(1, n_t)]
        n_rows = (me_t ^ jnp.arange(n_t)) * chunk_rows
    packed = pl.pallas_call(
        functools.partial(pack_kernel, dm),
        out_shape=out(part_rows, dm.wc, dtype=BF16),
        name="pack_weights",
    )(gate_proj, value_proj, shared_proj, step_proj.T, output_proj.T)
    w_list = [packed] + [along(packed, k) for k in range(1, n_hi)]
    w_list = w_list + [partner(part) for part in w_list]

    seg = segment_ids[0]
    segb = seg.reshape(nb, q)
    last = segb[:, -1]
    prev_last = jnp.concatenate([jnp.full((1,), -1, jnp.int32), last[:-1]])
    gap = jnp.full((3,), -1, jnp.int32)
    wide = jnp.concatenate([gap, seg, gap])
    rows = [seg.astype(F32)]
    rows += [(wide[3 - k : 3 - k + length] == seg).astype(F32) for k in range(1, 4)]
    rows += [(wide[3 + k : 3 + k + length] == seg).astype(F32) for k in range(1, 4)]
    rows += [
        (segb == prev_last[:, None]).astype(F32).reshape(-1),
        (segb == last[:, None]).astype(F32).reshape(-1),
    ]
    rows = jnp.concatenate([jnp.stack(rows), jnp.zeros((16 - len(rows), length), F32)], axis=0)
    keep = (last == prev_last).astype(jnp.int32)
    other = (hi - jnp.arange(n_hi)) % n_hi
    rel = (jnp.arange(nb) * q // chunk_rows) ^ me_t
    half = jnp.arange(nb) % (chunk_rows // q)
    if dm.halves == 2:
        group_of = jnp.array([[2, 2], [0, 2], [2, 1], [0, 1]])
        slot_of = jnp.array([[0, 2], [0, 3], [1, 0], [1, 1]])
        group, slot = group_of[rel, half], slot_of[rel, half]
        dm.group_sizes = (2, 2, 4)
    else:
        group, slot = rel, half
        dm.group_sizes = (chunk_rows // q,) * n_t
    scalars = jnp.concatenate(
        [
            (other * 2 + core) * part_rows,
            (other * 2 + 1 - core) * part_rows,
            n_rows,
            (me_t ^ jnp.arange(n_t)) * chunk_rows,
            keep,
            rel,
            group,
            slot,
            (hi + jnp.arange(n_hi)) % n_hi,
            core[None],
        ]
    ).astype(jnp.int32)

    conv = jnp.concatenate(
        [
            pad_cols(jnp.concatenate([conv_value_weight, conv_value_bias[None]]), ip),
            jnp.concatenate([conv_shared_weight, conv_shared_bias[None]]),
        ],
        axis=1,
    )
    conv = jnp.pad(conv, ((0, 3), (0, 0)))
    rate = -jnp.exp(decay_log)
    per_head = jnp.stack([pad_vec(step_bias, LANES), pad_vec(rate, LANES)])
    per_head = jnp.pad(per_head, ((0, 6), (0, 0)))
    per_lane = jnp.stack([pad_vec(jnp.repeat(skip_weight, hd), ip), pad_vec(gate_gain, ip)])
    per_lane = jnp.pad(per_lane, ((0, 6), (0, 0)))

    def const(*shape):
        return pl.BlockSpec(shape, lambda i, s: (0,) * len(shape))

    def fblock(cols):
        return pl.BlockSpec((q, cols), lambda i, s: (i, 0))

    def fsum(k):
        return pl.BlockSpec((None, k, q), lambda i, s: (i, 0, 0))

    def grid(steps, in_specs, out_specs, scratch):
        return pltpu.PrefetchScalarGridSpec(
            num_scalar_prefetch=1,
            grid=(steps,),
            in_specs=in_specs,
            out_specs=out_specs,
            scratch_shapes=scratch,
        )

    (gate, value, conved, scan, steps_raw, held, squares, normed_all, scaled, weights) = pl.pallas_call(
        functools.partial(forward_kernel, dm),
        out_shape=[
            out(length, ip),
            out(length, vs),
            out(length, vs),
            out(length, ip),
            out(length, LANES),
            out(nb * state, ip),
            out(nb, 1, q),
            out(length, width, dtype=BF16),
            out(length, ip, dtype=BF16),
            out(width, dm.wc, dtype=BF16),
        ],
        grid_spec=grid(
            nb,
            [hbm] * (n_dp + dm.pieces)
            + [
                pl.BlockSpec((16, q), lambda i, s: (0, i)),
                const(8, vs),
                const(8, LANES),
                const(8, ip),
            ],
            [
                fblock(ip),
                fblock(vs),
                fblock(vs),
                fblock(ip),
                fblock(LANES),
                pl.BlockSpec((state, ip), lambda i, s: (i, 0)),
                fsum(1),
                fblock(width),
                fblock(ip),
                hbm,
            ],
            [
                vmem((width, dm.wc), BF16),
                vmem((length, width), BF16),
                vmem((state, ip), F32),
                vmem((q + 8, vs), F32),
                vmem((q, q), BF16),
                vmem((q, q), F32),
                pltpu.SemaphoreType.DMA((n_dp,)),
                pltpu.SemaphoreType.DMA((dm.pieces,)),
                pltpu.SemaphoreType.DMA,
            ],
        ),
        compiler_params=params,
        cost_estimate=pl.CostEstimate(
            flops=30_000_000_000, bytes_accessed=30_000_000, transcendentals=0
        ),
        name="block_forward",
    )(scalars, *w_list, *n_list, rows, conv, per_head, per_lane)

    c_list = [out_cotangent] + [across(out_cotangent, k) for k in range(1, n_t)]
    w_cols = pl.BlockSpec((width, ip), lambda i, s: (0, dm.np // ip))
    sc, sums, cot_all = pl.pallas_call(
        functools.partial(cotangent_kernel, dm),
        out_shape=[
            out(length, ip, dtype=BF16),
            out(nb, 2, q),
            out(length, width, dtype=BF16),
        ],
        grid_spec=grid(
            nb,
            [hbm] * n_t + [w_cols, fblock(ip), fsum(1)],
            [fblock(ip), fsum(2), fblock(width)],
            [vmem((length, width), BF16), pltpu.SemaphoreType.DMA((n_t,))],
        ),
        compiler_params=params,
        cost_estimate=pl.CostEstimate(
            flops=3_000_000_000, bytes_accessed=10_000_000, transcendentals=0
        ),
        name="branch_cotangent",
    )(scalars, *c_list, weights, scaled, squares)
    total = sums
    for k in range(1, n_t):
        total = total + across(sums, k)
    branch = pl.pallas_call(
        functools.partial(branch_kernel, dm),
        out_shape=[out(chunk_rows // q, q, width, dtype=BF16)] * n_t,
        grid_spec=grid(
            nb,
            [w_cols, fblock(ip)],
            [hbm] * n_t,
            [vmem((2, q, width), BF16), pltpu.SemaphoreType.DMA((2,))],
        ),
        compiler_params=params,
        cost_estimate=pl.CostEstimate(
            flops=3_000_000_000, bytes_accessed=10_000_000, transcendentals=0
        ),
        name="branch_output",
    )(scalars, weights, scaled)
    root = lax.rsqrt(total[:, 0] / (inner * n_t) + EPS)
    pull = root * root * root * (total[:, 1] / (inner * n_t))
    rk = jnp.stack([root, pull], axis=1)
    branch_sum = branch[0].astype(F32)
    for k in range(1, n_t):
        branch_sum = branch_sum + across(branch[k], k).astype(F32)
    own_root = lax.dynamic_slice_in_dim(root.reshape(length), me_t * chunk_rows, chunk_rows)
    block_output = block_input + own_root[:, None] * branch_sum.reshape(chunk_rows, width)

    def bblock(cols):
        return pl.BlockSpec((q, cols), lambda i, s: (nb - 1 - i, 0))

    dgate, dscan, lanes, gate_rows, own_early, *early = pl.pallas_call(
        functools.partial(gate_kernel, dm),
        out_shape=[
            out(length, ip, dtype=BF16),
            out(length, ip),
            out(16, ip),
            out(8, width),
            out(2 * part_rows, 2 * ip),
        ]
        + [out(2 * part_rows, 2 * ip, dtype=BF16)] * (n_hi - 1),
        grid_spec=grid(
            nb,
            [
                const(width, ip),
                fsum(2),
                const(8, ip),
                fblock(ip),
                fblock(ip),
                fblock(ip),
                fblock(ip),
                fblock(width),
                fblock(width),
            ],
            [fblock(ip), fblock(ip), const(16, ip), const(8, width)]
            + [const(2 * part_rows, 2 * ip)] * n_hi,
            [vmem((width, 2 * ip), F32), vmem((q, ip), BF16)],
        ),
        compiler_params=params,
        cost_estimate=pl.CostEstimate(
            flops=6_000_000_000, bytes_accessed=20_000_000, transcendentals=0
        ),
        name="gate_backward",
    )(scalars, weights, rk, per_lane, gate, conved, scan, sc, normed_all, cot_all)
    early = [along(v, k + 1) for k, v in enumerate(early)]

    proj_cot, taps, head_sums, *nc = pl.pallas_call(
        functools.partial(backward_kernel, dm),
        out_shape=[out(length, vs + LANES, dtype=BF16), out(40, vs), out(16, LANES)]
        + [out(k, q, width, dtype=BF16) for k in dm.group_sizes],
        grid_spec=grid(
            nb,
            [
                hbm,
                pl.BlockSpec((16, q), lambda i, s: (0, nb - 1 - i)),
                const(8, vs),
                const(8, LANES),
                const(8, ip),
                bblock(ip),
                bblock(ip),
                bblock(vs),
                bblock(vs),
                bblock(ip),
                bblock(LANES),
                pl.BlockSpec((state, ip), lambda i, s: (nb - 1 - i, 0)),
            ],
            [bblock(vs + LANES), const(40, vs), const(16, LANES)] + [hbm] * len(dm.group_sizes),
            [
                vmem((width, dm.wc), BF16),
                vmem((state, ip), F32),
                vmem((q + 8, vs), F32),
                vmem((q, q), BF16),
                vmem((q, q), F32),
                vmem((q, q), F32),
                vmem((q, ip), F32),
                vmem((q, ip), F32),
                vmem((8, ip), F32),
                vmem((q, ip), F32),
                vmem((q, ip), F32),
                vmem((2, q, width), BF16),
                pltpu.SemaphoreType.DMA,
                pltpu.SemaphoreType.DMA((2,)),
            ],
        ),
        compiler_params=params,
        cost_estimate=pl.CostEstimate(
            flops=40_000_000_000, bytes_accessed=30_000_000, transcendentals=0
        ),
        name="block_backward",
    )(scalars, weights, rows, conv, per_head, per_lane, dgate, dscan, value, conved, scan, steps_raw, held)

    def slot_of_piece(k, at):
        return pl.BlockSpec(
            (None, part, width), lambda i: (at, jnp.clip(i - k * steps, 0, steps - 1), 0)
        )

    if dm.halves == 2:
        from_x, from_y, stay = across(nc[0], 1), across(nc[1], 2), nc[2]
        pass_y = (stay[1].astype(F32) + from_x[1].astype(F32)).astype(BF16)
        pass_x = (stay[3].astype(F32) + from_y[1].astype(F32)).astype(BF16)
        got_y, got_x = across(pass_y, 2), across(pass_x, 1)
        sets = (3, 3)
        terms = [stay, from_x, got_y, stay, from_y, got_x]
        specs = [slot_of_piece(0, 0), slot_of_piece(0, 0), turn(0)]
        specs += [slot_of_piece(1, 2), slot_of_piece(1, 0), turn(1)]
    else:
        sets = (n_t,)
        terms = [nc[0]] + [across(nc[k], k) for k in range(1, n_t)]
        terms = [v.reshape(chunk_rows, width) for v in terms]
        specs = [turn(0)] * n_t
    in_turn = pl.BlockSpec((part, width), lambda i: (i, 0))
    input_grad = pl.pallas_call(
        functools.partial(input_kernel, sets, steps),
        out_shape=out(chunk_rows, width),
        grid=(len(sets) * steps,),
        in_specs=[in_turn, in_turn, pl.BlockSpec((1, width), lambda i: (0, 0))] + specs,
        out_specs=in_turn,
        compiler_params=params,
        name="input_gradient",
    )(block_input, out_cotangent, gain, *terms)

    late = vs + LANES
    k_rows = 2 * q
    mine, theirs, small = pl.pallas_call(
        functools.partial(joined_kernel, dm),
        out_shape=[
            out(n_hi, part_rows, late),
            out(n_hi, part_rows, late, dtype=BF16),
            out(dm.small_rows, LANES),
        ],
        grid_spec=grid(
            length // k_rows,
            [
                pl.BlockSpec((k_rows, width), lambda i, s: (i, 0)),
                pl.BlockSpec((k_rows, late), lambda i, s: (i, 0)),
                const(width, dm.wc),
                const(40, vs),
                const(16, ip),
                const(16, LANES),
                const(8, width),
            ],
            [
                const(n_hi, part_rows, late),
                const(n_hi, part_rows, late),
                const(dm.small_rows, LANES),
            ],
            [vmem((width, late), F32)],
        ),
        compiler_params=params,
        cost_estimate=pl.CostEstimate(
            flops=6_000_000_000, bytes_accessed=20_000_000, transcendentals=0
        ),
        name="weight_gradients",
    )(scalars, normed_all, proj_cot, weights, taps, lanes, head_sums, gate_rows)

    theirs = partner(theirs)
    by_hi = pl.BlockSpec((None, part_rows, late), lambda i, s: (s[dm.at_hi + i], 0, 0))
    own, *others = pl.pallas_call(
        pair_kernel,
        out_shape=[out(part_rows, late)] + [out(part_rows, late, dtype=BF16)] * (n_hi - 1),
        grid_spec=grid(n_hi, [by_hi, by_hi], [const(part_rows, late)] * n_hi, []),
        compiler_params=params,
        name="core_sum",
    )(scalars, mine, theirs)
    others = [along(v, k + 1) for k, v in enumerate(others)]
    early_spec = const(2 * part_rows, 2 * ip)
    mine, theirs = pl.pallas_call(
        functools.partial(early_kernel, dm),
        out_shape=[out(part_rows, 2 * ip), out(part_rows, 2 * ip, dtype=BF16)],
        grid_spec=grid(
            1,
            [early_spec] * n_hi,
            [const(part_rows, 2 * ip)] * 2,
            [vmem((2 * part_rows, 2 * ip), F32)],
        ),
        compiler_params=params,
        name="early_sum",
    )(scalars, own_early, *early)
    theirs = partner(theirs)
    gate_proj_grad, value_proj_grad, step_proj_grad, outp_t, shared = pl.pallas_call(
        functools.partial(grads_kernel, dm),
        out_shape=[
            out(part_rows, inner),
            out(part_rows, inner),
            out(part_rows, heads),
            out(part_rows, inner),
            out(part_rows, 2 * state),
        ],
        name="gradient_sum",
    )(own, mine, theirs, *others)
    output_proj_grad = outp_t.T

    small = all_sum(small, "dp", n_dp)
    common = all_sum(small[dm.local_rows :], "tensor", n_t)
    shared_b = shared.astype(BF16)
    shared_proj_grad = shared
    for k in range(1, n_t):
        shared_proj_grad = shared_proj_grad + across(shared_b, k).astype(F32)

    flat = small[: dm.local_rows].reshape(-1)
    taps = flat[: 5 * ip].reshape(5, ip)
    lanes = flat[5 * ip : 7 * ip].reshape(2, ip)
    head_sums = flat[7 * ip : 7 * ip + 2 * LANES].reshape(2, LANES)
    flat = common.reshape(-1)
    shared_taps = flat[: 10 * state].reshape(5, 2 * state)
    norm_gain_grad = flat[10 * state : 10 * state + width] / norm_gain
    return (
        block_output,
        input_grad,
        norm_gain_grad,
        gate_proj_grad,
        value_proj_grad,
        shared_proj_grad,
        step_proj_grad,
        taps[:4, :inner],
        taps[4, :inner],
        shared_taps[:4],
        shared_taps[4],
        head_sums[0, :heads],
        head_sums[1, :heads] * rate,
        jnp.sum(lanes[1, :inner].reshape(heads, hd), axis=1),
        lanes[0, :inner],
        output_proj_grad,
    )


def solution(mesh):
    n_dp, n_t = mesh.shape["dp"], mesh.shape["tensor"]
    both = ("dp", "tensor")
    return jax.shard_map(
        functools.partial(body, n_dp, n_t),
        mesh=mesh,
        in_specs=(
            P(both, None),
            P("dp", None),
            P(),
            P("dp", "tensor"),
            P("dp", "tensor"),
            P("dp", None),
            P("dp", "tensor"),
            P(None, "tensor"),
            P("tensor"),
            P(),
            P(),
            P("tensor"),
            P("tensor"),
            P("tensor"),
            P("tensor"),
            P("tensor", "dp"),
            P(both, None),
        ),
        out_specs=(
            P(both, None),
            P(both, None),
            P(),
            P("dp", "tensor"),
            P("dp", "tensor"),
            P("dp", None),
            P("dp", "tensor"),
            P(None, "tensor"),
            P("tensor"),
            P(),
            P(),
            P("tensor"),
            P("tensor"),
            P("tensor"),
            P("tensor"),
            P("tensor", "dp"),
        ),
        check_vma=False,
    )
```

profile of v0, /device:TPU:0, one launch (start us, length us, event | category | flops | bytes accessed | tf_op | source)
XLA Modules:
  0.0 276.1 jit_solution(9935558570993923209)
XLA Ops:
  0.7 1.9 pack_weights.1.refs_0_
  2.6 3.1 %collective-permute-start.3 = (bf16[96,1536]{1,0:T(8,128)(2,1)}, bf16[96,1536]{1,0:T(8,128)(2,1)S(1)}, u32[]{:S(2)}, u32[]{:S(2)}) collective-permute-start(bf16[96,1536]{1,0:T(8,128)(2,1)} %pack_weights.1.refs_0_), channel_id=1, source_target_pairs={{0,8},{4,12},{8,16},{12,20},{16,24},{20,28},{24,0},{28,4},{1,9},{5... | collective-permute-start | bytes 884744 | tf_op jit(solution)/shard_map/ppermute | solution.py:668
  5.7 2.6 collective-permute-start.4
  8.3 1.3 collective-permute-start.5
  9.6 1.3 reshape.184.gain_ref
  10.9 3.9 %normalize.1 = (bf16[256,768]{1,0:T(8,128)(2,1)}, bf16[256,768]{1,0:T(8,128)(2,1)}) custom-call(f32[512,768]{1,0:T(8,128)} %x_ref.3, f32[1,768]{1,0:T(1,128)} %reshape.184.gain_ref), custom_call_target="tpu_custom_call" | custom-call | tf_op jit(solution)/shard_map/normalize/pallas_call | solution.py:692
  14.8 1.5 collective-permute-start.10
  16.3 1.5 collective-permute-start.13
  20.4 7.3 %collective-permute-done.4.refs_2_ = bf16[96,1536]{1,0:T(8,128)(2,1)S(1)} collective-permute-done((bf16[96,1536]{1,0:T(8,128)(2,1)}, bf16[96,1536]{1,0:T(8,128)(2,1)S(1)}, u32[]{:S(2)}, u32[]{:S(2)}) %collective-permute-start.4) | collective-permute-done | bytes 294944 | tf_op jit(solution)/shard_map/ppermute | solution.py:668
  27.7 1.5 collective-permute-start.12
  30.0 1.5 collective-permute-start.15
  33.0 1.4 concatenate.38.refs_16_.refs_1_
  35.5 4.4 %collective-permute-done.12.refs_12_ = bf16[256,768]{1,0:T(8,128)(2,1)S(1)} collective-permute-done((bf16[256,768]{1,0:T(8,128)(2,1)}, bf16[256,768]{1,0:T(8,128)(2,1)S(1)}, u32[]{:S(2)}, u32[]{:S(2)}) %collective-permute-start.12) | collective-permute-done | bytes 393248 | tf_op jit(solution)/shard_map/ppermute | solution.py:665
  41.8 1.6 collective-permute-start
  43.4 1.6 collective-permute-start.1
  45.5 2.9 %collective-permute-done.14.refs_14_ = bf16[256,768]{1,0:T(8,128)(2,1)} collective-permute-done((bf16[256,768]{1,0:T(8,128)(2,1)S(1)}, bf16[256,768]{1,0:T(8,128)(2,1)}, u32[]{:S(2)}, u32[]{:S(2)}) %collective-permute-start.14) | collective-permute-done | bytes 393248 | tf_op jit(solution)/shard_map/ppermute | solution.py:665
  48.5 25.2 %block_forward.1 = (f32[2048,384]{1,0:T(8,128)}, f32[2048,640]{1,0:T(8,128)}, f32[2048,640]{1,0:T(8,128)}, f32[2048,384]{1,0:T(8,128)}, f32[2048,128]{1,0:T(8,12...) custom-call(s32[57]{0:T(128)} %concatenate.35.scalars, ...), custom_call_target="tpu_custom_call" | custom-call | flops 30000001024 | bytes 30000000 | tf_op jit(solution)/shard_map/block_forward/pallas_call | solution.py:796
  73.7 7.3 %collective-permute-done.1.refs_2_ = bf16[512,768]{1,0:T(8,128)(2,1)S(1)} collective-permute-done((bf16[512,768]{1,0:T(8,128)(2,1)S(1)}, bf16[512,768]{1,0:T(8,128)(2,1)S(1)}, u32[]{:S(2)}, u32[]{:S(2)}) %collective-permute-start.1) | collective-permute-done | bytes 786464 | tf_op jit(solution)/shard_map/ppermute | solution.py:665
  81.0 0.9 copy-done.28
  82.1 10.3 %branch_cotangent.1 = (bf16[2048,384]{1,0:T(8,128)(2,1)}, f32[8,2,256]{2,1,0:T(2,128)}, bf16[2048,768]{1,0:T(8,128)(2,1)}) custom-call(s32[57]{0:T(128)} %concatenate.35.scalars, bf16[512,768]{1,0:T(8,128)(2,1)} %cot_ref.1, bf16[512,768]{1,0:T(8,128)(2,1)} %copy-done.27, bf16[512,768]{1,0:T(8,128)(2,1)} %copy-done.28, bf16[512,768]{1,0:T(8,128)(2,1)} %copy-done.29, ...), custom_call_target="tpu_custom_call" | custom-call | flops 3000000000 | bytes 10000000 | tf_op jit(solution)/shard_map/branch_cotangent/pallas_call | solution.py:852
  92.4 2.5 collective-permute-start.18
  96.0 1.4 collective-permute-done.18
  97.3 1.5 collective-permute-done.17
  100.7 16.0 %gate_backward.1 = (bf16[2048,384]{1,0:T(8,128)(2,1)}, f32[2048,384]{1,0:T(8,128)}, f32[16,384]{1,0:T(8,128)}, f32[8,768]{1,0:T(8,128)}, f32[192,768]{1,0:T(8,12...) custom-call(s32[57]{0:T(128)} %concatenate.35.scalars, ...), custom_call_target="tpu_custom_call" | custom-call | flops 6000000000 | bytes 20000000 | tf_op jit(solution)/shard_map/gate_backward/pallas_call | solution.py:901
  116.8 39.1 %block_backward.1 = (bf16[2048,768]{1,0:T(8,128)(2,1)}, f32[40,640]{1,0:T(8,128)}, f32[16,128]{1,0:T(8,128)}, bf16[2,256,768]{2,1,0:T(8,128)(2,1)}, bf16[2,256,7...) custom-call(s32[57]{0:T(128)} %concatenate.35.scalars, bf16[768,1536]{1,0:T(8,128)(2,1)} %get-tuple-element.65.refs_4_.w_ref.refs_0_, ...), custom_call_target="tpu_custom_call" | custom-call | flops 40000000000 | bytes 30000000 | tf_op jit(solution)/shard_map/block_backward/pallas_call | solution.py:936
  155.9 9.1 %weight_gradients.1 = (f32[4,96,768]{2,1,0:T(8,128)}, bf16[4,96,768]{2,1,0:T(8,128)(2,1)}, f32[40,128]{1,0:T(8,128)}) custom-call(s32[57]{0:T(128)} %concatenate.35.scalars, bf16[2048,768]{1,0:T(8,128)(2,1)} %get-tuple-element.77.refs_7_.nm_ref, bf16[2048,768]{1,0:T(8,128)(2,1)} %get-tuple-element.87.pj_ref, ...), custom_call_target="tpu_custom_call" | custom-call | flops 6000000000 | bytes 20000000 | tf_op jit(solution)/shard_map/weight_gradients/pallas_call | solution.py:1013
  164.9 1.4 collective-permute-done.26
  166.3 0.7 add.205
  167.0 4.2 %collective-permute-start.27 = (f32[40,128]{1,0:T(8,128)S(1)}, f32[40,128]{1,0:T(8,128)S(1)}, u32[]{:S(2)}, u32[]{:S(2)}) collective-permute-start(f32[40,128]{1,0:T(8,128)S(1)} %add.205), channel_id=1, source_target_pairs={{0,8},{4,12},{8,0},{12,4},{16,24},{20,28},{24,16},{28,20},{1,9},{5... | collective-permute-start | bytes 61448 | tf_op jit(solution)/shard_map/ppermute | solution.py:615
  171.2 1.8 collective-permute-done.27
  173.0 3.3 %collective-permute-start.28 = (f32[40,128]{1,0:T(8,128)S(1)}, f32[40,128]{1,0:T(8,128)S(1)}, u32[]{:S(2)}, u32[]{:S(2)}) collective-permute-start(f32[40,128]{1,0:T(8,128)S(1)} %add.206), channel_id=1, source_target_pairs={{0,16},{4,20},{8,24},{12,28},{16,0},{20,4},{24,8},{28,12},{1,17},{... | collective-permute-start | bytes 61448 | tf_op jit(solution)/shard_map/ppermute | solution.py:615
  176.2 1.8 collective-permute-done.28
  178.6 7.9 %branch_output.1 = (bf16[2,256,768]{2,1,0:T(8,128)(2,1)}, bf16[2,256,768]{2,1,0:T(8,128)(2,1)}, bf16[2,256,768]{2,1,0:T(8,128)(2,1)}, bf16[2,256,768]{2,1,0:T(8,128)(2,1)}) custom-call(s32[57]{0:T(128)} %concatenate.35.scalars, bf16[768,1536]{1,0:T(8,128)(2,1)} %get-tuple-element.65.refs_4_.w_ref.refs_0_, bf16[2048,384]{1,0:T(8,128)(2,1)} %get-tuple-element.66.refs_5_.sg_ref), custom_call_target="tpu_custom_call" | custom-call | flops 3000000000 | bytes 10000000 | tf_op jit(solution)/shard_map/branch_output/pallas_call | solution.py:874
  186.6 2.1 collective-permute-start.32
  188.6 2.9 %collective-permute-start.33 = (bf16[192,768]{1,0:T(8,128)(2,1)S(1)}, bf16[192,768]{1,0:T(8,128)(2,1)S(1)}, u32[]{:S(2)}, u32[]{:S(2)}) collective-permute-start(bf16[192,768]{1,0:T(8,128)(2,1)S(1)} %copy-done.36), channel_id=1, source_target_pairs={{0,16},{4,20},{8,24},{12,28},{16,0},{20,4},{24,8},{28,12},{1,17},{... | collective-permute-start | bytes 884744 | tf_op jit(solution)/shard_map/ppermute | solution.py:668
  191.6 0.9 collective-permute-start.34
  192.5 1.6 collective-permute-start.30
  196.0 2.9 %collective-permute-done.32.refs_0_ = bf16[192,768]{1,0:T(8,128)(2,1)S(1)} collective-permute-done((bf16[192,768]{1,0:T(8,128)(2,1)S(1)}, bf16[192,768]{1,0:T(8,128)(2,1)S(1)}, u32[]{:S(2)}, u32[]{:S(2)}) %collective-permute-start.32) | collective-permute-done | bytes 294944 | tf_op jit(solution)/shard_map/ppermute | solution.py:668
  198.9 2.5 collective-permute-start.21
  201.4 7.1 %collective-permute-done.33.refs_1_ = bf16[192,768]{1,0:T(8,128)(2,1)S(1)} collective-permute-done((bf16[192,768]{1,0:T(8,128)(2,1)S(1)}, bf16[192,768]{1,0:T(8,128)(2,1)S(1)}, u32[]{:S(2)}, u32[]{:S(2)}) %collective-permute-start.33) | collective-permute-done | bytes 294944 | tf_op jit(solution)/shard_map/ppermute | solution.py:668
  208.5 1.6 collective-permute-start.20
  210.1 1.5 collective-permute-start.19
  211.6 3.1 %early_sum.1 = (f32[96,768]{1,0:T(8,128)}, bf16[96,768]{1,0:T(8,128)(2,1)}) custom-call(s32[57]{0:T(128)} %concatenate.35.scalars, f32[192,768]{1,0:T(8,128)} %get-tuple-element.96.own_ref, bf16[192,768]{1,0:T(8,128)(2,1)} %copy-done.12, bf16[192,768]{1,0:T(8,128)(2,1)} %copy-done.13, bf16[192,768]{1,0:T(8,128)(2,1)} %copy-done.14), custom_call_target="tpu_custom_call" | custom-call | tf_op jit(solution)/shard_map/early_sum/pallas_call | solution.py:1056
  214.8 0.8 copy-done.7
  215.5 4.0 %core_sum.1 = (f32[96,768]{1,0:T(8,128)}, bf16[96,768]{1,0:T(8,128)(2,1)}, bf16[96,768]{1,0:T(8,128)(2,1)}, bf16[96,768]{1,0:T(8,128)(2,1)}) custom-call(s32[57]{0:T(128)} %concatenate.35.scalars, f32[4,96,768]{2,1,0:T(8,128)} %get-tuple-element.93.mine_ref, bf16[4,96,768]{2,1,0:T(8,128)(2,1)} %copy-done.7), custom_call_target="tpu_custom_call" | custom-call | tf_op jit(solution)/shard_map/core_sum/pallas_call | solution.py:1047
  219.5 5.2 %collective-permute-start.36 = (bf16[96,768]{1,0:T(8,128)(2,1)}, bf16[96,768]{1,0:T(8,128)(2,1)S(1)}, u32[]{:S(2)}, u32[]{:S(2)}) collective-permute-start(bf16[96,768]{1,0:T(8,128)(2,1)} %get-tuple-element.102), channel_id=1, source_target_pairs={{0,8},{4,12},{8,16},{12,20},{16,24},{20,28},{24,0},{28,4},{1,9},{5... | collective-permute-start | bytes 442376 | tf_op jit(solution)/shard_map/ppermute | solution.py:668
  225.3 3.0 %collective-permute-start.37 = (bf16[96,768]{1,0:T(8,128)(2,1)}, bf16[96,768]{1,0:T(8,128)(2,1)S(1)}, u32[]{:S(2)}, u32[]{:S(2)}) collective-permute-start(bf16[96,768]{1,0:T(8,128)(2,1)} %get-tuple-element.103), channel_id=1, source_target_pairs={{0,16},{4,20},{8,24},{12,28},{16,0},{20,4},{24,8},{28,12},{1,17},{... | collective-permute-start | bytes 442376 | tf_op jit(solution)/shard_map/ppermute | solution.py:668
  228.3 3.9 %collective-permute-done.36.refs_0_ = bf16[96,768]{1,0:T(8,128)(2,1)S(1)} collective-permute-done((bf16[96,768]{1,0:T(8,128)(2,1)}, bf16[96,768]{1,0:T(8,128)(2,1)S(1)}, u32[]{:S(2)}, u32[]{:S(2)}) %collective-permute-start.36) | collective-permute-done | bytes 147488 | tf_op jit(solution)/shard_map/ppermute | solution.py:668
  232.2 1.9 collective-permute-start.38
  235.2 2.4 collective-permute-done.37.refs_1_
  241.1 2.1 gradient_sum.1
  243.1 0.9 convert_element_type.98
  244.0 1.5 copy.45
  245.5 1.9 collective-permute-start.41
  247.8 1.2 collective-permute-start.39
  249.0 1.6 convert_add_fusion
  250.6 8.3 %collective-permute-done.22.refs_1_ = bf16[2,256,768]{2,1,0:T(8,128)(2,1)S(1)} collective-permute-done((bf16[2,256,768]{2,1,0:T(8,128)(2,1)}, bf16[2,256,768]{2,1,0:T(8,128)(2,1)S(1)}, u32[]{:S(2)}, u32[]{:S(2)}) %collective-permute-start.22) | collective-permute-done | bytes 786464 | tf_op jit(solution)/shard_map/ppermute | solution.py:665
  258.9 1.1 collective-permute-done.24.refs_4_
  259.9 1.2 fusion.2
  261.2 1.4 collective-permute-start.25
  262.6 1.4 fusion
  264.7 4.9 %collective-permute-done.23.refs_2_ = bf16[256,768]{1,0:T(8,128)(2,1)S(1)} collective-permute-done((bf16[256,768]{1,0:T(8,128)(2,1)S(1)}, bf16[256,768]{1,0:T(8,128)(2,1)S(1)}, u32[]{:S(2)}, u32[]{:S(2)}) %collective-permute-start.23) | collective-permute-done | bytes 393248 | tf_op jit(solution)/shard_map/ppermute | solution.py:665
  270.4 0.8 copy-done.9
  271.1 5.0 %input_gradient.1 = f32[512,768]{1,0:T(8,128)} custom-call(f32[512,768]{1,0:T(8,128)} %x_ref.3, bf16[512,768]{1,0:T(8,128)(2,1)} %cot_ref.1, f32[1,768]{1,0:T(1,128)} %reshape.184.gain_ref, bf16[4,256,768]{2,1,0:T(8,128)(2,1)} %get-tuple-element.84.refs_0_.refs_3_, bf16[2,256,768]{2,1,0:T(8,128)(2,1)} %copy-done.4, bf16[256,768]{1,0:T(8,128)(2,1)} %copy-done.8, ...), custom_call_target="tpu_custom_call" | custom-call | tf_op jit(solution)/shard_map/input_gradient/pallas_call | solution.py:1001
  (179 shorter events, 21.2 us)
Async XLA Ops:
  0.6 30.9 %copy-start.1 = (s32[4,2]{1,0:T(4,128)S(1)}, s32[4,2]{1,0:T(4,128)}, u32[]{:S(2)}) copy-start(s32[4,2]{1,0:T(4,128)} %constant.108.clone) | copy-start | bytes 100
  0.7 31.5 %copy-start = (s32[4,2]{1,0:T(4,128)S(1)}, s32[4,2]{1,0:T(4,128)}, u32[]{:S(2)}) copy-start(s32[4,2]{1,0:T(4,128)} %constant.109.clone) | copy-start | bytes 100
  0.7 17.6 %copy-start.18 = (s32[1,2048]{1,0:T(1,128)S(1)}, s32[1,2048]{1,0:T(1,128)}, u32[]{:S(2)}) copy-start(s32[1,2048]{1,0:T(1,128)} %param.20) | copy-start | bytes 24580
  0.7 19.0 %copy-start.41 = (f32[6]{0:T(128)S(1)}, f32[6]{0:T(128)}, u32[]{:S(2)}) copy-start(f32[6]{0:T(128)} %param.31) | copy-start | bytes 76
  0.7 19.1 %copy-start.26 = (f32[6]{0:T(128)S(1)}, f32[6]{0:T(128)}, u32[]{:S(2)}) copy-start(f32[6]{0:T(128)} %param.30) | copy-start | bytes 76
  2.6 26.7 %copy-start.11 = (bf16[96,1536]{1,0:T(8,128)(2,1)S(1)}, bf16[96,1536]{1,0:T(8,128)(2,1)}, u32[]{:S(2)}) copy-start(bf16[96,1536]{1,0:T(8,128)(2,1)} %pack_weights.1.refs_0_) | copy-start | bytes 884740
  2.6 30.2 %copy-start.22 = (f32[384]{0:T(512)S(1)}, f32[384]{0:T(512)}, u32[]{:S(2)}) copy-start(f32[384]{0:T(512)} %param.27) | copy-start | bytes 4612
  2.6 30.3 %copy-start.23 = (f32[384]{0:T(512)S(1)}, f32[384]{0:T(512)}, u32[]{:S(2)}) copy-start(f32[384]{0:T(512)} %param.33) | copy-start | bytes 4612
  2.6 30.3 %copy-start.25 = (f32[6]{0:T(128)S(1)}, f32[6]{0:T(128)}, u32[]{:S(2)}) copy-start(f32[6]{0:T(128)} %param.32) | copy-start | bytes 76
  2.6 17.2 %collective-permute-start.3 = (bf16[96,1536]{1,0:T(8,128)(2,1)}, bf16[96,1536]{1,0:T(8,128)(2,1)S(1)}, u32[]{:S(2)}, u32[]{:S(2)}) collective-permute-start(bf16[96,1536]{1,0:T(8,128)(2,1)} %pack_weights.1.refs_0_), channel_id=1, source_target_pairs={{0,8},{4,12},{8,16},{12,20},{16,24},{20,28},{24,0},{28,4},{1,9},{5... | collective-permute-start | bytes 884744 | tf_op jit(solution)/shard_map/ppermute | solution.py:668
  5.7 22.0 %collective-permute-start.4 = (bf16[96,1536]{1,0:T(8,128)(2,1)}, bf16[96,1536]{1,0:T(8,128)(2,1)S(1)}, u32[]{:S(2)}, u32[]{:S(2)}) collective-permute-start(bf16[96,1536]{1,0:T(8,128)(2,1)} %pack_weights.1.refs_0_), channel_id=1, source_target_pairs={{0,16},{4,20},{8,24},{12,28},{16,0},{20,4},{24,8},{28,12},{1,17},{... | collective-permute-start | bytes 884744 | tf_op jit(solution)/shard_map/ppermute | solution.py:668
  8.3 21.0 %collective-permute-start.5 = (bf16[96,1536]{1,0:T(8,128)(2,1)}, bf16[96,1536]{1,0:T(8,128)(2,1)S(1)}, u32[]{:S(2)}, u32[]{:S(2)}) collective-permute-start(bf16[96,1536]{1,0:T(8,128)(2,1)} %pack_weights.1.refs_0_), channel_id=1, source_target_pairs={{0,24},{4,28},{8,0},{12,4},{16,8},{20,12},{24,16},{28,20},{1,25},{... | collective-permute-start | bytes 884744 | tf_op jit(solution)/shard_map/ppermute | solution.py:668
  10.9 30.3 %copy-start.20 = (f32[4,384]{1,0:T(4,128)S(1)}, f32[4,384]{1,0:T(4,128)}, u32[]{:S(2)}) copy-start(f32[4,384]{1,0:T(4,128)} %param.26) | copy-start | bytes 18436
  10.9 30.3 %copy-start.21 = (f32[4,256]{1,0:T(4,128)S(1)}, f32[4,256]{1,0:T(4,128)}, u32[]{:S(2)}) copy-start(f32[4,256]{1,0:T(4,128)} %param.28) | copy-start | bytes 12292
  10.9 30.3 %copy-start.24 = (f32[256]{0:T(256)S(1)}, f32[256]{0:T(256)}, u32[]{:S(2)}) copy-start(f32[256]{0:T(256)} %param.29) | copy-start | bytes 3076
  10.9 30.9 %copy-start.6 = (bf16[512,768]{1,0:T(8,128)(2,1)S(1)}, bf16[512,768]{1,0:T(8,128)(2,1)}, u32[]{:S(2)}) copy-start(bf16[512,768]{1,0:T(8,128)(2,1)} %cot_ref.1) | copy-start | bytes 2359300
  14.8 14.7 %collective-permute-start.10 = (bf16[256,768]{1,0:T(8,128)(2,1)}, bf16[256,768]{1,0:T(8,128)(2,1)S(1)}, u32[]{:S(2)}, u32[]{:S(2)}) collective-permute-start(bf16[256,768]{1,0:T(8,128)(2,1)} %get-tuple-element.63.refs_8_), channel_id=1, source_target_pairs={{0,1},{1,0},{2,3},{3,2},{4,5},{5,4},{6,7},{7,6},{8,9},{9,8},{10,11... | collective-permute-start | bytes 1179656 | tf_op jit(solution)/shard_map/ppermute | solution.py:665
  16.3 13.7 %collective-permute-start.13 = (bf16[256,768]{1,0:T(8,128)(2,1)}, bf16[256,768]{1,0:T(8,128)(2,1)}, u32[]{:S(2)}, u32[]{:S(2)}) collective-permute-start(bf16[256,768]{1,0:T(8,128)(2,1)} %get-tuple-element.64.refs_9_), channel_id=1, source_target_pairs={{0,2},{1,3},{2,0},{3,1},{4,6},{5,7},{6,4},{7,5},{8,10},{9,11},{10,... | collective-permute-start | bytes 1179656 | tf_op jit(solution)/shard_map/ppermute | solution.py:665
  19.8 23.6 %copy-start.33 = (bf16[96,1536]{1,0:T(8,128)(2,1)}, bf16[96,1536]{1,0:T(8,128)(2,1)S(1)}, u32[]{:S(2)}) copy-start(bf16[96,1536]{1,0:T(8,128)(2,1)S(1)} %collective-permute-done.3.refs_1_) | copy-start | bytes 884740
  19.8 15.2 %collective-permute-start.11 = (bf16[256,768]{1,0:T(8,128)(2,1)}, bf16[256,768]{1,0:T(8,128)(2,1)S(1)}, u32[]{:S(2)}, u32[]{:S(2)}) collective-permute-start(bf16[256,768]{1,0:T(8,128)(2,1)} %get-tuple-element.64.refs_9_), channel_id=1, source_target_pairs={{0,1},{1,0},{2,3},{3,2},{4,5},{5,4},{6,7},{7,6},{8,9},{9,8},{10,11... | collective-permute-start | bytes 1179656 | tf_op jit(solution)/shard_map/ppermute | solution.py:665
  27.7 17.3 %copy-start.34 = (bf16[96,1536]{1,0:T(8,128)(2,1)}, bf16[96,1536]{1,0:T(8,128)(2,1)S(1)}, u32[]{:S(2)}) copy-start(bf16[96,1536]{1,0:T(8,128)(2,1)S(1)} %collective-permute-done.4.refs_2_) | copy-start | bytes 884740
  27.7 12.2 %collective-permute-start.12 = (bf16[256,768]{1,0:T(8,128)(2,1)}, bf16[256,768]{1,0:T(8,128)(2,1)S(1)}, u32[]{:S(2)}, u32[]{:S(2)}) collective-permute-start(bf16[256,768]{1,0:T(8,128)(2,1)} %get-tuple-element.63.refs_8_), channel_id=1, source_target_pairs={{0,2},{1,3},{2,0},{3,1},{4,6},{5,7},{6,4},{7,5},{8,10},{9,11},{10,... | collective-permute-start | bytes 1179656 | tf_op jit(solution)/shard_map/ppermute | solution.py:665
  29.3 15.7 %copy-start.35 = (bf16[96,1536]{1,0:T(8,128)(2,1)}, bf16[96,1536]{1,0:T(8,128)(2,1)S(1)}, u32[]{:S(2)}) copy-start(bf16[96,1536]{1,0:T(8,128)(2,1)S(1)} %collective-permute-done.5.refs_3_) | copy-start | bytes 884740
  29.3 5.7 %collective-permute-start.6 = (bf16[96,1536]{1,0:T(8,128)(2,1)S(1)}, bf16[96,1536]{1,0:T(8,128)(2,1)}, u32[]{:S(2)}, u32[]{:S(2)}) collective-permute-start(bf16[96,1536]{1,0:T(8,128)(2,1)S(1)} %copy-done.11), channel_id=1, source_target_pairs={{0,4},{4,0},{8,12},{12,8},{16,20},{20,16},{24,28},{28,24},{1,5},{5... | collective-permute-start | bytes 884744 | tf_op jit(solution)/shard_map/ppermute | solution.py:671
  29.4 19.0 %copy-start.30 = (bf16[256,768]{1,0:T(8,128)(2,1)}, bf16[256,768]{1,0:T(8,128)(2,1)S(1)}, u32[]{:S(2)}) copy-start(bf16[256,768]{1,0:T(8,128)(2,1)S(1)} %collective-permute-done.10.refs_10_) | copy-start | bytes 1179652
  29.4 19.0 %collective-permute-start.14 = (bf16[256,768]{1,0:T(8,128)(2,1)S(1)}, bf16[256,768]{1,0:T(8,128)(2,1)}, u32[]{:S(2)}, u32[]{:S(2)}) collective-permute-start(bf16[256,768]{1,0:T(8,128)(2,1)S(1)} %collective-permute-done.10.refs_10_), channel_id=1, source_target_pairs={{0,2},{1,3},{2,0},{3,1},{4,6},{5,7},{6,4},{7,5},{8,10},{9,11},{10,... | collective-permute-start | bytes 1179656 | tf_op jit(solution)/shard_map/ppermute | solution.py:665
  30.0 18.5 %collective-permute-start.15 = (bf16[256,768]{1,0:T(8,128)(2,1)}, bf16[256,768]{1,0:T(8,128)(2,1)}, u32[]{:S(2)}, u32[]{:S(2)}) collective-permute-start(bf16[256,768]{1,0:T(8,128)(2,1)} %collective-permute-done.13.refs_13_), channel_id=1, source_target_pairs={{0,1},{1,0},{2,3},{3,2},{4,5},{5,4},{6,7},{7,6},{8,9},{9,8},{10,11... | collective-permute-start | bytes 1179656 | tf_op jit(solution)/shard_map/ppermute | solution.py:665
  35.0 6.8 %collective-permute-start.7 = (bf16[96,1536]{1,0:T(8,128)(2,1)S(1)}, bf16[96,1536]{1,0:T(8,128)(2,1)S(1)}, u32[]{:S(2)}, u32[]{:S(2)}) collective-permute-start(bf16[96,1536]{1,0:T(8,128)(2,1)S(1)} %collective-permute-done.3.refs_1_), channel_id=1, source_target_pairs={{0,4},{4,0},{8,12},{12,8},{16,20},{20,16},{24,28},{28,24},{1,5},{5... | collective-permute-start | bytes 884744 | tf_op jit(solution)/shard_map/ppermute | solution.py:671
  35.0 8.4 %collective-permute-start.8 = (bf16[96,1536]{1,0:T(8,128)(2,1)S(1)}, bf16[96,1536]{1,0:T(8,128)(2,1)S(1)}, u32[]{:S(2)}, u32[]{:S(2)}) collective-permute-start(bf16[96,1536]{1,0:T(8,128)(2,1)S(1)} %collective-permute-done.4.refs_2_), channel_id=1, source_target_pairs={{0,4},{4,0},{8,12},{12,8},{16,20},{20,16},{24,28},{28,24},{1,5},{5... | collective-permute-start | bytes 884744 | tf_op jit(solution)/shard_map/ppermute | solution.py:671
  39.9 5.1 %collective-permute-start.9 = (bf16[96,1536]{1,0:T(8,128)(2,1)S(1)}, bf16[96,1536]{1,0:T(8,128)(2,1)S(1)}, u32[]{:S(2)}, u32[]{:S(2)}) collective-permute-start(bf16[96,1536]{1,0:T(8,128)(2,1)S(1)} %collective-permute-done.5.refs_3_), channel_id=1, source_target_pairs={{0,4},{4,0},{8,12},{12,8},{16,20},{20,16},{24,28},{28,24},{1,5},{5... | collective-permute-start | bytes 884744 | tf_op jit(solution)/shard_map/ppermute | solution.py:671
  41.8 31.8 %collective-permute-start = (bf16[512,768]{1,0:T(8,128)(2,1)S(1)}, bf16[512,768]{1,0:T(8,128)(2,1)S(1)}, u32[]{:S(2)}, u32[]{:S(2)}) collective-permute-start(bf16[512,768]{1,0:T(8,128)(2,1)S(1)} %copy-done.6), channel_id=1, source_target_pairs={{0,1},{1,0},{2,3},{3,2},{4,5},{5,4},{6,7},{7,6},{8,9},{9,8},{10,11... | collective-permute-start | bytes 2359304 | tf_op jit(solution)/shard_map/ppermute | solution.py:665
  43.4 37.6 %collective-permute-start.1 = (bf16[512,768]{1,0:T(8,128)(2,1)S(1)}, bf16[512,768]{1,0:T(8,128)(2,1)S(1)}, u32[]{:S(2)}, u32[]{:S(2)}) collective-permute-start(bf16[512,768]{1,0:T(8,128)(2,1)S(1)} %copy-done.6), channel_id=1, source_target_pairs={{0,2},{1,3},{2,0},{3,1},{4,6},{5,7},{6,4},{7,5},{8,10},{9,11},{10,... | collective-permute-start | bytes 2359304 | tf_op jit(solution)/shard_map/ppermute | solution.py:665
  45.0 36.0 %collective-permute-start.2 = (bf16[512,768]{1,0:T(8,128)(2,1)S(1)}, bf16[512,768]{1,0:T(8,128)(2,1)S(1)}, u32[]{:S(2)}, u32[]{:S(2)}) collective-permute-start(bf16[512,768]{1,0:T(8,128)(2,1)S(1)} %copy-done.6), channel_id=1, source_target_pairs={{0,3},{1,2},{2,1},{3,0},{4,7},{5,6},{6,5},{7,4},{8,11},{9,10},{10,... | collective-permute-start | bytes 2359304 | tf_op jit(solution)/shard_map/ppermute | solution.py:665
  92.4 4.9 %collective-permute-start.18 = (f32[8,2,256]{2,1,0:T(2,128)}, f32[8,2,256]{2,1,0:T(2,128)S(1)}, u32[]{:S(2)}, u32[]{:S(2)}) collective-permute-start(f32[8,2,256]{2,1,0:T(2,128)} %get-tuple-element.68), channel_id=1, source_target_pairs={{0,3},{1,2},{2,1},{3,0},{4,7},{5,6},{6,5},{7,4},{8,11},{9,10},{10,... | collective-permute-start | bytes 49160 | tf_op jit(solution)/shard_map/ppermute | solution.py:665
  94.9 3.9 %collective-permute-start.17 = (f32[8,2,256]{2,1,0:T(2,128)}, f32[8,2,256]{2,1,0:T(2,128)S(1)}, u32[]{:S(2)}, u32[]{:S(2)}) collective-permute-start(f32[8,2,256]{2,1,0:T(2,128)} %get-tuple-element.68), channel_id=1, source_target_pairs={{0,2},{1,3},{2,0},{3,1},{4,6},{5,7},{6,4},{7,5},{8,10},{9,11},{10,... | collective-permute-start | bytes 49160 | tf_op jit(solution)/shard_map/ppermute | solution.py:665
  95.4 3.9 %collective-permute-start.16 = (f32[8,2,256]{2,1,0:T(2,128)}, f32[8,2,256]{2,1,0:T(2,128)S(1)}, u32[]{:S(2)}, u32[]{:S(2)}) collective-permute-start(f32[8,2,256]{2,1,0:T(2,128)} %get-tuple-element.68), channel_id=1, source_target_pairs={{0,1},{1,0},{2,3},{3,2},{4,5},{5,4},{6,7},{7,6},{8,9},{9,8},{10,11... | collective-permute-start | bytes 49160 | tf_op jit(solution)/shard_map/ppermute | solution.py:665
  164.9 1.4 collective-permute-start.26
  167.0 5.9 %collective-permute-start.27 = (f32[40,128]{1,0:T(8,128)S(1)}, f32[40,128]{1,0:T(8,128)S(1)}, u32[]{:S(2)}, u32[]{:S(2)}) collective-permute-start(f32[40,128]{1,0:T(8,128)S(1)} %add.205), channel_id=1, source_target_pairs={{0,8},{4,12},{8,0},{12,4},{16,24},{20,28},{24,16},{28,20},{1,9},{5... | collective-permute-start | bytes 61448 | tf_op jit(solution)/shard_map/ppermute | solution.py:615
  173.0 5.0 %collective-permute-start.28 = (f32[40,128]{1,0:T(8,128)S(1)}, f32[40,128]{1,0:T(8,128)S(1)}, u32[]{:S(2)}, u32[]{:S(2)}) collective-permute-start(f32[40,128]{1,0:T(8,128)S(1)} %add.206), channel_id=1, source_target_pairs={{0,16},{4,20},{8,24},{12,28},{16,0},{20,4},{24,8},{28,12},{1,17},{... | collective-permute-start | bytes 61448 | tf_op jit(solution)/shard_map/ppermute | solution.py:615
  176.2 38.5 %collective-permute-start.31 = (bf16[4,96,768]{2,1,0:T(8,128)(2,1)}, bf16[4,96,768]{2,1,0:T(8,128)(2,1)S(1)}, u32[]{:S(2)}, u32[]{:S(2)}) collective-permute-start(bf16[4,96,768]{2,1,0:T(8,128)(2,1)} %get-tuple-element.94), channel_id=1, source_target_pairs={{0,4},{4,0},{8,12},{12,8},{16,20},{20,16},{24,28},{28,24},{1,5},{5... | collective-permute-start | bytes 1769480 | tf_op jit(solution)/shard_map/ppermute | solution.py:671
  178.0 14.5 %collective-permute-start.29 = (f32[16,128]{1,0:T(8,128)S(1)}, f32[16,128]{1,0:T(8,128)S(1)}, u32[]{:S(2)}, u32[]{:S(2)}) collective-permute-start(f32[16,128]{1,0:T(8,128)S(1)} %slice.153), channel_id=1, source_target_pairs={{0,1},{1,0},{2,3},{3,2},{4,5},{5,4},{6,7},{7,6},{8,9},{9,8},{10,11... | collective-permute-start | bytes 24584 | tf_op jit(solution)/shard_map/ppermute | solution.py:615
  186.6 12.3 %collective-permute-start.32 = (bf16[192,768]{1,0:T(8,128)(2,1)S(1)}, bf16[192,768]{1,0:T(8,128)(2,1)S(1)}, u32[]{:S(2)}, u32[]{:S(2)}) collective-permute-start(bf16[192,768]{1,0:T(8,128)(2,1)S(1)} %copy-done.37), channel_id=1, source_target_pairs={{0,8},{4,12},{8,16},{12,20},{16,24},{20,28},{24,0},{28,4},{1,9},{5... | collective-permute-start | bytes 884744 | tf_op jit(solution)/shard_map/ppermute | solution.py:668
  188.6 19.9 %collective-permute-start.33 = (bf16[192,768]{1,0:T(8,128)(2,1)S(1)}, bf16[192,768]{1,0:T(8,128)(2,1)S(1)}, u32[]{:S(2)}, u32[]{:S(2)}) collective-permute-start(bf16[192,768]{1,0:T(8,128)(2,1)S(1)} %copy-done.36), channel_id=1, source_target_pairs={{0,16},{4,20},{8,24},{12,28},{16,0},{20,4},{24,8},{28,12},{1,17},{... | collective-permute-start | bytes 884744 | tf_op jit(solution)/shard_map/ppermute | solution.py:668
  191.6 18.5 %collective-permute-start.34 = (bf16[192,768]{1,0:T(8,128)(2,1)}, bf16[192,768]{1,0:T(8,128)(2,1)S(1)}, u32[]{:S(2)}, u32[]{:S(2)}) collective-permute-start(bf16[192,768]{1,0:T(8,128)(2,1)} %get-tuple-element.99), channel_id=1, source_target_pairs={{0,24},{4,28},{8,0},{12,4},{16,8},{20,12},{24,16},{28,20},{1,25},{... | collective-permute-start | bytes 884744 | tf_op jit(solution)/shard_map/ppermute | solution.py:668
  192.5 27.0 %collective-permute-start.30 = (f32[16,128]{1,0:T(8,128)S(1)}, f32[16,128]{1,0:T(8,128)S(1)}, u32[]{:S(2)}, u32[]{:S(2)}) collective-permute-start(f32[16,128]{1,0:T(8,128)S(1)} %slice_add_fusion), channel_id=1, source_target_pairs={{0,2},{1,3},{2,0},{3,1},{4,6},{5,7},{6,4},{7,5},{8,10},{9,11},{10,... | collective-permute-start | bytes 24584 | tf_op jit(solution)/shard_map/ppermute | solution.py:615
  198.9 12.7 %copy-start.12 = (bf16[192,768]{1,0:T(8,128)(2,1)}, bf16[192,768]{1,0:T(8,128)(2,1)S(1)}, u32[]{:S(2)}) copy-start(bf16[192,768]{1,0:T(8,128)(2,1)S(1)} %collective-permute-done.32.refs_0_) | copy-start | bytes 884740
  198.9 46.6 %collective-permute-start.21 = (bf16[2,256,768]{2,1,0:T(8,128)(2,1)}, bf16[2,256,768]{2,1,0:T(8,128)(2,1)S(1)}, u32[]{:S(2)}, u32[]{:S(2)}) collective-permute-start(bf16[2,256,768]{2,1,0:T(8,128)(2,1)} %get-tuple-element.72), channel_id=1, source_target_pairs={{0,3},{1,2},{2,1},{3,0},{4,7},{5,6},{6,5},{7,4},{8,11},{9,10},{10,... | collective-permute-start | bytes 2359304 | tf_op jit(solution)/shard_map/ppermute | solution.py:665
  208.5 38.8 %collective-permute-start.20 = (bf16[2,256,768]{2,1,0:T(8,128)(2,1)}, bf16[2,256,768]{2,1,0:T(8,128)(2,1)S(1)}, u32[]{:S(2)}, u32[]{:S(2)}) collective-permute-start(bf16[2,256,768]{2,1,0:T(8,128)(2,1)} %get-tuple-element.71), channel_id=1, source_target_pairs={{0,2},{1,3},{2,0},{3,1},{4,6},{5,7},{6,4},{7,5},{8,10},{9,11},{10,... | collective-permute-start | bytes 2359304 | tf_op jit(solution)/shard_map/ppermute | solution.py:665
  210.1 37.7 %collective-permute-start.19 = (bf16[2,256,768]{2,1,0:T(8,128)(2,1)}, bf16[2,256,768]{2,1,0:T(8,128)(2,1)}, u32[]{:S(2)}, u32[]{:S(2)}) collective-permute-start(bf16[2,256,768]{2,1,0:T(8,128)(2,1)} %get-tuple-element.70), channel_id=1, source_target_pairs={{0,1},{1,0},{2,3},{3,2},{4,5},{5,4},{6,7},{7,6},{8,9},{9,8},{10,11... | collective-permute-start | bytes 2359304 | tf_op jit(solution)/shard_map/ppermute | solution.py:665
  211.6 28.9 %copy-start.19 = (f32[768]{0:T(1024)S(1)}, f32[768]{0:T(1024)}, u32[]{:S(2)}) copy-start(f32[768]{0:T(1024)} %param.21) | copy-start | bytes 9220
  214.7 10.6 %collective-permute-start.35 = (bf16[96,768]{1,0:T(8,128)(2,1)}, bf16[96,768]{1,0:T(8,128)(2,1)S(1)}, u32[]{:S(2)}, u32[]{:S(2)}) collective-permute-start(bf16[96,768]{1,0:T(8,128)(2,1)} %get-tuple-element.101), channel_id=1, source_target_pairs={{0,4},{4,0},{8,12},{12,8},{16,20},{20,16},{24,28},{28,24},{1,5},{5... | collective-permute-start | bytes 442376 | tf_op jit(solution)/shard_map/ppermute | solution.py:671
  215.5 33.4 %copy-start.5 = (bf16[2,256,768]{2,1,0:T(8,128)(2,1)S(1)}, bf16[2,256,768]{2,1,0:T(8,128)(2,1)}, u32[]{:S(2)}) copy-start(bf16[2,256,768]{2,1,0:T(8,128)(2,1)} %get-tuple-element.69) | copy-start | bytes 2359300
  219.5 12.7 %collective-permute-start.36 = (bf16[96,768]{1,0:T(8,128)(2,1)}, bf16[96,768]{1,0:T(8,128)(2,1)S(1)}, u32[]{:S(2)}, u32[]{:S(2)}) collective-permute-start(bf16[96,768]{1,0:T(8,128)(2,1)} %get-tuple-element.102), channel_id=1, source_target_pairs={{0,8},{4,12},{8,16},{12,20},{16,24},{20,28},{24,0},{28,4},{1,9},{5... | collective-permute-start | bytes 442376 | tf_op jit(solution)/shard_map/ppermute | solution.py:668
  225.3 15.8 %copy-start.15 = (bf16[96,768]{1,0:T(8,128)(2,1)}, bf16[96,768]{1,0:T(8,128)(2,1)S(1)}, u32[]{:S(2)}) copy-start(bf16[96,768]{1,0:T(8,128)(2,1)S(1)} %collective-permute-done.35.theirs_ref) | copy-start | bytes 442372
  225.3 12.3 %collective-permute-start.37 = (bf16[96,768]{1,0:T(8,128)(2,1)}, bf16[96,768]{1,0:T(8,128)(2,1)S(1)}, u32[]{:S(2)}, u32[]{:S(2)}) collective-permute-start(bf16[96,768]{1,0:T(8,128)(2,1)} %get-tuple-element.103), channel_id=1, source_target_pairs={{0,16},{4,20},{8,24},{12,28},{16,0},{20,4},{24,8},{28,12},{1,17},{... | collective-permute-start | bytes 442376 | tf_op jit(solution)/shard_map/ppermute | solution.py:668
  232.2 7.3 %collective-permute-start.38 = (bf16[96,768]{1,0:T(8,128)(2,1)}, bf16[96,768]{1,0:T(8,128)(2,1)}, u32[]{:S(2)}, u32[]{:S(2)}) collective-permute-start(bf16[96,768]{1,0:T(8,128)(2,1)} %get-tuple-element.104), channel_id=1, source_target_pairs={{0,24},{4,28},{8,0},{12,4},{16,8},{20,12},{24,16},{28,20},{1,25},{... | collective-permute-start | bytes 442376 | tf_op jit(solution)/shard_map/ppermute | solution.py:668
  238.3 20.6 %collective-permute-start.22 = (bf16[2,256,768]{2,1,0:T(8,128)(2,1)}, bf16[2,256,768]{2,1,0:T(8,128)(2,1)S(1)}, u32[]{:S(2)}, u32[]{:S(2)}) collective-permute-start(bf16[2,256,768]{2,1,0:T(8,128)(2,1)} %get-tuple-element.85), channel_id=1, source_target_pairs={{0,1},{1,0},{2,3},{3,2},{4,5},{5,4},{6,7},{7,6},{8,9},{9,8},{10,11... | collective-permute-start | bytes 2359304 | tf_op jit(solution)/shard_map/ppermute | solution.py:665
  239.5 20.5 %collective-permute-start.24 = (bf16[2,256,768]{2,1,0:T(8,128)(2,1)}, bf16[2,256,768]{2,1,0:T(8,128)(2,1)}, u32[]{:S(2)}, u32[]{:S(2)}) collective-permute-start(bf16[2,256,768]{2,1,0:T(8,128)(2,1)} %get-tuple-element.86), channel_id=1, source_target_pairs={{0,2},{1,3},{2,0},{3,1},{4,6},{5,7},{6,4},{7,5},{8,10},{9,11},{10,... | collective-permute-start | bytes 2359304 | tf_op jit(solution)/shard_map/ppermute | solution.py:665
  245.5 18.5 %collective-permute-start.41 = (bf16[96,256]{1,0:T(8,128)(2,1)S(1)}, bf16[96,256]{1,0:T(8,128)(2,1)S(1)}, u32[]{:S(2)}, u32[]{:S(2)}) collective-permute-start(bf16[96,256]{1,0:T(8,128)(2,1)S(1)} %convert_element_type.98), channel_id=1, source_target_pairs={{0,3},{1,2},{2,1},{3,0},{4,7},{5,6},{6,5},{7,4},{8,11},{9,10},{10,... | collective-permute-start | bytes 147464 | tf_op jit(solution)/shard_map/ppermute | solution.py:665
  247.4 16.7 %collective-permute-start.40 = (bf16[96,256]{1,0:T(8,128)(2,1)S(1)}, bf16[96,256]{1,0:T(8,128)(2,1)S(1)}, u32[]{:S(2)}, u32[]{:S(2)}) collective-permute-start(bf16[96,256]{1,0:T(8,128)(2,1)S(1)} %convert_element_type.98), channel_id=1, source_target_pairs={{0,2},{1,3},{2,0},{3,1},{4,6},{5,7},{6,4},{7,5},{8,10},{9,11},{10,... | collective-permute-start | bytes 147464 | tf_op jit(solution)/shard_map/ppermute | solution.py:665
  247.8 16.2 %collective-permute-start.39 = (bf16[96,256]{1,0:T(8,128)(2,1)S(1)}, bf16[96,256]{1,0:T(8,128)(2,1)S(1)}, u32[]{:S(2)}, u32[]{:S(2)}) collective-permute-start(bf16[96,256]{1,0:T(8,128)(2,1)S(1)} %convert_element_type.98), channel_id=1, source_target_pairs={{0,1},{1,0},{2,3},{3,2},{4,5},{5,4},{6,7},{7,6},{8,9},{9,8},{10,11... | collective-permute-start | bytes 147464 | tf_op jit(solution)/shard_map/ppermute | solution.py:665
  250.6 12.0 %copy-start.2 = (f32[512,768]{1,0:T(8,128)S(1)}, f32[512,768]{1,0:T(8,128)}, u32[]{:S(2)}) copy-start(f32[512,768]{1,0:T(8,128)} %x_ref.3) | copy-start | bytes 4718596
  261.2 8.5 %collective-permute-start.23 = (bf16[256,768]{1,0:T(8,128)(2,1)S(1)}, bf16[256,768]{1,0:T(8,128)(2,1)S(1)}, u32[]{:S(2)}, u32[]{:S(2)}) collective-permute-start(bf16[256,768]{1,0:T(8,128)(2,1)S(1)} %get-tuple-element.161), channel_id=1, source_target_pairs={{0,2},{1,3},{2,0},{3,1},{4,6},{5,7},{6,4},{7,5},{8,10},{9,11},{10,... | collective-permute-start | bytes 1179656 | tf_op jit(solution)/shard_map/ppermute | solution.py:665
  261.2 8.5 %collective-permute-start.25 = (bf16[256,768]{1,0:T(8,128)(2,1)S(1)}, bf16[256,768]{1,0:T(8,128)(2,1)S(1)}, u32[]{:S(2)}, u32[]{:S(2)}) collective-permute-start(bf16[256,768]{1,0:T(8,128)(2,1)S(1)} %get-tuple-element.160), channel_id=1, source_target_pairs={{0,1},{1,0},{2,3},{3,2},{4,5},{5,4},{6,7},{7,6},{8,9},{9,8},{10,11... | collective-permute-start | bytes 1179656 | tf_op jit(solution)/shard_map/ppermute | solution.py:665
  (20 other events, 89.3 us)
where the time goes:
time: 279 us; the launch traced here: 276 us
  Pallas kernels  127 us (46%)
  waiting for transfers between devices  61.5 us (22%)
  starting transfers between devices  59.3 us (21%)
  local copies, waits for them, and re-layouts  14.3 us (5%)
  other arithmetic  12.5 us (4%)
    pallas_call x1, Pallas kernels, body(): pl.pallas_call(functools.partial(backward_kernel, dm), out_shape=[out(len...  39.1 us
    ppermute x22, waiting for transfers between devices, across(): return lax.ppermute(v, 'tensor', swap(n_t, k))  32.5 us
    ppermute x22, starting transfers between devices, across(): return lax.ppermute(v, 'tensor', swap(n_t, k))  26 us
    pallas_call x1, Pallas kernels, body(): pl.pallas_call(functools.partial(forward_kernel, dm), out_shape=[out(leng...  25.2 us
    ppermute x9, waiting for transfers between devices, along(): return lax.ppermute(v, 'dp', shift_hi(n_dp, k))  24.1 us
    ppermute x9, starting transfers between devices, along(): return lax.ppermute(v, 'dp', shift_hi(n_dp, k))  23.1 us
    pallas_call x1, Pallas kernels, body(): pl.pallas_call(functools.partial(gate_kernel, dm), out_shape=[out(length,...  16 us
    pallas_call x1, Pallas kernels, body(): pl.pallas_call(functools.partial(cotangent_kernel, dm), out_shape=[out(le...  10.3 us
  transfers between devices with their start and end apart: 42, of which 19 were waited for; matrix products, arithmetic and copies ran while one was open for 7% of the time, Pallas kernels for 17%

commit v1 on v0

v1 whole, which is shorter than its diff:
```python
import functools
import math

import jax
import jax.numpy as jnp
from jax import lax
from jax.experimental import pallas as pl
from jax.experimental.pallas import tpu as pltpu
from jax.sharding import PartitionSpec as P


BLOCK = 256
LANES = 128
EPS = 1e-05
LOG2E = math.log2(math.e)
FAR = -1e30
F32 = jnp.float32
BF16 = jnp.bfloat16

MM = (((1,), (0,)), ((), ()))
MT = (((1,), (1,)), ((), ()))
TM = (((0,), (0,)), ((), ()))


def dot(a, b, dims=MM):
    return lax.dot_general(a, b, dims, preferred_element_type=F32)


def dot_split(exact, values, dims=MM):
    high = values.astype(BF16)
    low = (values - high.astype(F32)).astype(BF16)
    return dot(exact, high, dims) + dot(exact, low, dims)


def split_dot(values, exact, dims=MM):
    high = values.astype(BF16)
    low = (values - high.astype(F32)).astype(BF16)
    return dot(high, exact, dims) + dot(low, exact, dims)


def up(n, to=LANES):
    return -(-n // to) * to


def softplus(v):
    return jnp.maximum(v, 0.0) + jnp.log1p(jnp.exp(-jnp.abs(v)))


def sigmoid(v):
    return 0.5 + 0.5 * jnp.tanh(0.5 * v)


def colsum(v):
    return jnp.sum(v.reshape(v.shape[0] // 8, 8, v.shape[1]), axis=0)


def spread(cols, pair, hd):
    per = LANES // hd
    lane = lax.broadcasted_iota(jnp.int32, (cols.shape[0], LANES), 1)
    out = jnp.broadcast_to(cols[:, pair * per : pair * per + 1], lane.shape)
    for j in range(1, per):
        col = cols[:, pair * per + j : pair * per + j + 1]
        out = jnp.where(lane >= j * hd, jnp.broadcast_to(col, lane.shape), out)
    return out


def columns_of(rows):
    pad = jnp.zeros((LANES - rows.shape[0], rows.shape[1]), F32)
    return jnp.concatenate([rows, pad], axis=0).T


class Dims:
    def __init__(self, n_dp, n_t, length, width, inner, hd, state, part_rows, chunk_rows):
        self.length, self.width, self.state, self.hd = length, width, state, hd
        self.n_dp, self.n_t, self.n_hi = n_dp, n_t, n_dp // 2
        self.ip = up(inner)
        self.vs = self.ip + 2 * state
        self.np = self.ip + self.vs + LANES
        self.blocks = length // BLOCK
        self.part_rows, self.chunk_rows = part_rows, chunk_rows
        self.pairs = self.ip // LANES
        self.per = LANES // hd
        self.halves = 2 if n_t == 4 and chunk_rows == 2 * BLOCK else 1
        self.piece_rows = chunk_rows // self.halves
        self.pieces = n_t * self.halves
        self.at_n = n_dp
        self.at_c = self.at_n + self.pieces
        self.at_keep = self.at_c + n_t
        self.at_rel = self.at_keep + self.blocks
        self.at_group = self.at_rel + self.blocks
        self.at_slot = self.at_group + self.blocks
        self.at_hi = self.at_slot + self.blocks
        self.at_core = self.at_hi + self.n_hi
        self.at_from = self.at_core + 1
        self.at_side = self.at_from + self.n_hi
        self.late = self.vs + LANES
        self.local_rows = up(7 * self.pairs + 2, 8)


def load_parts(refs, target, sems, scalars, first, rows):
    return [
        pltpu.make_async_copy(
            ref, target.at[pl.ds(pl.multiple_of(scalars[first + k], rows), rows), :], sems.at[k]
        )
        for k, ref in enumerate(refs)
    ]


def decay_parts(raw, hp_ref, cols, tri):
    delta = softplus(raw + hp_ref[0:1, :])
    logs = dot_split(tri, delta * (hp_ref[1:2, :] * LOG2E))
    enter = jnp.exp2(logs) * cols[:, 7:8]
    ending = jnp.exp2(logs[BLOCK - 1 :, :] - logs) * cols[:, 8:9]
    return delta, logs, enter, ending


def norm_kernel(part, x_hbm, gain_ref, *refs):
    outs, (x_v, sem) = refs[:-2], refs[-2:]
    count = x_v.shape[0] // part
    copies = [
        pltpu.make_async_copy(
            x_hbm.at[pl.ds(k * part, part), :], x_v.at[pl.ds(k * part, part), :], sem.at[k]
        )
        for k in range(count)
    ]
    for copy in copies:
        copy.start()
    rows = outs[0].shape[0]
    for k, copy in enumerate(copies):
        copy.wait()
        x = x_v[k * part : (k + 1) * part]
        root = lax.rsqrt(jnp.mean(x * x, axis=1, keepdims=True) + EPS)
        first = k * part % rows
        outs[k * part // rows][first : first + part] = (x * root * gain_ref[...]).astype(BF16)


def pack_kernel(dm, gate_ref, value_ref, shared_ref, step_ref, out_ref):
    inner, heads, r = gate_ref.shape[1], step_ref.shape[0], step_ref.shape[1]
    if inner != dm.ip:
        out_ref[...] = jnp.zeros_like(out_ref)
    row = lax.broadcasted_iota(jnp.int32, (r, r), 0)
    col = lax.broadcasted_iota(jnp.int32, (r, r), 1)
    eye = jnp.where(row == col, 1.0, 0.0).astype(BF16)
    out_ref[:, :inner] = gate_ref[...]
    out_ref[:, dm.ip : dm.ip + inner] = value_ref[...]
    out_ref[:, 2 * dm.ip : dm.ip + dm.vs] = shared_ref[...]
    out_ref[:, dm.ip + dm.vs :] = jnp.zeros((r, LANES), BF16)
    out_ref[:, dm.ip + dm.vs : dm.ip + dm.vs + heads] = dot(eye, step_ref[...], MT).astype(BF16)


def forward_kernel(dm, scalars, *refs):
    q, ip, vs, st, hd = BLOCK, dm.ip, dm.vs, dm.state, dm.hd
    w_parts = refs[: dm.n_dp]
    n_parts = refs[dm.n_dp : dm.n_dp + dm.pieces]
    rest = refs[dm.n_dp + dm.pieces :]
    rows_ref, conv_ref, hp_ref, lane_ref = rest[:4]
    (g_out, v_out, cv_out, ys_out, st_out, h_out, sum_out, nm_out, sg_out, w_out) = rest[4:14]
    (w_v, nm_v, h_ref, vbuf, tri_ref, bias_ref, pbuf, w_sem, n_sem, o_sem) = rest[14:]
    i = pl.program_id(0)
    save = pltpu.make_async_copy(w_v, w_out, o_sem)

    def rows_at(k):
        return nm_v[pl.ds(pl.multiple_of(k * q, q), q), :]

    @pl.when(i == 0)
    def _():
        copies = load_parts(w_parts, w_v, w_sem, scalars, 0, dm.part_rows)
        copies += load_parts(n_parts, nm_v, n_sem, scalars, dm.at_n, dm.piece_rows)
        for copy in copies:
            copy.start()
        h_ref[...] = jnp.zeros_like(h_ref)
        vbuf[...] = jnp.zeros_like(vbuf)
        r = lax.broadcasted_iota(jnp.int32, (q, q), 0)
        c = lax.broadcasted_iota(jnp.int32, (q, q), 1)
        tri_ref[...] = jnp.where(r >= c, 1.0, 0.0).astype(BF16)
        for copy in copies:
            copy.wait()
        save.start()
        pbuf[...] = dot(nm_v[0:q, :], w_v[...])

    rows = rows_ref[...]
    cols = columns_of(rows)
    nm_out[...] = rows_at(i)
    vbuf[0:8, :] = vbuf[q : q + 8, :]
    vbuf[8 : 8 + q, :] = pbuf[:, ip : ip + vs]
    v_out[...] = pbuf[:, ip : ip + vs].astype(BF16)
    raw = pbuf[:, ip + vs :]
    gates = pbuf[:, :ip].astype(BF16)
    g_out[...] = gates
    st_out[...] = raw
    pbuf[...] = dot(rows_at(jnp.minimum(i + 1, dm.blocks - 1)), w_v[...])

    acts = []
    for c in range(vs // LANES):
        g = slice(c * LANES, (c + 1) * LANES)
        acc = conv_ref[4:5, g] + conv_ref[3:4, g] * vbuf[8 : 8 + q, g]
        for lag in range(1, 4):
            acc = acc + conv_ref[3 - lag : 4 - lag, g] * (
                vbuf[8 - lag : 8 - lag + q, g] * cols[:, lag : lag + 1]
            )
        rounded = acc.astype(BF16)
        cv_out[:, g] = rounded
        acc = rounded.astype(F32)
        acts.append(acc * sigmoid(acc))
    in_map = jnp.concatenate(acts[dm.pairs : dm.pairs + st // LANES], axis=1).astype(BF16)
    out_map = jnp.concatenate(acts[dm.pairs + st // LANES :], axis=1).astype(BF16)

    delta, logs, enter, ending = decay_parts(raw, hp_ref, cols, tri_ref[...])
    logs_t = logs.T
    r = lax.broadcasted_iota(jnp.int32, (q, q), 0)
    c = lax.broadcasted_iota(jnp.int32, (q, q), 1)
    bias_ref[...] = jnp.where((r >= c) & (cols[:, 0:1] == rows[0:1, :]), 0.0, FAR)
    scores = dot(out_map, in_map, MT)
    keep = scalars[dm.at_keep + i].astype(F32)
    total = jnp.exp2(logs[q - 1 :, :]) * keep
    lane = lax.broadcasted_iota(jnp.int32, (q, LANES), 1)
    h_out[...] = h_ref[...]
    in_map_t = in_map.T
    squares = jnp.zeros((q, LANES), F32)
    for p in range(dm.pairs):
        g = slice(p * LANES, (p + 1) * LANES)
        x = acts[p]
        u = x * spread(delta, p, hd)
        ub = u.astype(BF16)
        y = None
        for j in range(dm.per):
            h = p * dm.per + j
            decay = jnp.exp2(logs[:, h : h + 1] - logs_t[h : h + 1, :] + bias_ref[...])
            part = dot((decay * scores).astype(BF16), ub)
            y = part if y is None else jnp.where(lane >= j * hd, part, y)
        held = h_ref[:, g]
        y = y + dot(out_map, held.astype(BF16)) * spread(enter, p, hd)
        wu = (u * spread(ending, p, hd)).astype(BF16)
        h_ref[:, g] = held * spread(total, p, hd) + dot(in_map_t, wu)
        ys_out[:, g] = y
        gate = gates[:, g].astype(F32)
        gated = (y + lane_ref[0:1, g] * x) * (gate * sigmoid(gate))
        sg_out[:, g] = (gated * lane_ref[1:2, g]).astype(BF16)
        squares = squares + gated * gated
    sum_out[...] = jnp.sum(squares.T, axis=0, keepdims=True)

    @pl.when(i == dm.blocks - 1)
    def _():
        save.wait()


def cotangent_kernel(dm, scalars, *refs):
    q, n_dp, n_t = BLOCK, dm.n_dp, dm.n_t
    c_parts, w_parts = refs[:n_t], refs[n_t : n_t + n_dp]
    sg_hbm, sq_ref, sc_hbm, sum_out, ct_hbm, wo_out = refs[n_t + n_dp : n_t + n_dp + 6]
    ct_v, sg_v, sc_v, c_sem, w_sem, g_sem, o_sem, t_sem = refs[n_t + n_dp + 6 :]
    loads = load_parts(w_parts, wo_out, w_sem, scalars, 0, dm.part_rows)
    takes = load_parts(c_parts, ct_v, c_sem, scalars, dm.at_c, dm.chunk_rows)
    whole = pltpu.make_async_copy(sg_hbm, sg_v, g_sem)
    for copy in loads:
        copy.start()
    whole.start()
    for copy in takes:
        copy.start()
    for copy in loads:
        copy.wait()
    whole.wait()
    gives = []
    for k in range(n_t):
        takes[k].wait()
        chunk = pl.multiple_of(scalars[dm.at_c + k], dm.chunk_rows)
        for h in range(dm.chunk_rows // q):
            at = pl.ds(pl.multiple_of(chunk + h * q, q), q)
            sc = dot(ct_v[at, :], wo_out[...])
            sc_v[at, :] = sc.astype(BF16)
            prod = sc * sg_v[at, :].astype(F32)
            dots = prod[:, :LANES]
            for p in range(1, dm.pairs):
                dots = dots + prod[:, p * LANES : (p + 1) * LANES]
            blk = chunk // q + h
            sum_out[blk, 0:1, :] = sq_ref[blk]
            sum_out[blk, 1:2, :] = jnp.sum(dots.T, axis=0, keepdims=True)
        at = pl.ds(chunk, dm.chunk_rows)
        gives.append(pltpu.make_async_copy(sc_v.at[at, :], sc_hbm.at[at, :], o_sem.at[k]))
        gives.append(pltpu.make_async_copy(ct_v.at[at, :], ct_hbm.at[at, :], t_sem.at[k]))
        gives[-1].start()
        gives[-2].start()
    for copy in gives:
        copy.wait()


def branch_kernel(dm, scalars, w_ref, sg_ref, *refs):
    outs, (buf, sem) = refs[: dm.n_t], refs[dm.n_t :]
    per = dm.chunk_rows // BLOCK
    for i in range(dm.blocks):
        at = slice(i * BLOCK, (i + 1) * BLOCK)
        buf[i] = dot(sg_ref[at, :], w_ref[...], MT).astype(BF16)
        for k in range(dm.n_t):

            @pl.when(scalars[dm.at_rel + i] == k)
            def _():
                pltpu.make_async_copy(buf.at[i], outs[k].at[i % per], sem.at[i]).start()

    for i in range(dm.blocks):
        pltpu.make_async_copy(buf.at[i], outs[0].at[0], sem.at[i]).wait()


def gate_kernel(dm, scalars, *refs):
    q, ip, r = BLOCK, dm.ip, dm.part_rows
    (w_ref, rk_ref, lane_ref, g_in, cv_in, ys_in, sc_in, nm_in, ct_in) = refs[:9]
    dg_out, dy_out, lane_out, rows_out, own_out = refs[9:14]
    z_outs = refs[14 : 13 + dm.n_hi]
    acc, dg_s, both = refs[13 + dm.n_hi :]
    i = pl.program_id(0)

    @pl.when(i == 0)
    def _():
        lane_out[...] = jnp.zeros_like(lane_out)
        acc[...] = jnp.zeros_like(acc)

    def gather():
        acc[:, :ip] += dot(nm_in[...], dg_s[...], TM)
        acc[:, ip:] += dot(ct_in[...], both[...], TM)

    def gating():
        pad = jnp.zeros((LANES - 2, q), F32)
        cols = jnp.concatenate([rk_ref[...], pad], axis=0).T
        root, pull = cols[:, 0:1], cols[:, 1:2]
        for p in range(dm.pairs):
            g = slice(p * LANES, (p + 1) * LANES)
            gate, sc = g_in[:, g].astype(F32), sc_in[:, g].astype(F32)
            cv = cv_in[:, g].astype(F32)
            x = cv * sigmoid(cv)
            sig = sigmoid(gate)
            z = gate * sig
            y = ys_in[:, g] + lane_ref[0:1, g] * x
            gated = y * z
            scaled = gated * root
            cot = root * (lane_ref[1:2, g] * sc) - pull * gated
            lane_out[0:8, g] += colsum(sc * scaled)
            dy = cot * z
            dy_out[:, g] = dy.astype(BF16)
            dg = (cot * y * (sig + z * (1.0 - sig))).astype(BF16)
            dg_out[:, g] = dg
            dg_s[:, g] = dg
            lane_out[8:16, g] += colsum(dy * x)
            both[:, g] = (scaled * lane_ref[1:2, g]).astype(BF16)

    @pl.when(i == 0)
    def _():
        gating()

    @pl.when((i > 0) & (i < dm.blocks))
    def _():
        gather()
        gating()

    @pl.when(i == dm.blocks)
    def _():
        gather()
        prod = acc[:, :LANES] * w_ref[:, :LANES].astype(F32)
        for p in range(1, dm.pairs):
            g = slice(p * LANES, (p + 1) * LANES)
            prod = prod + acc[:, g] * w_ref[:, g].astype(F32)
        rows_out[...] = gain_rows(prod)
        hi = scalars[dm.at_hi]
        own_out[...] = acc[pl.ds(pl.multiple_of(hi * 2 * r, 8), 2 * r), :]
        for k, z_out in enumerate(z_outs):
            at = pl.multiple_of(scalars[dm.at_hi + k + 1] * 2 * r, 8)
            z_out[...] = acc[pl.ds(at, 2 * r), :].astype(BF16)


def backward_kernel(dm, scalars, *refs):
    q, ip, vs, st, hd, late_cols = BLOCK, dm.ip, dm.vs, dm.state, dm.hd, dm.late
    groups = dm.group_sizes
    w_ref, rows_ref, conv_ref, hp_ref, lane_ref, lanes_ref, gain_ref = refs[:7]
    dg_in, nm_in, dy_in, v_in, cv_in, ys_in, st_in, h_in = refs[7:15]
    mine_out, theirs_out = refs[15:17]
    nc_outs = refs[17 : 17 + len(groups)]
    (dh_ref, dbuf, tri_ref, bias_ref, ds_ref, u_s, dx_s, act_s, t1_s, t2_s) = refs[
        17 + len(groups) : 27 + len(groups)
    ]
    (pj_s, acc, tap_out, head_out, nc_buf, nc_sem) = refs[27 + len(groups) :]
    i = pl.program_id(0)
    blk = jnp.maximum(dm.blocks - 1 - i, 0)

    def send(k, at, row):
        return pltpu.make_async_copy(nc_buf.at[at], nc_outs[k].at[row], nc_sem.at[at])

    @pl.when(i == 0)
    def _():
        dh_ref[...] = jnp.zeros_like(dh_ref)
        dbuf[...] = jnp.zeros_like(dbuf)
        tap_out[...] = jnp.zeros_like(tap_out)
        head_out[...] = jnp.zeros_like(head_out)
        acc[...] = jnp.zeros_like(acc)
        r = lax.broadcasted_iota(jnp.int32, (q, q), 0)
        c = lax.broadcasted_iota(jnp.int32, (q, q), 1)
        tri_ref[...] = jnp.where(r >= c, 1.0, 0.0).astype(BF16)

    slot = lax.rem(i, 2)

    @pl.when(i >= 3)
    def _():
        send(0, slot, 0).wait()

    def project():
        nc = dot(dg_in[...], w_ref[:, :ip], MT) + dot(pj_s[...], w_ref[:, ip:], MT)
        nc_buf[slot] = nc.astype(BF16)
        acc[...] += dot(nm_in[...], pj_s[...], TM)

    def scan():
        rows = rows_ref[...]
        cols = columns_of(rows)
        raw = st_in[...]
        tri = tri_ref[...]
        delta, logs, enter, ending = decay_parts(raw, hp_ref, cols, tri)
        logs_t = logs.T
        lane = lax.broadcasted_iota(jnp.int32, (q, LANES), 1)

        acts, slopes = [], []
        for c in range(vs // LANES):
            g = slice(c * LANES, (c + 1) * LANES)
            cv = cv_in[:, g].astype(F32)
            sig = sigmoid(cv)
            act = cv * sig
            acts.append(act)
            slopes.append(sig + act * (1.0 - sig))
        in_map = jnp.concatenate(acts[dm.pairs : dm.pairs + st // LANES], axis=1).astype(BF16)
        out_map = jnp.concatenate(acts[dm.pairs + st // LANES :], axis=1).astype(BF16)

        for p in range(dm.pairs):
            g = slice(p * LANES, (p + 1) * LANES)
            u_s[:, g] = acts[p] * spread(delta, p, hd)

        r = lax.broadcasted_iota(jnp.int32, (q, q), 0)
        c = lax.broadcasted_iota(jnp.int32, (q, q), 1)
        bias_ref[...] = jnp.where((r <= c) & (cols[:, 0:1] == rows[0:1, :]), 0.0, FAR)
        scores = dot(in_map, out_map, MT)
        dh_b = dh_ref[...].astype(BF16)
        h_b = h_in[...].astype(BF16)
        out_map_t = out_map.T
        keep = scalars[dm.at_keep + blk].astype(F32)
        total = jnp.exp2(logs[q - 1 :, :]) * keep
        d_in = jnp.zeros((q, st), F32)
        d_out = jnp.zeros((q, st), F32)
        for p in range(dm.pairs):
            g = slice(p * LANES, (p + 1) * LANES)
            u, dyb = u_s[:, g], dy_in[:, g]
            ub, dy = u.astype(BF16), dyb.astype(F32)
            du = None
            for j in range(dm.per):
                h = p * dm.per + j
                mine = (lane >= j * hd) & (lane < (j + 1) * hd)
                decay = jnp.exp2(logs_t[h : h + 1, :] - logs[:, h : h + 1] + bias_ref[...])
                part = dot((decay * scores).astype(BF16), dyb)
                du = part if du is None else jnp.where(lane >= j * hd, part, du)
                dm_t = dot(jnp.where(mine, u, 0.0).astype(BF16), dyb, MT)
                if p == 0 and j == 0:
                    ds_ref[...] = dm_t * decay
                else:
                    ds_ref[...] += dm_t * decay
            end_e = spread(ending, p, hd)
            late = end_e * dot(in_map, dh_b[:, g])
            du = du + late
            wu = (u * end_e).astype(BF16)
            edy = (dy * spread(enter, p, hd)).astype(BF16)
            d_in = d_in + dot(wu, dh_b[:, g], MT)
            d_out = d_out + dot(edy, h_b[:, g], MT)
            u32 = ub.astype(F32)
            t1_s[:, g] = dy * ys_in[:, g] - u32 * du
            t2_s[:, g] = du * acts[p]
            kept = dh_ref[:, g] * spread(total, p, hd)
            act_s[:, g] = colsum(u32 * late) + colsum(h_in[:, g] * kept)
            dh_ref[:, g] = kept + dot(out_map_t, edy)
            dx_s[:, g] = (spread(delta, p, hd) * du + lane_ref[0:1, g] * dy) * slopes[p]
        ds_b = ds_ref[...].astype(BF16)
        d_in = d_in + dot(ds_b, out_map)
        d_out = d_out + dot(ds_b, in_map, TM)

        hr = lax.broadcasted_iota(jnp.int32, (ip, LANES), 0)
        hc = lax.broadcasted_iota(jnp.int32, (ip, LANES), 1)
        pick = jnp.where(hr // hd == hc, 1.0, 0.0).astype(BF16)
        d_log = split_dot(t1_s[...], pick)
        last = split_dot(jnp.sum(act_s[...], axis=0, keepdims=True), pick)
        row = lax.broadcasted_iota(jnp.int32, (q, LANES), 0)
        d_log = d_log + jnp.where(row == q - 1, last, 0.0)
        d_step = dot_split(tri, d_log, TM)
        head_out[8:16, :] += colsum(d_step * delta)
        d_delta = hp_ref[1:2, :] * d_step + split_dot(t2_s[...], pick)
        d_raw = d_delta * sigmoid(raw + hp_ref[0:1, :])
        head_out[0:8, :] += colsum(d_raw)
        pj_s[:, vs:] = d_raw.astype(BF16)

        dbuf[q : q + 8, :] = dbuf[0:8, :]
        for c in range(vs // LANES):
            g = slice(c * LANES, (c + 1) * LANES)
            if c < dm.pairs:
                dbuf[0:q, g] = dx_s[:, g]
            else:
                k = (c - dm.pairs) * LANES
                source = d_in[:, k : k + LANES] if k < st else d_out[:, k - st : k - st + LANES]
                dbuf[0:q, g] = source * slopes[c]
        for c in range(vs // LANES):
            g = slice(c * LANES, (c + 1) * LANES)
            v = v_in[:, g].astype(F32)
            shifted = dbuf[0:q, g]
            tap_out[32:40, g] += colsum(shifted)
            tap_out[24:32, g] += colsum(shifted * v)
            dv = conv_ref[3:4, g] * shifted
            for lag in range(1, 4):
                shifted = dbuf[lag : lag + q, g] * cols[:, 3 + lag : 4 + lag]
                tap_out[24 - 8 * lag : 32 - 8 * lag, g] += colsum(shifted * v)
                dv = dv + conv_ref[3 - lag : 4 - lag, g] * shifted
            pj_s[:, g] = dv.astype(BF16)


    @pl.when(i == 0)
    def _():
        scan()

    @pl.when((i > 0) & (i < dm.blocks))
    def _():
        project()
        scan()

    @pl.when(i == dm.blocks)
    def _():
        project()

    before = jnp.minimum(blk + 1, dm.blocks - 1)
    before = jnp.where(i == dm.blocks, 0, before)
    for k in range(len(groups)):

        @pl.when((i > 0) & (scalars[dm.at_group + before] == k))
        def _():
            send(k, slot, scalars[dm.at_slot + before]).start()

    @pl.when(i == dm.blocks)
    def _():
        core, r = scalars[dm.at_core], dm.part_rows
        for h in range(dm.n_hi):
            at = pl.multiple_of((2 * h + core) * r, 8)
            mine_out[h * r : (h + 1) * r, :] = acc[pl.ds(at, r), :]
            at = pl.multiple_of((2 * h + 1 - core) * r, 8)
            theirs_out[h * r : (h + 1) * r, :] = acc[pl.ds(at, r), :].astype(BF16)
        small = []

        def put(v):
            for c in range(v.shape[1] // LANES):
                small.append(jnp.sum(v[:, c * LANES : (c + 1) * LANES], axis=0, keepdims=True))

        for k in range(5):
            put(tap_out[8 * k : 8 * k + 8, :ip])
        for k in range(2):
            put(lanes_ref[8 * k : 8 * k + 8, :])
        for k in range(2):
            put(head_out[8 * k : 8 * k + 8, :])
        zero = jnp.zeros((1, LANES), F32)
        small.extend([zero] * (dm.local_rows - len(small)))
        for k in range(5):
            put(tap_out[8 * k : 8 * k + 8, ip:])
        prod = acc[:, :LANES] * w_ref[:, ip : ip + LANES].astype(F32)
        for p in range(1, late_cols // LANES):
            g = slice(p * LANES, (p + 1) * LANES)
            o = slice(ip + p * LANES, ip + (p + 1) * LANES)
            prod = prod + acc[:, g] * w_ref[:, o].astype(F32)
        prod = gain_rows(prod)
        for c in range(dm.width // LANES):
            g = slice(c * LANES, (c + 1) * LANES)
            small.append(prod[0:1, g] + gain_ref[0:1, g])
        small.extend([zero] * (late_cols // 16 - len(small)))
        for c in range(late_cols // LANES):
            g = slice(c * LANES, (c + 1) * LANES)
            theirs_out[dm.n_hi * r :, g] = two_parts(jnp.concatenate(small[8 * c : 8 * c + 8], axis=0))
        send(0, 1 - slot, 0).wait()
        send(0, slot, 0).wait()


def two_parts(v):
    high = v.astype(BF16).astype(F32)
    return jnp.concatenate([high, v - high], axis=0).astype(BF16)


def one_part(v):
    return v[0:8, :].astype(F32) + v[8:16, :].astype(F32)


def gain_rows(acc):
    high = acc.astype(BF16)
    rest = acc - high.astype(F32)
    mid = rest.astype(BF16)
    low = (rest - mid.astype(F32)).astype(BF16)
    one = jnp.ones((8, LANES), BF16)
    return dot(one, high, MT) + dot(one, mid, MT) + dot(one, low, MT)


def pair_kernel(dm, scalars, mine_ref, kept_ref, theirs_ref, own_out, *outs):
    r = dm.part_rows
    tail = dm.n_hi * r
    small = one_part(kept_ref[...]) + one_part(theirs_ref[tail:, :])
    small = two_parts(small)
    for k in range(dm.n_hi):
        at = pl.multiple_of(scalars[dm.at_hi + k] * r, 8)
        both = mine_ref[pl.ds(at, r), :] + theirs_ref[pl.ds(at, r), :].astype(F32)
        if k == 0:
            own_out[...] = both
        else:
            outs[k][0:r, :] = both.astype(BF16)
        if k > 0:
            outs[k][r:, :] = small
        else:
            outs[0][...] = small


def early_kernel(dm, scalars, own_ref, *refs):
    parts, (mine_out, theirs_out, total) = refs[: dm.n_hi - 1], refs[dm.n_hi - 1 :]
    r = dm.part_rows
    both = own_ref[...]
    for part in parts:
        both = both + part[...].astype(F32)
    total[...] = both
    core = scalars[dm.at_core]
    mine_out[...] = total[pl.ds(pl.multiple_of(core * r, 8), r), :]
    theirs_out[...] = total[pl.ds(pl.multiple_of((1 - core) * r, 8), r), :].astype(BF16)


def grads_kernel(dm, scalars, hp_ref, own_ref, kept_ref, mine_ref, theirs_ref, *refs):
    n, r, st2 = dm.n_hi, dm.part_rows, 2 * dm.state
    parts = refs[: n - 1]
    (gate_out, value_out, step_out, outp_out, share_out) = refs[n - 1 : n + 4]
    (tap_out, tapb_out, gain_out, skip_out, sb_out, dl_out, hold) = refs[n + 4 :]
    total = own_ref[...]
    for part in parts:
        total = total + part[0:r, :].astype(F32)
    early = mine_ref[...] + theirs_ref[...].astype(F32)
    inner, heads = gate_out.shape[1], step_out.shape[0]
    gate_out[...] = early[:, :inner]
    outp_out[...] = early[:, dm.ip : dm.ip + inner]
    value_out[...] = total[:, :inner]
    share_out[0:r, :] = total[:, dm.ip : dm.vs].astype(BF16)
    step_out[...] = total[:, dm.vs :].T[0:heads, :]
    hold[0] = one_part(kept_ref[...])
    for k, part in enumerate(parts):
        hold[k + 1] = one_part(part[r:, :])
    small = hold[scalars[dm.at_from]]
    for k in range(1, n):
        small = small + hold[scalars[dm.at_from + k]]
    flat = [
        small[j : j + 1, c * LANES : (c + 1) * LANES]
        for c in range(dm.late // LANES)
        for j in range(8)
    ]

    def take(first, width):
        return jnp.concatenate(flat[first : first + dm.pairs], axis=1)[:, :width]

    for k in range(4):
        tap_out[k : k + 1, :] = take(k * dm.pairs, inner)
    tapb_out[...] = take(4 * dm.pairs, inner)
    gain_out[...] = take(5 * dm.pairs, inner)
    lane = lax.broadcasted_iota(jnp.int32, (1, LANES), 1)
    skip = jnp.zeros((1, LANES), F32)
    for h in range(heads):
        row = flat[6 * dm.pairs + h // dm.per]
        mine = lane // dm.hd == h % dm.per
        one = jnp.sum(jnp.where(mine, row, 0.0), axis=1, keepdims=True)
        skip = jnp.where(lane == h, one, skip)
    skip_out[...] = skip[:, :heads]
    sb_out[...] = flat[7 * dm.pairs][:, :heads]
    dl_out[...] = (flat[7 * dm.pairs + 1] * hp_ref[1:2, :])[:, :heads]
    first = dm.local_rows // 8
    for c in range(st2 // LANES):
        g = slice((first + c) * LANES, (first + c + 1) * LANES)
        share_out[r:, c * LANES : (c + 1) * LANES] = two_parts(small[:, g])


def share_kernel(dm, scalars, norm_ref, *refs):
    r, st2 = dm.part_rows, 2 * dm.state
    parts = refs[: dm.n_t]
    shared_out, tap_out, tapb_out, norm_out, hold = refs[dm.n_t :]
    for k, part in enumerate(parts):
        hold[k] = part[...]
    shared, common = None, None
    for k in range(dm.n_t):
        part = hold[scalars[dm.at_side + k]]
        share, small = part[0:r, :].astype(F32), one_part(part[r:, :])
        shared = share if shared is None else shared + share
        common = small if common is None else common + small
    shared_out[...] = shared
    flat = [
        common[j : j + 1, c * LANES : (c + 1) * LANES] for c in range(st2 // LANES) for j in range(8)
    ]
    per = st2 // LANES
    for k in range(4):
        tap_out[k : k + 1, :] = jnp.concatenate(flat[k * per : (k + 1) * per], axis=1)
    tapb_out[...] = jnp.concatenate(flat[4 * per : 5 * per], axis=1)
    rows = flat[5 * per : 5 * per + dm.width // LANES]
    norm_out[...] = jnp.concatenate(rows, axis=1) / norm_ref[...]


def input_kernel(sets, steps, x_ref, cot_ref, gain_ref, *refs):
    out = refs[-1]
    x = x_ref[...]
    root = lax.rsqrt(jnp.mean(x * x, axis=1, keepdims=True) + EPS)
    first = 0
    for k, count in enumerate(sets):
        parts = refs[first : first + count]
        first += count

        @pl.when(pl.program_id(0) // steps == k)
        def _():
            nc = parts[0][...].astype(F32)
            for part in parts[1:]:
                nc = nc + part[...].astype(F32)
            hat = nc * gain_ref[...]
            mean = jnp.mean(hat * x, axis=1, keepdims=True)
            out[...] = cot_ref[...].astype(F32) + root * hat - x * (root * root * root * mean)


def shift_hi(n, k):
    return [(i, ((i // 2 + k) % (n // 2)) * 2 + i % 2) for i in range(n)]


def swap(n, k):
    return [(i, i ^ k) for i in range(n)]


def pad_cols(v, to):
    return jnp.pad(v, ((0, 0), (0, to - v.shape[1])))


def pad_vec(v, to):
    return jnp.pad(v, (0, to - v.shape[0]))


def body(
    n_dp,
    n_t,
    block_input,
    segment_ids,
    norm_gain,
    gate_proj,
    value_proj,
    shared_proj,
    step_proj,
    conv_value_weight,
    conv_value_bias,
    conv_shared_weight,
    conv_shared_bias,
    step_bias,
    decay_log,
    skip_weight,
    gate_gain,
    output_proj,
    out_cotangent,
):
    q = BLOCK
    chunk_rows, width = block_input.shape
    length = segment_ids.shape[1]
    inner, heads = gate_proj.shape[1], step_proj.shape[1]
    part_rows = gate_proj.shape[0]
    state = shared_proj.shape[1] // 2
    hd = inner // heads
    dm = Dims(n_dp, n_t, length, width, inner, hd, state, part_rows, chunk_rows)
    ip, vs, nb, n_hi = dm.ip, dm.vs, dm.blocks, dm.n_hi
    me_t = lax.axis_index("tensor")
    me_dp = lax.axis_index("dp")
    hi, core = me_dp // 2, me_dp % 2

    def across(v, k):
        return lax.ppermute(v, "tensor", swap(n_t, k))

    def along(v, k):
        return lax.ppermute(v, "dp", shift_hi(n_dp, k))

    def partner(v):
        return lax.ppermute(v, "dp", swap(n_dp, 1))

    def vmem(shape, dtype):
        return pltpu.VMEM(shape, dtype)

    limit = 60 * 1024 * 1024
    params = pltpu.CompilerParams(dimension_semantics=("arbitrary",), vmem_limit_bytes=limit)
    hbm = pl.BlockSpec(memory_space=pl.ANY)

    def out(*shape, dtype=F32):
        return jax.ShapeDtypeStruct(shape, dtype)

    gain = norm_gain.reshape(1, width)
    part = min(LANES, dm.piece_rows)
    normed = pl.pallas_call(
        functools.partial(norm_kernel, part),
        out_shape=[out(dm.piece_rows, width, dtype=BF16)] * dm.halves,
        in_specs=[hbm, pl.BlockSpec(memory_space=pltpu.VMEM)],
        scratch_shapes=[
            vmem((chunk_rows, width), F32),
            pltpu.SemaphoreType.DMA((chunk_rows // part,)),
        ],
        compiler_params=pltpu.CompilerParams(vmem_limit_bytes=limit),
        name="normalize",
    )(block_input, gain)
    if dm.halves == 2:
        a, b = normed
        xa, yb = across(a, 1), across(b, 2)
        ya, xb = across(a, 2), across(b, 1)
        n_list = [a, b, xa, xb, ya, yb, across(xa, 2), across(yb, 1)]
        n_rows = jnp.concatenate(
            [(me_t ^ k) * chunk_rows + jnp.arange(2) * dm.piece_rows for k in range(4)]
        )
    else:
        n_list = [normed[0]] + [across(normed[0], k) for k in range(1, n_t)]
        n_rows = (me_t ^ jnp.arange(n_t)) * chunk_rows
    packed = pl.pallas_call(
        functools.partial(pack_kernel, dm),
        out_shape=out(part_rows, dm.np, dtype=BF16),
        name="pack_weights",
    )(gate_proj, value_proj, shared_proj, step_proj.T)
    w_list = [packed] + [along(packed, k) for k in range(1, n_hi)]
    w_list = w_list + [partner(v) for v in w_list]
    outp = pad_cols(output_proj.T, ip)
    o_list = [outp] + [along(outp, k) for k in range(1, n_hi)]
    o_list = o_list + [partner(v) for v in o_list]

    seg = segment_ids[0]
    segb = seg.reshape(nb, q)
    last = segb[:, -1]
    prev_last = jnp.concatenate([jnp.full((1,), -1, jnp.int32), last[:-1]])
    gap = jnp.full((3,), -1, jnp.int32)
    wide = jnp.concatenate([gap, seg, gap])
    rows = [seg.astype(F32)]
    rows += [(wide[3 - k : 3 - k + length] == seg).astype(F32) for k in range(1, 4)]
    rows += [(wide[3 + k : 3 + k + length] == seg).astype(F32) for k in range(1, 4)]
    rows += [
        (segb == prev_last[:, None]).astype(F32).reshape(-1),
        (segb == last[:, None]).astype(F32).reshape(-1),
    ]
    rows = jnp.concatenate([jnp.stack(rows), jnp.zeros((16 - len(rows), length), F32)], axis=0)
    keep = (last == prev_last).astype(jnp.int32)
    other = (hi - jnp.arange(n_hi)) % n_hi
    rel = (jnp.arange(nb) * q // chunk_rows) ^ me_t
    half = jnp.arange(nb) % (chunk_rows // q)
    if dm.halves == 2:
        group_of = jnp.array([[2, 2], [0, 2], [2, 1], [0, 1]])
        slot_of = jnp.array([[0, 2], [0, 3], [1, 0], [1, 1]])
        group, slot = group_of[rel, half], slot_of[rel, half]
        dm.group_sizes = (2, 2, 4)
    else:
        group, slot = rel, half
        dm.group_sizes = (chunk_rows // q,) * n_t
    scalars = jnp.concatenate(
        [
            (other * 2 + core) * part_rows,
            (other * 2 + 1 - core) * part_rows,
            n_rows,
            (me_t ^ jnp.arange(n_t)) * chunk_rows,
            keep,
            rel,
            group,
            slot,
            (hi + jnp.arange(n_hi)) % n_hi,
            core[None],
            (hi - jnp.arange(n_hi)) % n_hi,
            me_t ^ jnp.arange(n_t),
        ]
    ).astype(jnp.int32)

    conv = jnp.concatenate(
        [
            pad_cols(jnp.concatenate([conv_value_weight, conv_value_bias[None]]), ip),
            jnp.concatenate([conv_shared_weight, conv_shared_bias[None]]),
        ],
        axis=1,
    )
    conv = jnp.pad(conv, ((0, 3), (0, 0)))
    rate = -jnp.exp(decay_log)
    per_head = jnp.stack([pad_vec(step_bias, LANES), pad_vec(rate, LANES)])
    per_head = jnp.pad(per_head, ((0, 6), (0, 0)))
    per_lane = jnp.stack([pad_vec(jnp.repeat(skip_weight, hd), ip), pad_vec(gate_gain, ip)])
    per_lane = jnp.pad(per_lane, ((0, 6), (0, 0)))

    def const(*shape):
        return pl.BlockSpec(shape, lambda i, s: (0,) * len(shape))

    def fblock(cols):
        return pl.BlockSpec((q, cols), lambda i, s: (i, 0))

    def fsum(k):
        return pl.BlockSpec((None, k, q), lambda i, s: (i, 0, 0))

    def grid(steps, in_specs, out_specs, scratch):
        return pltpu.PrefetchScalarGridSpec(
            num_scalar_prefetch=1,
            grid=(steps,),
            in_specs=in_specs,
            out_specs=out_specs,
            scratch_shapes=scratch,
        )

    (gate, value, conved, scan, steps_raw, held, squares, normed_all, scaled, weights) = pl.pallas_call(
        functools.partial(forward_kernel, dm),
        out_shape=[
            out(length, ip, dtype=BF16),
            out(length, vs, dtype=BF16),
            out(length, vs, dtype=BF16),
            out(length, ip),
            out(length, LANES),
            out(nb * state, ip),
            out(nb, 1, q),
            out(length, width, dtype=BF16),
            out(length, ip, dtype=BF16),
            out(width, dm.np, dtype=BF16),
        ],
        grid_spec=grid(
            nb,
            [hbm] * (n_dp + dm.pieces)
            + [
                pl.BlockSpec((16, q), lambda i, s: (0, i)),
                const(8, vs),
                const(8, LANES),
                const(8, ip),
            ],
            [
                fblock(ip),
                fblock(vs),
                fblock(vs),
                fblock(ip),
                fblock(LANES),
                pl.BlockSpec((state, ip), lambda i, s: (i, 0)),
                fsum(1),
                fblock(width),
                fblock(ip),
                hbm,
            ],
            [
                vmem((width, dm.np), BF16),
                vmem((length, width), BF16),
                vmem((state, ip), F32),
                vmem((q + 8, vs), F32),
                vmem((q, q), BF16),
                vmem((q, q), F32),
                vmem((q, dm.np), F32),
                pltpu.SemaphoreType.DMA((n_dp,)),
                pltpu.SemaphoreType.DMA((dm.pieces,)),
                pltpu.SemaphoreType.DMA,
            ],
        ),
        compiler_params=params,
        cost_estimate=pl.CostEstimate(
            flops=30_000_000_000, bytes_accessed=30_000_000, transcendentals=0
        ),
        name="block_forward",
    )(scalars, *w_list, *n_list, rows, conv, per_head, per_lane)

    c_list = [out_cotangent] + [across(out_cotangent, k) for k in range(1, n_t)]
    in_vmem = pl.BlockSpec(memory_space=pltpu.VMEM)
    sc, sums, cot_all, w_back = pl.pallas_call(
        functools.partial(cotangent_kernel, dm),
        out_shape=[
            out(length, ip, dtype=BF16),
            out(nb, 2, q),
            out(length, width, dtype=BF16),
            out(width, ip, dtype=BF16),
        ],
        grid_spec=grid(
            1,
            [hbm] * (n_t + n_dp + 1) + [in_vmem],
            [hbm, in_vmem, hbm, in_vmem],
            [
                vmem((length, width), BF16),
                vmem((length, ip), BF16),
                vmem((length, ip), BF16),
                pltpu.SemaphoreType.DMA((n_t,)),
                pltpu.SemaphoreType.DMA((n_dp,)),
                pltpu.SemaphoreType.DMA,
                pltpu.SemaphoreType.DMA((n_t,)),
                pltpu.SemaphoreType.DMA((n_t,)),
            ],
        ),
        compiler_params=params,
        cost_estimate=pl.CostEstimate(
            flops=3_000_000_000, bytes_accessed=10_000_000, transcendentals=0
        ),
        name="branch_cotangent",
    )(scalars, *c_list, *o_list, scaled, squares)
    total = sums
    for k in range(1, n_t):
        total = total + across(sums, k)
    branch = pl.pallas_call(
        functools.partial(branch_kernel, dm),
        out_shape=[out(chunk_rows // q, q, width, dtype=BF16)] * n_t,
        grid_spec=grid(
            1,
            [in_vmem, in_vmem],
            [hbm] * n_t,
            [vmem((nb, q, width), BF16), pltpu.SemaphoreType.DMA((nb,))],
        ),
        compiler_params=params,
        cost_estimate=pl.CostEstimate(
            flops=3_000_000_000, bytes_accessed=10_000_000, transcendentals=0
        ),
        name="branch_output",
    )(scalars, w_back, scaled)
    root = lax.rsqrt(total[:, 0] / (inner * n_t) + EPS)
    pull = root * root * root * (total[:, 1] / (inner * n_t))
    rk = jnp.stack([root, pull], axis=1)
    branch_sum = branch[0].astype(F32)
    for k in range(1, n_t):
        branch_sum = branch_sum + across(branch[k], k).astype(F32)
    own_root = lax.dynamic_slice_in_dim(root.reshape(length), me_t * chunk_rows, chunk_rows)
    block_output = block_input + own_root[:, None] * branch_sum.reshape(chunk_rows, width)

    def bblock(cols):
        return pl.BlockSpec((q, cols), lambda i, s: (jnp.maximum(nb - 1 - i, 0), 0))

    def bago(cols):
        return pl.BlockSpec((q, cols), lambda i, s: (jnp.minimum(nb - i, nb - 1), 0))

    def now(cols):
        return pl.BlockSpec((q, cols), lambda i, s: (jnp.minimum(i, nb - 1), 0))

    def ago(cols):
        return pl.BlockSpec((q, cols), lambda i, s: (jnp.maximum(i - 1, 0), 0))

    dgate, dscan, lanes, gate_rows, own_early, *early = pl.pallas_call(
        functools.partial(gate_kernel, dm),
        out_shape=[
            out(length, ip, dtype=BF16),
            out(length, ip, dtype=BF16),
            out(16, ip),
            out(8, width),
            out(2 * part_rows, 2 * ip),
        ]
        + [out(2 * part_rows, 2 * ip, dtype=BF16)] * (n_hi - 1),
        grid_spec=grid(
            nb + 1,
            [
                const(width, ip),
                pl.BlockSpec((None, 2, q), lambda i, s: (jnp.minimum(i, nb - 1), 0, 0)),
                const(8, ip),
                now(ip),
                now(ip),
                now(ip),
                now(ip),
                ago(width),
                ago(width),
            ],
            [now(ip), now(ip), const(16, ip), const(8, width)]
            + [const(2 * part_rows, 2 * ip)] * n_hi,
            [vmem((width, 2 * ip), F32), vmem((q, ip), BF16), vmem((q, ip), BF16)],
        ),
        compiler_params=params,
        cost_estimate=pl.CostEstimate(
            flops=6_000_000_000, bytes_accessed=20_000_000, transcendentals=0
        ),
        name="gate_backward",
    )(scalars, weights, rk, per_lane, gate, conved, scan, sc, normed_all, cot_all)
    early = [along(v, k + 1) for k, v in enumerate(early)]

    r_all = n_hi * part_rows
    mine, theirs, *nc = pl.pallas_call(
        functools.partial(backward_kernel, dm),
        out_shape=[out(r_all, dm.late), out(r_all + 16, dm.late, dtype=BF16)]
        + [out(k, q, width, dtype=BF16) for k in dm.group_sizes],
        grid_spec=grid(
            nb + 1,
            [
                const(width, dm.np),
                pl.BlockSpec((16, q), lambda i, s: (0, jnp.maximum(nb - 1 - i, 0))),
                const(8, vs),
                const(8, LANES),
                const(8, ip),
                const(16, ip),
                const(8, width),
                bago(ip),
                bago(width),
                bblock(ip),
                bblock(vs),
                bblock(vs),
                bblock(ip),
                bblock(LANES),
                pl.BlockSpec((state, ip), lambda i, s: (jnp.maximum(nb - 1 - i, 0), 0)),
            ],
            [const(r_all, dm.late), const(r_all + 16, dm.late)] + [hbm] * len(dm.group_sizes),
            [
                vmem((state, ip), F32),
                vmem((q + 8, vs), F32),
                vmem((q, q), BF16),
                vmem((q, q), F32),
                vmem((q, q), F32),
                vmem((q, ip), F32),
                vmem((q, ip), F32),
                vmem((8, ip), F32),
                vmem((q, ip), F32),
                vmem((q, ip), F32),
                vmem((q, dm.late), BF16),
                vmem((width, dm.late), F32),
                vmem((40, vs), F32),
                vmem((16, LANES), F32),
                vmem((2, q, width), BF16),
                pltpu.SemaphoreType.DMA((2,)),
            ],
        ),
        compiler_params=params,
        cost_estimate=pl.CostEstimate(
            flops=40_000_000_000, bytes_accessed=30_000_000, transcendentals=0
        ),
        name="block_backward",
    )(
        scalars,
        weights,
        rows,
        conv,
        per_head,
        per_lane,
        lanes,
        gate_rows,
        dgate,
        normed_all,
        dscan,
        value,
        conved,
        scan,
        steps_raw,
        held,
    )

    part = min(q, dm.piece_rows)
    steps = dm.piece_rows // part

    def turn(k):
        return pl.BlockSpec((part, width), lambda i: (jnp.clip(i - k * steps, 0, steps - 1), 0))

    def slot_of_piece(k, at):
        return pl.BlockSpec(
            (None, part, width), lambda i: (at, jnp.clip(i - k * steps, 0, steps - 1), 0)
        )

    if dm.halves == 2:
        from_x, from_y, stay = across(nc[0], 1), across(nc[1], 2), nc[2]
        pass_y = (stay[1].astype(F32) + from_x[1].astype(F32)).astype(BF16)
        pass_x = (stay[3].astype(F32) + from_y[1].astype(F32)).astype(BF16)
        got_y, got_x = across(pass_y, 2), across(pass_x, 1)
        sets = (3, 3)
        terms = [stay, from_x, got_y, stay, from_y, got_x]
        specs = [slot_of_piece(0, 0), slot_of_piece(0, 0), turn(0)]
        specs += [slot_of_piece(1, 2), slot_of_piece(1, 0), turn(1)]
    else:
        sets = (n_t,)
        terms = [nc[0]] + [across(nc[k], k) for k in range(1, n_t)]
        terms = [v.reshape(chunk_rows, width) for v in terms]
        specs = [turn(0)] * n_t
    in_turn = pl.BlockSpec((part, width), lambda i: (i, 0))
    input_grad = pl.pallas_call(
        functools.partial(input_kernel, sets, steps),
        out_shape=out(chunk_rows, width),
        grid=(len(sets) * steps,),
        in_specs=[in_turn, in_turn, pl.BlockSpec((1, width), lambda i: (0, 0))] + specs,
        out_specs=in_turn,
        compiler_params=params,
        name="input_gradient",
    )(block_input, out_cotangent, gain, *terms)

    late = dm.late
    kept = theirs[r_all:]
    theirs = partner(theirs)
    own, own_small, *others = pl.pallas_call(
        functools.partial(pair_kernel, dm),
        out_shape=[out(part_rows, late), out(16, late, dtype=BF16)]
        + [out(part_rows + 16, late, dtype=BF16)] * (n_hi - 1),
        grid_spec=grid(1, [in_vmem] * 3, [in_vmem] * (n_hi + 1), []),
        compiler_params=params,
        name="core_sum",
    )(scalars, mine, kept, theirs)
    others = [along(v, k + 1) for k, v in enumerate(others)]
    early_mine, early_theirs = pl.pallas_call(
        functools.partial(early_kernel, dm),
        out_shape=[out(part_rows, 2 * ip), out(part_rows, 2 * ip, dtype=BF16)],
        grid_spec=grid(
            1, [in_vmem] * n_hi, [in_vmem] * 2, [vmem((2 * part_rows, 2 * ip), F32)]
        ),
        compiler_params=params,
        name="early_sum",
    )(scalars, own_early, *early)
    early_theirs = partner(early_theirs)
    (
        gate_proj_grad,
        value_proj_grad,
        step_t,
        outp_t,
        share,
        conv_value_weight_grad,
        conv_value_bias_grad,
        gate_gain_grad,
        skip_weight_grad,
        step_bias_grad,
        decay_log_grad,
    ) = pl.pallas_call(
        functools.partial(grads_kernel, dm),
        out_shape=[
            out(part_rows, inner),
            out(part_rows, inner),
            out(heads, part_rows),
            out(part_rows, inner),
            out(part_rows + 16, 2 * state, dtype=BF16),
            out(4, inner),
            out(1, inner),
            out(1, inner),
            out(1, heads),
            out(1, heads),
            out(1, heads),
        ],
        grid_spec=grid(1, [in_vmem] * (n_hi + 4), [in_vmem] * 11, [vmem((n_hi, 8, late), F32)]),
        compiler_params=params,
        name="gradient_sum",
    )(scalars, per_head, own, own_small, early_mine, early_theirs, *others)
    shares = [share] + [across(share, k) for k in range(1, n_t)]
    shared_proj_grad, conv_shared_weight_grad, conv_shared_bias_grad, norm_gain_grad = pl.pallas_call(
        functools.partial(share_kernel, dm),
        out_shape=[out(part_rows, 2 * state), out(4, 2 * state), out(1, 2 * state), out(1, width)],
        grid_spec=grid(
            1,
            [in_vmem] * (n_t + 1),
            [in_vmem] * 4,
            [vmem((n_t, part_rows + 16, 2 * state), BF16)],
        ),
        compiler_params=params,
        name="shared_sum",
    )(scalars, gain, *shares)
    return (
        block_output,
        input_grad,
        norm_gain_grad.reshape(width),
        gate_proj_grad,
        value_proj_grad,
        shared_proj_grad,
        step_t.T,
        conv_value_weight_grad,
        conv_value_bias_grad.reshape(inner),
        conv_shared_weight_grad,
        conv_shared_bias_grad.reshape(2 * state),
        step_bias_grad.reshape(heads),
        decay_log_grad.reshape(heads),
        skip_weight_grad.reshape(heads),
        gate_gain_grad.reshape(inner),
        outp_t.T,
    )


def solution(mesh):
    n_dp, n_t = mesh.shape["dp"], mesh.shape["tensor"]
    both = ("dp", "tensor")
    return jax.shard_map(
        functools.partial(body, n_dp, n_t),
        mesh=mesh,
        in_specs=(
            P(both, None),
            P("dp", None),
            P(),
            P("dp", "tensor"),
            P("dp", "tensor"),
            P("dp", None),
            P("dp", "tensor"),
            P(None, "tensor"),
            P("tensor"),
            P(),
            P(),
            P("tensor"),
            P("tensor"),
            P("tensor"),
            P("tensor"),
            P("tensor", "dp"),
            P(both, None),
        ),
        out_specs=(
            P(both, None),
            P(both, None),
            P(),
            P("dp", "tensor"),
            P("dp", "tensor"),
            P("dp", None),
            P("dp", "tensor"),
            P(None, "tensor"),
            P("tensor"),
            P(),
            P(),
            P("tensor"),
            P("tensor"),
            P("tensor"),
            P("tensor"),
            P("tensor", "dp"),
        ),
        check_vma=False,
    )
```

time: 279 us -> 248 us (0.89)
  Pallas kernels: 127 us -> 111 us
  starting transfers between devices: 59.3 us -> 48.3 us
  local copies, waits for them, and re-layouts: 14.3 us -> 9.87 us
    ppermute x5 -> x0, starting transfers between devices: 9.6 us -> none  [all_sum(): v = v + lax.ppermute(v, axis, swap(n, k))]
    pallas_call x4, Pallas kernels: 56 us -> 46.7 us  [the longest x1 38 us: body(): pl.pallas_call(functools.partial(backward_kernel, dm), out_shape=[out(r_a...]
    ppermute x22, waiting for transfers between devices: 32.5 us -> 40.3 us  [across(): return lax.ppermute(v, 'tensor', swap(n_t, k))]
    ppermute x5 -> x0, waiting for transfers between devices: 4.92 us -> none  [all_sum(): v = v + lax.ppermute(v, axis, swap(n, k))]
    ppermute x9 -> x12, waiting for transfers between devices: 24.1 us -> 20.8 us  [along(): return lax.ppermute(v, 'dp', shift_hi(n_dp, k))]
    pallas_call x1, Pallas kernels: 7.92 us -> 4.92 us  [body(): pl.pallas_call(functools.partial(branch_kernel, dm), out_shape=[out(chunk...]
    unnamed x92 -> x111, local copies, waits for them, and re-layouts: 6.35 us -> 3.54 us
    ppermute x9 -> x12, starting transfers between devices: 23.1 us -> 22.1 us  [along(): return lax.ppermute(v, 'dp', shift_hi(n_dp, k))]
  transfers between devices with their start and end apart: 42 -> 44, of which waited for: 19 -> 14; matrix products, arithmetic and copies ran while one was open for 7% -> 8% of each run, Pallas kernels for 17% -> 19%
where the time goes in v1:
time: 248 us; the launch traced here: 247 us
  Pallas kernels  111 us (45%)
  waiting for transfers between devices  62.4 us (25%)
  starting transfers between devices  48.3 us (19%)
  other arithmetic  13.7 us (6%)
  local copies, waits for them, and re-layouts  9.87 us (4%)
    ppermute x22, waiting for transfers between devices, across(): return lax.ppermute(v, 'tensor', swap(n_t, k))  40.3 us
    pallas_call x1, Pallas kernels, body(): pl.pallas_call(functools.partial(backward_kernel, dm), out_shape=[out(r_a...  38 us
    pallas_call x1, Pallas kernels, body(): pl.pallas_call(functools.partial(forward_kernel, dm), out_shape=[out(leng...  25.1 us
    ppermute x22, starting transfers between devices, across(): return lax.ppermute(v, 'tensor', swap(n_t, k))  24.8 us
    ppermute x12, starting transfers between devices, along(): return lax.ppermute(v, 'dp', shift_hi(n_dp, k))  22.1 us
    ppermute x12, waiting for transfers between devices, along(): return lax.ppermute(v, 'dp', shift_hi(n_dp, k))  20.8 us
    pallas_call x1, Pallas kernels, body(): pl.pallas_call(functools.partial(gate_kernel, dm), out_shape=[out(length,...  14.8 us
    pallas_call x1, Pallas kernels, body(): pl.pallas_call(functools.partial(cotangent_kernel, dm), out_shape=[out(le...  8.4 us
  transfers between devices with their start and end apart: 44, of which 14 were waited for; matrix products, arithmetic and copies ran while one was open for 8% of the time, Pallas kernels for 19%

profile of v1, /device:TPU:0, one launch (start us, length us, event | category | flops | bytes accessed | tf_op | source)
XLA Modules:
  0.0 246.9 jit_solution(8827950658771877009)
XLA Ops:
  0.7 3.1 %collective-permute-start.3 = (bf16[96,384]{1,0:T(8,128)(2,1)}, bf16[96,384]{1,0:T(8,128)(2,1)S(1)}, u32[]{:S(2)}, u32[]{:S(2)}) collective-permute-start(bf16[96,384]{1,0:T(8,128)(2,1)} %bitcast.69), channel_id=1, source_target_pairs={{0,8},{4,12},{8,16},{12,20},{16,24},{20,28},{24,0},{28,4},{1,9},{5... | collective-permute-start | bytes 221192 | tf_op jit(solution)/shard_map/ppermute | solution.py:770
  3.8 2.6 %collective-permute-start.4 = (bf16[96,384]{1,0:T(8,128)(2,1)}, bf16[96,384]{1,0:T(8,128)(2,1)S(1)}, u32[]{:S(2)}, u32[]{:S(2)}) collective-permute-start(bf16[96,384]{1,0:T(8,128)(2,1)} %bitcast.70), channel_id=1, source_target_pairs={{0,16},{4,20},{8,24},{12,28},{16,0},{20,4},{24,8},{28,12},{1,17},{... | collective-permute-start | bytes 221192 | tf_op jit(solution)/shard_map/ppermute | solution.py:770
  6.4 1.3 collective-permute-start.5
  7.7 1.8 pack_weights.1.refs_0_
  9.5 0.7 collective-permute-start.10
  10.8 1.4 fusion.33
  12.7 1.3 reshape.180.gain_ref.norm_ref
  14.0 1.0 fusion.13
  15.2 0.7 exponential_negate_fusion
  15.9 3.2 %normalize.1 = (bf16[256,768]{1,0:T(8,128)(2,1)}, bf16[256,768]{1,0:T(8,128)(2,1)}) custom-call(f32[512,768]{1,0:T(8,128)} %x_ref.1, f32[1,768]{1,0:T(1,128)} %reshape.180.gain_ref.norm_ref), custom_call_target="tpu_custom_call" | custom-call | tf_op jit(solution)/shard_map/normalize/pallas_call | solution.py:787
  19.5 1.5 collective-permute-start.17
  21.0 1.5 collective-permute-start.20
  22.7 1.2 collective-permute-done.7.refs_9_
  23.9 2.9 %collective-permute-start.12 = (bf16[96,1152]{1,0:T(8,128)(2,1)S(1)}, bf16[96,1152]{1,0:T(8,128)(2,1)S(1)}, u32[]{:S(2)}, u32[]{:S(2)}) collective-permute-start(bf16[96,1152]{1,0:T(8,128)(2,1)S(1)} %copy-done.13), channel_id=1, source_target_pairs={{0,24},{4,28},{8,0},{12,4},{16,8},{20,12},{24,16},{28,20},{1,25},{... | collective-permute-start | bytes 663560 | tf_op jit(solution)/shard_map/ppermute | solution.py:770
  27.4 5.6 %collective-permute-done.11.refs_2_ = bf16[96,1152]{1,0:T(8,128)(2,1)S(1)} collective-permute-done((bf16[96,1152]{1,0:T(8,128)(2,1)S(1)}, bf16[96,1152]{1,0:T(8,128)(2,1)S(1)}, u32[]{:S(2)}, u32[]{:S(2)}) %collective-permute-start.11) | collective-permute-done | bytes 221216 | tf_op jit(solution)/shard_map/ppermute | solution.py:770
  33.0 1.5 collective-permute-start.19
  34.6 2.5 %collective-permute-done.12.refs_3_ = bf16[96,1152]{1,0:T(8,128)(2,1)S(1)} collective-permute-done((bf16[96,1152]{1,0:T(8,128)(2,1)S(1)}, bf16[96,1152]{1,0:T(8,128)(2,1)S(1)}, u32[]{:S(2)}, u32[]{:S(2)}) %collective-permute-start.12) | collective-permute-done | bytes 221216 | tf_op jit(solution)/shard_map/ppermute | solution.py:770
  38.3 0.7 gather_fusion
  39.0 0.7 gather_fusion.1
  39.8 1.4 concatenate.38.refs_16_.refs_1_
  41.2 0.6 concatenate.35.scalars
  43.0 2.3 collective-permute-done.19.refs_12_
  45.2 0.6 select_maximum_fusion.3.refs_18_.refs_3_.hp_ref
  46.5 1.6 collective-permute-start
  48.1 1.6 collective-permute-start.1
  50.2 2.1 collective-permute-done.21.refs_14_
  53.0 25.1 %block_forward.1 = (bf16[2048,384]{1,0:T(8,128)(2,1)}, bf16[2048,640]{1,0:T(8,128)(2,1)}, bf16[2048,640]{1,0:T(8,128)(2,1)}, f32[2048,384]{1,0:T(8,128)}, f32[20...) custom-call(s32[65]{0:T(128)} %concatenate.35.scalars, ...), custom_call_target="tpu_custom_call" | custom-call | flops 30000001024 | bytes 30000000 | tf_op jit(solution)/shard_map/block_forward/pallas_call | solution.py:895
  78.1 7.2 %collective-permute-done.1.refs_2_ = bf16[512,768]{1,0:T(8,128)(2,1)S(1)} collective-permute-done((bf16[512,768]{1,0:T(8,128)(2,1)S(1)}, bf16[512,768]{1,0:T(8,128)(2,1)S(1)}, u32[]{:S(2)}, u32[]{:S(2)}) %collective-permute-start.1) | collective-permute-done | bytes 786464 | tf_op jit(solution)/shard_map/ppermute | solution.py:767
  85.3 0.9 copy-done.29
  86.5 8.4 %branch_cotangent.1 = (bf16[2048,384]{1,0:T(8,128)(2,1)}, f32[8,2,256]{2,1,0:T(2,128)}, bf16[2048,768]{1,0:T(8,128)(2,1)}, bf16[768,384]{1,0:T(8,128)(2,1)}) custom-call(s32[65]{0:T(128)} %concatenate.35.scalars, bf16[512,768]{1,0:T(8,128)(2,1)} %cot_ref.1, bf16[512,768]{1,0:T(8,128)(2,1)} %copy-done.28, bf16[512,768]{1,0:T(8,128)(2,1)} %copy-done.29, ...), custom_call_target="tpu_custom_call" | custom-call | flops 3000000000 | bytes 10000000 | tf_op jit(solution)/shard_map/branch_cotangent/pallas_call | solution.py:952
  94.9 2.5 %collective-permute-start.25 = (f32[8,2,256]{2,1,0:T(2,128)}, f32[8,2,256]{2,1,0:T(2,128)S(1)}, u32[]{:S(2)}, u32[]{:S(2)}) collective-permute-start(f32[8,2,256]{2,1,0:T(2,128)} %get-tuple-element.75), channel_id=1, source_target_pairs={{0,3},{1,2},{2,1},{3,0},{4,7},{5,6},{6,5},{7,4},{8,11},{9,10},{10,... | collective-permute-start | bytes 49160 | tf_op jit(solution)/shard_map/ppermute | solution.py:767
  98.4 1.5 collective-permute-done.25
  99.9 1.4 collective-permute-done.24
  101.8 0.7 add_add_fusion
  102.5 0.6 pad_maximum_fusion.refs_1_
  103.2 14.8 %gate_backward.1 = (bf16[2048,384]{1,0:T(8,128)(2,1)}, bf16[2048,384]{1,0:T(8,128)(2,1)}, f32[16,384]{1,0:T(8,128)}, f32[8,768]{1,0:T(8,128)}, f32[192,768]{1,0:...) custom-call(s32[65]{0:T(128)} %concatenate.35.scalars, ...), custom_call_target="tpu_custom_call" | custom-call | flops 6000000000 | bytes 20000000 | tf_op jit(solution)/shard_map/gate_backward/pallas_call | solution.py:1020
  118.0 38.0 %block_backward.1 = (f32[384,768]{1,0:T(8,128)}, bf16[400,768]{1,0:T(8,128)(2,1)}, bf16[2,256,768]{2,1,0:T(8,128)(2,1)}, bf16[2,256,768]{2,1,0:T(8,128)(2,1)}, bf16[4,256,768]{2,1,0:T(8,128)(2,1)}) custom-call(s32[65]{0:T(128)} %concatenate.35.scalars, bf16[768,1152]{1,0:T(8,128)(2,1)} %get-tuple-element.81.refs_0_, ...), custom_call_target="tpu_custom_call" | custom-call | flops 40000000000 | bytes 30000000 | tf_op jit(solution)/shard_map/block_backward/pallas_call | solution.py:1056
  156.1 3.7 %collective-permute-start.34 = (bf16[192,768]{1,0:T(8,128)(2,1)S(1)}, bf16[192,768]{1,0:T(8,128)(2,1)S(1)}, u32[]{:S(2)}, u32[]{:S(2)}) collective-permute-start(bf16[192,768]{1,0:T(8,128)(2,1)S(1)} %copy-done.37), channel_id=1, source_target_pairs={{0,8},{4,12},{8,16},{12,20},{16,24},{20,28},{24,0},{28,4},{1,9},{5... | collective-permute-start | bytes 884744 | tf_op jit(solution)/shard_map/ppermute | solution.py:770
  159.7 3.4 %collective-permute-start.35 = (bf16[192,768]{1,0:T(8,128)(2,1)S(1)}, bf16[192,768]{1,0:T(8,128)(2,1)S(1)}, u32[]{:S(2)}, u32[]{:S(2)}) collective-permute-start(bf16[192,768]{1,0:T(8,128)(2,1)S(1)} %copy-done.36), channel_id=1, source_target_pairs={{0,16},{4,20},{8,24},{12,28},{16,0},{20,4},{24,8},{28,12},{1,17},{... | collective-permute-start | bytes 884744 | tf_op jit(solution)/shard_map/ppermute | solution.py:770
  163.7 6.8 %collective-permute-done.34.refs_0_ = bf16[192,768]{1,0:T(8,128)(2,1)S(1)} collective-permute-done((bf16[192,768]{1,0:T(8,128)(2,1)S(1)}, bf16[192,768]{1,0:T(8,128)(2,1)S(1)}, u32[]{:S(2)}, u32[]{:S(2)}) %collective-permute-start.34) | collective-permute-done | bytes 294944 | tf_op jit(solution)/shard_map/ppermute | solution.py:770
  170.6 1.6 collective-permute-start.31
  172.2 4.9 %branch_output.1 = (bf16[2,256,768]{2,1,0:T(8,128)(2,1)}, bf16[2,256,768]{2,1,0:T(8,128)(2,1)}, bf16[2,256,768]{2,1,0:T(8,128)(2,1)}, bf16[2,256,768]{2,1,0:T(8,128)(2,1)}) custom-call(s32[65]{0:T(128)} %concatenate.35.scalars, bf16[768,384]{1,0:T(8,128)(2,1)} %get-tuple-element.76.w_ref, bf16[2048,384]{1,0:T(8,128)(2,1)} %get-tuple-element.73.refs_12_.sg_ref), custom_call_target="tpu_custom_call" | custom-call | flops 3000000000 | bytes 10000000 | tf_op jit(solution)/shard_map/branch_output/pallas_call | solution.py:984
  177.1 5.8 %collective-permute-done.35.refs_1_ = bf16[192,768]{1,0:T(8,128)(2,1)S(1)} collective-permute-done((bf16[192,768]{1,0:T(8,128)(2,1)S(1)}, bf16[192,768]{1,0:T(8,128)(2,1)S(1)}, u32[]{:S(2)}, u32[]{:S(2)}) %collective-permute-start.35) | collective-permute-done | bytes 294944 | tf_op jit(solution)/shard_map/ppermute | solution.py:770
  182.9 1.5 collective-permute-start.28
  185.0 1.5 collective-permute-start.26
  186.5 1.3 slice.70.kept_ref
  187.9 3.1 %early_sum.1 = (f32[96,768]{1,0:T(8,128)}, bf16[96,768]{1,0:T(8,128)(2,1)}) custom-call(s32[65]{0:T(128)} %concatenate.35.scalars, f32[192,768]{1,0:T(8,128)} %get-tuple-element.102.own_ref, bf16[192,768]{1,0:T(8,128)(2,1)} %copy-done.10, bf16[192,768]{1,0:T(8,128)(2,1)} %copy-done.11, bf16[192,768]{1,0:T(8,128)(2,1)} %copy-done.12), custom_call_target="tpu_custom_call" | custom-call | tf_op jit(solution)/shard_map/early_sum/pallas_call | solution.py:1171
  191.0 3.2 %core_sum.1 = (f32[96,768]{1,0:T(8,128)}, bf16[16,768]{1,0:T(8,128)(2,1)}, bf16[112,768]{1,0:T(8,128)(2,1)}, bf16[112,768]{1,0:T(8,128)(2,1)}, bf16[112,768]{1,0:T(8,128)(2,1)}) custom-call(s32[65]{0:T(128)} %concatenate.35.scalars, f32[384,768]{1,0:T(8,128)} %get-tuple-element.98.mine_ref, bf16[16,768]{1,0:T(8,128)(2,1)} %slice.70.kept_ref, ...), custom_call_target="tpu_custom_call" | custom-call | tf_op jit(solution)/shard_map/core_sum/pallas_call | solution.py:1162
  194.4 13.7 %collective-permute-done.31.refs_4_ = bf16[2,256,768]{2,1,0:T(8,128)(2,1)S(1)} collective-permute-done((bf16[2,256,768]{2,1,0:T(8,128)(2,1)}, bf16[2,256,768]{2,1,0:T(8,128)(2,1)S(1)}, u32[]{:S(2)}, u32[]{:S(2)}) %collective-permute-start.31) | collective-permute-done | bytes 786464 | tf_op jit(solution)/shard_map/ppermute | solution.py:767
  208.1 1.1 fusion.2
  209.2 1.4 collective-permute-start.39
  210.6 2.5 %collective-permute-start.40 = (bf16[112,768]{1,0:T(8,128)(2,1)S(1)}, bf16[112,768]{1,0:T(8,128)(2,1)}, u32[]{:S(2)}, u32[]{:S(2)}) collective-permute-start(bf16[112,768]{1,0:T(8,128)(2,1)S(1)} %copy-done.44), channel_id=1, source_target_pairs={{0,24},{4,28},{8,0},{12,4},{16,8},{20,12},{24,16},{28,20},{1,25},{... | collective-permute-start | bytes 516104 | tf_op jit(solution)/shard_map/ppermute | solution.py:770
  213.1 10.5 %collective-permute-done.27 = bf16[2,256,768]{2,1,0:T(8,128)(2,1)} collective-permute-done((bf16[2,256,768]{2,1,0:T(8,128)(2,1)}, bf16[2,256,768]{2,1,0:T(8,128)(2,1)}, u32[]{:S(2)}, u32[]{:S(2)}) %collective-permute-start.27) | collective-permute-done | bytes 786464 | tf_op jit(solution)/shard_map/ppermute | solution.py:767
  223.6 1.6 collective-permute-start.30
  225.7 2.1 convert_add_fusion
  227.9 2.8 %gradient_sum.1 = (f32[96,384]{1,0:T(8,128)}, f32[96,384]{1,0:T(8,128)}, f32[6,96]{1,0:T(8,128)}, f32[96,384]{1,0:T(8,128)}, bf16[112,256]{1,0:T(8,128)(2,1)}, /...) custom-call(s32[65]{0:T(128)} %concatenate.35.scalars, ...), custom_call_target="tpu_custom_call" | custom-call | tf_op jit(solution)/shard_map/gradient_sum/pallas_call | solution.py:1193
  230.7 1.6 collective-permute-start.41
  232.8 1.5 collective-permute-start.43
  234.3 1.4 fusion
  236.9 1.2 collective-permute-done.43.refs_3_
  238.7 2.3 shared_sum.1
  240.9 1.3 reduce.1
  242.2 0.7 copy-done.9
  243.0 3.9 %input_gradient.1 = f32[512,768]{1,0:T(8,128)} custom-call(f32[512,768]{1,0:T(8,128)} %x_ref.1, bf16[512,768]{1,0:T(8,128)(2,1)} %cot_ref.1, f32[1,768]{1,0:T(1,128)} %reshape.180.gain_ref.norm_ref, bf16[4,256,768]{2,1,0:T(8,128)(2,1)} %get-tuple-element.95.refs_0_.refs_3_, bf16[2,256,768]{2,1,0:T(8,128)(2,1)} %copy-done.4, bf16[256,768]{1,0:T(8,128)(2,1)} %copy-done.9, ...), custom_call_target="tpu_custom_call" | custom-call | tf_op jit(solution)/shard_map/input_gradient/pallas_call | solution.py:1149
  (188 shorter events, 12.5 us)
Async XLA Ops:
  0.6 37.7 %copy-start.1 = (s32[4,2]{1,0:T(4,128)S(1)}, s32[4,2]{1,0:T(4,128)}, u32[]{:S(2)}) copy-start(s32[4,2]{1,0:T(4,128)} %constant.110.clone) | copy-start | bytes 100
  0.7 38.3 %copy-start = (s32[4,2]{1,0:T(4,128)S(1)}, s32[4,2]{1,0:T(4,128)}, u32[]{:S(2)}) copy-start(s32[4,2]{1,0:T(4,128)} %constant.111.clone) | copy-start | bytes 100
  0.7 33.9 %copy-start.27 = (f32[6]{0:T(128)S(1)}, f32[6]{0:T(128)}, u32[]{:S(2)}) copy-start(f32[6]{0:T(128)} %param.30) | copy-start | bytes 76
  0.7 18.4 %collective-permute-start.3 = (bf16[96,384]{1,0:T(8,128)(2,1)}, bf16[96,384]{1,0:T(8,128)(2,1)S(1)}, u32[]{:S(2)}, u32[]{:S(2)}) collective-permute-start(bf16[96,384]{1,0:T(8,128)(2,1)} %bitcast.69), channel_id=1, source_target_pairs={{0,8},{4,12},{8,16},{12,20},{16,24},{20,28},{24,0},{28,4},{1,9},{5... | collective-permute-start | bytes 221192 | tf_op jit(solution)/shard_map/ppermute | solution.py:770
  3.8 15.7 %collective-permute-start.4 = (bf16[96,384]{1,0:T(8,128)(2,1)}, bf16[96,384]{1,0:T(8,128)(2,1)S(1)}, u32[]{:S(2)}, u32[]{:S(2)}) collective-permute-start(bf16[96,384]{1,0:T(8,128)(2,1)} %bitcast.70), channel_id=1, source_target_pairs={{0,16},{4,20},{8,24},{12,28},{16,0},{20,4},{24,8},{28,12},{1,17},{... | collective-permute-start | bytes 221192 | tf_op jit(solution)/shard_map/ppermute | solution.py:770
  6.4 14.6 %collective-permute-start.5 = (bf16[96,384]{1,0:T(8,128)(2,1)}, bf16[96,384]{1,0:T(8,128)(2,1)S(1)}, u32[]{:S(2)}, u32[]{:S(2)}) collective-permute-start(bf16[96,384]{1,0:T(8,128)(2,1)} %bitcast.71), channel_id=1, source_target_pairs={{0,24},{4,28},{8,0},{12,4},{16,8},{20,12},{24,16},{28,20},{1,25},{... | collective-permute-start | bytes 221192 | tf_op jit(solution)/shard_map/ppermute | solution.py:770
  7.7 14.8 %collective-permute-start.6 = (bf16[96,384]{1,0:T(8,128)(2,1)}, bf16[96,384]{1,0:T(8,128)(2,1)S(1)}, u32[]{:S(2)}, u32[]{:S(2)}) collective-permute-start(bf16[96,384]{1,0:T(8,128)(2,1)} %bitcast.72), channel_id=1, source_target_pairs={{0,4},{4,0},{8,12},{12,8},{16,20},{20,16},{24,28},{28,24},{1,5},{5... | collective-permute-start | bytes 221192 | tf_op jit(solution)/shard_map/ppermute | solution.py:773
  9.5 30.1 %copy-start.21 = (f32[384]{0:T(512)S(1)}, f32[384]{0:T(512)}, u32[]{:S(2)}) copy-start(f32[384]{0:T(512)} %param.27) | copy-start | bytes 4612
  9.5 30.1 %copy-start.22 = (f32[384]{0:T(512)S(1)}, f32[384]{0:T(512)}, u32[]{:S(2)}) copy-start(f32[384]{0:T(512)} %param.33) | copy-start | bytes 4612
  9.5 30.2 %copy-start.26 = (f32[6]{0:T(128)S(1)}, f32[6]{0:T(128)}, u32[]{:S(2)}) copy-start(f32[6]{0:T(128)} %param.32) | copy-start | bytes 76
  9.5 17.3 %collective-permute-start.10 = (bf16[96,1152]{1,0:T(8,128)(2,1)}, bf16[96,1152]{1,0:T(8,128)(2,1)S(1)}, u32[]{:S(2)}, u32[]{:S(2)}) collective-permute-start(bf16[96,1152]{1,0:T(8,128)(2,1)} %pack_weights.1.refs_0_), channel_id=1, source_target_pairs={{0,8},{4,12},{8,16},{12,20},{16,24},{20,28},{24,0},{28,4},{1,9},{5... | collective-permute-start | bytes 663560 | tf_op jit(solution)/shard_map/ppermute | solution.py:770
  15.2 30.7 %copy-start.19 = (f32[4,384]{1,0:T(4,128)S(1)}, f32[4,384]{1,0:T(4,128)}, u32[]{:S(2)}) copy-start(f32[4,384]{1,0:T(4,128)} %param.26) | copy-start | bytes 18436
  15.2 30.7 %copy-start.20 = (f32[4,256]{1,0:T(4,128)S(1)}, f32[4,256]{1,0:T(4,128)}, u32[]{:S(2)}) copy-start(f32[4,256]{1,0:T(4,128)} %param.28) | copy-start | bytes 12292
  15.2 30.7 %copy-start.25 = (f32[256]{0:T(256)S(1)}, f32[256]{0:T(256)}, u32[]{:S(2)}) copy-start(f32[256]{0:T(256)} %param.29) | copy-start | bytes 3076
  15.9 30.6 %copy-start.7 = (bf16[512,768]{1,0:T(8,128)(2,1)S(1)}, bf16[512,768]{1,0:T(8,128)(2,1)}, u32[]{:S(2)}) copy-start(bf16[512,768]{1,0:T(8,128)(2,1)} %cot_ref.1) | copy-start | bytes 2359300
  19.1 59.0 %copy-start.47 = (bf16[96,384]{1,0:T(8,128)(2,1)}, bf16[96,384]{1,0:T(8,128)(2,1)S(1)}, u32[]{:S(2)}) copy-start(bf16[96,384]{1,0:T(8,128)(2,1)S(1)} %collective-permute-done.3.refs_5_) | copy-start | bytes 221188
  19.1 13.9 %collective-permute-start.11 = (bf16[96,1152]{1,0:T(8,128)(2,1)S(1)}, bf16[96,1152]{1,0:T(8,128)(2,1)S(1)}, u32[]{:S(2)}, u32[]{:S(2)}) collective-permute-start(bf16[96,1152]{1,0:T(8,128)(2,1)S(1)} %copy-done.13), channel_id=1, source_target_pairs={{0,16},{4,20},{8,24},{12,28},{16,0},{20,4},{24,8},{28,12},{1,17},{... | collective-permute-start | bytes 663560 | tf_op jit(solution)/shard_map/ppermute | solution.py:770
  19.5 58.5 %copy-start.48 = (bf16[96,384]{1,0:T(8,128)(2,1)}, bf16[96,384]{1,0:T(8,128)(2,1)S(1)}, u32[]{:S(2)}) copy-start(bf16[96,384]{1,0:T(8,128)(2,1)S(1)} %collective-permute-done.4.refs_6_) | copy-start | bytes 221188
  19.5 17.7 %collective-permute-start.17 = (bf16[256,768]{1,0:T(8,128)(2,1)}, bf16[256,768]{1,0:T(8,128)(2,1)S(1)}, u32[]{:S(2)}, u32[]{:S(2)}) collective-permute-start(bf16[256,768]{1,0:T(8,128)(2,1)} %get-tuple-element.71.refs_8_), channel_id=1, source_target_pairs={{0,1},{1,0},{2,3},{3,2},{4,5},{5,4},{6,7},{7,6},{8,9},{9,8},{10,11... | collective-permute-start | bytes 1179656 | tf_op jit(solution)/shard_map/ppermute | solution.py:767
  21.0 28.6 %copy-start.49 = (bf16[96,384]{1,0:T(8,128)(2,1)}, bf16[96,384]{1,0:T(8,128)(2,1)S(1)}, u32[]{:S(2)}) copy-start(bf16[96,384]{1,0:T(8,128)(2,1)S(1)} %collective-permute-done.5.refs_7_) | copy-start | bytes 221188
  21.0 16.7 %collective-permute-start.20 = (bf16[256,768]{1,0:T(8,128)(2,1)}, bf16[256,768]{1,0:T(8,128)(2,1)S(1)}, u32[]{:S(2)}, u32[]{:S(2)}) collective-permute-start(bf16[256,768]{1,0:T(8,128)(2,1)} %get-tuple-element.72.refs_9_), channel_id=1, source_target_pairs={{0,2},{1,3},{2,0},{3,1},{4,6},{5,7},{6,4},{7,5},{8,10},{9,11},{10,... | collective-permute-start | bytes 1179656 | tf_op jit(solution)/shard_map/ppermute | solution.py:767
  22.6 1.3 collective-permute-start.7
  23.9 13.2 %collective-permute-start.12 = (bf16[96,1152]{1,0:T(8,128)(2,1)S(1)}, bf16[96,1152]{1,0:T(8,128)(2,1)S(1)}, u32[]{:S(2)}, u32[]{:S(2)}) collective-permute-start(bf16[96,1152]{1,0:T(8,128)(2,1)S(1)} %copy-done.13), channel_id=1, source_target_pairs={{0,24},{4,28},{8,0},{12,4},{16,8},{20,12},{24,16},{28,20},{1,25},{... | collective-permute-start | bytes 663560 | tf_op jit(solution)/shard_map/ppermute | solution.py:770
  26.8 22.9 %copy-start.38 = (bf16[96,1152]{1,0:T(8,128)(2,1)}, bf16[96,1152]{1,0:T(8,128)(2,1)S(1)}, u32[]{:S(2)}) copy-start(bf16[96,1152]{1,0:T(8,128)(2,1)S(1)} %collective-permute-done.10.refs_1_) | copy-start | bytes 663556
  26.8 15.6 %collective-permute-start.18 = (bf16[256,768]{1,0:T(8,128)(2,1)}, bf16[256,768]{1,0:T(8,128)(2,1)S(1)}, u32[]{:S(2)}, u32[]{:S(2)}) collective-permute-start(bf16[256,768]{1,0:T(8,128)(2,1)} %get-tuple-element.72.refs_9_), channel_id=1, source_target_pairs={{0,1},{1,0},{2,3},{3,2},{4,5},{5,4},{6,7},{7,6},{8,9},{9,8},{10,11... | collective-permute-start | bytes 1179656 | tf_op jit(solution)/shard_map/ppermute | solution.py:767
  33.0 12.2 %collective-permute-start.19 = (bf16[256,768]{1,0:T(8,128)(2,1)}, bf16[256,768]{1,0:T(8,128)(2,1)S(1)}, u32[]{:S(2)}, u32[]{:S(2)}) collective-permute-start(bf16[256,768]{1,0:T(8,128)(2,1)} %get-tuple-element.71.refs_8_), channel_id=1, source_target_pairs={{0,2},{1,3},{2,0},{3,1},{4,6},{5,7},{6,4},{7,5},{8,10},{9,11},{10,... | collective-permute-start | bytes 1179656 | tf_op jit(solution)/shard_map/ppermute | solution.py:767
  37.1 5.3 %collective-permute-start.13 = (bf16[96,1152]{1,0:T(8,128)(2,1)S(1)}, bf16[96,1152]{1,0:T(8,128)(2,1)}, u32[]{:S(2)}, u32[]{:S(2)}) collective-permute-start(bf16[96,1152]{1,0:T(8,128)(2,1)S(1)} %copy-done.13), channel_id=1, source_target_pairs={{0,4},{4,0},{8,12},{12,8},{16,20},{20,16},{24,28},{28,24},{1,5},{5... | collective-permute-start | bytes 663560 | tf_op jit(solution)/shard_map/ppermute | solution.py:773
  37.2 15.2 %collective-permute-start.21 = (bf16[256,768]{1,0:T(8,128)(2,1)S(1)}, bf16[256,768]{1,0:T(8,128)(2,1)}, u32[]{:S(2)}, u32[]{:S(2)}) collective-permute-start(bf16[256,768]{1,0:T(8,128)(2,1)S(1)} %collective-permute-done.17.refs_10_), channel_id=1, source_target_pairs={{0,2},{1,3},{2,0},{3,1},{4,6},{5,7},{6,4},{7,5},{8,10},{9,11},{10,... | collective-permute-start | bytes 1179656 | tf_op jit(solution)/shard_map/ppermute | solution.py:767
  37.8 14.6 %collective-permute-start.22 = (bf16[256,768]{1,0:T(8,128)(2,1)S(1)}, bf16[256,768]{1,0:T(8,128)(2,1)}, u32[]{:S(2)}, u32[]{:S(2)}) collective-permute-start(bf16[256,768]{1,0:T(8,128)(2,1)S(1)} %collective-permute-done.20.refs_13_), channel_id=1, source_target_pairs={{0,1},{1,0},{2,3},{3,2},{4,5},{5,4},{6,7},{7,6},{8,9},{9,8},{10,11... | collective-permute-start | bytes 1179656 | tf_op jit(solution)/shard_map/ppermute | solution.py:767
  42.4 4.1 %collective-permute-start.14 = (bf16[96,1152]{1,0:T(8,128)(2,1)S(1)}, bf16[96,1152]{1,0:T(8,128)(2,1)S(1)}, u32[]{:S(2)}, u32[]{:S(2)}) collective-permute-start(bf16[96,1152]{1,0:T(8,128)(2,1)S(1)} %collective-permute-done.10.refs_1_), channel_id=1, source_target_pairs={{0,4},{4,0},{8,12},{12,8},{16,20},{20,16},{24,28},{28,24},{1,5},{5... | collective-permute-start | bytes 663560 | tf_op jit(solution)/shard_map/ppermute | solution.py:773
  42.5 5.6 %collective-permute-start.15 = (bf16[96,1152]{1,0:T(8,128)(2,1)S(1)}, bf16[96,1152]{1,0:T(8,128)(2,1)S(1)}, u32[]{:S(2)}, u32[]{:S(2)}) collective-permute-start(bf16[96,1152]{1,0:T(8,128)(2,1)S(1)} %collective-permute-done.11.refs_2_), channel_id=1, source_target_pairs={{0,4},{4,0},{8,12},{12,8},{16,20},{20,16},{24,28},{28,24},{1,5},{5... | collective-permute-start | bytes 663560 | tf_op jit(solution)/shard_map/ppermute | solution.py:773
  45.2 4.4 %collective-permute-start.16 = (bf16[96,1152]{1,0:T(8,128)(2,1)}, bf16[96,1152]{1,0:T(8,128)(2,1)S(1)}, u32[]{:S(2)}, u32[]{:S(2)}) collective-permute-start(bf16[96,1152]{1,0:T(8,128)(2,1)} %copy-done.40), channel_id=1, source_target_pairs={{0,4},{4,0},{8,12},{12,8},{16,20},{20,16},{24,28},{28,24},{1,5},{5... | collective-permute-start | bytes 663560 | tf_op jit(solution)/shard_map/ppermute | solution.py:773
  46.5 31.6 %collective-permute-start = (bf16[512,768]{1,0:T(8,128)(2,1)S(1)}, bf16[512,768]{1,0:T(8,128)(2,1)S(1)}, u32[]{:S(2)}, u32[]{:S(2)}) collective-permute-start(bf16[512,768]{1,0:T(8,128)(2,1)S(1)} %copy-done.7), channel_id=1, source_target_pairs={{0,1},{1,0},{2,3},{3,2},{4,5},{5,4},{6,7},{7,6},{8,9},{9,8},{10,11... | collective-permute-start | bytes 2359304 | tf_op jit(solution)/shard_map/ppermute | solution.py:767
  48.1 37.2 %collective-permute-start.1 = (bf16[512,768]{1,0:T(8,128)(2,1)S(1)}, bf16[512,768]{1,0:T(8,128)(2,1)S(1)}, u32[]{:S(2)}, u32[]{:S(2)}) collective-permute-start(bf16[512,768]{1,0:T(8,128)(2,1)S(1)} %copy-done.7), channel_id=1, source_target_pairs={{0,2},{1,3},{2,0},{3,1},{4,6},{5,7},{6,4},{7,5},{8,10},{9,11},{10,... | collective-permute-start | bytes 2359304 | tf_op jit(solution)/shard_map/ppermute | solution.py:767
  49.7 35.6 %collective-permute-start.2 = (bf16[512,768]{1,0:T(8,128)(2,1)S(1)}, bf16[512,768]{1,0:T(8,128)(2,1)S(1)}, u32[]{:S(2)}, u32[]{:S(2)}) collective-permute-start(bf16[512,768]{1,0:T(8,128)(2,1)S(1)} %copy-done.7), channel_id=1, source_target_pairs={{0,3},{1,2},{2,1},{3,0},{4,7},{5,6},{6,5},{7,4},{8,11},{9,10},{10,... | collective-permute-start | bytes 2359304 | tf_op jit(solution)/shard_map/ppermute | solution.py:767
  52.4 25.7 %collective-permute-start.8 = (bf16[96,384]{1,0:T(8,128)(2,1)S(1)}, bf16[96,384]{1,0:T(8,128)(2,1)}, u32[]{:S(2)}, u32[]{:S(2)}) collective-permute-start(bf16[96,384]{1,0:T(8,128)(2,1)S(1)} %collective-permute-done.4.refs_6_), channel_id=1, source_target_pairs={{0,4},{4,0},{8,12},{12,8},{16,20},{20,16},{24,28},{28,24},{1,5},{5... | collective-permute-start | bytes 221192 | tf_op jit(solution)/shard_map/ppermute | solution.py:773
  52.4 25.7 %collective-permute-start.9 = (bf16[96,384]{1,0:T(8,128)(2,1)}, bf16[96,384]{1,0:T(8,128)(2,1)}, u32[]{:S(2)}, u32[]{:S(2)}) collective-permute-start(bf16[96,384]{1,0:T(8,128)(2,1)} %copy-done.49), channel_id=1, source_target_pairs={{0,4},{4,0},{8,12},{12,8},{16,20},{20,16},{24,28},{28,24},{1,5},{5... | collective-permute-start | bytes 221192 | tf_op jit(solution)/shard_map/ppermute | solution.py:773
  94.9 5.1 %collective-permute-start.25 = (f32[8,2,256]{2,1,0:T(2,128)}, f32[8,2,256]{2,1,0:T(2,128)S(1)}, u32[]{:S(2)}, u32[]{:S(2)}) collective-permute-start(f32[8,2,256]{2,1,0:T(2,128)} %get-tuple-element.75), channel_id=1, source_target_pairs={{0,3},{1,2},{2,1},{3,0},{4,7},{5,6},{6,5},{7,4},{8,11},{9,10},{10,... | collective-permute-start | bytes 49160 | tf_op jit(solution)/shard_map/ppermute | solution.py:767
  97.4 3.9 %collective-permute-start.24 = (f32[8,2,256]{2,1,0:T(2,128)}, f32[8,2,256]{2,1,0:T(2,128)S(1)}, u32[]{:S(2)}, u32[]{:S(2)}) collective-permute-start(f32[8,2,256]{2,1,0:T(2,128)} %get-tuple-element.75), channel_id=1, source_target_pairs={{0,2},{1,3},{2,0},{3,1},{4,6},{5,7},{6,4},{7,5},{8,10},{9,11},{10,... | collective-permute-start | bytes 49160 | tf_op jit(solution)/shard_map/ppermute | solution.py:767
  97.8 3.9 %collective-permute-start.23 = (f32[8,2,256]{2,1,0:T(2,128)}, f32[8,2,256]{2,1,0:T(2,128)S(1)}, u32[]{:S(2)}, u32[]{:S(2)}) collective-permute-start(f32[8,2,256]{2,1,0:T(2,128)} %get-tuple-element.75), channel_id=1, source_target_pairs={{0,1},{1,0},{2,3},{3,2},{4,5},{5,4},{6,7},{7,6},{8,9},{9,8},{10,11... | collective-permute-start | bytes 49160 | tf_op jit(solution)/shard_map/ppermute | solution.py:767
  117.9 38.1 %copy-start.37 = (bf16[192,768]{1,0:T(8,128)(2,1)S(1)}, bf16[192,768]{1,0:T(8,128)(2,1)}, u32[]{:S(2)}) copy-start(bf16[192,768]{1,0:T(8,128)(2,1)} %get-tuple-element.103) | copy-start | bytes 884740
  117.9 41.8 %copy-start.36 = (bf16[192,768]{1,0:T(8,128)(2,1)S(1)}, bf16[192,768]{1,0:T(8,128)(2,1)}, u32[]{:S(2)}) copy-start(bf16[192,768]{1,0:T(8,128)(2,1)} %get-tuple-element.104) | copy-start | bytes 884740
  117.9 45.2 %copy-start.35 = (bf16[192,768]{1,0:T(8,128)(2,1)S(1)}, bf16[192,768]{1,0:T(8,128)(2,1)}, u32[]{:S(2)}) copy-start(bf16[192,768]{1,0:T(8,128)(2,1)} %get-tuple-element.105) | copy-start | bytes 884740
  156.0 29.0 %collective-permute-start.33 = (bf16[400,768]{1,0:T(8,128)(2,1)}, bf16[400,768]{1,0:T(8,128)(2,1)S(1)}, u32[]{:S(2)}, u32[]{:S(2)}) collective-permute-start(bf16[400,768]{1,0:T(8,128)(2,1)} %get-tuple-element.99), channel_id=1, source_target_pairs={{0,4},{4,0},{8,12},{12,8},{16,20},{20,16},{24,28},{28,24},{1,5},{5... | collective-permute-start | bytes 1843208 | tf_op jit(solution)/shard_map/ppermute | solution.py:773
  156.1 14.5 %collective-permute-start.34 = (bf16[192,768]{1,0:T(8,128)(2,1)S(1)}, bf16[192,768]{1,0:T(8,128)(2,1)S(1)}, u32[]{:S(2)}, u32[]{:S(2)}) collective-permute-start(bf16[192,768]{1,0:T(8,128)(2,1)S(1)} %copy-done.37), channel_id=1, source_target_pairs={{0,8},{4,12},{8,16},{12,20},{16,24},{20,28},{24,0},{28,4},{1,9},{5... | collective-permute-start | bytes 884744 | tf_op jit(solution)/shard_map/ppermute | solution.py:770
  159.7 23.2 %collective-permute-start.35 = (bf16[192,768]{1,0:T(8,128)(2,1)S(1)}, bf16[192,768]{1,0:T(8,128)(2,1)S(1)}, u32[]{:S(2)}, u32[]{:S(2)}) collective-permute-start(bf16[192,768]{1,0:T(8,128)(2,1)S(1)} %copy-done.36), channel_id=1, source_target_pairs={{0,16},{4,20},{8,24},{12,28},{16,0},{20,4},{24,8},{28,12},{1,17},{... | collective-permute-start | bytes 884744 | tf_op jit(solution)/shard_map/ppermute | solution.py:770
  163.1 21.3 %collective-permute-start.36 = (bf16[192,768]{1,0:T(8,128)(2,1)S(1)}, bf16[192,768]{1,0:T(8,128)(2,1)S(1)}, u32[]{:S(2)}, u32[]{:S(2)}) collective-permute-start(bf16[192,768]{1,0:T(8,128)(2,1)S(1)} %copy-done.35), channel_id=1, source_target_pairs={{0,24},{4,28},{8,0},{12,4},{16,8},{20,12},{24,16},{28,20},{1,25},{... | collective-permute-start | bytes 884744 | tf_op jit(solution)/shard_map/ppermute | solution.py:770
  163.1 31.1 %collective-permute-start.29 = (bf16[2,256,768]{2,1,0:T(8,128)(2,1)}, bf16[2,256,768]{2,1,0:T(8,128)(2,1)S(1)}, u32[]{:S(2)}, u32[]{:S(2)}) collective-permute-start(bf16[2,256,768]{2,1,0:T(8,128)(2,1)} %get-tuple-element.96), channel_id=1, source_target_pairs={{0,1},{1,0},{2,3},{3,2},{4,5},{5,4},{6,7},{7,6},{8,9},{9,8},{10,11... | collective-permute-start | bytes 2359304 | tf_op jit(solution)/shard_map/ppermute | solution.py:767
  170.6 37.5 %collective-permute-start.31 = (bf16[2,256,768]{2,1,0:T(8,128)(2,1)}, bf16[2,256,768]{2,1,0:T(8,128)(2,1)S(1)}, u32[]{:S(2)}, u32[]{:S(2)}) collective-permute-start(bf16[2,256,768]{2,1,0:T(8,128)(2,1)} %get-tuple-element.97), channel_id=1, source_target_pairs={{0,2},{1,3},{2,0},{3,1},{4,6},{5,7},{6,4},{7,5},{8,10},{9,11},{10,... | collective-permute-start | bytes 2359304 | tf_op jit(solution)/shard_map/ppermute | solution.py:767
  182.9 27.7 %collective-permute-start.28 = (bf16[2,256,768]{2,1,0:T(8,128)(2,1)}, bf16[2,256,768]{2,1,0:T(8,128)(2,1)}, u32[]{:S(2)}, u32[]{:S(2)}) collective-permute-start(bf16[2,256,768]{2,1,0:T(8,128)(2,1)} %get-tuple-element.80), channel_id=1, source_target_pairs={{0,3},{1,2},{2,1},{3,0},{4,7},{5,6},{6,5},{7,4},{8,11},{9,10},{10,... | collective-permute-start | bytes 2359304 | tf_op jit(solution)/shard_map/ppermute | solution.py:767
  184.4 39.2 %collective-permute-start.27 = (bf16[2,256,768]{2,1,0:T(8,128)(2,1)}, bf16[2,256,768]{2,1,0:T(8,128)(2,1)}, u32[]{:S(2)}, u32[]{:S(2)}) collective-permute-start(bf16[2,256,768]{2,1,0:T(8,128)(2,1)} %get-tuple-element.79), channel_id=1, source_target_pairs={{0,2},{1,3},{2,0},{3,1},{4,6},{5,7},{6,4},{7,5},{8,10},{9,11},{10,... | collective-permute-start | bytes 2359304 | tf_op jit(solution)/shard_map/ppermute | solution.py:767
  185.0 40.2 %collective-permute-start.26 = (bf16[2,256,768]{2,1,0:T(8,128)(2,1)}, bf16[2,256,768]{2,1,0:T(8,128)(2,1)}, u32[]{:S(2)}, u32[]{:S(2)}) collective-permute-start(bf16[2,256,768]{2,1,0:T(8,128)(2,1)} %get-tuple-element.78), channel_id=1, source_target_pairs={{0,1},{1,0},{2,3},{3,2},{4,5},{5,4},{6,7},{7,6},{8,9},{9,8},{10,11... | collective-permute-start | bytes 2359304 | tf_op jit(solution)/shard_map/ppermute | solution.py:767
  187.9 20.2 %copy-start.3 = (bf16[4,256,768]{2,1,0:T(8,128)(2,1)S(1)}, bf16[4,256,768]{2,1,0:T(8,128)(2,1)}, u32[]{:S(2)}) copy-start(bf16[4,256,768]{2,1,0:T(8,128)(2,1)} %get-tuple-element.95.refs_0_.refs_3_) | copy-start | bytes 4718596
  194.2 31.5 %copy-start.6 = (bf16[2,256,768]{2,1,0:T(8,128)(2,1)S(1)}, bf16[2,256,768]{2,1,0:T(8,128)(2,1)}, u32[]{:S(2)}) copy-start(bf16[2,256,768]{2,1,0:T(8,128)(2,1)} %get-tuple-element.77) | copy-start | bytes 2359300
  194.3 31.4 %copy-start.4 = (bf16[2,256,768]{2,1,0:T(8,128)(2,1)}, bf16[2,256,768]{2,1,0:T(8,128)(2,1)S(1)}, u32[]{:S(2)}) copy-start(bf16[2,256,768]{2,1,0:T(8,128)(2,1)S(1)} %collective-permute-done.29.refs_1_) | copy-start | bytes 2359300
  194.3 14.9 %collective-permute-start.37 = (bf16[96,768]{1,0:T(8,128)(2,1)S(1)}, bf16[96,768]{1,0:T(8,128)(2,1)S(1)}, u32[]{:S(2)}, u32[]{:S(2)}) collective-permute-start(bf16[96,768]{1,0:T(8,128)(2,1)S(1)} %copy-done.46), channel_id=1, source_target_pairs={{0,4},{4,0},{8,12},{12,8},{16,20},{20,16},{24,28},{28,24},{1,5},{5... | collective-permute-start | bytes 442376 | tf_op jit(solution)/shard_map/ppermute | solution.py:773
  208.1 19.8 %collective-permute-start.38 = (bf16[112,768]{1,0:T(8,128)(2,1)}, bf16[112,768]{1,0:T(8,128)(2,1)}, u32[]{:S(2)}, u32[]{:S(2)}) collective-permute-start(bf16[112,768]{1,0:T(8,128)(2,1)} %get-tuple-element.108), channel_id=1, source_target_pairs={{0,8},{4,12},{8,16},{12,20},{16,24},{20,28},{24,0},{28,4},{1,9},{5... | collective-permute-start | bytes 516104 | tf_op jit(solution)/shard_map/ppermute | solution.py:770
  209.2 18.7 %collective-permute-start.39 = (bf16[112,768]{1,0:T(8,128)(2,1)S(1)}, bf16[112,768]{1,0:T(8,128)(2,1)}, u32[]{:S(2)}, u32[]{:S(2)}) collective-permute-start(bf16[112,768]{1,0:T(8,128)(2,1)S(1)} %copy-done.45), channel_id=1, source_target_pairs={{0,16},{4,20},{8,24},{12,28},{16,0},{20,4},{24,8},{28,12},{1,17},{... | collective-permute-start | bytes 516104 | tf_op jit(solution)/shard_map/ppermute | solution.py:770
  210.6 17.2 %collective-permute-start.40 = (bf16[112,768]{1,0:T(8,128)(2,1)S(1)}, bf16[112,768]{1,0:T(8,128)(2,1)}, u32[]{:S(2)}, u32[]{:S(2)}) collective-permute-start(bf16[112,768]{1,0:T(8,128)(2,1)S(1)} %copy-done.44), channel_id=1, source_target_pairs={{0,24},{4,28},{8,0},{12,4},{16,8},{20,12},{24,16},{28,20},{1,25},{... | collective-permute-start | bytes 516104 | tf_op jit(solution)/shard_map/ppermute | solution.py:770
  223.6 18.6 %collective-permute-start.30 = (bf16[256,768]{1,0:T(8,128)(2,1)}, bf16[256,768]{1,0:T(8,128)(2,1)S(1)}, u32[]{:S(2)}, u32[]{:S(2)}) collective-permute-start(bf16[256,768]{1,0:T(8,128)(2,1)} %get-tuple-element.129), channel_id=1, source_target_pairs={{0,2},{1,3},{2,0},{3,1},{4,6},{5,7},{6,4},{7,5},{8,10},{9,11},{10,... | collective-permute-start | bytes 1179656 | tf_op jit(solution)/shard_map/ppermute | solution.py:767
  225.2 17.0 %collective-permute-start.32 = (bf16[256,768]{1,0:T(8,128)(2,1)}, bf16[256,768]{1,0:T(8,128)(2,1)}, u32[]{:S(2)}, u32[]{:S(2)}) collective-permute-start(bf16[256,768]{1,0:T(8,128)(2,1)} %get-tuple-element.128), channel_id=1, source_target_pairs={{0,1},{1,0},{2,3},{3,2},{4,5},{5,4},{6,7},{7,6},{8,9},{9,8},{10,11... | collective-permute-start | bytes 1179656 | tf_op jit(solution)/shard_map/ppermute | solution.py:767
  230.7 6.1 %collective-permute-start.41 = (bf16[112,256]{1,0:T(8,128)(2,1)}, bf16[112,256]{1,0:T(8,128)(2,1)S(1)}, u32[]{:S(2)}, u32[]{:S(2)}) collective-permute-start(bf16[112,256]{1,0:T(8,128)(2,1)} %get-tuple-element.111.refs_0_), channel_id=1, source_target_pairs={{0,1},{1,0},{2,3},{3,2},{4,5},{5,4},{6,7},{7,6},{8,9},{9,8},{10,11... | collective-permute-start | bytes 172040 | tf_op jit(solution)/shard_map/ppermute | solution.py:767
  232.3 4.5 %collective-permute-start.42 = (bf16[112,256]{1,0:T(8,128)(2,1)}, bf16[112,256]{1,0:T(8,128)(2,1)S(1)}, u32[]{:S(2)}, u32[]{:S(2)}) collective-permute-start(bf16[112,256]{1,0:T(8,128)(2,1)} %get-tuple-element.111.refs_0_), channel_id=1, source_target_pairs={{0,2},{1,3},{2,0},{3,1},{4,6},{5,7},{6,4},{7,5},{8,10},{9,11},{10,... | collective-permute-start | bytes 172040 | tf_op jit(solution)/shard_map/ppermute | solution.py:767
  232.8 5.3 %collective-permute-start.43 = (bf16[112,256]{1,0:T(8,128)(2,1)}, bf16[112,256]{1,0:T(8,128)(2,1)S(1)}, u32[]{:S(2)}, u32[]{:S(2)}) collective-permute-start(bf16[112,256]{1,0:T(8,128)(2,1)} %get-tuple-element.111.refs_0_), channel_id=1, source_target_pairs={{0,3},{1,2},{2,1},{3,0},{4,7},{5,6},{6,5},{7,4},{8,11},{9,10},{10,... | collective-permute-start | bytes 172040 | tf_op jit(solution)/shard_map/ppermute | solution.py:767
  (32 other events, 221.1 us)

commit v2 on v1

--- a/solution.py
+++ b/solution.py
@@ -131,7 +131,7 @@
         x = x_v[k * part : (k + 1) * part]
         root = lax.rsqrt(jnp.mean(x * x, axis=1, keepdims=True) + EPS)
         first = k * part % rows
-        outs[k * part // rows][first : first + part] = (x * root * gain_ref[...]).astype(BF16)
+        outs[k * part // rows][first : first + part] = (x * root * gain_ref[...][None]).astype(BF16)
 
 
 def pack_kernel(dm, gate_ref, value_ref, shared_ref, step_ref, out_ref):
@@ -244,68 +244,71 @@
         save.wait()
 
 
-def cotangent_kernel(dm, scalars, *refs):
-    q, n_dp, n_t = BLOCK, dm.n_dp, dm.n_t
-    c_parts, w_parts = refs[:n_t], refs[n_t : n_t + n_dp]
-    sg_hbm, sq_ref, sc_hbm, sum_out, ct_hbm, wo_out = refs[n_t + n_dp : n_t + n_dp + 6]
-    ct_v, sg_v, sc_v, c_sem, w_sem, g_sem, o_sem, t_sem = refs[n_t + n_dp + 6 :]
-    loads = load_parts(w_parts, wo_out, w_sem, scalars, 0, dm.part_rows)
-    takes = load_parts(c_parts, ct_v, c_sem, scalars, dm.at_c, dm.chunk_rows)
+def branch_kernel(dm, scalars, *refs):
+    n_dp, n_t = dm.n_dp, dm.n_t
+    w_parts, sg_hbm = refs[:n_dp], refs[n_dp]
+    w_out, outs = refs[n_dp + 1], refs[n_dp + 2 : n_dp + 2 + n_t]
+    sg_v, buf, w_sem, g_sem, sem = refs[n_dp + 2 + n_t :]
+    per = dm.chunk_rows // BLOCK
+    loads = load_parts(w_parts, w_out, w_sem, scalars, 0, dm.part_rows)
     whole = pltpu.make_async_copy(sg_hbm, sg_v, g_sem)
     for copy in loads:
         copy.start()
     whole.start()
-    for copy in takes:
-        copy.start()
     for copy in loads:
         copy.wait()
     whole.wait()
+    for i in range(dm.blocks):
+        at = slice(i * BLOCK, (i + 1) * BLOCK)
+        buf[i] = dot(sg_v[at, :], w_out[...], MT).astype(BF16)
+        for k in range(n_t):
+
+            @pl.when(scalars[dm.at_rel + i] == k)
+            def _():
+                pltpu.make_async_copy(buf.at[i], outs[k].at[i % per], sem.at[i]).start()
+
+    for i in range(dm.blocks):
+        pltpu.make_async_copy(buf.at[i], outs[0].at[0], sem.at[i]).wait()
+
+
+def dots_kernel(dm, scalars, *refs):
+    q, n_t = BLOCK, dm.n_t
+    c_parts, b_parts = refs[:n_t], refs[n_t : 2 * n_t]
+    sq_ref, sum_out, ct_hbm = refs[2 * n_t : 2 * n_t + 3]
+    ct_v, br_v, c_sem, b_sem, t_sem = refs[2 * n_t + 3 :]
+    takes = [pltpu.make_async_copy(c_parts[k], ct_v.at[k], c_sem.at[k]) for k in range(n_t)]
+    takes += [pltpu.make_async_copy(b_parts[k], br_v.at[k], b_sem.at[k]) for k in range(n_t)]
+    for copy in takes:
+        copy.start()
     gives = []
     for k in range(n_t):
         takes[k].wait()
+        takes[n_t + k].wait()
         chunk = pl.multiple_of(scalars[dm.at_c + k], dm.chunk_rows)
+        gives.append(
+            pltpu.make_async_copy(ct_v.at[k], ct_hbm.at[pl.ds(chunk, dm.chunk_rows), :], t_sem.at[k])
+        )
+        gives[-1].start()
         for h in range(dm.chunk_rows // q):
-            at = pl.ds(pl.multiple_of(chunk + h * q, q), q)
-            sc = dot(ct_v[at, :], wo_out[...])
-            sc_v[at, :] = sc.astype(BF16)
-            prod = sc * sg_v[at, :].astype(F32)
-            dots = prod[:, :LANES]
-            for p in range(1, dm.pairs):
-                dots = dots + prod[:, p * LANES : (p + 1) * LANES]
+            dots = None
+            for c in range(dm.width // LANES):
+                g = slice(c * LANES, (c + 1) * LANES)
+                cot = ct_v[k, h * q : (h + 1) * q, g].astype(F32)
+                prod = cot * br_v[k, h, :, g].astype(F32)
+                dots = prod if dots is None else dots + prod
             blk = chunk // q + h
             sum_out[blk, 0:1, :] = sq_ref[blk]
             sum_out[blk, 1:2, :] = jnp.sum(dots.T, axis=0, keepdims=True)
-        at = pl.ds(chunk, dm.chunk_rows)
-        gives.append(pltpu.make_async_copy(sc_v.at[at, :], sc_hbm.at[at, :], o_sem.at[k]))
-        gives.append(pltpu.make_async_copy(ct_v.at[at, :], ct_hbm.at[at, :], t_sem.at[k]))
-        gives[-1].start()
-        gives[-2].start()
     for copy in gives:
         copy.wait()
 
 
-def branch_kernel(dm, scalars, w_ref, sg_ref, *refs):
-    outs, (buf, sem) = refs[: dm.n_t], refs[dm.n_t :]
-    per = dm.chunk_rows // BLOCK
-    for i in range(dm.blocks):
-        at = slice(i * BLOCK, (i + 1) * BLOCK)
-        buf[i] = dot(sg_ref[at, :], w_ref[...], MT).astype(BF16)
-        for k in range(dm.n_t):
-
-            @pl.when(scalars[dm.at_rel + i] == k)
-            def _():
-                pltpu.make_async_copy(buf.at[i], outs[k].at[i % per], sem.at[i]).start()
-
-    for i in range(dm.blocks):
-        pltpu.make_async_copy(buf.at[i], outs[0].at[0], sem.at[i]).wait()
-
-
 def gate_kernel(dm, scalars, *refs):
     q, ip, r = BLOCK, dm.ip, dm.part_rows
-    (w_ref, rk_ref, lane_ref, g_in, cv_in, ys_in, sc_in, nm_in, ct_in) = refs[:9]
-    dg_out, dy_out, lane_out, rows_out, own_out = refs[9:14]
-    z_outs = refs[14 : 13 + dm.n_hi]
-    acc, dg_s, both = refs[13 + dm.n_hi :]
+    (w_ref, wo_ref, rk_ref, lane_ref, g_in, cv_in, ys_in, cot_in, nm_in, ct_in) = refs[:10]
+    dg_out, dy_out, lane_out, rows_out, own_out = refs[10:15]
+    z_outs = refs[15 : 14 + dm.n_hi]
+    acc, dg_s, both = refs[14 + dm.n_hi :]
     i = pl.program_id(0)
 
     @pl.when(i == 0)
@@ -321,9 +324,10 @@
         pad = jnp.zeros((LANES - 2, q), F32)
         cols = jnp.concatenate([rk_ref[...], pad], axis=0).T
         root, pull = cols[:, 0:1], cols[:, 1:2]
+        scaled_cot = dot(cot_in[...], wo_ref[...])
         for p in range(dm.pairs):
             g = slice(p * LANES, (p + 1) * LANES)
-            gate, sc = g_in[:, g].astype(F32), sc_in[:, g].astype(F32)
+            gate, sc = g_in[:, g].astype(F32), scaled_cot[:, g]
             cv = cv_in[:, g].astype(F32)
             x = cv * sigmoid(cv)
             sig = sigmoid(gate)
@@ -370,12 +374,12 @@
     groups = dm.group_sizes
     w_ref, rows_ref, conv_ref, hp_ref, lane_ref, lanes_ref, gain_ref = refs[:7]
     dg_in, nm_in, dy_in, v_in, cv_in, ys_in, st_in, h_in = refs[7:15]
-    mine_out, theirs_out = refs[15:17]
-    nc_outs = refs[17 : 17 + len(groups)]
+    mine_out, theirs_out, kept_out = refs[15:18]
+    nc_outs = refs[18 : 18 + len(groups)]
     (dh_ref, dbuf, tri_ref, bias_ref, ds_ref, u_s, dx_s, act_s, t1_s, t2_s) = refs[
-        17 + len(groups) : 27 + len(groups)
+        18 + len(groups) : 28 + len(groups)
     ]
-    (pj_s, acc, tap_out, head_out, nc_buf, nc_sem) = refs[27 + len(groups) :]
+    (pj_s, acc, tap_out, head_out, nc_buf, nc_sem) = refs[28 + len(groups) :]
     i = pl.program_id(0)
     blk = jnp.maximum(dm.blocks - 1 - i, 0)
 
@@ -567,7 +571,9 @@
         small.extend([zero] * (late_cols // 16 - len(small)))
         for c in range(late_cols // LANES):
             g = slice(c * LANES, (c + 1) * LANES)
-            theirs_out[dm.n_hi * r :, g] = two_parts(jnp.concatenate(small[8 * c : 8 * c + 8], axis=0))
+            parts = two_parts(jnp.concatenate(small[8 * c : 8 * c + 8], axis=0))
+            theirs_out[dm.n_hi * r :, g] = parts
+            kept_out[:, g] = parts
         send(0, 1 - slot, 0).wait()
         send(0, slot, 0).wait()
 
@@ -652,8 +658,8 @@
 
     for k in range(4):
         tap_out[k : k + 1, :] = take(k * dm.pairs, inner)
-    tapb_out[...] = take(4 * dm.pairs, inner)
-    gain_out[...] = take(5 * dm.pairs, inner)
+    tapb_out[...] = take(4 * dm.pairs, inner)[0]
+    gain_out[...] = take(5 * dm.pairs, inner)[0]
     lane = lax.broadcasted_iota(jnp.int32, (1, LANES), 1)
     skip = jnp.zeros((1, LANES), F32)
     for h in range(heads):
@@ -661,9 +667,9 @@
         mine = lane // dm.hd == h % dm.per
         one = jnp.sum(jnp.where(mine, row, 0.0), axis=1, keepdims=True)
         skip = jnp.where(lane == h, one, skip)
-    skip_out[...] = skip[:, :heads]
-    sb_out[...] = flat[7 * dm.pairs][:, :heads]
-    dl_out[...] = (flat[7 * dm.pairs + 1] * hp_ref[1:2, :])[:, :heads]
+    skip_out[...] = skip[0, :heads]
+    sb_out[...] = flat[7 * dm.pairs][0, :heads]
+    dl_out[...] = (flat[7 * dm.pairs + 1] * hp_ref[1:2, :])[0, :heads]
     first = dm.local_rows // 8
     for c in range(st2 // LANES):
         g = slice((first + c) * LANES, (first + c + 1) * LANES)
@@ -689,9 +695,9 @@
     per = st2 // LANES
     for k in range(4):
         tap_out[k : k + 1, :] = jnp.concatenate(flat[k * per : (k + 1) * per], axis=1)
-    tapb_out[...] = jnp.concatenate(flat[4 * per : 5 * per], axis=1)
+    tapb_out[...] = jnp.concatenate(flat[4 * per : 5 * per], axis=1)[0]
     rows = flat[5 * per : 5 * per + dm.width // LANES]
-    norm_out[...] = jnp.concatenate(rows, axis=1) / norm_ref[...]
+    norm_out[...] = jnp.concatenate(rows, axis=1)[0] / norm_ref[...]
 
 
 def input_kernel(sets, steps, x_ref, cot_ref, gain_ref, *refs):
@@ -708,7 +714,7 @@
             nc = parts[0][...].astype(F32)
             for part in parts[1:]:
                 nc = nc + part[...].astype(F32)
-            hat = nc * gain_ref[...]
+            hat = nc * gain_ref[...][None]
             mean = jnp.mean(hat * x, axis=1, keepdims=True)
             out[...] = cot_ref[...].astype(F32) + root * hat - x * (root * root * root * mean)
 
@@ -782,7 +788,6 @@
     def out(*shape, dtype=F32):
         return jax.ShapeDtypeStruct(shape, dtype)
 
-    gain = norm_gain.reshape(1, width)
     part = min(LANES, dm.piece_rows)
     normed = pl.pallas_call(
         functools.partial(norm_kernel, part),
@@ -794,7 +799,7 @@
         ],
         compiler_params=pltpu.CompilerParams(vmem_limit_bytes=limit),
         name="normalize",
-    )(block_input, gain)
+    )(block_input, norm_gain)
     if dm.halves == 2:
         a, b = normed
         xa, yb = across(a, 1), across(b, 2)
@@ -806,11 +811,12 @@
     else:
         n_list = [normed[0]] + [across(normed[0], k) for k in range(1, n_t)]
         n_rows = (me_t ^ jnp.arange(n_t)) * chunk_rows
+    step_first, _ = lax.optimization_barrier((step_proj.T, normed[0]))
     packed = pl.pallas_call(
         functools.partial(pack_kernel, dm),
         out_shape=out(part_rows, dm.np, dtype=BF16),
         name="pack_weights",
-    )(gate_proj, value_proj, shared_proj, step_proj.T)
+    )(gate_proj, value_proj, shared_proj, step_first)
     w_list = [packed] + [along(packed, k) for k in range(1, n_hi)]
     w_list = w_list + [partner(v) for v in w_list]
     outp = pad_cols(output_proj.T, ip)
@@ -949,25 +955,39 @@
 
     c_list = [out_cotangent] + [across(out_cotangent, k) for k in range(1, n_t)]
     in_vmem = pl.BlockSpec(memory_space=pltpu.VMEM)
-    sc, sums, cot_all, w_back = pl.pallas_call(
-        functools.partial(cotangent_kernel, dm),
-        out_shape=[
-            out(length, ip, dtype=BF16),
-            out(nb, 2, q),
-            out(length, width, dtype=BF16),
-            out(width, ip, dtype=BF16),
-        ],
+    w_back, *branch = pl.pallas_call(
+        functools.partial(branch_kernel, dm),
+        out_shape=[out(width, ip, dtype=BF16)]
+        + [out(chunk_rows // q, q, width, dtype=BF16)] * n_t,
         grid_spec=grid(
             1,
-            [hbm] * (n_t + n_dp + 1) + [in_vmem],
-            [hbm, in_vmem, hbm, in_vmem],
+            [hbm] * (n_dp + 1),
+            [in_vmem] + [hbm] * n_t,
             [
-                vmem((length, width), BF16),
                 vmem((length, ip), BF16),
-                vmem((length, ip), BF16),
-                pltpu.SemaphoreType.DMA((n_t,)),
+                vmem((nb, q, width), BF16),
                 pltpu.SemaphoreType.DMA((n_dp,)),
                 pltpu.SemaphoreType.DMA,
+                pltpu.SemaphoreType.DMA((nb,)),
+            ],
+        ),
+        compiler_params=params,
+        cost_estimate=pl.CostEstimate(
+            flops=3_000_000_000, bytes_accessed=10_000_000, transcendentals=0
+        ),
+        name="branch_output",
+    )(scalars, *o_list, scaled)
+    sums, cot_all = pl.pallas_call(
+        functools.partial(dots_kernel, dm),
+        out_shape=[out(nb, 2, q), out(length, width, dtype=BF16)],
+        grid_spec=grid(
+            1,
+            [hbm] * (2 * n_t) + [in_vmem],
+            [in_vmem, hbm],
+            [
+                vmem((n_t, chunk_rows, width), BF16),
+                vmem((n_t, chunk_rows // q, q, width), BF16),
+                pltpu.SemaphoreType.DMA((n_t,)),
                 pltpu.SemaphoreType.DMA((n_t,)),
                 pltpu.SemaphoreType.DMA((n_t,)),
             ],
@@ -976,26 +996,11 @@
         cost_estimate=pl.CostEstimate(
             flops=3_000_000_000, bytes_accessed=10_000_000, transcendentals=0
         ),
-        name="branch_cotangent",
-    )(scalars, *c_list, *o_list, scaled, squares)
+        name="branch_dots",
+    )(scalars, *c_list, *branch, squares)
     total = sums
     for k in range(1, n_t):
         total = total + across(sums, k)
-    branch = pl.pallas_call(
-        functools.partial(branch_kernel, dm),
-        out_shape=[out(chunk_rows // q, q, width, dtype=BF16)] * n_t,
-        grid_spec=grid(
-            1,
-            [in_vmem, in_vmem],
-            [hbm] * n_t,
-            [vmem((nb, q, width), BF16), pltpu.SemaphoreType.DMA((nb,))],
-        ),
-        compiler_params=params,
-        cost_estimate=pl.CostEstimate(
-            flops=3_000_000_000, bytes_accessed=10_000_000, transcendentals=0
-        ),
-        name="branch_output",
-    )(scalars, w_back, scaled)
     root = lax.rsqrt(total[:, 0] / (inner * n_t) + EPS)
     pull = root * root * root * (total[:, 1] / (inner * n_t))
     rk = jnp.stack([root, pull], axis=1)
@@ -1031,12 +1036,13 @@
             nb + 1,
             [
                 const(width, ip),
+                const(width, ip),
                 pl.BlockSpec((None, 2, q), lambda i, s: (jnp.minimum(i, nb - 1), 0, 0)),
                 const(8, ip),
                 now(ip),
                 now(ip),
                 now(ip),
-                now(ip),
+                now(width),
                 ago(width),
                 ago(width),
             ],
@@ -1049,13 +1055,17 @@
             flops=6_000_000_000, bytes_accessed=20_000_000, transcendentals=0
         ),
         name="gate_backward",
-    )(scalars, weights, rk, per_lane, gate, conved, scan, sc, normed_all, cot_all)
+    )(scalars, weights, w_back, rk, per_lane, gate, conved, scan, cot_all, normed_all, cot_all)
     early = [along(v, k + 1) for k, v in enumerate(early)]
 
     r_all = n_hi * part_rows
-    mine, theirs, *nc = pl.pallas_call(
+    mine, theirs, kept, *nc = pl.pallas_call(
         functools.partial(backward_kernel, dm),
-        out_shape=[out(r_all, dm.late), out(r_all + 16, dm.late, dtype=BF16)]
+        out_shape=[
+            out(r_all, dm.late),
+            out(r_all + 16, dm.late, dtype=BF16),
+            out(16, dm.late, dtype=BF16),
+        ]
         + [out(k, q, width, dtype=BF16) for k in dm.group_sizes],
         grid_spec=grid(
             nb + 1,
@@ -1076,7 +1086,8 @@
                 bblock(LANES),
                 pl.BlockSpec((state, ip), lambda i, s: (jnp.maximum(nb - 1 - i, 0), 0)),
             ],
-            [const(r_all, dm.late), const(r_all + 16, dm.late)] + [hbm] * len(dm.group_sizes),
+            [const(r_all, dm.late), const(r_all + 16, dm.late), const(16, dm.late)]
+            + [hbm] * len(dm.group_sizes),
             [
                 vmem((state, ip), F32),
                 vmem((q + 8, vs), F32),
@@ -1150,14 +1161,13 @@
         functools.partial(input_kernel, sets, steps),
         out_shape=out(chunk_rows, width),
         grid=(len(sets) * steps,),
-        in_specs=[in_turn, in_turn, pl.BlockSpec((1, width), lambda i: (0, 0))] + specs,
+        in_specs=[in_turn, in_turn, pl.BlockSpec((width,), lambda i: (0,))] + specs,
         out_specs=in_turn,
         compiler_params=params,
         name="input_gradient",
-    )(block_input, out_cotangent, gain, *terms)
+    )(block_input, out_cotangent, norm_gain, *terms)
 
     late = dm.late
-    kept = theirs[r_all:]
     theirs = partner(theirs)
     own, own_small, *others = pl.pallas_call(
         functools.partial(pair_kernel, dm),
@@ -1199,11 +1209,11 @@
             out(part_rows, inner),
             out(part_rows + 16, 2 * state, dtype=BF16),
             out(4, inner),
-            out(1, inner),
-            out(1, inner),
-            out(1, heads),
-            out(1, heads),
-            out(1, heads),
+            out(inner),
+            out(inner),
+            out(heads),
+            out(heads),
+            out(heads),
         ],
         grid_spec=grid(1, [in_vmem] * (n_hi + 4), [in_vmem] * 11, [vmem((n_hi, 8, late), F32)]),
         compiler_params=params,
@@ -1212,7 +1222,7 @@
     shares = [share] + [across(share, k) for k in range(1, n_t)]
     shared_proj_grad, conv_shared_weight_grad, conv_shared_bias_grad, norm_gain_grad = pl.pallas_call(
         functools.partial(share_kernel, dm),
-        out_shape=[out(part_rows, 2 * state), out(4, 2 * state), out(1, 2 * state), out(1, width)],
+        out_shape=[out(part_rows, 2 * state), out(4, 2 * state), out(2 * state), out(width)],
         grid_spec=grid(
             1,
             [in_vmem] * (n_t + 1),
@@ -1221,23 +1231,23 @@
         ),
         compiler_params=params,
         name="shared_sum",
-    )(scalars, gain, *shares)
+    )(scalars, norm_gain, *shares)
     return (
         block_output,
         input_grad,
-        norm_gain_grad.reshape(width),
+        norm_gain_grad,
         gate_proj_grad,
         value_proj_grad,
         shared_proj_grad,
         step_t.T,
         conv_value_weight_grad,
-        conv_value_bias_grad.reshape(inner),
+        conv_value_bias_grad,
         conv_shared_weight_grad,
-        conv_shared_bias_grad.reshape(2 * state),
-        step_bias_grad.reshape(heads),
-        decay_log_grad.reshape(heads),
-        skip_weight_grad.reshape(heads),
-        gate_gain_grad.reshape(inner),
+        conv_shared_bias_grad,
+        step_bias_grad,
+        decay_log_grad,
+        skip_weight_grad,
+        gate_gain_grad,
         outp_t.T,
     )
 

time: 248 us -> 244 us (0.984)
  other arithmetic: 13.7 us -> 8.85 us
  waiting for transfers between devices: 62.4 us -> 65.9 us
    ppermute x12, waiting for transfers between devices: 20.8 us -> 25.6 us  [along(): return lax.ppermute(v, 'dp', shift_hi(n_dp, k))]
  transfers between devices with their start and end apart: 44 -> 44, of which waited for: 14 -> 16; matrix products, arithmetic and copies ran while one was open for 8% -> 5% of each run, Pallas kernels for 19% -> 19%
where the time goes in v2:
time: 244 us; the launch traced here: 243 us
  Pallas kernels  112 us (46%)
  waiting for transfers between devices  65.9 us (27%)
  starting transfers between devices  47.6 us (20%)
  other arithmetic  8.85 us (4%)
  local copies, waits for them, and re-layouts  7.79 us (3%)
    ppermute x22, waiting for transfers between devices, across(): return lax.ppermute(v, 'tensor', swap(n_t, k))  39 us
    pallas_call x1, Pallas kernels, body(): pl.pallas_call(functools.partial(backward_kernel, dm), out_shape=[out(r_a...  37.9 us
    ppermute x22, starting transfers between devices, across(): return lax.ppermute(v, 'tensor', swap(n_t, k))  26.3 us
    ppermute x12, waiting for transfers between devices, along(): return lax.ppermute(v, 'dp', shift_hi(n_dp, k))  25.6 us
    pallas_call x1, Pallas kernels, body(): pl.pallas_call(functools.partial(forward_kernel, dm), out_shape=[out(leng...  25.1 us
    ppermute x12, starting transfers between devices, along(): return lax.ppermute(v, 'dp', shift_hi(n_dp, k))  20.1 us
    pallas_call x1, Pallas kernels, body(): pl.pallas_call(functools.partial(gate_kernel, dm), out_shape=[out(length,...  16 us
    pallas_call x1, Pallas kernels, body(): pl.pallas_call(functools.partial(dots_kernel, dm), out_shape=[out(nb, 2,...  6.45 us
  transfers between devices with their start and end apart: 44, of which 16 were waited for; matrix products, arithmetic and copies ran while one was open for 5% of the time, Pallas kernels for 19%

profile of v2, /device:TPU:0, one launch (start us, length us, event | category | flops | bytes accessed | tf_op | source)
XLA Modules:
  0.0 243.0 jit_solution(5189559586226889669)
XLA Ops:
  0.8 3.1 %collective-permute-start.3 = (bf16[96,384]{1,0:T(8,128)(2,1)}, bf16[96,384]{1,0:T(8,128)(2,1)S(1)}, u32[]{:S(2)}, u32[]{:S(2)}) collective-permute-start(bf16[96,384]{1,0:T(8,128)(2,1)} %bitcast.65), channel_id=1, source_target_pairs={{0,8},{4,12},{8,16},{12,20},{16,24},{20,28},{24,0},{28,4},{1,9},{5... | collective-permute-start | bytes 221192 | tf_op jit(solution)/shard_map/ppermute | solution.py:776
  3.9 2.6 %collective-permute-start.4 = (bf16[96,384]{1,0:T(8,128)(2,1)}, bf16[96,384]{1,0:T(8,128)(2,1)S(1)}, u32[]{:S(2)}, u32[]{:S(2)}) collective-permute-start(bf16[96,384]{1,0:T(8,128)(2,1)} %bitcast.66), channel_id=1, source_target_pairs={{0,16},{4,20},{8,24},{12,28},{16,0},{20,4},{24,8},{28,12},{1,17},{... | collective-permute-start | bytes 221192 | tf_op jit(solution)/shard_map/ppermute | solution.py:776
  6.5 1.3 collective-permute-start.5
  7.8 3.0 %normalize.1 = (bf16[256,768]{1,0:T(8,128)(2,1)}, bf16[256,768]{1,0:T(8,128)(2,1)}) custom-call(f32[512,768]{1,0:T(8,128)} %x_ref.1, f32[768]{0:T(1024)} %norm_ref.1), custom_call_target="tpu_custom_call" | custom-call | tf_op jit(solution)/shard_map/normalize/pallas_call | solution.py:792
  10.8 1.8 pack_weights.1.refs_0_
  12.6 0.7 collective-permute-start.10
  13.8 0.7 fusion.33
  15.7 1.5 collective-permute-start.17
  17.2 1.5 collective-permute-start.20
  18.8 1.2 collective-permute-done.7.refs_5_
  20.1 2.9 %collective-permute-start.12 = (bf16[96,1152]{1,0:T(8,128)(2,1)}, bf16[96,1152]{1,0:T(8,128)(2,1)S(1)}, u32[]{:S(2)}, u32[]{:S(2)}) collective-permute-start(bf16[96,1152]{1,0:T(8,128)(2,1)} %pack_weights.1.refs_0_), channel_id=1, source_target_pairs={{0,24},{4,28},{8,0},{12,4},{16,8},{20,12},{24,16},{28,20},{1,25},{... | collective-permute-start | bytes 663560 | tf_op jit(solution)/shard_map/ppermute | solution.py:776
  23.0 1.5 collective-permute-start.18
  24.5 7.5 %collective-permute-done.11.refs_2_ = bf16[96,1152]{1,0:T(8,128)(2,1)S(1)} collective-permute-done((bf16[96,1152]{1,0:T(8,128)(2,1)}, bf16[96,1152]{1,0:T(8,128)(2,1)S(1)}, u32[]{:S(2)}, u32[]{:S(2)}) %collective-permute-start.11) | collective-permute-done | bytes 221216 | tf_op jit(solution)/shard_map/ppermute | solution.py:776
  32.0 1.5 collective-permute-start.19
  34.7 1.1 collective-permute-start.22
  35.8 0.7 gather_fusion
  36.5 0.7 gather_fusion.1
  37.3 1.4 concatenate.38.refs_16_.refs_1_
  38.7 0.6 concatenate.35.scalars
  39.3 0.6 select_maximum_fusion.2.refs_19_.refs_3_.refs_4_
  40.5 3.8 %collective-permute-done.19.refs_12_ = bf16[256,768]{1,0:T(8,128)(2,1)S(1)} collective-permute-done((bf16[256,768]{1,0:T(8,128)(2,1)}, bf16[256,768]{1,0:T(8,128)(2,1)S(1)}, u32[]{:S(2)}, u32[]{:S(2)}) %collective-permute-start.19) | collective-permute-done | bytes 393248 | tf_op jit(solution)/shard_map/ppermute | solution.py:773
  44.2 0.6 select_maximum_fusion.3.refs_18_.refs_3_.hp_ref
  44.9 0.6 fusion.3.refs_17_.refs_2_
  45.5 1.6 collective-permute-start
  47.1 1.6 collective-permute-start.1
  49.3 3.5 %collective-permute-done.21.refs_14_ = bf16[256,768]{1,0:T(8,128)(2,1)} collective-permute-done((bf16[256,768]{1,0:T(8,128)(2,1)S(1)}, bf16[256,768]{1,0:T(8,128)(2,1)}, u32[]{:S(2)}, u32[]{:S(2)}) %collective-permute-start.21) | collective-permute-done | bytes 393248 | tf_op jit(solution)/shard_map/ppermute | solution.py:773
  53.3 25.1 %block_forward.1 = (bf16[2048,384]{1,0:T(8,128)(2,1)}, bf16[2048,640]{1,0:T(8,128)(2,1)}, bf16[2048,640]{1,0:T(8,128)(2,1)}, f32[2048,384]{1,0:T(8,128)}, f32[20...) custom-call(s32[65]{0:T(128)} %concatenate.35.scalars, ...), custom_call_target="tpu_custom_call" | custom-call | flops 30000001024 | bytes 30000000 | tf_op jit(solution)/shard_map/block_forward/pallas_call | solution.py:901
  78.4 0.6 copy-done.47
  79.0 6.1 %branch_output.1 = (bf16[768,384]{1,0:T(8,128)(2,1)}, bf16[2,256,768]{2,1,0:T(8,128)(2,1)}, bf16[2,256,768]{2,1,0:T(8,128)(2,1)}, bf16[2,256,768]{2,1,0:T(8,128)(2,1)}, bf16[2,256,768]{2,1,0:T(8,128)(2,1)}) custom-call(s32[65]{0:T(128)} %concatenate.35.scalars, bf16[96,384]{1,0:T(8,128)(2,1)} %bitcast.69, bf16[96,384]{1,0:T(8,128)(2,1)} %copy-done.42, ...), custom_call_target="tpu_custom_call" | custom-call | flops 3000000000 | bytes 10000000 | tf_op jit(solution)/shard_map/branch_output/pallas_call | solution.py:958
  85.4 0.6 copy-done.25
  86.6 6.5 %branch_dots.1 = (f32[8,2,256]{2,1,0:T(2,128)}, bf16[2048,768]{1,0:T(8,128)(2,1)}) custom-call(s32[65]{0:T(128)} %concatenate.35.scalars, bf16[512,768]{1,0:T(8,128)(2,1)} %cot_ref.1, bf16[512,768]{1,0:T(8,128)(2,1)} %copy-done.25, bf16[512,768]{1,0:T(8,128)(2,1)} %copy-done.26, bf16[512,768]{1,0:T(8,128)(2,1)} %copy-done.27, ...), custom_call_target="tpu_custom_call" | custom-call | flops 3000000000 | bytes 10000000 | tf_op jit(solution)/shard_map/branch_dots/pallas_call | solution.py:980
  93.0 2.6 %collective-permute-start.25 = (f32[8,2,256]{2,1,0:T(2,128)}, f32[8,2,256]{2,1,0:T(2,128)S(1)}, u32[]{:S(2)}, u32[]{:S(2)}) collective-permute-start(f32[8,2,256]{2,1,0:T(2,128)} %get-tuple-element.81), channel_id=1, source_target_pairs={{0,3},{1,2},{2,1},{3,0},{4,7},{5,6},{6,5},{7,4},{8,11},{9,10},{10,... | collective-permute-start | bytes 49160 | tf_op jit(solution)/shard_map/ppermute | solution.py:773
  96.6 1.4 collective-permute-done.25
  97.9 1.6 collective-permute-done.24
  100.0 0.7 add_add_fusion
  100.8 0.6 pad_maximum_fusion.refs_2_
  101.4 16.0 %gate_backward.1 = (bf16[2048,384]{1,0:T(8,128)(2,1)}, bf16[2048,384]{1,0:T(8,128)(2,1)}, f32[16,384]{1,0:T(8,128)}, f32[8,768]{1,0:T(8,128)}, f32[192,768]{1,0:...) custom-call(s32[65]{0:T(128)} %concatenate.35.scalars, ...), custom_call_target="tpu_custom_call" | custom-call | flops 6000000000 | bytes 20000000 | tf_op jit(solution)/shard_map/gate_backward/pallas_call | solution.py:1025
  117.4 37.9 %block_backward.1 = (f32[384,768]{1,0:T(8,128)}, bf16[400,768]{1,0:T(8,128)(2,1)}, bf16[16,768]{1,0:T(8,128)(2,1)}, bf16[2,256,768]{2,1,0:T(8,128)(2,1)}, bf16[2...) custom-call(s32[65]{0:T(128)} %concatenate.35.scalars, bf16[768,1152]{1,0:T(8,128)(2,1)} %get-tuple-element.82.refs_0_, ...), custom_call_target="tpu_custom_call" | custom-call | flops 40000000000 | bytes 30000000 | tf_op jit(solution)/shard_map/block_backward/pallas_call | solution.py:1062
  155.4 1.9 collective-permute-start.34
  157.3 3.3 %collective-permute-start.35 = (bf16[192,768]{1,0:T(8,128)(2,1)}, bf16[192,768]{1,0:T(8,128)(2,1)S(1)}, u32[]{:S(2)}, u32[]{:S(2)}) collective-permute-start(bf16[192,768]{1,0:T(8,128)(2,1)} %get-tuple-element.106), channel_id=1, source_target_pairs={{0,16},{4,20},{8,24},{12,28},{16,0},{20,4},{24,8},{28,12},{1,17},{... | collective-permute-start | bytes 884744 | tf_op jit(solution)/shard_map/ppermute | solution.py:776
  161.2 6.8 %collective-permute-done.34.refs_0_ = bf16[192,768]{1,0:T(8,128)(2,1)S(1)} collective-permute-done((bf16[192,768]{1,0:T(8,128)(2,1)S(1)}, bf16[192,768]{1,0:T(8,128)(2,1)S(1)}, u32[]{:S(2)}, u32[]{:S(2)}) %collective-permute-start.34) | collective-permute-done | bytes 294944 | tf_op jit(solution)/shard_map/ppermute | solution.py:776
  168.1 1.6 collective-permute-start.31
  169.6 10.8 %collective-permute-done.35.refs_1_ = bf16[192,768]{1,0:T(8,128)(2,1)S(1)} collective-permute-done((bf16[192,768]{1,0:T(8,128)(2,1)}, bf16[192,768]{1,0:T(8,128)(2,1)S(1)}, u32[]{:S(2)}, u32[]{:S(2)}) %collective-permute-start.35) | collective-permute-done | bytes 294944 | tf_op jit(solution)/shard_map/ppermute | solution.py:776
  180.4 1.5 collective-permute-start.28
  182.5 1.4 collective-permute-start.26
  184.0 3.1 %early_sum.1 = (f32[96,768]{1,0:T(8,128)}, bf16[96,768]{1,0:T(8,128)(2,1)}) custom-call(s32[65]{0:T(128)} %concatenate.35.scalars, f32[192,768]{1,0:T(8,128)} %get-tuple-element.104.own_ref, bf16[192,768]{1,0:T(8,128)(2,1)} %copy-done.9, bf16[192,768]{1,0:T(8,128)(2,1)} %copy-done.10, bf16[192,768]{1,0:T(8,128)(2,1)} %copy-done.11), custom_call_target="tpu_custom_call" | custom-call | tf_op jit(solution)/shard_map/early_sum/pallas_call | solution.py:1181
  187.1 3.2 %core_sum.1 = (f32[96,768]{1,0:T(8,128)}, bf16[16,768]{1,0:T(8,128)(2,1)}, bf16[112,768]{1,0:T(8,128)(2,1)}, bf16[112,768]{1,0:T(8,128)(2,1)}, bf16[112,768]{1,0:T(8,128)(2,1)}) custom-call(s32[65]{0:T(128)} %concatenate.35.scalars, f32[384,768]{1,0:T(8,128)} %get-tuple-element.99.mine_ref, bf16[16,768]{1,0:T(8,128)(2,1)} %get-tuple-element.100.kept_ref, ...), custom_call_target="tpu_custom_call" | custom-call | tf_op jit(solution)/shard_map/core_sum/pallas_call | solution.py:1172
  190.4 15.1 %collective-permute-done.31.refs_4_ = bf16[2,256,768]{2,1,0:T(8,128)(2,1)S(1)} collective-permute-done((bf16[2,256,768]{2,1,0:T(8,128)(2,1)}, bf16[2,256,768]{2,1,0:T(8,128)(2,1)S(1)}, u32[]{:S(2)}, u32[]{:S(2)}) %collective-permute-start.31) | collective-permute-done | bytes 786464 | tf_op jit(solution)/shard_map/ppermute | solution.py:773
  205.6 1.1 fusion.2
  206.7 1.0 collective-permute-start.39
  207.7 2.9 %collective-permute-start.40 = (bf16[112,768]{1,0:T(8,128)(2,1)S(1)}, bf16[112,768]{1,0:T(8,128)(2,1)}, u32[]{:S(2)}, u32[]{:S(2)}) collective-permute-start(bf16[112,768]{1,0:T(8,128)(2,1)S(1)} %copy-done.39), channel_id=1, source_target_pairs={{0,24},{4,28},{8,0},{12,4},{16,8},{20,12},{24,16},{28,20},{1,25},{... | collective-permute-start | bytes 516104 | tf_op jit(solution)/shard_map/ppermute | solution.py:776
  210.6 10.5 %collective-permute-done.27 = bf16[2,256,768]{2,1,0:T(8,128)(2,1)} collective-permute-done((bf16[2,256,768]{2,1,0:T(8,128)(2,1)}, bf16[2,256,768]{2,1,0:T(8,128)(2,1)}, u32[]{:S(2)}, u32[]{:S(2)}) %collective-permute-start.27) | collective-permute-done | bytes 786464 | tf_op jit(solution)/shard_map/ppermute | solution.py:773
  221.1 1.6 collective-permute-start.30
  223.3 2.1 convert_add_fusion
  225.4 0.6 copy-done.12
  226.1 2.8 %gradient_sum.1 = (f32[96,384]{1,0:T(8,128)}, f32[96,384]{1,0:T(8,128)}, f32[6,96]{1,0:T(8,128)}, f32[96,384]{1,0:T(8,128)}, bf16[112,256]{1,0:T(8,128)(2,1)}, /...) custom-call(s32[65]{0:T(128)} %concatenate.35.scalars, ...), custom_call_target="tpu_custom_call" | custom-call | tf_op jit(solution)/shard_map/gradient_sum/pallas_call | solution.py:1203
  228.9 1.6 collective-permute-start.41
  230.9 1.5 collective-permute-start.43
  232.5 1.4 fusion
  234.2 0.6 collective-permute-done.42.refs_2_
  234.9 1.4 collective-permute-done.43.refs_3_
  236.2 0.6 copy-done.17
  236.8 2.3 shared_sum.1
  239.1 3.9 %input_gradient.1 = f32[512,768]{1,0:T(8,128)} custom-call(f32[512,768]{1,0:T(8,128)} %x_ref.1, bf16[512,768]{1,0:T(8,128)(2,1)} %cot_ref.1, f32[768]{0:T(1024)} %norm_ref.1, bf16[4,256,768]{2,1,0:T(8,128)(2,1)} %get-tuple-element.96.refs_0_.refs_3_, bf16[2,256,768]{2,1,0:T(8,128)(2,1)} %copy-done.4, bf16[256,768]{1,0:T(8,128)(2,1)} %collective-permute-done.30.refs_2_, ...), custom_call_target="tpu_custom_call" | custom-call | tf_op jit(solution)/shard_map/input_gradient/pallas_call | solution.py:1160
  (177 shorter events, 9.8 us)
Async XLA Ops:
  0.6 35.2 %copy-start.1 = (s32[4,2]{1,0:T(4,128)S(1)}, s32[4,2]{1,0:T(4,128)}, u32[]{:S(2)}) copy-start(s32[4,2]{1,0:T(4,128)} %constant.110.clone) | copy-start | bytes 100
  0.7 35.8 %copy-start = (s32[4,2]{1,0:T(4,128)S(1)}, s32[4,2]{1,0:T(4,128)}, u32[]{:S(2)}) copy-start(s32[4,2]{1,0:T(4,128)} %constant.111.clone) | copy-start | bytes 100
  0.7 32.9 %copy-start.24 = (f32[6]{0:T(128)S(1)}, f32[6]{0:T(128)}, u32[]{:S(2)}) copy-start(f32[6]{0:T(128)} %param.30) | copy-start | bytes 76
  0.7 36.4 %copy-start.20 = (f32[384]{0:T(512)S(1)}, f32[384]{0:T(512)}, u32[]{:S(2)}) copy-start(f32[384]{0:T(512)} %param.27) | copy-start | bytes 4612
  0.7 36.4 %copy-start.21 = (f32[384]{0:T(512)S(1)}, f32[384]{0:T(512)}, u32[]{:S(2)}) copy-start(f32[384]{0:T(512)} %param.33) | copy-start | bytes 4612
  0.7 36.4 %copy-start.23 = (f32[6]{0:T(128)S(1)}, f32[6]{0:T(128)}, u32[]{:S(2)}) copy-start(f32[6]{0:T(128)} %param.32) | copy-start | bytes 76
  0.7 44.2 %copy-start.18 = (f32[4,384]{1,0:T(4,128)S(1)}, f32[4,384]{1,0:T(4,128)}, u32[]{:S(2)}) copy-start(f32[4,384]{1,0:T(4,128)} %param.26) | copy-start | bytes 18436
  0.7 44.2 %copy-start.19 = (f32[4,256]{1,0:T(4,128)S(1)}, f32[4,256]{1,0:T(4,128)}, u32[]{:S(2)}) copy-start(f32[4,256]{1,0:T(4,128)} %param.28) | copy-start | bytes 12292
  0.8 44.1 %copy-start.22 = (f32[256]{0:T(256)S(1)}, f32[256]{0:T(256)}, u32[]{:S(2)}) copy-start(f32[256]{0:T(256)} %param.29) | copy-start | bytes 3076
  0.8 44.8 %copy-start.6 = (bf16[512,768]{1,0:T(8,128)(2,1)S(1)}, bf16[512,768]{1,0:T(8,128)(2,1)}, u32[]{:S(2)}) copy-start(bf16[512,768]{1,0:T(8,128)(2,1)} %cot_ref.1) | copy-start | bytes 2359300
  0.8 14.5 %collective-permute-start.3 = (bf16[96,384]{1,0:T(8,128)(2,1)}, bf16[96,384]{1,0:T(8,128)(2,1)S(1)}, u32[]{:S(2)}, u32[]{:S(2)}) collective-permute-start(bf16[96,384]{1,0:T(8,128)(2,1)} %bitcast.65), channel_id=1, source_target_pairs={{0,8},{4,12},{8,16},{12,20},{16,24},{20,28},{24,0},{28,4},{1,9},{5... | collective-permute-start | bytes 221192 | tf_op jit(solution)/shard_map/ppermute | solution.py:776
  3.9 11.8 %collective-permute-start.4 = (bf16[96,384]{1,0:T(8,128)(2,1)}, bf16[96,384]{1,0:T(8,128)(2,1)S(1)}, u32[]{:S(2)}, u32[]{:S(2)}) collective-permute-start(bf16[96,384]{1,0:T(8,128)(2,1)} %bitcast.66), channel_id=1, source_target_pairs={{0,16},{4,20},{8,24},{12,28},{16,0},{20,4},{24,8},{28,12},{1,17},{... | collective-permute-start | bytes 221192 | tf_op jit(solution)/shard_map/ppermute | solution.py:776
  6.5 10.8 %collective-permute-start.5 = (bf16[96,384]{1,0:T(8,128)(2,1)}, bf16[96,384]{1,0:T(8,128)(2,1)S(1)}, u32[]{:S(2)}, u32[]{:S(2)}) collective-permute-start(bf16[96,384]{1,0:T(8,128)(2,1)} %bitcast.67), channel_id=1, source_target_pairs={{0,24},{4,28},{8,0},{12,4},{16,8},{20,12},{24,16},{28,20},{1,25},{... | collective-permute-start | bytes 221192 | tf_op jit(solution)/shard_map/ppermute | solution.py:776
  7.8 10.9 %collective-permute-start.6 = (bf16[96,384]{1,0:T(8,128)(2,1)}, bf16[96,384]{1,0:T(8,128)(2,1)S(1)}, u32[]{:S(2)}, u32[]{:S(2)}) collective-permute-start(bf16[96,384]{1,0:T(8,128)(2,1)} %bitcast.68), channel_id=1, source_target_pairs={{0,4},{4,0},{8,12},{12,8},{16,20},{20,16},{24,28},{28,24},{1,5},{5... | collective-permute-start | bytes 221192 | tf_op jit(solution)/shard_map/ppermute | solution.py:779
  12.6 10.4 %collective-permute-start.10 = (bf16[96,1152]{1,0:T(8,128)(2,1)}, bf16[96,1152]{1,0:T(8,128)(2,1)S(1)}, u32[]{:S(2)}, u32[]{:S(2)}) collective-permute-start(bf16[96,1152]{1,0:T(8,128)(2,1)} %pack_weights.1.refs_0_), channel_id=1, source_target_pairs={{0,8},{4,12},{8,16},{12,20},{16,24},{20,28},{24,0},{28,4},{1,9},{5... | collective-permute-start | bytes 663560 | tf_op jit(solution)/shard_map/ppermute | solution.py:776
  15.3 16.7 %collective-permute-start.11 = (bf16[96,1152]{1,0:T(8,128)(2,1)}, bf16[96,1152]{1,0:T(8,128)(2,1)S(1)}, u32[]{:S(2)}, u32[]{:S(2)}) collective-permute-start(bf16[96,1152]{1,0:T(8,128)(2,1)} %pack_weights.1.refs_0_), channel_id=1, source_target_pairs={{0,16},{4,20},{8,24},{12,28},{16,0},{20,4},{24,8},{28,12},{1,17},{... | collective-permute-start | bytes 663560 | tf_op jit(solution)/shard_map/ppermute | solution.py:776
  15.7 18.3 %collective-permute-start.17 = (bf16[256,768]{1,0:T(8,128)(2,1)}, bf16[256,768]{1,0:T(8,128)(2,1)S(1)}, u32[]{:S(2)}, u32[]{:S(2)}) collective-permute-start(bf16[256,768]{1,0:T(8,128)(2,1)} %get-tuple-element.72.refs_8_), channel_id=1, source_target_pairs={{0,1},{1,0},{2,3},{3,2},{4,5},{5,4},{6,7},{7,6},{8,9},{9,8},{10,11... | collective-permute-start | bytes 1179656 | tf_op jit(solution)/shard_map/ppermute | solution.py:773
  17.2 17.4 %collective-permute-start.20 = (bf16[256,768]{1,0:T(8,128)(2,1)}, bf16[256,768]{1,0:T(8,128)(2,1)}, u32[]{:S(2)}, u32[]{:S(2)}) collective-permute-start(bf16[256,768]{1,0:T(8,128)(2,1)} %get-tuple-element.74.refs_9_), channel_id=1, source_target_pairs={{0,2},{1,3},{2,0},{3,1},{4,6},{5,7},{6,4},{7,5},{8,10},{9,11},{10,... | collective-permute-start | bytes 1179656 | tf_op jit(solution)/shard_map/ppermute | solution.py:773
  18.8 1.3 collective-permute-start.7
  20.1 14.0 %collective-permute-start.12 = (bf16[96,1152]{1,0:T(8,128)(2,1)}, bf16[96,1152]{1,0:T(8,128)(2,1)S(1)}, u32[]{:S(2)}, u32[]{:S(2)}) collective-permute-start(bf16[96,1152]{1,0:T(8,128)(2,1)} %pack_weights.1.refs_0_), channel_id=1, source_target_pairs={{0,24},{4,28},{8,0},{12,4},{16,8},{20,12},{24,16},{28,20},{1,25},{... | collective-permute-start | bytes 663560 | tf_op jit(solution)/shard_map/ppermute | solution.py:776
  23.0 24.1 %copy-start.33 = (bf16[96,1152]{1,0:T(8,128)(2,1)}, bf16[96,1152]{1,0:T(8,128)(2,1)S(1)}, u32[]{:S(2)}) copy-start(bf16[96,1152]{1,0:T(8,128)(2,1)S(1)} %collective-permute-done.10.refs_1_) | copy-start | bytes 663556
  23.0 16.9 %collective-permute-start.18 = (bf16[256,768]{1,0:T(8,128)(2,1)}, bf16[256,768]{1,0:T(8,128)(2,1)S(1)}, u32[]{:S(2)}, u32[]{:S(2)}) collective-permute-start(bf16[256,768]{1,0:T(8,128)(2,1)} %get-tuple-element.74.refs_9_), channel_id=1, source_target_pairs={{0,1},{1,0},{2,3},{3,2},{4,5},{5,4},{6,7},{7,6},{8,9},{9,8},{10,11... | collective-permute-start | bytes 1179656 | tf_op jit(solution)/shard_map/ppermute | solution.py:773
  32.0 12.2 %collective-permute-start.19 = (bf16[256,768]{1,0:T(8,128)(2,1)}, bf16[256,768]{1,0:T(8,128)(2,1)S(1)}, u32[]{:S(2)}, u32[]{:S(2)}) collective-permute-start(bf16[256,768]{1,0:T(8,128)(2,1)} %get-tuple-element.72.refs_8_), channel_id=1, source_target_pairs={{0,2},{1,3},{2,0},{3,1},{4,6},{5,7},{6,4},{7,5},{8,10},{9,11},{10,... | collective-permute-start | bytes 1179656 | tf_op jit(solution)/shard_map/ppermute | solution.py:773
  34.1 5.9 %collective-permute-start.13 = (bf16[96,1152]{1,0:T(8,128)(2,1)}, bf16[96,1152]{1,0:T(8,128)(2,1)S(1)}, u32[]{:S(2)}, u32[]{:S(2)}) collective-permute-start(bf16[96,1152]{1,0:T(8,128)(2,1)} %pack_weights.1.refs_0_), channel_id=1, source_target_pairs={{0,4},{4,0},{8,12},{12,8},{16,20},{20,16},{24,28},{28,24},{1,5},{5... | collective-permute-start | bytes 663560 | tf_op jit(solution)/shard_map/ppermute | solution.py:779
  34.1 19.2 %copy-start.28 = (bf16[256,768]{1,0:T(8,128)(2,1)}, bf16[256,768]{1,0:T(8,128)(2,1)S(1)}, u32[]{:S(2)}) copy-start(bf16[256,768]{1,0:T(8,128)(2,1)S(1)} %collective-permute-done.17.refs_10_) | copy-start | bytes 1179652
  34.1 18.7 %collective-permute-start.21 = (bf16[256,768]{1,0:T(8,128)(2,1)S(1)}, bf16[256,768]{1,0:T(8,128)(2,1)}, u32[]{:S(2)}, u32[]{:S(2)}) collective-permute-start(bf16[256,768]{1,0:T(8,128)(2,1)S(1)} %collective-permute-done.17.refs_10_), channel_id=1, source_target_pairs={{0,2},{1,3},{2,0},{3,1},{4,6},{5,7},{6,4},{7,5},{8,10},{9,11},{10,... | collective-permute-start | bytes 1179656 | tf_op jit(solution)/shard_map/ppermute | solution.py:773
  34.7 18.1 %collective-permute-start.22 = (bf16[256,768]{1,0:T(8,128)(2,1)}, bf16[256,768]{1,0:T(8,128)(2,1)}, u32[]{:S(2)}, u32[]{:S(2)}) collective-permute-start(bf16[256,768]{1,0:T(8,128)(2,1)} %collective-permute-done.20.refs_13_), channel_id=1, source_target_pairs={{0,1},{1,0},{2,3},{3,2},{4,5},{5,4},{6,7},{7,6},{8,9},{9,8},{10,11... | collective-permute-start | bytes 1179656 | tf_op jit(solution)/shard_map/ppermute | solution.py:773
  39.9 5.6 %collective-permute-start.14 = (bf16[96,1152]{1,0:T(8,128)(2,1)S(1)}, bf16[96,1152]{1,0:T(8,128)(2,1)S(1)}, u32[]{:S(2)}, u32[]{:S(2)}) collective-permute-start(bf16[96,1152]{1,0:T(8,128)(2,1)S(1)} %collective-permute-done.10.refs_1_), channel_id=1, source_target_pairs={{0,4},{4,0},{8,12},{12,8},{16,20},{20,16},{24,28},{28,24},{1,5},{5... | collective-permute-start | bytes 663560 | tf_op jit(solution)/shard_map/ppermute | solution.py:779
  40.0 7.1 %collective-permute-start.15 = (bf16[96,1152]{1,0:T(8,128)(2,1)S(1)}, bf16[96,1152]{1,0:T(8,128)(2,1)S(1)}, u32[]{:S(2)}, u32[]{:S(2)}) collective-permute-start(bf16[96,1152]{1,0:T(8,128)(2,1)S(1)} %collective-permute-done.11.refs_2_), channel_id=1, source_target_pairs={{0,4},{4,0},{8,12},{12,8},{16,20},{20,16},{24,28},{28,24},{1,5},{5... | collective-permute-start | bytes 663560 | tf_op jit(solution)/shard_map/ppermute | solution.py:779
  44.2 4.5 %collective-permute-start.16 = (bf16[96,1152]{1,0:T(8,128)(2,1)S(1)}, bf16[96,1152]{1,0:T(8,128)(2,1)}, u32[]{:S(2)}, u32[]{:S(2)}) collective-permute-start(bf16[96,1152]{1,0:T(8,128)(2,1)S(1)} %collective-permute-done.12.refs_3_), channel_id=1, source_target_pairs={{0,4},{4,0},{8,12},{12,8},{16,20},{20,16},{24,28},{28,24},{1,5},{5... | collective-permute-start | bytes 663560 | tf_op jit(solution)/shard_map/ppermute | solution.py:779
  45.5 39.6 %collective-permute-start = (bf16[512,768]{1,0:T(8,128)(2,1)S(1)}, bf16[512,768]{1,0:T(8,128)(2,1)S(1)}, u32[]{:S(2)}, u32[]{:S(2)}) collective-permute-start(bf16[512,768]{1,0:T(8,128)(2,1)S(1)} %copy-done.6), channel_id=1, source_target_pairs={{0,1},{1,0},{2,3},{3,2},{4,5},{5,4},{6,7},{7,6},{8,9},{9,8},{10,11... | collective-permute-start | bytes 2359304 | tf_op jit(solution)/shard_map/ppermute | solution.py:773
  47.1 38.3 %collective-permute-start.1 = (bf16[512,768]{1,0:T(8,128)(2,1)S(1)}, bf16[512,768]{1,0:T(8,128)(2,1)S(1)}, u32[]{:S(2)}, u32[]{:S(2)}) collective-permute-start(bf16[512,768]{1,0:T(8,128)(2,1)S(1)} %copy-done.6), channel_id=1, source_target_pairs={{0,2},{1,3},{2,0},{3,1},{4,6},{5,7},{6,4},{7,5},{8,10},{9,11},{10,... | collective-permute-start | bytes 2359304 | tf_op jit(solution)/shard_map/ppermute | solution.py:773
  48.7 36.7 %collective-permute-start.2 = (bf16[512,768]{1,0:T(8,128)(2,1)S(1)}, bf16[512,768]{1,0:T(8,128)(2,1)S(1)}, u32[]{:S(2)}, u32[]{:S(2)}) collective-permute-start(bf16[512,768]{1,0:T(8,128)(2,1)S(1)} %copy-done.6), channel_id=1, source_target_pairs={{0,3},{1,2},{2,1},{3,0},{4,7},{5,6},{6,5},{7,4},{8,11},{9,10},{10,... | collective-permute-start | bytes 2359304 | tf_op jit(solution)/shard_map/ppermute | solution.py:773
  52.8 25.6 %collective-permute-start.8 = (bf16[96,384]{1,0:T(8,128)(2,1)}, bf16[96,384]{1,0:T(8,128)(2,1)S(1)}, u32[]{:S(2)}, u32[]{:S(2)}) collective-permute-start(bf16[96,384]{1,0:T(8,128)(2,1)} %copy-done.43), channel_id=1, source_target_pairs={{0,4},{4,0},{8,12},{12,8},{16,20},{20,16},{24,28},{28,24},{1,5},{5... | collective-permute-start | bytes 221192 | tf_op jit(solution)/shard_map/ppermute | solution.py:779
  52.8 25.6 %collective-permute-start.9 = (bf16[96,384]{1,0:T(8,128)(2,1)}, bf16[96,384]{1,0:T(8,128)(2,1)}, u32[]{:S(2)}, u32[]{:S(2)}) collective-permute-start(bf16[96,384]{1,0:T(8,128)(2,1)} %copy-done.44), channel_id=1, source_target_pairs={{0,4},{4,0},{8,12},{12,8},{16,20},{20,16},{24,28},{28,24},{1,5},{5... | collective-permute-start | bytes 221192 | tf_op jit(solution)/shard_map/ppermute | solution.py:779
  93.0 4.9 %collective-permute-start.25 = (f32[8,2,256]{2,1,0:T(2,128)}, f32[8,2,256]{2,1,0:T(2,128)S(1)}, u32[]{:S(2)}, u32[]{:S(2)}) collective-permute-start(f32[8,2,256]{2,1,0:T(2,128)} %get-tuple-element.81), channel_id=1, source_target_pairs={{0,3},{1,2},{2,1},{3,0},{4,7},{5,6},{6,5},{7,4},{8,11},{9,10},{10,... | collective-permute-start | bytes 49160 | tf_op jit(solution)/shard_map/ppermute | solution.py:773
  95.6 3.9 %collective-permute-start.24 = (f32[8,2,256]{2,1,0:T(2,128)}, f32[8,2,256]{2,1,0:T(2,128)S(1)}, u32[]{:S(2)}, u32[]{:S(2)}) collective-permute-start(f32[8,2,256]{2,1,0:T(2,128)} %get-tuple-element.81), channel_id=1, source_target_pairs={{0,2},{1,3},{2,0},{3,1},{4,6},{5,7},{6,4},{7,5},{8,10},{9,11},{10,... | collective-permute-start | bytes 49160 | tf_op jit(solution)/shard_map/ppermute | solution.py:773
  96.1 3.9 %collective-permute-start.23 = (f32[8,2,256]{2,1,0:T(2,128)}, f32[8,2,256]{2,1,0:T(2,128)S(1)}, u32[]{:S(2)}, u32[]{:S(2)}) collective-permute-start(f32[8,2,256]{2,1,0:T(2,128)} %get-tuple-element.81), channel_id=1, source_target_pairs={{0,1},{1,0},{2,3},{3,2},{4,5},{5,4},{6,7},{7,6},{8,9},{9,8},{10,11... | collective-permute-start | bytes 49160 | tf_op jit(solution)/shard_map/ppermute | solution.py:773
  117.4 38.0 %copy-start.32 = (bf16[192,768]{1,0:T(8,128)(2,1)S(1)}, bf16[192,768]{1,0:T(8,128)(2,1)}, u32[]{:S(2)}) copy-start(bf16[192,768]{1,0:T(8,128)(2,1)} %get-tuple-element.105) | copy-start | bytes 884740
  117.4 43.2 %copy-start.31 = (bf16[192,768]{1,0:T(8,128)(2,1)S(1)}, bf16[192,768]{1,0:T(8,128)(2,1)}, u32[]{:S(2)}) copy-start(bf16[192,768]{1,0:T(8,128)(2,1)} %get-tuple-element.107) | copy-start | bytes 884740
  155.4 27.1 %collective-permute-start.33 = (bf16[400,768]{1,0:T(8,128)(2,1)}, bf16[400,768]{1,0:T(8,128)(2,1)S(1)}, u32[]{:S(2)}, u32[]{:S(2)}) collective-permute-start(bf16[400,768]{1,0:T(8,128)(2,1)} %get-tuple-element.101), channel_id=1, source_target_pairs={{0,4},{4,0},{8,12},{12,8},{16,20},{20,16},{24,28},{28,24},{1,5},{5... | collective-permute-start | bytes 1843208 | tf_op jit(solution)/shard_map/ppermute | solution.py:779
  155.4 12.6 %collective-permute-start.34 = (bf16[192,768]{1,0:T(8,128)(2,1)S(1)}, bf16[192,768]{1,0:T(8,128)(2,1)S(1)}, u32[]{:S(2)}, u32[]{:S(2)}) collective-permute-start(bf16[192,768]{1,0:T(8,128)(2,1)S(1)} %copy-done.32), channel_id=1, source_target_pairs={{0,8},{4,12},{8,16},{12,20},{16,24},{20,28},{24,0},{28,4},{1,9},{5... | collective-permute-start | bytes 884744 | tf_op jit(solution)/shard_map/ppermute | solution.py:776
  157.3 23.0 %collective-permute-start.35 = (bf16[192,768]{1,0:T(8,128)(2,1)}, bf16[192,768]{1,0:T(8,128)(2,1)S(1)}, u32[]{:S(2)}, u32[]{:S(2)}) collective-permute-start(bf16[192,768]{1,0:T(8,128)(2,1)} %get-tuple-element.106), channel_id=1, source_target_pairs={{0,16},{4,20},{8,24},{12,28},{16,0},{20,4},{24,8},{28,12},{1,17},{... | collective-permute-start | bytes 884744 | tf_op jit(solution)/shard_map/ppermute | solution.py:776
  160.6 21.3 %collective-permute-start.36 = (bf16[192,768]{1,0:T(8,128)(2,1)S(1)}, bf16[192,768]{1,0:T(8,128)(2,1)S(1)}, u32[]{:S(2)}, u32[]{:S(2)}) collective-permute-start(bf16[192,768]{1,0:T(8,128)(2,1)S(1)} %copy-done.31), channel_id=1, source_target_pairs={{0,24},{4,28},{8,0},{12,4},{16,8},{20,12},{24,16},{28,20},{1,25},{... | collective-permute-start | bytes 884744 | tf_op jit(solution)/shard_map/ppermute | solution.py:776
  160.6 29.7 %collective-permute-start.29 = (bf16[2,256,768]{2,1,0:T(8,128)(2,1)}, bf16[2,256,768]{2,1,0:T(8,128)(2,1)S(1)}, u32[]{:S(2)}, u32[]{:S(2)}) collective-permute-start(bf16[2,256,768]{2,1,0:T(8,128)(2,1)} %get-tuple-element.97), channel_id=1, source_target_pairs={{0,1},{1,0},{2,3},{3,2},{4,5},{5,4},{6,7},{7,6},{8,9},{9,8},{10,11... | collective-permute-start | bytes 2359304 | tf_op jit(solution)/shard_map/ppermute | solution.py:773
  168.1 37.5 %collective-permute-start.31 = (bf16[2,256,768]{2,1,0:T(8,128)(2,1)}, bf16[2,256,768]{2,1,0:T(8,128)(2,1)S(1)}, u32[]{:S(2)}, u32[]{:S(2)}) collective-permute-start(bf16[2,256,768]{2,1,0:T(8,128)(2,1)} %get-tuple-element.98), channel_id=1, source_target_pairs={{0,2},{1,3},{2,0},{3,1},{4,6},{5,7},{6,4},{7,5},{8,10},{9,11},{10,... | collective-permute-start | bytes 2359304 | tf_op jit(solution)/shard_map/ppermute | solution.py:773
  180.4 27.3 %collective-permute-start.28 = (bf16[2,256,768]{2,1,0:T(8,128)(2,1)}, bf16[2,256,768]{2,1,0:T(8,128)(2,1)}, u32[]{:S(2)}, u32[]{:S(2)}) collective-permute-start(bf16[2,256,768]{2,1,0:T(8,128)(2,1)} %get-tuple-element.79.refs_7_), channel_id=1, source_target_pairs={{0,3},{1,2},{2,1},{3,0},{4,7},{5,6},{6,5},{7,4},{8,11},{9,10},{10,... | collective-permute-start | bytes 2359304 | tf_op jit(solution)/shard_map/ppermute | solution.py:773
  181.9 39.2 %collective-permute-start.27 = (bf16[2,256,768]{2,1,0:T(8,128)(2,1)}, bf16[2,256,768]{2,1,0:T(8,128)(2,1)}, u32[]{:S(2)}, u32[]{:S(2)}) collective-permute-start(bf16[2,256,768]{2,1,0:T(8,128)(2,1)} %get-tuple-element.78.refs_6_), channel_id=1, source_target_pairs={{0,2},{1,3},{2,0},{3,1},{4,6},{5,7},{6,4},{7,5},{8,10},{9,11},{10,... | collective-permute-start | bytes 2359304 | tf_op jit(solution)/shard_map/ppermute | solution.py:773
  182.5 40.2 %collective-permute-start.26 = (bf16[2,256,768]{2,1,0:T(8,128)(2,1)}, bf16[2,256,768]{2,1,0:T(8,128)(2,1)}, u32[]{:S(2)}, u32[]{:S(2)}) collective-permute-start(bf16[2,256,768]{2,1,0:T(8,128)(2,1)} %get-tuple-element.77.refs_5_), channel_id=1, source_target_pairs={{0,1},{1,0},{2,3},{3,2},{4,5},{5,4},{6,7},{7,6},{8,9},{9,8},{10,11... | collective-permute-start | bytes 2359304 | tf_op jit(solution)/shard_map/ppermute | solution.py:773
  184.0 21.6 %copy-start.3 = (bf16[4,256,768]{2,1,0:T(8,128)(2,1)S(1)}, bf16[4,256,768]{2,1,0:T(8,128)(2,1)}, u32[]{:S(2)}) copy-start(bf16[4,256,768]{2,1,0:T(8,128)(2,1)} %get-tuple-element.96.refs_0_.refs_3_) | copy-start | bytes 4718596
  190.3 16.4 %copy-start.40 = (bf16[112,768]{1,0:T(8,128)(2,1)S(1)}, bf16[112,768]{1,0:T(8,128)(2,1)}, u32[]{:S(2)}) copy-start(bf16[112,768]{1,0:T(8,128)(2,1)} %get-tuple-element.111) | copy-start | bytes 516100
  190.3 17.4 %copy-start.39 = (bf16[112,768]{1,0:T(8,128)(2,1)S(1)}, bf16[112,768]{1,0:T(8,128)(2,1)}, u32[]{:S(2)}) copy-start(bf16[112,768]{1,0:T(8,128)(2,1)} %get-tuple-element.112) | copy-start | bytes 516100
  190.3 32.9 %copy-start.7 = (bf16[2,256,768]{2,1,0:T(8,128)(2,1)S(1)}, bf16[2,256,768]{2,1,0:T(8,128)(2,1)}, u32[]{:S(2)}) copy-start(bf16[2,256,768]{2,1,0:T(8,128)(2,1)} %get-tuple-element.76.refs_4_) | copy-start | bytes 2359300
  190.3 35.1 %copy-start.4 = (bf16[2,256,768]{2,1,0:T(8,128)(2,1)}, bf16[2,256,768]{2,1,0:T(8,128)(2,1)S(1)}, u32[]{:S(2)}) copy-start(bf16[2,256,768]{2,1,0:T(8,128)(2,1)S(1)} %collective-permute-done.29.refs_1_) | copy-start | bytes 2359300
  190.4 16.3 %collective-permute-start.37 = (bf16[96,768]{1,0:T(8,128)(2,1)S(1)}, bf16[96,768]{1,0:T(8,128)(2,1)S(1)}, u32[]{:S(2)}, u32[]{:S(2)}) collective-permute-start(bf16[96,768]{1,0:T(8,128)(2,1)S(1)} %copy-done.41), channel_id=1, source_target_pairs={{0,4},{4,0},{8,12},{12,8},{16,20},{20,16},{24,28},{28,24},{1,5},{5... | collective-permute-start | bytes 442376 | tf_op jit(solution)/shard_map/ppermute | solution.py:779
  205.5 17.1 %copy-start.5 = (bf16[2,256,768]{2,1,0:T(8,128)(2,1)}, bf16[2,256,768]{2,1,0:T(8,128)(2,1)S(1)}, u32[]{:S(2)}) copy-start(bf16[2,256,768]{2,1,0:T(8,128)(2,1)S(1)} %collective-permute-done.31.refs_4_) | copy-start | bytes 2359300
  205.5 19.9 %collective-permute-start.38 = (bf16[112,768]{1,0:T(8,128)(2,1)}, bf16[112,768]{1,0:T(8,128)(2,1)S(1)}, u32[]{:S(2)}, u32[]{:S(2)}) collective-permute-start(bf16[112,768]{1,0:T(8,128)(2,1)} %get-tuple-element.110), channel_id=1, source_target_pairs={{0,8},{4,12},{8,16},{12,20},{16,24},{20,28},{24,0},{28,4},{1,9},{5... | collective-permute-start | bytes 516104 | tf_op jit(solution)/shard_map/ppermute | solution.py:776
  206.7 18.7 %collective-permute-start.39 = (bf16[112,768]{1,0:T(8,128)(2,1)S(1)}, bf16[112,768]{1,0:T(8,128)(2,1)}, u32[]{:S(2)}, u32[]{:S(2)}) collective-permute-start(bf16[112,768]{1,0:T(8,128)(2,1)S(1)} %copy-done.40), channel_id=1, source_target_pairs={{0,16},{4,20},{8,24},{12,28},{16,0},{20,4},{24,8},{28,12},{1,17},{... | collective-permute-start | bytes 516104 | tf_op jit(solution)/shard_map/ppermute | solution.py:776
  207.7 17.7 %collective-permute-start.40 = (bf16[112,768]{1,0:T(8,128)(2,1)S(1)}, bf16[112,768]{1,0:T(8,128)(2,1)}, u32[]{:S(2)}, u32[]{:S(2)}) collective-permute-start(bf16[112,768]{1,0:T(8,128)(2,1)S(1)} %copy-done.39), channel_id=1, source_target_pairs={{0,24},{4,28},{8,0},{12,4},{16,8},{20,12},{24,16},{28,20},{1,25},{... | collective-permute-start | bytes 516104 | tf_op jit(solution)/shard_map/ppermute | solution.py:776
  221.1 18.0 %collective-permute-start.30 = (bf16[256,768]{1,0:T(8,128)(2,1)}, bf16[256,768]{1,0:T(8,128)(2,1)}, u32[]{:S(2)}, u32[]{:S(2)}) collective-permute-start(bf16[256,768]{1,0:T(8,128)(2,1)} %get-tuple-element.131), channel_id=1, source_target_pairs={{0,2},{1,3},{2,0},{3,1},{4,6},{5,7},{6,4},{7,5},{8,10},{9,11},{10,... | collective-permute-start | bytes 1179656 | tf_op jit(solution)/shard_map/ppermute | solution.py:773
  222.7 16.5 %collective-permute-start.32 = (bf16[256,768]{1,0:T(8,128)(2,1)}, bf16[256,768]{1,0:T(8,128)(2,1)}, u32[]{:S(2)}, u32[]{:S(2)}) collective-permute-start(bf16[256,768]{1,0:T(8,128)(2,1)} %get-tuple-element.130), channel_id=1, source_target_pairs={{0,1},{1,0},{2,3},{3,2},{4,5},{5,4},{6,7},{7,6},{8,9},{9,8},{10,11... | collective-permute-start | bytes 1179656 | tf_op jit(solution)/shard_map/ppermute | solution.py:773
  228.9 5.3 %collective-permute-start.41 = (bf16[112,256]{1,0:T(8,128)(2,1)}, bf16[112,256]{1,0:T(8,128)(2,1)S(1)}, u32[]{:S(2)}, u32[]{:S(2)}) collective-permute-start(bf16[112,256]{1,0:T(8,128)(2,1)} %get-tuple-element.113.refs_0_), channel_id=1, source_target_pairs={{0,1},{1,0},{2,3},{3,2},{4,5},{5,4},{6,7},{7,6},{8,9},{9,8},{10,11... | collective-permute-start | bytes 172040 | tf_op jit(solution)/shard_map/ppermute | solution.py:773
  230.5 4.4 %collective-permute-start.42 = (bf16[112,256]{1,0:T(8,128)(2,1)}, bf16[112,256]{1,0:T(8,128)(2,1)S(1)}, u32[]{:S(2)}, u32[]{:S(2)}) collective-permute-start(bf16[112,256]{1,0:T(8,128)(2,1)} %get-tuple-element.113.refs_0_), channel_id=1, source_target_pairs={{0,2},{1,3},{2,0},{3,1},{4,6},{5,7},{6,4},{7,5},{8,10},{9,11},{10,... | collective-permute-start | bytes 172040 | tf_op jit(solution)/shard_map/ppermute | solution.py:773
  230.9 5.3 %collective-permute-start.43 = (bf16[112,256]{1,0:T(8,128)(2,1)}, bf16[112,256]{1,0:T(8,128)(2,1)S(1)}, u32[]{:S(2)}, u32[]{:S(2)}) collective-permute-start(bf16[112,256]{1,0:T(8,128)(2,1)} %get-tuple-element.113.refs_0_), channel_id=1, source_target_pairs={{0,3},{1,2},{2,1},{3,0},{4,7},{5,6},{6,5},{7,4},{8,11},{9,10},{10,... | collective-permute-start | bytes 172040 | tf_op jit(solution)/shard_map/ppermute | solution.py:773
  (29 other events, 174.6 us)

commit v3 on v2

--- a/solution.py
+++ b/solution.py
@@ -10,6 +10,7 @@
 
 
 BLOCK = 256
+SUB = 128
 LANES = 128
 EPS = 1e-05
 LOG2E = math.log2(math.e)
@@ -86,7 +87,7 @@
         self.at_n = n_dp
         self.at_c = self.at_n + self.pieces
         self.at_keep = self.at_c + n_t
-        self.at_rel = self.at_keep + self.blocks
+        self.at_rel = self.at_keep + length // SUB
         self.at_group = self.at_rel + self.blocks
         self.at_slot = self.at_group + self.blocks
         self.at_hi = self.at_slot + self.blocks
@@ -110,8 +111,20 @@
     delta = softplus(raw + hp_ref[0:1, :])
     logs = dot_split(tri, delta * (hp_ref[1:2, :] * LOG2E))
     enter = jnp.exp2(logs) * cols[:, 7:8]
-    ending = jnp.exp2(logs[BLOCK - 1 :, :] - logs) * cols[:, 8:9]
+    left = [logs[k + SUB - 1 : k + SUB, :] - logs[k : k + SUB, :] for k in range(0, BLOCK, SUB)]
+    ending = jnp.exp2(jnp.concatenate(left, axis=0)) * cols[:, 8:9]
     return delta, logs, enter, ending
+
+
+def lower_blocks():
+    r = lax.broadcasted_iota(jnp.int32, (BLOCK, BLOCK), 0)
+    c = lax.broadcasted_iota(jnp.int32, (BLOCK, BLOCK), 1)
+    return jnp.where((r >= c) & (r // SUB == c // SUB), 1.0, 0.0).astype(BF16)
+
+
+def head_masks(dm):
+    lane = lax.broadcasted_iota(jnp.int32, (1, LANES), 1)
+    return [jnp.where(lane // dm.hd == j, 1.0, 0.0).astype(BF16) for j in range(dm.per)]
 
 
 def norm_kernel(part, x_hbm, gain_ref, *refs):
@@ -155,7 +168,7 @@
     rest = refs[dm.n_dp + dm.pieces :]
     rows_ref, conv_ref, hp_ref, lane_ref = rest[:4]
     (g_out, v_out, cv_out, ys_out, st_out, h_out, sum_out, nm_out, sg_out, w_out) = rest[4:14]
-    (w_v, nm_v, h_ref, vbuf, tri_ref, bias_ref, pbuf, w_sem, n_sem, o_sem) = rest[14:]
+    (w_v, nm_v, h_ref, vbuf, tri_ref, pbuf, w_sem, n_sem, o_sem) = rest[14:]
     i = pl.program_id(0)
     save = pltpu.make_async_copy(w_v, w_out, o_sem)
 
@@ -170,9 +183,7 @@
             copy.start()
         h_ref[...] = jnp.zeros_like(h_ref)
         vbuf[...] = jnp.zeros_like(vbuf)
-        r = lax.broadcasted_iota(jnp.int32, (q, q), 0)
-        c = lax.broadcasted_iota(jnp.int32, (q, q), 1)
-        tri_ref[...] = jnp.where(r >= c, 1.0, 0.0).astype(BF16)
+        tri_ref[...] = lower_blocks()
         for copy in copies:
             copy.wait()
         save.start()
@@ -181,63 +192,75 @@
     rows = rows_ref[...]
     cols = columns_of(rows)
     nm_out[...] = rows_at(i)
-    vbuf[0:8, :] = vbuf[q : q + 8, :]
-    vbuf[8 : 8 + q, :] = pbuf[:, ip : ip + vs]
+    for c in range(vs // LANES):
+        vbuf[c, 0:8, :] = vbuf[c, q : q + 8, :]
+        vbuf[c, 8 : 8 + q, :] = pbuf[:, ip + c * LANES : ip + (c + 1) * LANES]
     v_out[...] = pbuf[:, ip : ip + vs].astype(BF16)
     raw = pbuf[:, ip + vs :]
-    gates = pbuf[:, :ip].astype(BF16)
-    g_out[...] = gates
+    g_out[...] = pbuf[:, :ip].astype(BF16)
     st_out[...] = raw
-    pbuf[...] = dot(rows_at(jnp.minimum(i + 1, dm.blocks - 1)), w_v[...])
 
     acts = []
-    for c in range(vs // LANES):
+    count = vs // LANES
+    edges = [k * dm.np // count // LANES * LANES for k in range(count)] + [dm.np]
+    following = rows_at(jnp.minimum(i + 1, dm.blocks - 1))
+    for c in range(count):
         g = slice(c * LANES, (c + 1) * LANES)
-        acc = conv_ref[4:5, g] + conv_ref[3:4, g] * vbuf[8 : 8 + q, g]
+        acc = conv_ref[4:5, g] + conv_ref[3:4, g] * vbuf[c, 8 : 8 + q, :]
         for lag in range(1, 4):
             acc = acc + conv_ref[3 - lag : 4 - lag, g] * (
-                vbuf[8 - lag : 8 - lag + q, g] * cols[:, lag : lag + 1]
+                vbuf[c, 8 - lag : 8 - lag + q, :] * cols[:, lag : lag + 1]
             )
         rounded = acc.astype(BF16)
         cv_out[:, g] = rounded
         acc = rounded.astype(F32)
         acts.append(acc * sigmoid(acc))
+        n = slice(edges[c], edges[c + 1])
+        pbuf[:, n] = dot(following, w_v[:, n])
     in_map = jnp.concatenate(acts[dm.pairs : dm.pairs + st // LANES], axis=1).astype(BF16)
     out_map = jnp.concatenate(acts[dm.pairs + st // LANES :], axis=1).astype(BF16)
 
     delta, logs, enter, ending = decay_parts(raw, hp_ref, cols, tri_ref[...])
     logs_t = logs.T
-    r = lax.broadcasted_iota(jnp.int32, (q, q), 0)
-    c = lax.broadcasted_iota(jnp.int32, (q, q), 1)
-    bias_ref[...] = jnp.where((r >= c) & (cols[:, 0:1] == rows[0:1, :]), 0.0, FAR)
-    scores = dot(out_map, in_map, MT)
-    keep = scalars[dm.at_keep + i].astype(F32)
-    total = jnp.exp2(logs[q - 1 :, :]) * keep
-    lane = lax.broadcasted_iota(jnp.int32, (q, LANES), 1)
-    h_out[...] = h_ref[...]
-    in_map_t = in_map.T
-    squares = jnp.zeros((q, LANES), F32)
-    for p in range(dm.pairs):
-        g = slice(p * LANES, (p + 1) * LANES)
-        x = acts[p]
-        u = x * spread(delta, p, hd)
-        ub = u.astype(BF16)
-        y = None
-        for j in range(dm.per):
-            h = p * dm.per + j
-            decay = jnp.exp2(logs[:, h : h + 1] - logs_t[h : h + 1, :] + bias_ref[...])
-            part = dot((decay * scores).astype(BF16), ub)
-            y = part if y is None else jnp.where(lane >= j * hd, part, y)
-        held = h_ref[:, g]
-        y = y + dot(out_map, held.astype(BF16)) * spread(enter, p, hd)
-        wu = (u * spread(ending, p, hd)).astype(BF16)
-        h_ref[:, g] = held * spread(total, p, hd) + dot(in_map_t, wu)
-        ys_out[:, g] = y
-        gate = gates[:, g].astype(F32)
-        gated = (y + lane_ref[0:1, g] * x) * (gate * sigmoid(gate))
-        sg_out[:, g] = (gated * lane_ref[1:2, g]).astype(BF16)
-        squares = squares + gated * gated
-    sum_out[...] = jnp.sum(squares.T, axis=0, keepdims=True)
+    r = lax.broadcasted_iota(jnp.int32, (SUB, SUB), 0)
+    c = lax.broadcasted_iota(jnp.int32, (SUB, SUB), 1)
+    masks = head_masks(dm)
+    squares = []
+    for k in range(q // SUB):
+        a = slice(k * SUB, (k + 1) * SUB)
+        bias = jnp.where((r >= c) & (cols[a, 0:1] == rows[0:1, a]), 0.0, FAR)
+        source, target = in_map[a], out_map[a]
+        scores = dot(target, source, MT)
+        source_t = source.T
+        keep = scalars[dm.at_keep + i * (q // SUB) + k].astype(F32)
+        total = jnp.exp2(logs[a][SUB - 1 :, :]) * keep
+        h_out[k * st : (k + 1) * st, :] = h_ref[...]
+        square = None
+        for p in range(dm.pairs):
+            g = slice(p * LANES, (p + 1) * LANES)
+            x = acts[p][a]
+            u = x * spread(delta[a], p, hd)
+            ub = u.astype(BF16)
+            mixing = []
+            for j in range(dm.per):
+                h = p * dm.per + j
+                decay = jnp.exp2(logs[a, h : h + 1] - logs_t[h : h + 1, a] + bias)
+                mixing.append((decay * scores).astype(BF16))
+            y = dot(
+                jnp.concatenate(mixing, axis=1),
+                jnp.concatenate([ub * mask for mask in masks], axis=0),
+            )
+            held = h_ref[:, g]
+            y = y + dot(target, held.astype(BF16)) * spread(enter[a], p, hd)
+            wu = (u * spread(ending[a], p, hd)).astype(BF16)
+            h_ref[:, g] = held * spread(total, p, hd) + dot(source_t, wu)
+            ys_out[a, g] = y
+            gate = g_out[a, g].astype(F32)
+            gated = (y + lane_ref[0:1, g] * x) * (gate * sigmoid(gate))
+            sg_out[a, g] = (gated * lane_ref[1:2, g]).astype(BF16)
+            square = gated * gated if square is None else square + gated * gated
+        squares.append(square)
+    sum_out[...] = jnp.sum(jnp.concatenate(squares, axis=0).T, axis=0, keepdims=True)
 
     @pl.when(i == dm.blocks - 1)
     def _():
@@ -376,12 +399,11 @@
     dg_in, nm_in, dy_in, v_in, cv_in, ys_in, st_in, h_in = refs[7:15]
     mine_out, theirs_out, kept_out = refs[15:18]
     nc_outs = refs[18 : 18 + len(groups)]
-    (dh_ref, dbuf, tri_ref, bias_ref, ds_ref, u_s, dx_s, act_s, t1_s, t2_s) = refs[
-        18 + len(groups) : 28 + len(groups)
-    ]
-    (pj_s, acc, tap_out, head_out, nc_buf, nc_sem) = refs[28 + len(groups) :]
+    (dh_ref, dbuf, tri_ref, dx_s, act_s, t1_s, t2_s) = refs[18 + len(groups) : 25 + len(groups)]
+    (pj_s, full, acc, tap_out, head_out, nc_buf, nc_sem) = refs[25 + len(groups) :]
     i = pl.program_id(0)
     blk = jnp.maximum(dm.blocks - 1 - i, 0)
+    subs = q // SUB
 
     def send(k, at, row):
         return pltpu.make_async_copy(nc_buf.at[at], nc_outs[k].at[row], nc_sem.at[at])
@@ -393,9 +415,7 @@
         tap_out[...] = jnp.zeros_like(tap_out)
         head_out[...] = jnp.zeros_like(head_out)
         acc[...] = jnp.zeros_like(acc)
-        r = lax.broadcasted_iota(jnp.int32, (q, q), 0)
-        c = lax.broadcasted_iota(jnp.int32, (q, q), 1)
-        tri_ref[...] = jnp.where(r >= c, 1.0, 0.0).astype(BF16)
+        tri_ref[...] = lower_blocks()
 
     slot = lax.rem(i, 2)
 
@@ -403,19 +423,35 @@
     def _():
         send(0, slot, 0).wait()
 
-    def project():
-        nc = dot(dg_in[...], w_ref[:, :ip], MT) + dot(pj_s[...], w_ref[:, ip:], MT)
-        nc_buf[slot] = nc.astype(BF16)
-        acc[...] += dot(nm_in[...], pj_s[...], TM)
-
-    def scan():
+    third = dm.width // 3
+
+    def cotangent_piece(n):
+        def run():
+            g = slice(n * third, (n + 1) * third)
+            nc_buf[slot, :, g] = dot(full[...], w_ref[g, :], MT).astype(BF16)
+
+        return run
+
+    def gradient_piece(n):
+        def run():
+            g = slice(n * third, (n + 1) * third)
+            acc[g, :] += dot(nm_in[:, g], full[:, ip:], TM)
+
+        return run
+
+    pieces = [make(n) for n in range(3) for make in (cotangent_piece, gradient_piece)]
+
+    def take_over():
+        full[:, :ip] = dg_in[...]
+        full[:, ip:] = pj_s[...]
+
+    def scan(between):
         rows = rows_ref[...]
         cols = columns_of(rows)
         raw = st_in[...]
         tri = tri_ref[...]
         delta, logs, enter, ending = decay_parts(raw, hp_ref, cols, tri)
         logs_t = logs.T
-        lane = lax.broadcasted_iota(jnp.int32, (q, LANES), 1)
 
         acts, slopes = [], []
         for c in range(vs // LANES):
@@ -428,62 +464,67 @@
         in_map = jnp.concatenate(acts[dm.pairs : dm.pairs + st // LANES], axis=1).astype(BF16)
         out_map = jnp.concatenate(acts[dm.pairs + st // LANES :], axis=1).astype(BF16)
 
-        for p in range(dm.pairs):
-            g = slice(p * LANES, (p + 1) * LANES)
-            u_s[:, g] = acts[p] * spread(delta, p, hd)
-
-        r = lax.broadcasted_iota(jnp.int32, (q, q), 0)
-        c = lax.broadcasted_iota(jnp.int32, (q, q), 1)
-        bias_ref[...] = jnp.where((r <= c) & (cols[:, 0:1] == rows[0:1, :]), 0.0, FAR)
-        scores = dot(in_map, out_map, MT)
-        dh_b = dh_ref[...].astype(BF16)
-        h_b = h_in[...].astype(BF16)
-        out_map_t = out_map.T
-        keep = scalars[dm.at_keep + blk].astype(F32)
-        total = jnp.exp2(logs[q - 1 :, :]) * keep
-        d_in = jnp.zeros((q, st), F32)
-        d_out = jnp.zeros((q, st), F32)
-        for p in range(dm.pairs):
-            g = slice(p * LANES, (p + 1) * LANES)
-            u, dyb = u_s[:, g], dy_in[:, g]
-            ub, dy = u.astype(BF16), dyb.astype(F32)
-            du = None
-            for j in range(dm.per):
-                h = p * dm.per + j
-                mine = (lane >= j * hd) & (lane < (j + 1) * hd)
-                decay = jnp.exp2(logs_t[h : h + 1, :] - logs[:, h : h + 1] + bias_ref[...])
-                part = dot((decay * scores).astype(BF16), dyb)
-                du = part if du is None else jnp.where(lane >= j * hd, part, du)
-                dm_t = dot(jnp.where(mine, u, 0.0).astype(BF16), dyb, MT)
-                if p == 0 and j == 0:
-                    ds_ref[...] = dm_t * decay
-                else:
-                    ds_ref[...] += dm_t * decay
-            end_e = spread(ending, p, hd)
-            late = end_e * dot(in_map, dh_b[:, g])
-            du = du + late
-            wu = (u * end_e).astype(BF16)
-            edy = (dy * spread(enter, p, hd)).astype(BF16)
-            d_in = d_in + dot(wu, dh_b[:, g], MT)
-            d_out = d_out + dot(edy, h_b[:, g], MT)
-            u32 = ub.astype(F32)
-            t1_s[:, g] = dy * ys_in[:, g] - u32 * du
-            t2_s[:, g] = du * acts[p]
-            kept = dh_ref[:, g] * spread(total, p, hd)
-            act_s[:, g] = colsum(u32 * late) + colsum(h_in[:, g] * kept)
-            dh_ref[:, g] = kept + dot(out_map_t, edy)
-            dx_s[:, g] = (spread(delta, p, hd) * du + lane_ref[0:1, g] * dy) * slopes[p]
-        ds_b = ds_ref[...].astype(BF16)
-        d_in = d_in + dot(ds_b, out_map)
-        d_out = d_out + dot(ds_b, in_map, TM)
+        r = lax.broadcasted_iota(jnp.int32, (SUB, SUB), 0)
+        c = lax.broadcasted_iota(jnp.int32, (SUB, SUB), 1)
+        masks = head_masks(dm)
+        d_in, d_out = [None] * subs, [None] * subs
+        for k in reversed(range(subs)):
+            a = slice(k * SUB, (k + 1) * SUB)
+            bias = jnp.where((r <= c) & (cols[a, 0:1] == rows[0:1, a]), 0.0, FAR)
+            source, target = in_map[a], out_map[a]
+            scores = dot(source, target, MT)
+            target_t = target.T
+            keep = scalars[dm.at_keep + blk * subs + k].astype(F32)
+            total = jnp.exp2(logs[a][SUB - 1 :, :]) * keep
+            ds = None
+            for p in range(dm.pairs):
+                g = slice(p * LANES, (p + 1) * LANES)
+                x, dyb = acts[p][a], dy_in[a, g]
+                delta_e = spread(delta[a], p, hd)
+                u = x * delta_e
+                ub, dy = u.astype(BF16), dyb.astype(F32)
+                decays = []
+                for j in range(dm.per):
+                    h = p * dm.per + j
+                    decays.append(jnp.exp2(logs_t[h : h + 1, a] - logs[a, h : h + 1] + bias))
+                du = dot(
+                    jnp.concatenate([(d * scores).astype(BF16) for d in decays], axis=1),
+                    jnp.concatenate([dyb * mask for mask in masks], axis=0),
+                )
+                dm_t = dot(jnp.concatenate([ub * mask for mask in masks], axis=0), dyb, MT)
+                for j, d in enumerate(decays):
+                    part = dm_t[j * SUB : (j + 1) * SUB] * d
+                    ds = part if ds is None else ds + part
+                dh, h_rows = dh_ref[:, g], h_in[k * st : (k + 1) * st, g]
+                dh_b = dh.astype(BF16)
+                end_e = spread(ending[a], p, hd)
+                late = end_e * dot(source, dh_b)
+                du = du + late
+                wu = (u * end_e).astype(BF16)
+                edy = (dy * spread(enter[a], p, hd)).astype(BF16)
+                from_wu, from_dy = dot(wu, dh_b, MT), dot(edy, h_rows.astype(BF16), MT)
+                d_in[k] = from_wu if p == 0 else d_in[k] + from_wu
+                d_out[k] = from_dy if p == 0 else d_out[k] + from_dy
+                u32 = ub.astype(F32)
+                t1_s[a, g] = dy * ys_in[a, g] - u32 * du
+                t2_s[a, g] = du * x
+                kept = dh * spread(total, p, hd)
+                act_s[8 * k : 8 * k + 8, g] = colsum(u32 * late) + colsum(h_rows * kept)
+                dh_ref[:, g] = kept + dot(target_t, edy)
+                dx_s[a, g] = (delta_e * du + lane_ref[0:1, g] * dy) * slopes[p][a]
+            ds_b = ds.astype(BF16)
+            d_in[k] = d_in[k] + dot(ds_b, target)
+            d_out[k] = d_out[k] + dot(ds_b, source, TM)
 
         hr = lax.broadcasted_iota(jnp.int32, (ip, LANES), 0)
         hc = lax.broadcasted_iota(jnp.int32, (ip, LANES), 1)
         pick = jnp.where(hr // hd == hc, 1.0, 0.0).astype(BF16)
         d_log = split_dot(t1_s[...], pick)
-        last = split_dot(jnp.sum(act_s[...], axis=0, keepdims=True), pick)
+        last = split_dot(act_s[...], pick)
         row = lax.broadcasted_iota(jnp.int32, (q, LANES), 0)
-        d_log = d_log + jnp.where(row == q - 1, last, 0.0)
+        for k in range(subs):
+            end = jnp.sum(last[8 * k : 8 * k + 8, :], axis=0, keepdims=True)
+            d_log = d_log + jnp.where(row == (k + 1) * SUB - 1, end, 0.0)
         d_step = dot_split(tri, d_log, TM)
         head_out[8:16, :] += colsum(d_step * delta)
         d_delta = hp_ref[1:2, :] * d_step + split_dot(t2_s[...], pick)
@@ -491,41 +532,47 @@
         head_out[0:8, :] += colsum(d_raw)
         pj_s[:, vs:] = d_raw.astype(BF16)
 
-        dbuf[q : q + 8, :] = dbuf[0:8, :]
-        for c in range(vs // LANES):
-            g = slice(c * LANES, (c + 1) * LANES)
-            if c < dm.pairs:
-                dbuf[0:q, g] = dx_s[:, g]
-            else:
-                k = (c - dm.pairs) * LANES
-                source = d_in[:, k : k + LANES] if k < st else d_out[:, k - st : k - st + LANES]
-                dbuf[0:q, g] = source * slopes[c]
-        for c in range(vs // LANES):
+        count = vs // LANES
+        for c in range(count):
+            dbuf[c, q : q + 8, :] = dbuf[c, 0:8, :]
+            for k in range(subs):
+                a = slice(k * SUB, (k + 1) * SUB)
+                if c < dm.pairs:
+                    dbuf[c, a, :] = dx_s[a, c * LANES : (c + 1) * LANES]
+                else:
+                    n = (c - dm.pairs) * LANES
+                    part = d_in[k][:, n : n + LANES] if n < st else d_out[k][:, n - st : n - st + LANES]
+                    dbuf[c, a, :] = part * slopes[c][a]
+        for c in range(count):
             g = slice(c * LANES, (c + 1) * LANES)
             v = v_in[:, g].astype(F32)
-            shifted = dbuf[0:q, g]
+            shifted = dbuf[c, 0:q, :]
             tap_out[32:40, g] += colsum(shifted)
             tap_out[24:32, g] += colsum(shifted * v)
             dv = conv_ref[3:4, g] * shifted
             for lag in range(1, 4):
-                shifted = dbuf[lag : lag + q, g] * cols[:, 3 + lag : 4 + lag]
+                shifted = dbuf[c, lag : lag + q, :] * cols[:, 3 + lag : 4 + lag]
                 tap_out[24 - 8 * lag : 32 - 8 * lag, g] += colsum(shifted * v)
                 dv = dv + conv_ref[3 - lag : 4 - lag, g] * shifted
             pj_s[:, g] = dv.astype(BF16)
-
+            first, stop = c * len(between) // count, (c + 1) * len(between) // count
+            for run in between[first:stop]:
+                run()
 
     @pl.when(i == 0)
     def _():
-        scan()
+        scan([])
 
     @pl.when((i > 0) & (i < dm.blocks))
     def _():
-        project()
-        scan()
+        take_over()
+        scan(pieces)
 
     @pl.when(i == dm.blocks)
     def _():
-        project()
+        take_over()
+        for run in pieces:
+            run()
 
     before = jnp.minimum(blk + 1, dm.blocks - 1)
     before = jnp.where(i == dm.blocks, 0, before)
@@ -781,7 +828,7 @@
     def vmem(shape, dtype):
         return pltpu.VMEM(shape, dtype)
 
-    limit = 60 * 1024 * 1024
+    limit = 20 * 1024 * 1024
     params = pltpu.CompilerParams(dimension_semantics=("arbitrary",), vmem_limit_bytes=limit)
     hbm = pl.BlockSpec(memory_space=pl.ANY)
 
@@ -824,7 +871,8 @@
     o_list = o_list + [partner(v) for v in o_list]
 
     seg = segment_ids[0]
-    segb = seg.reshape(nb, q)
+    subs = q // SUB
+    segb = seg.reshape(nb * subs, SUB)
     last = segb[:, -1]
     prev_last = jnp.concatenate([jnp.full((1,), -1, jnp.int32), last[:-1]])
     gap = jnp.full((3,), -1, jnp.int32)
@@ -906,7 +954,7 @@
             out(length, vs, dtype=BF16),
             out(length, ip),
             out(length, LANES),
-            out(nb * state, ip),
+            out(nb * subs * state, ip),
             out(nb, 1, q),
             out(length, width, dtype=BF16),
             out(length, ip, dtype=BF16),
@@ -927,7 +975,7 @@
                 fblock(vs),
                 fblock(ip),
                 fblock(LANES),
-                pl.BlockSpec((state, ip), lambda i, s: (i, 0)),
+                pl.BlockSpec((subs * state, ip), lambda i, s: (i, 0)),
                 fsum(1),
                 fblock(width),
                 fblock(ip),
@@ -937,9 +985,8 @@
                 vmem((width, dm.np), BF16),
                 vmem((length, width), BF16),
                 vmem((state, ip), F32),
-                vmem((q + 8, vs), F32),
+                vmem((vs // LANES, q + 8, LANES), F32),
                 vmem((q, q), BF16),
-                vmem((q, q), F32),
                 vmem((q, dm.np), F32),
                 pltpu.SemaphoreType.DMA((n_dp,)),
                 pltpu.SemaphoreType.DMA((dm.pieces,)),
@@ -1084,22 +1131,20 @@
                 bblock(vs),
                 bblock(ip),
                 bblock(LANES),
-                pl.BlockSpec((state, ip), lambda i, s: (jnp.maximum(nb - 1 - i, 0), 0)),
+                pl.BlockSpec((subs * state, ip), lambda i, s: (jnp.maximum(nb - 1 - i, 0), 0)),
             ],
             [const(r_all, dm.late), const(r_all + 16, dm.late), const(16, dm.late)]
             + [hbm] * len(dm.group_sizes),
             [
                 vmem((state, ip), F32),
-                vmem((q + 8, vs), F32),
+                vmem((vs // LANES, q + 8, LANES), F32),
                 vmem((q, q), BF16),
-                vmem((q, q), F32),
-                vmem((q, q), F32),
                 vmem((q, ip), F32),
-                vmem((q, ip), F32),
-                vmem((8, ip), F32),
+                vmem((8 * subs, ip), F32),
                 vmem((q, ip), F32),
                 vmem((q, ip), F32),
                 vmem((q, dm.late), BF16),
+                vmem((q, dm.np), BF16),
                 vmem((width, dm.late), F32),
                 vmem((40, vs), F32),
                 vmem((16, LANES), F32),

time: 244 us -> 229 us (0.939)
  Pallas kernels: 112 us -> 87.2 us
  local copies, waits for them, and re-layouts: 7.79 us -> 24.5 us
  waiting for transfers between devices: 65.9 us -> 58.4 us
    unnamed x105 -> x84, local copies, waits for them, and re-layouts: 4.08 us -> 17.7 us
    ppermute x22, waiting for transfers between devices: 39 us -> 31.1 us  [across(): return lax.ppermute(v, 'tensor', swap(n_t, k))]
    pallas_call x1, Pallas kernels: 37.9 us -> 33.2 us  [body(): pl.pallas_call(functools.partial(backward_kernel, dm), out_shape=[out(r_a...]
    pallas_call x1, Pallas kernels: 16 us -> 11.7 us  [body(): pl.pallas_call(functools.partial(gate_kernel, dm), out_shape=[out(length,...]
    pallas_call x1, Pallas kernels: 6.45 us -> 3.05 us  [body(): pl.pallas_call(functools.partial(dots_kernel, dm), out_shape=[out(nb, 2,...]
    pallas_call x1, Pallas kernels: 3.23 us -> 0.64 us  [body(): pl.pallas_call(functools.partial(pair_kernel, dm), out_shape=[out(part_ro...]
    ppermute x22, starting transfers between devices: 26.3 us -> 23.8 us  [across(): return lax.ppermute(v, 'tensor', swap(n_t, k))]
  transfers between devices with their start and end apart: 44 -> 44, of which waited for: 16 -> 12; matrix products, arithmetic and copies ran while one was open for 5% -> 8% of each run, Pallas kernels for 19% -> 16%
where the time goes in v3:
time: 229 us; the launch traced here: 228 us
  Pallas kernels  87.2 us (38%)
  waiting for transfers between devices  58.4 us (26%)
  starting transfers between devices  46.3 us (20%)
  local copies, waits for them, and re-layouts  24.5 us (11%)
  other arithmetic  10.9 us (5%)
    pallas_call x1, Pallas kernels, body(): pl.pallas_call(functools.partial(backward_kernel, dm), out_shape=[out(r_a...  33.2 us
    ppermute x22, waiting for transfers between devices, across(): return lax.ppermute(v, 'tensor', swap(n_t, k))  31.1 us
    ppermute x12, waiting for transfers between devices, along(): return lax.ppermute(v, 'dp', shift_hi(n_dp, k))  26.6 us
    ppermute x22, starting transfers between devices, across(): return lax.ppermute(v, 'tensor', swap(n_t, k))  23.8 us
    pallas_call x1, Pallas kernels, body(): pl.pallas_call(functools.partial(forward_kernel, dm), out_shape=[out(leng...  23.4 us
    ppermute x12, starting transfers between devices, along(): return lax.ppermute(v, 'dp', shift_hi(n_dp, k))  21.4 us
    unnamed x84, local copies, waits for them, and re-layouts  17.7 us
    pallas_call x1, Pallas kernels, body(): pl.pallas_call(functools.partial(gate_kernel, dm), out_shape=[out(length,...  11.7 us
  transfers between devices with their start and end apart: 44, of which 12 were waited for; matrix products, arithmetic and copies ran while one was open for 8% of the time, Pallas kernels for 16%

profile of v3, /device:TPU:0, one launch (start us, length us, event | category | flops | bytes accessed | tf_op | source)
XLA Modules:
  0.0 228.5 jit_solution(8085338143359867765)
XLA Ops:
  0.7 3.1 %collective-permute-start.3 = (bf16[96,384]{1,0:T(8,128)(2,1)}, bf16[96,384]{1,0:T(8,128)(2,1)S(1)}, u32[]{:S(2)}, u32[]{:S(2)}) collective-permute-start(bf16[96,384]{1,0:T(8,128)(2,1)} %bitcast.40), channel_id=1, source_target_pairs={{0,8},{4,12},{8,16},{12,20},{16,24},{20,28},{24,0},{28,4},{1,9},{5... | collective-permute-start | bytes 221192 | tf_op jit(solution)/shard_map/ppermute | solution.py:823
  3.8 2.6 %collective-permute-start.4 = (bf16[96,384]{1,0:T(8,128)(2,1)}, bf16[96,384]{1,0:T(8,128)(2,1)S(1)}, u32[]{:S(2)}, u32[]{:S(2)}) collective-permute-start(bf16[96,384]{1,0:T(8,128)(2,1)} %bitcast.41), channel_id=1, source_target_pairs={{0,16},{4,20},{8,24},{12,28},{16,0},{20,4},{24,8},{28,12},{1,17},{... | collective-permute-start | bytes 221192 | tf_op jit(solution)/shard_map/ppermute | solution.py:823
  6.4 1.3 collective-permute-start.5
  7.8 1.4 copy-done
  9.9 1.3 normalize.1
  11.2 1.9 pack_weights.1.refs_0_
  18.2 1.5 collective-permute-start.17
  19.7 1.5 collective-permute-start.20
  23.0 2.9 %collective-permute-start.12 = (bf16[96,1152]{1,0:T(8,128)(2,1)}, bf16[96,1152]{1,0:T(8,128)(2,1)}, u32[]{:S(2)}, u32[]{:S(2)}) collective-permute-start(bf16[96,1152]{1,0:T(8,128)(2,1)} %pack_weights.1.refs_0_), channel_id=1, source_target_pairs={{0,24},{4,28},{8,0},{12,4},{16,8},{20,12},{24,16},{28,20},{1,25},{... | collective-permute-start | bytes 663560 | tf_op jit(solution)/shard_map/ppermute | solution.py:823
  26.4 6.2 %collective-permute-done.11.refs_2_ = bf16[96,1152]{1,0:T(8,128)(2,1)} collective-permute-done((bf16[96,1152]{1,0:T(8,128)(2,1)}, bf16[96,1152]{1,0:T(8,128)(2,1)}, u32[]{:S(2)}, u32[]{:S(2)}) %collective-permute-start.11) | collective-permute-done | bytes 221216 | tf_op jit(solution)/shard_map/ppermute | solution.py:823
  32.6 1.5 collective-permute-start.19
  35.2 1.9 collective-permute-done.12.refs_3_
  38.8 1.2 gather_fusion
  40.0 1.2 gather_fusion.1
  42.0 1.8 concatenate.38.refs_16_.refs_1_
  43.8 0.9 concatenate.35.scalars
  46.7 0.8 copy-done.23
  48.8 1.6 collective-permute-start
  50.4 1.5 collective-permute-start.1
  52.9 1.0 copy-done.20
  53.9 1.0 copy-done.22
  54.9 1.0 copy-done.24
  55.9 0.9 copy-done.26
  56.8 0.9 copy-done.28
  57.8 23.4 %block_forward.1 = (bf16[2048,384]{1,0:T(8,128)(2,1)S(1)}, bf16[2048,640]{1,0:T(8,128)(2,1)S(1)}, bf16[2048,640]{1,0:T(8,128)(2,1)S(1)}, f32[2048,384]{1,0:T(8,1...) custom-call(s32[73]{0:T(128)S(1)} %concatenate.35.scalars, ...), custom_call_target="tpu_custom_call" | custom-call | flops 30000001024 | bytes 30000000 | tf_op jit(solution)/shard_map/block_forward/pallas_call | solution.py:949
  81.2 6.7 %branch_output.1 = (bf16[768,384]{1,0:T(8,128)(2,1)S(1)}, bf16[2,256,768]{2,1,0:T(8,128)(2,1)S(1)}, bf16[2,256,768]{2,1,0:T(8,128)(2,1)}, bf16[2,256,768]{2,1,0:T(8,128)(2,1)}, bf16[2,256,768]{2,1,0:T(8,128)(2,1)}) custom-call(s32[73]{0:T(128)S(1)} %concatenate.35.scalars, bf16[96,384]{1,0:T(8,128)(2,1)S(1)} %bitcast.44, ...), custom_call_target="tpu_custom_call" | custom-call | flops 3000000000 | bytes 10000000 | tf_op jit(solution)/shard_map/branch_output/pallas_call | solution.py:1005
  88.0 3.0 %branch_dots.1 = (f32[8,2,256]{2,1,0:T(2,128)S(1)}, bf16[2048,768]{1,0:T(8,128)(2,1)S(1)}) custom-call(s32[73]{0:T(128)S(1)} %concatenate.35.scalars, bf16[512,768]{1,0:T(8,128)(2,1)S(1)} %copy-done.4, bf16[512,768]{1,0:T(8,128)(2,1)S(1)} %collective-permute-done.refs_1_, bf16[512,768]{1,0:T(8,128)(2,1)S(1)} %collective-permute-done.1.refs_2_, ...), custom_call_target="tpu_custom_call" | custom-call | flops 3000000000 | bytes 10000000 | tf_op jit(solution)/shard_map/branch_dots/pallas_call | solution.py:1027
  91.1 1.8 collective-permute-start.25
  92.9 1.2 collective-permute-start.24
  94.6 1.1 collective-permute-done.25
  95.8 0.8 collective-permute-done.24
  96.6 1.2 collective-permute-done.23
  97.9 11.7 %gate_backward.1 = (bf16[2048,384]{1,0:T(8,128)(2,1)S(1)}, bf16[2048,384]{1,0:T(8,128)(2,1)S(1)}, f32[16,384]{1,0:T(8,128)S(1)}, f32[8,768]{1,0:T(8,128)S(1)}, f...) custom-call(s32[73]{0:T(128)S(1)} %concatenate.35.scalars, ...), custom_call_target="tpu_custom_call" | custom-call | flops 6000000000 | bytes 20000000 | tf_op jit(solution)/shard_map/gate_backward/pallas_call | solution.py:1072
  109.6 0.9 copy-done.10
  110.5 33.2 %block_backward.1 = (f32[384,768]{1,0:T(8,128)S(1)}, bf16[400,768]{1,0:T(8,128)(2,1)S(1)}, bf16[16,768]{1,0:T(8,128)(2,1)S(1)}, bf16[2,256,768]{2,1,0:T(8,128)(2...) custom-call(s32[73]{0:T(128)S(1)} %concatenate.35.scalars, ...), custom_call_target="tpu_custom_call" | custom-call | flops 40000000000 | bytes 30000000 | tf_op jit(solution)/shard_map/block_backward/pallas_call | solution.py:1109
  143.7 1.0 copy-done.2
  144.7 2.4 %collective-permute-start.34 = (bf16[192,768]{1,0:T(8,128)(2,1)S(1)}, bf16[192,768]{1,0:T(8,128)(2,1)S(1)}, u32[]{:S(2)}, u32[]{:S(2)}) collective-permute-start(bf16[192,768]{1,0:T(8,128)(2,1)S(1)} %get-tuple-element.105), channel_id=1, source_target_pairs={{0,8},{4,12},{8,16},{12,20},{16,24},{20,28},{24,0},{28,4},{1,9},{5... | collective-permute-start | bytes 884744 | tf_op jit(solution)/shard_map/ppermute | solution.py:823
  147.0 4.2 %collective-permute-start.35 = (bf16[192,768]{1,0:T(8,128)(2,1)S(1)}, bf16[192,768]{1,0:T(8,128)(2,1)S(1)}, u32[]{:S(2)}, u32[]{:S(2)}) collective-permute-start(bf16[192,768]{1,0:T(8,128)(2,1)S(1)} %get-tuple-element.106), channel_id=1, source_target_pairs={{0,16},{4,20},{8,24},{12,28},{16,0},{20,4},{24,8},{28,12},{1,17},{... | collective-permute-start | bytes 884744 | tf_op jit(solution)/shard_map/ppermute | solution.py:823
  151.8 6.8 %collective-permute-done.34.refs_0_ = bf16[192,768]{1,0:T(8,128)(2,1)S(1)} collective-permute-done((bf16[192,768]{1,0:T(8,128)(2,1)S(1)}, bf16[192,768]{1,0:T(8,128)(2,1)S(1)}, u32[]{:S(2)}, u32[]{:S(2)}) %collective-permute-start.34) | collective-permute-done | bytes 294944 | tf_op jit(solution)/shard_map/ppermute | solution.py:823
  158.6 0.8 collective-permute-start.31
  159.4 11.6 %collective-permute-done.35.refs_1_ = bf16[192,768]{1,0:T(8,128)(2,1)S(1)} collective-permute-done((bf16[192,768]{1,0:T(8,128)(2,1)S(1)}, bf16[192,768]{1,0:T(8,128)(2,1)S(1)}, u32[]{:S(2)}, u32[]{:S(2)}) %collective-permute-start.35) | collective-permute-done | bytes 294944 | tf_op jit(solution)/shard_map/ppermute | solution.py:823
  171.8 1.6 collective-permute-start.28
  174.6 0.8 copy-done.8
  175.4 1.4 collective-permute-start.26
  176.9 1.1 copy-done.11
  178.1 1.0 copy-done.13
  179.0 1.0 copy-done.15
  180.0 0.8 early_sum.1
  180.8 1.1 copy-done.9
  182.6 13.5 %collective-permute-done.31.refs_4_ = bf16[2,256,768]{2,1,0:T(8,128)(2,1)S(1)} collective-permute-done((bf16[2,256,768]{2,1,0:T(8,128)(2,1)}, bf16[2,256,768]{2,1,0:T(8,128)(2,1)S(1)}, u32[]{:S(2)}, u32[]{:S(2)}) %collective-permute-start.31) | collective-permute-done | bytes 786464 | tf_op jit(solution)/shard_map/ppermute | solution.py:820
  196.3 1.5 collective-permute-start.39
  197.8 2.5 %collective-permute-start.40 = (bf16[112,768]{1,0:T(8,128)(2,1)S(1)}, bf16[112,768]{1,0:T(8,128)(2,1)S(1)}, u32[]{:S(2)}, u32[]{:S(2)}) collective-permute-start(bf16[112,768]{1,0:T(8,128)(2,1)S(1)} %get-tuple-element.112), channel_id=1, source_target_pairs={{0,24},{4,28},{8,0},{12,4},{16,8},{20,12},{24,16},{28,20},{1,25},{... | collective-permute-start | bytes 516104 | tf_op jit(solution)/shard_map/ppermute | solution.py:823
  200.3 11.5 %collective-permute-done.27 = bf16[2,256,768]{2,1,0:T(8,128)(2,1)} collective-permute-done((bf16[2,256,768]{2,1,0:T(8,128)(2,1)}, bf16[2,256,768]{2,1,0:T(8,128)(2,1)}, u32[]{:S(2)}, u32[]{:S(2)}) %collective-permute-start.27) | collective-permute-done | bytes 786464 | tf_op jit(solution)/shard_map/ppermute | solution.py:820
  211.8 0.8 collective-permute-start.30
  212.6 1.4 collective-permute-start.32
  213.9 2.1 convert_add_fusion
  216.1 1.4 gradient_sum.1
  218.3 1.2 collective-permute-start.42
  219.5 1.6 collective-permute-start.43
  221.1 1.4 fusion
  222.5 1.5 collective-permute-done.41.refs_1_
  224.0 1.3 collective-permute-done.43.refs_3_
  225.3 1.2 shared_sum.1
  226.5 1.9 input_gradient.1
  (157 shorter events, 20.9 us)
Async XLA Ops:
  0.6 38.1 %copy-start.33 = (s32[4,2]{1,0:T(4,128)S(1)}, s32[4,2]{1,0:T(4,128)}, u32[]{:S(2)}) copy-start(s32[4,2]{1,0:T(4,128)} %constant.110.clone) | copy-start | bytes 100
  0.7 39.3 %copy-start.32 = (s32[4,2]{1,0:T(4,128)S(1)}, s32[4,2]{1,0:T(4,128)}, u32[]{:S(2)}) copy-start(s32[4,2]{1,0:T(4,128)} %constant.111.clone) | copy-start | bytes 100
  0.7 15.9 %copy-start.40 = (f32[6]{0:T(128)S(1)}, f32[6]{0:T(128)}, u32[]{:S(2)}) copy-start(f32[6]{0:T(128)} %param.31) | copy-start | bytes 76
  0.7 34.0 %copy-start.39 = (f32[6]{0:T(128)S(1)}, f32[6]{0:T(128)}, u32[]{:S(2)}) copy-start(f32[6]{0:T(128)} %param.30) | copy-start | bytes 76
  0.7 40.5 %copy-start.38 = (f32[6]{0:T(128)S(1)}, f32[6]{0:T(128)}, u32[]{:S(2)}) copy-start(f32[6]{0:T(128)} %param.32) | copy-start | bytes 76
  0.7 17.2 %collective-permute-start.3 = (bf16[96,384]{1,0:T(8,128)(2,1)}, bf16[96,384]{1,0:T(8,128)(2,1)S(1)}, u32[]{:S(2)}, u32[]{:S(2)}) collective-permute-start(bf16[96,384]{1,0:T(8,128)(2,1)} %bitcast.40), channel_id=1, source_target_pairs={{0,8},{4,12},{8,16},{12,20},{16,24},{20,28},{24,0},{28,4},{1,9},{5... | collective-permute-start | bytes 221192 | tf_op jit(solution)/shard_map/ppermute | solution.py:823
  3.8 14.4 %collective-permute-start.4 = (bf16[96,384]{1,0:T(8,128)(2,1)}, bf16[96,384]{1,0:T(8,128)(2,1)S(1)}, u32[]{:S(2)}, u32[]{:S(2)}) collective-permute-start(bf16[96,384]{1,0:T(8,128)(2,1)} %bitcast.41), channel_id=1, source_target_pairs={{0,16},{4,20},{8,24},{12,28},{16,0},{20,4},{24,8},{28,12},{1,17},{... | collective-permute-start | bytes 221192 | tf_op jit(solution)/shard_map/ppermute | solution.py:823
  6.4 13.3 %collective-permute-start.5 = (bf16[96,384]{1,0:T(8,128)(2,1)}, bf16[96,384]{1,0:T(8,128)(2,1)S(1)}, u32[]{:S(2)}, u32[]{:S(2)}) collective-permute-start(bf16[96,384]{1,0:T(8,128)(2,1)} %bitcast.42), channel_id=1, source_target_pairs={{0,24},{4,28},{8,0},{12,4},{16,8},{20,12},{24,16},{28,20},{1,25},{... | collective-permute-start | bytes 221192 | tf_op jit(solution)/shard_map/ppermute | solution.py:823
  7.7 14.0 %collective-permute-start.6 = (bf16[96,384]{1,0:T(8,128)(2,1)}, bf16[96,384]{1,0:T(8,128)(2,1)S(1)}, u32[]{:S(2)}, u32[]{:S(2)}) collective-permute-start(bf16[96,384]{1,0:T(8,128)(2,1)} %bitcast.43), channel_id=1, source_target_pairs={{0,4},{4,0},{8,12},{12,8},{16,20},{20,16},{24,28},{28,24},{1,5},{5... | collective-permute-start | bytes 221192 | tf_op jit(solution)/shard_map/ppermute | solution.py:826
  9.8 4.4 %copy-start.34 = (s32[1,2048]{1,0:T(1,128)S(1)}, s32[1,2048]{1,0:T(1,128)}, u32[]{:S(2)}) copy-start(s32[1,2048]{1,0:T(1,128)} %param.20) | copy-start | bytes 24580
  9.8 31.3 %copy-start.36 = (f32[384]{0:T(512)S(1)}, f32[384]{0:T(512)}, u32[]{:S(2)}) copy-start(f32[384]{0:T(512)} %param.27) | copy-start | bytes 4612
  9.9 31.3 %copy-start.37 = (f32[384]{0:T(512)S(1)}, f32[384]{0:T(512)}, u32[]{:S(2)}) copy-start(f32[384]{0:T(512)} %param.33) | copy-start | bytes 4612
  9.9 38.2 %copy-start.35 = (f32[4,256]{1,0:T(4,128)S(1)}, f32[4,256]{1,0:T(4,128)}, u32[]{:S(2)}) copy-start(f32[4,256]{1,0:T(4,128)} %param.28) | copy-start | bytes 12292
  9.9 38.9 %copy-start.4 = (bf16[512,768]{1,0:T(8,128)(2,1)S(1)}, bf16[512,768]{1,0:T(8,128)(2,1)}, u32[]{:S(2)}) copy-start(bf16[512,768]{1,0:T(8,128)(2,1)} %cot_ref.1) | copy-start | bytes 2359300
  11.2 39.2 %copy-start.19 = (bf16[256,768]{1,0:T(8,128)(2,1)}, bf16[256,768]{1,0:T(8,128)(2,1)S(1)}, u32[]{:S(2)}) copy-start(bf16[256,768]{1,0:T(8,128)(2,1)S(1)} %get-tuple-element.74.refs_9_) | copy-start | bytes 1179652
  13.1 39.8 %copy-start.16 = (bf16[96,1152]{1,0:T(8,128)(2,1)S(1)}, bf16[96,1152]{1,0:T(8,128)(2,1)}, u32[]{:S(2)}) copy-start(bf16[96,1152]{1,0:T(8,128)(2,1)} %pack_weights.1.refs_0_) | copy-start | bytes 663556
  13.1 12.8 %collective-permute-start.10 = (bf16[96,1152]{1,0:T(8,128)(2,1)}, bf16[96,1152]{1,0:T(8,128)(2,1)S(1)}, u32[]{:S(2)}, u32[]{:S(2)}) collective-permute-start(bf16[96,1152]{1,0:T(8,128)(2,1)} %pack_weights.1.refs_0_), channel_id=1, source_target_pairs={{0,8},{4,12},{8,16},{12,20},{16,24},{20,28},{24,0},{28,4},{1,9},{5... | collective-permute-start | bytes 663560 | tf_op jit(solution)/shard_map/ppermute | solution.py:823
  17.9 14.8 %collective-permute-start.11 = (bf16[96,1152]{1,0:T(8,128)(2,1)}, bf16[96,1152]{1,0:T(8,128)(2,1)}, u32[]{:S(2)}, u32[]{:S(2)}) collective-permute-start(bf16[96,1152]{1,0:T(8,128)(2,1)} %pack_weights.1.refs_0_), channel_id=1, source_target_pairs={{0,16},{4,20},{8,24},{12,28},{16,0},{20,4},{24,8},{28,12},{1,17},{... | collective-permute-start | bytes 663560 | tf_op jit(solution)/shard_map/ppermute | solution.py:823
  18.2 18.9 %collective-permute-start.17 = (bf16[256,768]{1,0:T(8,128)(2,1)S(1)}, bf16[256,768]{1,0:T(8,128)(2,1)}, u32[]{:S(2)}, u32[]{:S(2)}) collective-permute-start(bf16[256,768]{1,0:T(8,128)(2,1)S(1)} %get-tuple-element.72.refs_8_), channel_id=1, source_target_pairs={{0,1},{1,0},{2,3},{3,2},{4,5},{5,4},{6,7},{7,6},{8,9},{9,8},{10,11... | collective-permute-start | bytes 1179656 | tf_op jit(solution)/shard_map/ppermute | solution.py:820
  19.7 17.9 %collective-permute-start.20 = (bf16[256,768]{1,0:T(8,128)(2,1)S(1)}, bf16[256,768]{1,0:T(8,128)(2,1)}, u32[]{:S(2)}, u32[]{:S(2)}) collective-permute-start(bf16[256,768]{1,0:T(8,128)(2,1)S(1)} %get-tuple-element.74.refs_9_), channel_id=1, source_target_pairs={{0,2},{1,3},{2,0},{3,1},{4,6},{5,7},{6,4},{7,5},{8,10},{9,11},{10,... | collective-permute-start | bytes 1179656 | tf_op jit(solution)/shard_map/ppermute | solution.py:820
  21.7 1.3 collective-permute-start.7
  23.0 20.8 %copy-start.30 = (bf16[96,384]{1,0:T(8,128)(2,1)}, bf16[96,384]{1,0:T(8,128)(2,1)S(1)}, u32[]{:S(2)}) copy-start(bf16[96,384]{1,0:T(8,128)(2,1)S(1)} %collective-permute-done.7.refs_5_) | copy-start | bytes 221188
  23.0 14.1 %collective-permute-start.12 = (bf16[96,1152]{1,0:T(8,128)(2,1)}, bf16[96,1152]{1,0:T(8,128)(2,1)}, u32[]{:S(2)}, u32[]{:S(2)}) collective-permute-start(bf16[96,1152]{1,0:T(8,128)(2,1)} %pack_weights.1.refs_0_), channel_id=1, source_target_pairs={{0,24},{4,28},{8,0},{12,4},{16,8},{20,12},{24,16},{28,20},{1,25},{... | collective-permute-start | bytes 663560 | tf_op jit(solution)/shard_map/ppermute | solution.py:823
  25.9 22.9 %copy-start.25 = (bf16[96,1152]{1,0:T(8,128)(2,1)}, bf16[96,1152]{1,0:T(8,128)(2,1)S(1)}, u32[]{:S(2)}) copy-start(bf16[96,1152]{1,0:T(8,128)(2,1)S(1)} %collective-permute-done.10.refs_1_) | copy-start | bytes 663556
  25.9 19.5 %collective-permute-start.18 = (bf16[256,768]{1,0:T(8,128)(2,1)S(1)}, bf16[256,768]{1,0:T(8,128)(2,1)S(1)}, u32[]{:S(2)}, u32[]{:S(2)}) collective-permute-start(bf16[256,768]{1,0:T(8,128)(2,1)S(1)} %get-tuple-element.74.refs_9_), channel_id=1, source_target_pairs={{0,1},{1,0},{2,3},{3,2},{4,5},{5,4},{6,7},{7,6},{8,9},{9,8},{10,11... | collective-permute-start | bytes 1179656 | tf_op jit(solution)/shard_map/ppermute | solution.py:820
  32.6 14.0 %collective-permute-start.19 = (bf16[256,768]{1,0:T(8,128)(2,1)S(1)}, bf16[256,768]{1,0:T(8,128)(2,1)S(1)}, u32[]{:S(2)}, u32[]{:S(2)}) collective-permute-start(bf16[256,768]{1,0:T(8,128)(2,1)S(1)} %get-tuple-element.72.refs_8_), channel_id=1, source_target_pairs={{0,2},{1,3},{2,0},{3,1},{4,6},{5,7},{6,4},{7,5},{8,10},{9,11},{10,... | collective-permute-start | bytes 1179656 | tf_op jit(solution)/shard_map/ppermute | solution.py:820
  37.1 7.6 %collective-permute-start.13 = (bf16[96,1152]{1,0:T(8,128)(2,1)}, bf16[96,1152]{1,0:T(8,128)(2,1)S(1)}, u32[]{:S(2)}, u32[]{:S(2)}) collective-permute-start(bf16[96,1152]{1,0:T(8,128)(2,1)} %pack_weights.1.refs_0_), channel_id=1, source_target_pairs={{0,4},{4,0},{8,12},{12,8},{16,20},{20,16},{24,28},{28,24},{1,5},{5... | collective-permute-start | bytes 663560 | tf_op jit(solution)/shard_map/ppermute | solution.py:826
  37.1 15.3 %collective-permute-start.21 = (bf16[256,768]{1,0:T(8,128)(2,1)}, bf16[256,768]{1,0:T(8,128)(2,1)}, u32[]{:S(2)}, u32[]{:S(2)}) collective-permute-start(bf16[256,768]{1,0:T(8,128)(2,1)} %collective-permute-done.17.refs_10_), channel_id=1, source_target_pairs={{0,2},{1,3},{2,0},{3,1},{4,6},{5,7},{6,4},{7,5},{8,10},{9,11},{10,... | collective-permute-start | bytes 1179656 | tf_op jit(solution)/shard_map/ppermute | solution.py:820
  37.6 14.8 %collective-permute-start.22 = (bf16[256,768]{1,0:T(8,128)(2,1)}, bf16[256,768]{1,0:T(8,128)(2,1)}, u32[]{:S(2)}, u32[]{:S(2)}) collective-permute-start(bf16[256,768]{1,0:T(8,128)(2,1)} %collective-permute-done.20.refs_13_), channel_id=1, source_target_pairs={{0,1},{1,0},{2,3},{3,2},{4,5},{5,4},{6,7},{7,6},{8,9},{9,8},{10,11... | collective-permute-start | bytes 1179656 | tf_op jit(solution)/shard_map/ppermute | solution.py:820
  45.4 3.4 %collective-permute-start.14 = (bf16[96,1152]{1,0:T(8,128)(2,1)S(1)}, bf16[96,1152]{1,0:T(8,128)(2,1)S(1)}, u32[]{:S(2)}, u32[]{:S(2)}) collective-permute-start(bf16[96,1152]{1,0:T(8,128)(2,1)S(1)} %collective-permute-done.10.refs_1_), channel_id=1, source_target_pairs={{0,4},{4,0},{8,12},{12,8},{16,20},{20,16},{24,28},{28,24},{1,5},{5... | collective-permute-start | bytes 663560 | tf_op jit(solution)/shard_map/ppermute | solution.py:826
  46.2 4.2 %collective-permute-start.15 = (bf16[96,1152]{1,0:T(8,128)(2,1)}, bf16[96,1152]{1,0:T(8,128)(2,1)S(1)}, u32[]{:S(2)}, u32[]{:S(2)}) collective-permute-start(bf16[96,1152]{1,0:T(8,128)(2,1)} %collective-permute-done.11.refs_2_), channel_id=1, source_target_pairs={{0,4},{4,0},{8,12},{12,8},{16,20},{20,16},{24,28},{28,24},{1,5},{5... | collective-permute-start | bytes 663560 | tf_op jit(solution)/shard_map/ppermute | solution.py:826
  47.4 4.5 %collective-permute-start.16 = (bf16[96,1152]{1,0:T(8,128)(2,1)}, bf16[96,1152]{1,0:T(8,128)(2,1)S(1)}, u32[]{:S(2)}, u32[]{:S(2)}) collective-permute-start(bf16[96,1152]{1,0:T(8,128)(2,1)} %collective-permute-done.12.refs_3_), channel_id=1, source_target_pairs={{0,4},{4,0},{8,12},{12,8},{16,20},{20,16},{24,28},{28,24},{1,5},{5... | collective-permute-start | bytes 663560 | tf_op jit(solution)/shard_map/ppermute | solution.py:826
  48.8 39.2 %collective-permute-start = (bf16[512,768]{1,0:T(8,128)(2,1)S(1)}, bf16[512,768]{1,0:T(8,128)(2,1)S(1)}, u32[]{:S(2)}, u32[]{:S(2)}) collective-permute-start(bf16[512,768]{1,0:T(8,128)(2,1)S(1)} %copy-done.4), channel_id=1, source_target_pairs={{0,1},{1,0},{2,3},{3,2},{4,5},{5,4},{6,7},{7,6},{8,9},{9,8},{10,11... | collective-permute-start | bytes 2359304 | tf_op jit(solution)/shard_map/ppermute | solution.py:820
  50.4 37.6 %collective-permute-start.1 = (bf16[512,768]{1,0:T(8,128)(2,1)S(1)}, bf16[512,768]{1,0:T(8,128)(2,1)S(1)}, u32[]{:S(2)}, u32[]{:S(2)}) collective-permute-start(bf16[512,768]{1,0:T(8,128)(2,1)S(1)} %copy-done.4), channel_id=1, source_target_pairs={{0,2},{1,3},{2,0},{3,1},{4,6},{5,7},{6,4},{7,5},{8,10},{9,11},{10,... | collective-permute-start | bytes 2359304 | tf_op jit(solution)/shard_map/ppermute | solution.py:820
  51.9 36.1 %collective-permute-start.2 = (bf16[512,768]{1,0:T(8,128)(2,1)S(1)}, bf16[512,768]{1,0:T(8,128)(2,1)S(1)}, u32[]{:S(2)}, u32[]{:S(2)}) collective-permute-start(bf16[512,768]{1,0:T(8,128)(2,1)S(1)} %copy-done.4), channel_id=1, source_target_pairs={{0,3},{1,2},{2,1},{3,0},{4,7},{5,6},{6,5},{7,4},{8,11},{9,10},{10,... | collective-permute-start | bytes 2359304 | tf_op jit(solution)/shard_map/ppermute | solution.py:820
  52.4 28.8 %collective-permute-start.8 = (bf16[96,384]{1,0:T(8,128)(2,1)S(1)}, bf16[96,384]{1,0:T(8,128)(2,1)S(1)}, u32[]{:S(2)}, u32[]{:S(2)}) collective-permute-start(bf16[96,384]{1,0:T(8,128)(2,1)S(1)} %collective-permute-done.4.refs_2_), channel_id=1, source_target_pairs={{0,4},{4,0},{8,12},{12,8},{16,20},{20,16},{24,28},{28,24},{1,5},{5... | collective-permute-start | bytes 221192 | tf_op jit(solution)/shard_map/ppermute | solution.py:826
  52.4 28.8 %collective-permute-start.9 = (bf16[96,384]{1,0:T(8,128)(2,1)S(1)}, bf16[96,384]{1,0:T(8,128)(2,1)S(1)}, u32[]{:S(2)}, u32[]{:S(2)}) collective-permute-start(bf16[96,384]{1,0:T(8,128)(2,1)S(1)} %collective-permute-done.5.refs_3_), channel_id=1, source_target_pairs={{0,4},{4,0},{8,12},{12,8},{16,20},{20,16},{24,28},{28,24},{1,5},{5... | collective-permute-start | bytes 221192 | tf_op jit(solution)/shard_map/ppermute | solution.py:826
  57.7 23.5 %copy-start.29 = (bf16[384,96]{0,1:T(8,128)(2,1)S(1)}, bf16[384,96]{0,1:T(8,128)(2,1)}, u32[]{:S(2)}) copy-start(bf16[384,96]{0,1:T(8,128)(2,1)} %param.34) | copy-start | bytes 221188
  57.7 23.5 %copy-start.31 = (bf16[96,384]{1,0:T(8,128)(2,1)S(1)}, bf16[96,384]{1,0:T(8,128)(2,1)}, u32[]{:S(2)}) copy-start(bf16[96,384]{1,0:T(8,128)(2,1)} %copy-done.30) | copy-start | bytes 221188
  91.1 4.7 %collective-permute-start.25 = (f32[8,2,256]{2,1,0:T(2,128)S(1)}, f32[8,2,256]{2,1,0:T(2,128)S(1)}, u32[]{:S(2)}, u32[]{:S(2)}) collective-permute-start(f32[8,2,256]{2,1,0:T(2,128)S(1)} %get-tuple-element.81), channel_id=1, source_target_pairs={{0,3},{1,2},{2,1},{3,0},{4,7},{5,6},{6,5},{7,4},{8,11},{9,10},{10,... | collective-permute-start | bytes 49160 | tf_op jit(solution)/shard_map/ppermute | solution.py:820
  92.9 3.7 %collective-permute-start.24 = (f32[8,2,256]{2,1,0:T(2,128)S(1)}, f32[8,2,256]{2,1,0:T(2,128)S(1)}, u32[]{:S(2)}, u32[]{:S(2)}) collective-permute-start(f32[8,2,256]{2,1,0:T(2,128)S(1)} %get-tuple-element.81), channel_id=1, source_target_pairs={{0,2},{1,3},{2,0},{3,1},{4,6},{5,7},{6,4},{7,5},{8,10},{9,11},{10,... | collective-permute-start | bytes 49160 | tf_op jit(solution)/shard_map/ppermute | solution.py:820
  94.1 3.7 %collective-permute-start.23 = (f32[8,2,256]{2,1,0:T(2,128)S(1)}, f32[8,2,256]{2,1,0:T(2,128)S(1)}, u32[]{:S(2)}, u32[]{:S(2)}) collective-permute-start(f32[8,2,256]{2,1,0:T(2,128)S(1)} %get-tuple-element.81), channel_id=1, source_target_pairs={{0,1},{1,0},{2,3},{3,2},{4,5},{5,4},{6,7},{7,6},{8,9},{9,8},{10,11... | collective-permute-start | bytes 49160 | tf_op jit(solution)/shard_map/ppermute | solution.py:820
  144.7 29.9 %collective-permute-start.33 = (bf16[400,768]{1,0:T(8,128)(2,1)S(1)}, bf16[400,768]{1,0:T(8,128)(2,1)S(1)}, u32[]{:S(2)}, u32[]{:S(2)}) collective-permute-start(bf16[400,768]{1,0:T(8,128)(2,1)S(1)} %get-tuple-element.101), channel_id=1, source_target_pairs={{0,4},{4,0},{8,12},{12,8},{16,20},{20,16},{24,28},{28,24},{1,5},{5... | collective-permute-start | bytes 1843208 | tf_op jit(solution)/shard_map/ppermute | solution.py:826
  144.7 14.0 %collective-permute-start.34 = (bf16[192,768]{1,0:T(8,128)(2,1)S(1)}, bf16[192,768]{1,0:T(8,128)(2,1)S(1)}, u32[]{:S(2)}, u32[]{:S(2)}) collective-permute-start(bf16[192,768]{1,0:T(8,128)(2,1)S(1)} %get-tuple-element.105), channel_id=1, source_target_pairs={{0,8},{4,12},{8,16},{12,20},{16,24},{20,28},{24,0},{28,4},{1,9},{5... | collective-permute-start | bytes 884744 | tf_op jit(solution)/shard_map/ppermute | solution.py:823
  147.0 24.0 %collective-permute-start.35 = (bf16[192,768]{1,0:T(8,128)(2,1)S(1)}, bf16[192,768]{1,0:T(8,128)(2,1)S(1)}, u32[]{:S(2)}, u32[]{:S(2)}) collective-permute-start(bf16[192,768]{1,0:T(8,128)(2,1)S(1)} %get-tuple-element.106), channel_id=1, source_target_pairs={{0,16},{4,20},{8,24},{12,28},{16,0},{20,4},{24,8},{28,12},{1,17},{... | collective-permute-start | bytes 884744 | tf_op jit(solution)/shard_map/ppermute | solution.py:823
  151.2 22.2 %collective-permute-start.36 = (bf16[192,768]{1,0:T(8,128)(2,1)S(1)}, bf16[192,768]{1,0:T(8,128)(2,1)S(1)}, u32[]{:S(2)}, u32[]{:S(2)}) collective-permute-start(bf16[192,768]{1,0:T(8,128)(2,1)S(1)} %get-tuple-element.107), channel_id=1, source_target_pairs={{0,24},{4,28},{8,0},{12,4},{16,8},{20,12},{24,16},{28,20},{1,25},{... | collective-permute-start | bytes 884744 | tf_op jit(solution)/shard_map/ppermute | solution.py:823
  151.2 31.3 %collective-permute-start.29 = (bf16[2,256,768]{2,1,0:T(8,128)(2,1)}, bf16[2,256,768]{2,1,0:T(8,128)(2,1)S(1)}, u32[]{:S(2)}, u32[]{:S(2)}) collective-permute-start(bf16[2,256,768]{2,1,0:T(8,128)(2,1)} %get-tuple-element.97), channel_id=1, source_target_pairs={{0,1},{1,0},{2,3},{3,2},{4,5},{5,4},{6,7},{7,6},{8,9},{9,8},{10,11... | collective-permute-start | bytes 2359304 | tf_op jit(solution)/shard_map/ppermute | solution.py:820
  158.6 37.5 %collective-permute-start.31 = (bf16[2,256,768]{2,1,0:T(8,128)(2,1)}, bf16[2,256,768]{2,1,0:T(8,128)(2,1)S(1)}, u32[]{:S(2)}, u32[]{:S(2)}) collective-permute-start(bf16[2,256,768]{2,1,0:T(8,128)(2,1)} %get-tuple-element.98), channel_id=1, source_target_pairs={{0,2},{1,3},{2,0},{3,1},{4,6},{5,7},{6,4},{7,5},{8,10},{9,11},{10,... | collective-permute-start | bytes 2359304 | tf_op jit(solution)/shard_map/ppermute | solution.py:820
  171.8 26.1 %collective-permute-start.28 = (bf16[2,256,768]{2,1,0:T(8,128)(2,1)}, bf16[2,256,768]{2,1,0:T(8,128)(2,1)}, u32[]{:S(2)}, u32[]{:S(2)}) collective-permute-start(bf16[2,256,768]{2,1,0:T(8,128)(2,1)} %get-tuple-element.79.refs_7_), channel_id=1, source_target_pairs={{0,3},{1,2},{2,1},{3,0},{4,7},{5,6},{6,5},{7,4},{8,11},{9,10},{10,... | collective-permute-start | bytes 2359304 | tf_op jit(solution)/shard_map/ppermute | solution.py:820
  174.1 37.7 %collective-permute-start.27 = (bf16[2,256,768]{2,1,0:T(8,128)(2,1)}, bf16[2,256,768]{2,1,0:T(8,128)(2,1)}, u32[]{:S(2)}, u32[]{:S(2)}) collective-permute-start(bf16[2,256,768]{2,1,0:T(8,128)(2,1)} %get-tuple-element.78.refs_6_), channel_id=1, source_target_pairs={{0,2},{1,3},{2,0},{3,1},{4,6},{5,7},{6,4},{7,5},{8,10},{9,11},{10,... | collective-permute-start | bytes 2359304 | tf_op jit(solution)/shard_map/ppermute | solution.py:820
  175.4 37.1 %collective-permute-start.26 = (bf16[2,256,768]{2,1,0:T(8,128)(2,1)}, bf16[2,256,768]{2,1,0:T(8,128)(2,1)}, u32[]{:S(2)}, u32[]{:S(2)}) collective-permute-start(bf16[2,256,768]{2,1,0:T(8,128)(2,1)} %get-tuple-element.77.refs_5_), channel_id=1, source_target_pairs={{0,1},{1,0},{2,3},{3,2},{4,5},{5,4},{6,7},{7,6},{8,9},{9,8},{10,11... | collective-permute-start | bytes 2359304 | tf_op jit(solution)/shard_map/ppermute | solution.py:820
  182.5 31.5 %copy-start.7 = (bf16[2,256,768]{2,1,0:T(8,128)(2,1)S(1)}, bf16[2,256,768]{2,1,0:T(8,128)(2,1)}, u32[]{:S(2)}) copy-start(bf16[2,256,768]{2,1,0:T(8,128)(2,1)} %copy-done.6) | copy-start | bytes 2359300
  182.5 13.8 %collective-permute-start.37 = (bf16[96,768]{1,0:T(8,128)(2,1)S(1)}, bf16[96,768]{1,0:T(8,128)(2,1)S(1)}, u32[]{:S(2)}, u32[]{:S(2)}) collective-permute-start(bf16[96,768]{1,0:T(8,128)(2,1)S(1)} %get-tuple-element.109), channel_id=1, source_target_pairs={{0,4},{4,0},{8,12},{12,8},{16,20},{20,16},{24,28},{28,24},{1,5},{5... | collective-permute-start | bytes 442376 | tf_op jit(solution)/shard_map/ppermute | solution.py:826
  196.1 20.0 %collective-permute-start.38 = (bf16[112,768]{1,0:T(8,128)(2,1)S(1)}, bf16[112,768]{1,0:T(8,128)(2,1)S(1)}, u32[]{:S(2)}, u32[]{:S(2)}) collective-permute-start(bf16[112,768]{1,0:T(8,128)(2,1)S(1)} %get-tuple-element.110), channel_id=1, source_target_pairs={{0,8},{4,12},{8,16},{12,20},{16,24},{20,28},{24,0},{28,4},{1,9},{5... | collective-permute-start | bytes 516104 | tf_op jit(solution)/shard_map/ppermute | solution.py:823
  196.3 19.8 %collective-permute-start.39 = (bf16[112,768]{1,0:T(8,128)(2,1)S(1)}, bf16[112,768]{1,0:T(8,128)(2,1)S(1)}, u32[]{:S(2)}, u32[]{:S(2)}) collective-permute-start(bf16[112,768]{1,0:T(8,128)(2,1)S(1)} %get-tuple-element.111), channel_id=1, source_target_pairs={{0,16},{4,20},{8,24},{12,28},{16,0},{20,4},{24,8},{28,12},{1,17},{... | collective-permute-start | bytes 516104 | tf_op jit(solution)/shard_map/ppermute | solution.py:823
  197.8 18.3 %collective-permute-start.40 = (bf16[112,768]{1,0:T(8,128)(2,1)S(1)}, bf16[112,768]{1,0:T(8,128)(2,1)S(1)}, u32[]{:S(2)}, u32[]{:S(2)}) collective-permute-start(bf16[112,768]{1,0:T(8,128)(2,1)S(1)} %get-tuple-element.112), channel_id=1, source_target_pairs={{0,24},{4,28},{8,0},{12,4},{16,8},{20,12},{24,16},{28,20},{1,25},{... | collective-permute-start | bytes 516104 | tf_op jit(solution)/shard_map/ppermute | solution.py:823
  211.8 14.7 %collective-permute-start.30 = (bf16[256,768]{1,0:T(8,128)(2,1)S(1)}, bf16[256,768]{1,0:T(8,128)(2,1)S(1)}, u32[]{:S(2)}, u32[]{:S(2)}) collective-permute-start(bf16[256,768]{1,0:T(8,128)(2,1)S(1)} %get-tuple-element.131), channel_id=1, source_target_pairs={{0,2},{1,3},{2,0},{3,1},{4,6},{5,7},{6,4},{7,5},{8,10},{9,11},{10,... | collective-permute-start | bytes 1179656 | tf_op jit(solution)/shard_map/ppermute | solution.py:820
  212.6 14.0 %collective-permute-start.32 = (bf16[256,768]{1,0:T(8,128)(2,1)S(1)}, bf16[256,768]{1,0:T(8,128)(2,1)S(1)}, u32[]{:S(2)}, u32[]{:S(2)}) collective-permute-start(bf16[256,768]{1,0:T(8,128)(2,1)S(1)} %get-tuple-element.130), channel_id=1, source_target_pairs={{0,1},{1,0},{2,3},{3,2},{4,5},{5,4},{6,7},{7,6},{8,9},{9,8},{10,11... | collective-permute-start | bytes 1179656 | tf_op jit(solution)/shard_map/ppermute | solution.py:820
  213.9 7.1 %copy-start.1 = (f32[512,768]{1,0:T(8,128)S(1)}, f32[512,768]{1,0:T(8,128)}, u32[]{:S(2)}) copy-start(f32[512,768]{1,0:T(8,128)} %x_ref.1) | copy-start | bytes 4718596
  217.5 7.8 %copy-start.18 = (f32[768]{0:T(1024)S(1)}, f32[768]{0:T(1024)}, u32[]{:S(2)}) copy-start(f32[768]{0:T(1024)} %norm_ref.1) | copy-start | bytes 9220
  217.5 9.0 %copy-start.5 = (bf16[512,768]{1,0:T(8,128)(2,1)S(1)}, bf16[512,768]{1,0:T(8,128)(2,1)}, u32[]{:S(2)}) copy-start(bf16[512,768]{1,0:T(8,128)(2,1)} %cot_ref.1) | copy-start | bytes 2359300
  217.5 6.5 %collective-permute-start.41 = (bf16[112,256]{1,0:T(8,128)(2,1)S(1)}, bf16[112,256]{1,0:T(8,128)(2,1)S(1)}, u32[]{:S(2)}, u32[]{:S(2)}) collective-permute-start(bf16[112,256]{1,0:T(8,128)(2,1)S(1)} %get-tuple-element.113.refs_0_), channel_id=1, source_target_pairs={{0,1},{1,0},{2,3},{3,2},{4,5},{5,4},{6,7},{7,6},{8,9},{9,8},{10,11... | collective-permute-start | bytes 172040 | tf_op jit(solution)/shard_map/ppermute | solution.py:820
  218.3 5.7 %collective-permute-start.42 = (bf16[112,256]{1,0:T(8,128)(2,1)S(1)}, bf16[112,256]{1,0:T(8,128)(2,1)S(1)}, u32[]{:S(2)}, u32[]{:S(2)}) collective-permute-start(bf16[112,256]{1,0:T(8,128)(2,1)S(1)} %get-tuple-element.113.refs_0_), channel_id=1, source_target_pairs={{0,2},{1,3},{2,0},{3,1},{4,6},{5,7},{6,4},{7,5},{8,10},{9,11},{10,... | collective-permute-start | bytes 172040 | tf_op jit(solution)/shard_map/ppermute | solution.py:820
  219.5 5.8 %collective-permute-start.43 = (bf16[112,256]{1,0:T(8,128)(2,1)S(1)}, bf16[112,256]{1,0:T(8,128)(2,1)S(1)}, u32[]{:S(2)}, u32[]{:S(2)}) collective-permute-start(bf16[112,256]{1,0:T(8,128)(2,1)S(1)} %get-tuple-element.113.refs_0_), channel_id=1, source_target_pairs={{0,3},{1,2},{2,1},{3,0},{4,7},{5,6},{6,5},{7,4},{8,11},{9,10},{10,... | collective-permute-start | bytes 172040 | tf_op jit(solution)/shard_map/ppermute | solution.py:820
  (21 other events, 24.5 us)

commit v4 on v3

--- a/solution.py
+++ b/solution.py
@@ -122,6 +122,18 @@
     return jnp.where((r >= c) & (r // SUB == c // SUB), 1.0, 0.0).astype(BF16)
 
 
+def lane_pick(dm):
+    r = lax.broadcasted_iota(jnp.int32, (2 * LANES, dm.ip), 0)
+    c = lax.broadcasted_iota(jnp.int32, (2 * LANES, dm.ip), 1)
+    return jnp.where(r % LANES == c // dm.hd, 1.0, 0.0).astype(BF16)
+
+
+def to_lanes(cols, pick):
+    high = cols.astype(BF16)
+    low = (cols - high.astype(F32)).astype(BF16)
+    return dot(jnp.concatenate([high, low], axis=1), pick)
+
+
 def head_masks(dm):
     lane = lax.broadcasted_iota(jnp.int32, (1, LANES), 1)
     return [jnp.where(lane // dm.hd == j, 1.0, 0.0).astype(BF16) for j in range(dm.per)]
@@ -167,8 +179,10 @@
     n_parts = refs[dm.n_dp : dm.n_dp + dm.pieces]
     rest = refs[dm.n_dp + dm.pieces :]
     rows_ref, conv_ref, hp_ref, lane_ref = rest[:4]
-    (g_out, v_out, cv_out, ys_out, st_out, h_out, sum_out, nm_out, sg_out, w_out) = rest[4:14]
-    (w_v, nm_v, h_ref, vbuf, tri_ref, pbuf, w_sem, n_sem, o_sem) = rest[14:]
+    (z_out, e_out, gd_out, v_out, cv_out, ys_out, st_out, h_out, sum_out, nm_out, sg_out, w_out) = rest[
+        4:16
+    ]
+    (w_v, nm_v, h_ref, vbuf, tri_ref, pick_ref, pbuf, gate_s, w_sem, n_sem, o_sem) = rest[16:]
     i = pl.program_id(0)
     save = pltpu.make_async_copy(w_v, w_out, o_sem)
 
@@ -184,6 +198,7 @@
         h_ref[...] = jnp.zeros_like(h_ref)
         vbuf[...] = jnp.zeros_like(vbuf)
         tri_ref[...] = lower_blocks()
+        pick_ref[...] = lane_pick(dm)
         for copy in copies:
             copy.wait()
         save.start()
@@ -197,7 +212,7 @@
         vbuf[c, 8 : 8 + q, :] = pbuf[:, ip + c * LANES : ip + (c + 1) * LANES]
     v_out[...] = pbuf[:, ip : ip + vs].astype(BF16)
     raw = pbuf[:, ip + vs :]
-    g_out[...] = pbuf[:, :ip].astype(BF16)
+    gate_s[...] = pbuf[:, :ip]
     st_out[...] = raw
 
     acts = []
@@ -222,6 +237,7 @@
 
     delta, logs, enter, ending = decay_parts(raw, hp_ref, cols, tri_ref[...])
     logs_t = logs.T
+    delta_e, enter_e, ending_e = [to_lanes(v, pick_ref[...]) for v in (delta, enter, ending)]
     r = lax.broadcasted_iota(jnp.int32, (SUB, SUB), 0)
     c = lax.broadcasted_iota(jnp.int32, (SUB, SUB), 1)
     masks = head_masks(dm)
@@ -234,12 +250,12 @@
         source_t = source.T
         keep = scalars[dm.at_keep + i * (q // SUB) + k].astype(F32)
         total = jnp.exp2(logs[a][SUB - 1 :, :]) * keep
-        h_out[k * st : (k + 1) * st, :] = h_ref[...]
+        h_out[k * st : (k + 1) * st, :] = h_ref[...].astype(BF16)
         square = None
         for p in range(dm.pairs):
             g = slice(p * LANES, (p + 1) * LANES)
             x = acts[p][a]
-            u = x * spread(delta[a], p, hd)
+            u = x * delta_e[a, g]
             ub = u.astype(BF16)
             mixing = []
             for j in range(dm.per):
@@ -251,12 +267,18 @@
                 jnp.concatenate([ub * mask for mask in masks], axis=0),
             )
             held = h_ref[:, g]
-            y = y + dot(target, held.astype(BF16)) * spread(enter[a], p, hd)
-            wu = (u * spread(ending[a], p, hd)).astype(BF16)
+            y = y + dot(target, held.astype(BF16)) * enter_e[a, g]
+            wu = (u * ending_e[a, g]).astype(BF16)
             h_ref[:, g] = held * spread(total, p, hd) + dot(source_t, wu)
             ys_out[a, g] = y
-            gate = g_out[a, g].astype(F32)
-            gated = (y + lane_ref[0:1, g] * x) * (gate * sigmoid(gate))
+            gate = gate_s[a, g]
+            sig = sigmoid(gate)
+            z = gate * sig
+            y = y + lane_ref[0:1, g] * x
+            gated = y * z
+            z_out[a, g] = z
+            gd_out[a, g] = gated
+            e_out[a, g] = (y * (sig + z * (1.0 - sig))).astype(BF16)
             sg_out[a, g] = (gated * lane_ref[1:2, g]).astype(BF16)
             square = gated * gated if square is None else square + gated * gated
         squares.append(square)
@@ -268,70 +290,48 @@
 
 
 def branch_kernel(dm, scalars, *refs):
-    n_dp, n_t = dm.n_dp, dm.n_t
-    w_parts, sg_hbm = refs[:n_dp], refs[n_dp]
-    w_out, outs = refs[n_dp + 1], refs[n_dp + 2 : n_dp + 2 + n_t]
-    sg_v, buf, w_sem, g_sem, sem = refs[n_dp + 2 + n_t :]
-    per = dm.chunk_rows // BLOCK
+    n_dp, n_t, q = dm.n_dp, dm.n_t, BLOCK
+    w_parts, sg_ref = refs[:n_dp], refs[n_dp]
+    w_out, outs, (w_sem,) = refs[n_dp + 1], refs[n_dp + 2 : n_dp + 2 + n_t], refs[n_dp + 2 + n_t :]
     loads = load_parts(w_parts, w_out, w_sem, scalars, 0, dm.part_rows)
-    whole = pltpu.make_async_copy(sg_hbm, sg_v, g_sem)
     for copy in loads:
         copy.start()
-    whole.start()
     for copy in loads:
         copy.wait()
-    whole.wait()
-    for i in range(dm.blocks):
-        at = slice(i * BLOCK, (i + 1) * BLOCK)
-        buf[i] = dot(sg_v[at, :], w_out[...], MT).astype(BF16)
-        for k in range(n_t):
-
-            @pl.when(scalars[dm.at_rel + i] == k)
-            def _():
-                pltpu.make_async_copy(buf.at[i], outs[k].at[i % per], sem.at[i]).start()
-
-    for i in range(dm.blocks):
-        pltpu.make_async_copy(buf.at[i], outs[0].at[0], sem.at[i]).wait()
-
-
-def dots_kernel(dm, scalars, *refs):
+    for k in range(n_t):
+        chunk = pl.multiple_of(scalars[dm.at_c + k], dm.chunk_rows)
+        for h in range(dm.chunk_rows // q):
+            at = pl.ds(pl.multiple_of(chunk + h * q, q), q)
+            outs[k][h] = dot(sg_ref[at, :], w_out[...], MT).astype(BF16)
+
+
+def scaled_kernel(dm, scalars, *refs):
     q, n_t = BLOCK, dm.n_t
-    c_parts, b_parts = refs[:n_t], refs[n_t : 2 * n_t]
-    sq_ref, sum_out, ct_hbm = refs[2 * n_t : 2 * n_t + 3]
-    ct_v, br_v, c_sem, b_sem, t_sem = refs[2 * n_t + 3 :]
-    takes = [pltpu.make_async_copy(c_parts[k], ct_v.at[k], c_sem.at[k]) for k in range(n_t)]
-    takes += [pltpu.make_async_copy(b_parts[k], br_v.at[k], b_sem.at[k]) for k in range(n_t)]
-    for copy in takes:
-        copy.start()
-    gives = []
+    c_parts = refs[:n_t]
+    w_ref, lane_ref, gd_ref, sq_ref, sc_out, sum_out, ct_out = refs[n_t:]
     for k in range(n_t):
-        takes[k].wait()
-        takes[n_t + k].wait()
         chunk = pl.multiple_of(scalars[dm.at_c + k], dm.chunk_rows)
-        gives.append(
-            pltpu.make_async_copy(ct_v.at[k], ct_hbm.at[pl.ds(chunk, dm.chunk_rows), :], t_sem.at[k])
-        )
-        gives[-1].start()
         for h in range(dm.chunk_rows // q):
-            dots = None
-            for c in range(dm.width // LANES):
-                g = slice(c * LANES, (c + 1) * LANES)
-                cot = ct_v[k, h * q : (h + 1) * q, g].astype(F32)
-                prod = cot * br_v[k, h, :, g].astype(F32)
-                dots = prod if dots is None else dots + prod
+            at = pl.ds(pl.multiple_of(chunk + h * q, q), q)
+            cot = c_parts[k][h * q : (h + 1) * q, :]
+            ct_out[at, :] = cot
+            sc = (dot(cot, w_ref[...]) * lane_ref[1:2, :]).astype(BF16)
+            sc_out[at, :] = sc
+            prod = sc.astype(F32) * gd_ref[at, :]
+            dots = prod[:, :LANES]
+            for p in range(1, dm.pairs):
+                dots = dots + prod[:, p * LANES : (p + 1) * LANES]
             blk = chunk // q + h
             sum_out[blk, 0:1, :] = sq_ref[blk]
             sum_out[blk, 1:2, :] = jnp.sum(dots.T, axis=0, keepdims=True)
-    for copy in gives:
-        copy.wait()
 
 
 def gate_kernel(dm, scalars, *refs):
     q, ip, r = BLOCK, dm.ip, dm.part_rows
-    (w_ref, wo_ref, rk_ref, lane_ref, g_in, cv_in, ys_in, cot_in, nm_in, ct_in) = refs[:10]
-    dg_out, dy_out, lane_out, rows_out, own_out = refs[10:15]
-    z_outs = refs[15 : 14 + dm.n_hi]
-    acc, dg_s, both = refs[14 + dm.n_hi :]
+    (w_ref, rk_ref, lane_ref, z_in, e_in, gd_in, sc_in, nm_in, ct_in) = refs[:9]
+    dg_out, dy_out, lane_out, rows_out, own_out = refs[9:14]
+    z_outs = refs[14 : 13 + dm.n_hi]
+    acc, dg_s, both = refs[13 + dm.n_hi :]
     i = pl.program_id(0)
 
     @pl.when(i == 0)
@@ -346,26 +346,18 @@
     def gating():
         pad = jnp.zeros((LANES - 2, q), F32)
         cols = jnp.concatenate([rk_ref[...], pad], axis=0).T
-        root, pull = cols[:, 0:1], cols[:, 1:2]
-        scaled_cot = dot(cot_in[...], wo_ref[...])
+        root, pull = [jnp.broadcast_to(cols[:, k : k + 1], (q, LANES)) for k in range(2)]
         for p in range(dm.pairs):
             g = slice(p * LANES, (p + 1) * LANES)
-            gate, sc = g_in[:, g].astype(F32), scaled_cot[:, g]
-            cv = cv_in[:, g].astype(F32)
-            x = cv * sigmoid(cv)
-            sig = sigmoid(gate)
-            z = gate * sig
-            y = ys_in[:, g] + lane_ref[0:1, g] * x
-            gated = y * z
+            sc, gated = sc_in[:, g].astype(F32), gd_in[:, g]
             scaled = gated * root
-            cot = root * (lane_ref[1:2, g] * sc) - pull * gated
-            lane_out[0:8, g] += colsum(sc * scaled)
-            dy = cot * z
+            cot = root * sc - pull * gated
+            lane_out[:, g] += colsum(sc * scaled)
+            dy = cot * z_in[:, g]
             dy_out[:, g] = dy.astype(BF16)
-            dg = (cot * y * (sig + z * (1.0 - sig))).astype(BF16)
+            dg = (cot * e_in[:, g].astype(F32)).astype(BF16)
             dg_out[:, g] = dg
             dg_s[:, g] = dg
-            lane_out[8:16, g] += colsum(dy * x)
             both[:, g] = (scaled * lane_ref[1:2, g]).astype(BF16)
 
     @pl.when(i == 0)
@@ -380,6 +372,7 @@
     @pl.when(i == dm.blocks)
     def _():
         gather()
+        lane_out[...] = lane_out[...] / lane_ref[1:2, :]
         prod = acc[:, :LANES] * w_ref[:, :LANES].astype(F32)
         for p in range(1, dm.pairs):
             g = slice(p * LANES, (p + 1) * LANES)
@@ -400,7 +393,7 @@
     mine_out, theirs_out, kept_out = refs[15:18]
     nc_outs = refs[18 : 18 + len(groups)]
     (dh_ref, dbuf, tri_ref, dx_s, act_s, t1_s, t2_s) = refs[18 + len(groups) : 25 + len(groups)]
-    (pj_s, full, acc, tap_out, head_out, nc_buf, nc_sem) = refs[25 + len(groups) :]
+    (pick_ref, skip_s, pj_s, full, acc, tap_out, head_out, nc_buf, nc_sem) = refs[25 + len(groups) :]
     i = pl.program_id(0)
     blk = jnp.maximum(dm.blocks - 1 - i, 0)
     subs = q // SUB
@@ -414,8 +407,10 @@
         dbuf[...] = jnp.zeros_like(dbuf)
         tap_out[...] = jnp.zeros_like(tap_out)
         head_out[...] = jnp.zeros_like(head_out)
+        skip_s[...] = jnp.zeros_like(skip_s)
         acc[...] = jnp.zeros_like(acc)
         tri_ref[...] = lower_blocks()
+        pick_ref[...] = lane_pick(dm)
 
     slot = lax.rem(i, 2)
 
@@ -452,6 +447,7 @@
         tri = tri_ref[...]
         delta, logs, enter, ending = decay_parts(raw, hp_ref, cols, tri)
         logs_t = logs.T
+        deltas, enters, endings = [to_lanes(v, pick_ref[...]) for v in (delta, enter, ending)]
 
         acts, slopes = [], []
         for c in range(vs // LANES):
@@ -480,7 +476,7 @@
             for p in range(dm.pairs):
                 g = slice(p * LANES, (p + 1) * LANES)
                 x, dyb = acts[p][a], dy_in[a, g]
-                delta_e = spread(delta[a], p, hd)
+                delta_e = deltas[a, g]
                 u = x * delta_e
                 ub, dy = u.astype(BF16), dyb.astype(F32)
                 decays = []
@@ -497,19 +493,20 @@
                     ds = part if ds is None else ds + part
                 dh, h_rows = dh_ref[:, g], h_in[k * st : (k + 1) * st, g]
                 dh_b = dh.astype(BF16)
-                end_e = spread(ending[a], p, hd)
+                end_e = endings[a, g]
                 late = end_e * dot(source, dh_b)
                 du = du + late
                 wu = (u * end_e).astype(BF16)
-                edy = (dy * spread(enter[a], p, hd)).astype(BF16)
-                from_wu, from_dy = dot(wu, dh_b, MT), dot(edy, h_rows.astype(BF16), MT)
+                edy = (dy * enters[a, g]).astype(BF16)
+                from_wu, from_dy = dot(wu, dh_b, MT), dot(edy, h_rows, MT)
                 d_in[k] = from_wu if p == 0 else d_in[k] + from_wu
                 d_out[k] = from_dy if p == 0 else d_out[k] + from_dy
                 u32 = ub.astype(F32)
                 t1_s[a, g] = dy * ys_in[a, g] - u32 * du
                 t2_s[a, g] = du * x
+                skip_s[:, g] += colsum(dy * x)
                 kept = dh * spread(total, p, hd)
-                act_s[8 * k : 8 * k + 8, g] = colsum(u32 * late) + colsum(h_rows * kept)
+                act_s[8 * k : 8 * k + 8, g] = colsum(u32 * late) + colsum(h_rows.astype(F32) * kept)
                 dh_ref[:, g] = kept + dot(target_t, edy)
                 dx_s[a, g] = (delta_e * du + lane_ref[0:1, g] * dy) * slopes[p][a]
             ds_b = ds.astype(BF16)
@@ -527,7 +524,7 @@
             d_log = d_log + jnp.where(row == (k + 1) * SUB - 1, end, 0.0)
         d_step = dot_split(tri, d_log, TM)
         head_out[8:16, :] += colsum(d_step * delta)
-        d_delta = hp_ref[1:2, :] * d_step + split_dot(t2_s[...], pick)
+        d_delta = hp_ref[1:2, :] * d_step + dot(t2_s[...].astype(BF16), pick)
         d_raw = d_delta * sigmoid(raw + hp_ref[0:1, :])
         head_out[0:8, :] += colsum(d_raw)
         pj_s[:, vs:] = d_raw.astype(BF16)
@@ -598,8 +595,8 @@
 
         for k in range(5):
             put(tap_out[8 * k : 8 * k + 8, :ip])
-        for k in range(2):
-            put(lanes_ref[8 * k : 8 * k + 8, :])
+        put(lanes_ref[...])
+        put(skip_s[...])
         for k in range(2):
             put(head_out[8 * k : 8 * k + 8, :])
         zero = jnp.zeros((1, LANES), F32)
@@ -828,7 +825,7 @@
     def vmem(shape, dtype):
         return pltpu.VMEM(shape, dtype)
 
-    limit = 20 * 1024 * 1024
+    limit = 16 * 1024 * 1024
     params = pltpu.CompilerParams(dimension_semantics=("arbitrary",), vmem_limit_bytes=limit)
     hbm = pl.BlockSpec(memory_space=pl.ANY)
 
@@ -858,12 +855,11 @@
     else:
         n_list = [normed[0]] + [across(normed[0], k) for k in range(1, n_t)]
         n_rows = (me_t ^ jnp.arange(n_t)) * chunk_rows
-    step_first, _ = lax.optimization_barrier((step_proj.T, normed[0]))
     packed = pl.pallas_call(
         functools.partial(pack_kernel, dm),
         out_shape=out(part_rows, dm.np, dtype=BF16),
         name="pack_weights",
-    )(gate_proj, value_proj, shared_proj, step_first)
+    )(gate_proj, value_proj, shared_proj, step_proj.T)
     w_list = [packed] + [along(packed, k) for k in range(1, n_hi)]
     w_list = w_list + [partner(v) for v in w_list]
     outp = pad_cols(output_proj.T, ip)
@@ -925,7 +921,7 @@
     rate = -jnp.exp(decay_log)
     per_head = jnp.stack([pad_vec(step_bias, LANES), pad_vec(rate, LANES)])
     per_head = jnp.pad(per_head, ((0, 6), (0, 0)))
-    per_lane = jnp.stack([pad_vec(jnp.repeat(skip_weight, hd), ip), pad_vec(gate_gain, ip)])
+    per_lane = jnp.stack([pad_vec(jnp.repeat(skip_weight, hd), ip), jnp.pad(gate_gain, (0, ip - inner), constant_values=1.0)])
     per_lane = jnp.pad(per_lane, ((0, 6), (0, 0)))
 
     def const(*shape):
@@ -946,15 +942,17 @@
             scratch_shapes=scratch,
         )
 
-    (gate, value, conved, scan, steps_raw, held, squares, normed_all, scaled, weights) = pl.pallas_call(
+    (gate, slope, gated, value, conved, scan, steps_raw, held, squares, normed_all, scaled, weights) = pl.pallas_call(
         functools.partial(forward_kernel, dm),
         out_shape=[
+            out(length, ip),
             out(length, ip, dtype=BF16),
+            out(length, ip),
             out(length, vs, dtype=BF16),
             out(length, vs, dtype=BF16),
             out(length, ip),
             out(length, LANES),
-            out(nb * subs * state, ip),
+            out(nb * subs * state, ip, dtype=BF16),
             out(nb, 1, q),
             out(length, width, dtype=BF16),
             out(length, ip, dtype=BF16),
@@ -970,6 +968,8 @@
                 const(8, ip),
             ],
             [
+                fblock(ip),
+                fblock(ip),
                 fblock(ip),
                 fblock(vs),
                 fblock(vs),
@@ -987,7 +987,9 @@
                 vmem((state, ip), F32),
                 vmem((vs // LANES, q + 8, LANES), F32),
                 vmem((q, q), BF16),
+                vmem((2 * LANES, ip), BF16),
                 vmem((q, dm.np), F32),
+                vmem((q, ip), F32),
                 pltpu.SemaphoreType.DMA((n_dp,)),
                 pltpu.SemaphoreType.DMA((dm.pieces,)),
                 pltpu.SemaphoreType.DMA,
@@ -1008,15 +1010,9 @@
         + [out(chunk_rows // q, q, width, dtype=BF16)] * n_t,
         grid_spec=grid(
             1,
-            [hbm] * (n_dp + 1),
-            [in_vmem] + [hbm] * n_t,
-            [
-                vmem((length, ip), BF16),
-                vmem((nb, q, width), BF16),
-                pltpu.SemaphoreType.DMA((n_dp,)),
-                pltpu.SemaphoreType.DMA,
-                pltpu.SemaphoreType.DMA((nb,)),
-            ],
+            [hbm] * n_dp + [in_vmem],
+            [in_vmem] * (n_t + 1),
+            [pltpu.SemaphoreType.DMA((n_dp,))],
         ),
         compiler_params=params,
         cost_estimate=pl.CostEstimate(
@@ -1024,27 +1020,20 @@
         ),
         name="branch_output",
     )(scalars, *o_list, scaled)
-    sums, cot_all = pl.pallas_call(
-        functools.partial(dots_kernel, dm),
-        out_shape=[out(nb, 2, q), out(length, width, dtype=BF16)],
-        grid_spec=grid(
-            1,
-            [hbm] * (2 * n_t) + [in_vmem],
-            [in_vmem, hbm],
-            [
-                vmem((n_t, chunk_rows, width), BF16),
-                vmem((n_t, chunk_rows // q, q, width), BF16),
-                pltpu.SemaphoreType.DMA((n_t,)),
-                pltpu.SemaphoreType.DMA((n_t,)),
-                pltpu.SemaphoreType.DMA((n_t,)),
-            ],
-        ),
+    sc, sums, cot_all = pl.pallas_call(
+        functools.partial(scaled_kernel, dm),
+        out_shape=[
+            out(length, ip, dtype=BF16),
+            out(nb, 2, q),
+            out(length, width, dtype=BF16),
+        ],
+        grid_spec=grid(1, [in_vmem] * (n_t + 4), [in_vmem] * 3, []),
         compiler_params=params,
         cost_estimate=pl.CostEstimate(
             flops=3_000_000_000, bytes_accessed=10_000_000, transcendentals=0
         ),
-        name="branch_dots",
-    )(scalars, *c_list, *branch, squares)
+        name="scaled_cotangent",
+    )(scalars, *c_list, w_back, per_lane, gated, squares)
     total = sums
     for k in range(1, n_t):
         total = total + across(sums, k)
@@ -1074,7 +1063,7 @@
         out_shape=[
             out(length, ip, dtype=BF16),
             out(length, ip, dtype=BF16),
-            out(16, ip),
+            out(8, ip),
             out(8, width),
             out(2 * part_rows, 2 * ip),
         ]
@@ -1083,17 +1072,16 @@
             nb + 1,
             [
                 const(width, ip),
-                const(width, ip),
                 pl.BlockSpec((None, 2, q), lambda i, s: (jnp.minimum(i, nb - 1), 0, 0)),
                 const(8, ip),
                 now(ip),
                 now(ip),
                 now(ip),
-                now(width),
+                now(ip),
                 ago(width),
                 ago(width),
             ],
-            [now(ip), now(ip), const(16, ip), const(8, width)]
+            [now(ip), now(ip), const(8, ip), const(8, width)]
             + [const(2 * part_rows, 2 * ip)] * n_hi,
             [vmem((width, 2 * ip), F32), vmem((q, ip), BF16), vmem((q, ip), BF16)],
         ),
@@ -1102,7 +1090,7 @@
             flops=6_000_000_000, bytes_accessed=20_000_000, transcendentals=0
         ),
         name="gate_backward",
-    )(scalars, weights, w_back, rk, per_lane, gate, conved, scan, cot_all, normed_all, cot_all)
+    )(scalars, weights, rk, per_lane, gate, slope, gated, sc, normed_all, cot_all)
     early = [along(v, k + 1) for k, v in enumerate(early)]
 
     r_all = n_hi * part_rows
@@ -1122,7 +1110,7 @@
                 const(8, vs),
                 const(8, LANES),
                 const(8, ip),
-                const(16, ip),
+                const(8, ip),
                 const(8, width),
                 bago(ip),
                 bago(width),
@@ -1143,6 +1131,8 @@
                 vmem((8 * subs, ip), F32),
                 vmem((q, ip), F32),
                 vmem((q, ip), F32),
+                vmem((2 * LANES, ip), BF16),
+                vmem((8, ip), F32),
                 vmem((q, dm.late), BF16),
                 vmem((q, dm.np), BF16),
                 vmem((width, dm.late), F32),

time: 229 us -> 235 us (1.026)
  the two profiles are of different devices: /device:TPU:0 before, /device:TPU:16 now
where the time goes in v4:
time: 235 us; the launch traced here: 234 us
  Pallas kernels  76.7 us (33%)
  waiting for transfers between devices  66.4 us (28%)
  starting transfers between devices  44.4 us (19%)
  local copies, waits for them, and re-layouts  30.3 us (13%)
  other arithmetic  14.9 us (6%)
    ppermute x22, waiting for transfers between devices, across(): return lax.ppermute(v, 'tensor', swap(n_t, k))  38.6 us
    pallas_call x1, Pallas kernels, body(): pl.pallas_call(functools.partial(backward_kernel, dm), out_shape=[out(r_a...  31.2 us
    ppermute x12, waiting for transfers between devices, along(): return lax.ppermute(v, 'dp', shift_hi(n_dp, k))  27 us
    ppermute x22, starting transfers between devices, across(): return lax.ppermute(v, 'tensor', swap(n_t, k))  25.8 us
    pallas_call x1, Pallas kernels, body(): pl.pallas_call(functools.partial(forward_kernel, dm), out_shape=[out(leng...  21.7 us
    unnamed x96, local copies, waits for them, and re-layouts  19.4 us
    ppermute x12, starting transfers between devices, along(): return lax.ppermute(v, 'dp', shift_hi(n_dp, k))  17.4 us
    pallas_call x1, Pallas kernels, body(): pl.pallas_call(functools.partial(gate_kernel, dm), out_shape=[out(length,...  7.94 us
  transfers between devices with their start and end apart: 44, of which 12 were waited for; matrix products, arithmetic and copies ran while one was open for 11% of the time, Pallas kernels for 14%

profile of v4, /device:TPU:16, one launch (start us, length us, event | category | flops | bytes accessed | tf_op | source)
XLA Modules:
  0.0 233.9 jit_solution(9040762511185618530)
XLA Ops:
  1.3 3.5 %collective-permute-start.4 = (bf16[96,384]{1,0:T(8,128)(2,1)}, bf16[96,384]{1,0:T(8,128)(2,1)S(1)}, u32[]{:S(2)}, u32[]{:S(2)}) collective-permute-start(bf16[96,384]{1,0:T(8,128)(2,1)} %bitcast.42), channel_id=1, source_target_pairs={{0,16},{4,20},{8,24},{12,28},{16,0},{20,4},{24,8},{28,12},{1,17},{... | collective-permute-start | bytes 221192 | tf_op jit(solution)/shard_map/ppermute | solution.py:820
  4.8 1.7 pack_weights.1.refs_0_
  8.6 1.2 exponential_negate_fusion
  11.1 1.6 fusion.13
  12.9 1.3 compare_convert_fusion
  14.2 1.4 copy-done
  16.3 1.3 normalize.1
  18.2 2.0 collective-permute-start.12
  20.3 1.5 collective-permute-start.17
  21.8 1.5 collective-permute-start.20
  25.7 1.8 collective-permute-start.11
  29.6 6.8 %collective-permute-done.11.refs_2_ = bf16[96,1152]{1,0:T(8,128)(2,1)S(1)} collective-permute-done((bf16[96,1152]{1,0:T(8,128)(2,1)S(1)}, bf16[96,1152]{1,0:T(8,128)(2,1)S(1)}, u32[]{:S(2)}, u32[]{:S(2)}) %collective-permute-start.11) | collective-permute-done | bytes 221216 | tf_op jit(solution)/shard_map/ppermute | solution.py:820
  36.4 2.4 %collective-permute-start.10 = (bf16[96,1152]{1,0:T(8,128)(2,1)S(1)}, bf16[96,1152]{1,0:T(8,128)(2,1)}, u32[]{:S(2)}, u32[]{:S(2)}) collective-permute-start(bf16[96,1152]{1,0:T(8,128)(2,1)S(1)} %copy-done.16), channel_id=1, source_target_pairs={{0,8},{4,12},{8,16},{12,20},{16,24},{20,28},{24,0},{28,4},{1,9},{5... | collective-permute-start | bytes 663560 | tf_op jit(solution)/shard_map/ppermute | solution.py:820
  38.8 1.5 collective-permute-start.21
  40.3 1.5 collective-permute-start.22
  42.9 1.3 gather_fusion.1
  44.2 1.3 gather_fusion
  48.9 1.8 concatenate.38.refs_16_.refs_1_
  50.7 0.9 concatenate.35.scalars
  56.3 1.6 collective-permute-start.1
  57.9 1.5 collective-permute-start
  59.9 1.0 copy-done.20
  60.9 1.0 copy-done.22
  61.9 1.0 copy-done.24
  62.9 0.9 copy-done.26
  63.8 0.9 copy-done.28
  64.8 0.9 copy-done.30
  65.7 21.7 %block_forward.1 = (f32[2048,384]{1,0:T(8,128)S(1)}, bf16[2048,384]{1,0:T(8,128)(2,1)S(1)}, f32[2048,384]{1,0:T(8,128)S(1)}, bf16[2048,640]{1,0:T(8,128)(2,1)S(1...) custom-call(s32[73]{0:T(128)S(1)} %concatenate.35.scalars, ...), custom_call_target="tpu_custom_call" | custom-call | flops 30000001024 | bytes 30000000 | tf_op jit(solution)/shard_map/block_forward/pallas_call | solution.py:945
  87.5 4.3 %branch_output.1 = (bf16[768,384]{1,0:T(8,128)(2,1)S(1)}, bf16[2,256,768]{2,1,0:T(8,128)(2,1)S(1)}, bf16[2,256,768]{2,1,0:T(8,128)(2,1)}, bf16[2,256,768]{2,1,0:T(8,128)(2,1)}, bf16[2,256,768]{2,1,0:T(8,128)(2,1)}) custom-call(s32[73]{0:T(128)S(1)} %concatenate.35.scalars, bf16[96,384]{1,0:T(8,128)(2,1)S(1)} %bitcast.44, bf16[96,384]{1,0:T(8,128)(2,1)S(1)} %copy-done.35, ...), custom_call_target="tpu_custom_call" | custom-call | flops 3000000000 | bytes 10000000 | tf_op jit(solution)/shard_map/branch_output/pallas_call | solution.py:1007
  91.8 0.9 copy-done.6
  92.9 2.6 %scaled_cotangent.1 = (bf16[2048,384]{1,0:T(8,128)(2,1)S(1)}, f32[8,2,256]{2,1,0:T(2,128)S(1)}, bf16[2048,768]{1,0:T(8,128)(2,1)S(1)}) custom-call(s32[73]{0:T(128)S(1)} %concatenate.35.scalars, bf16[512,768]{1,0:T(8,128)(2,1)S(1)} %copy-done.4, bf16[512,768]{1,0:T(8,128)(2,1)S(1)} %collective-permute-done.refs_1_, ...), custom_call_target="tpu_custom_call" | custom-call | flops 3000000000 | bytes 10000000 | tf_op jit(solution)/shard_map/scaled_cotangent/pallas_call | solution.py:1023
  95.5 1.2 collective-permute-start.25
  96.7 1.4 collective-permute-start.24
  98.1 0.9 collective-permute-start.23
  99.0 1.1 collective-permute-done.25
  100.5 1.4 collective-permute-done.23
  102.0 7.9 %gate_backward.1 = (bf16[2048,384]{1,0:T(8,128)(2,1)S(1)}, bf16[2048,384]{1,0:T(8,128)(2,1)S(1)}, f32[8,384]{1,0:T(8,128)S(1)}, f32[8,768]{1,0:T(8,128)S(1)}, f3...) custom-call(s32[73]{0:T(128)S(1)} %concatenate.35.scalars, ...), custom_call_target="tpu_custom_call" | custom-call | flops 6000000000 | bytes 20000000 | tf_op jit(solution)/shard_map/gate_backward/pallas_call | solution.py:1061
  110.7 31.2 %block_backward.1 = (f32[384,768]{1,0:T(8,128)S(1)}, bf16[400,768]{1,0:T(8,128)(2,1)S(1)}, bf16[16,768]{1,0:T(8,128)(2,1)S(1)}, bf16[2,256,768]{2,1,0:T(8,128)(2...) custom-call(s32[73]{0:T(128)S(1)} %concatenate.35.scalars, ...), custom_call_target="tpu_custom_call" | custom-call | flops 40000000000 | bytes 30000000 | tf_op jit(solution)/shard_map/block_backward/pallas_call | solution.py:1097
  142.0 1.0 copy-done.2
  143.0 1.5 collective-permute-start.34
  144.5 1.5 collective-permute-start.36
  146.0 1.1 collective-permute-start.29
  147.2 18.3 %collective-permute-done.34.refs_0_ = bf16[192,768]{1,0:T(8,128)(2,1)S(1)} collective-permute-done((bf16[192,768]{1,0:T(8,128)(2,1)S(1)}, bf16[192,768]{1,0:T(8,128)(2,1)S(1)}, u32[]{:S(2)}, u32[]{:S(2)}) %collective-permute-start.34) | collective-permute-done | bytes 294944 | tf_op jit(solution)/shard_map/ppermute | solution.py:820
  166.8 1.6 collective-permute-start.26
  168.4 1.8 collective-permute-done.36.refs_2_
  170.9 1.4 collective-permute-start.27
  173.2 1.2 collective-permute-start.28
  174.4 1.1 copy-done.11
  175.6 1.0 copy-done.13
  176.5 1.0 copy-done.15
  178.3 1.1 copy-done.9
  180.1 7.9 %collective-permute-done.31.refs_4_ = bf16[2,256,768]{2,1,0:T(8,128)(2,1)S(1)} collective-permute-done((bf16[2,256,768]{2,1,0:T(8,128)(2,1)}, bf16[2,256,768]{2,1,0:T(8,128)(2,1)S(1)}, u32[]{:S(2)}, u32[]{:S(2)}) %collective-permute-start.31) | collective-permute-done | bytes 786464 | tf_op jit(solution)/shard_map/ppermute | solution.py:817
  188.3 4.0 %collective-permute-start.40 = (bf16[112,768]{1,0:T(8,128)(2,1)S(1)}, bf16[112,768]{1,0:T(8,128)(2,1)S(1)}, u32[]{:S(2)}, u32[]{:S(2)}) collective-permute-start(bf16[112,768]{1,0:T(8,128)(2,1)S(1)} %get-tuple-element.116), channel_id=1, source_target_pairs={{0,24},{4,28},{8,0},{12,4},{16,8},{20,12},{24,16},{28,20},{1,25},{... | collective-permute-start | bytes 516104 | tf_op jit(solution)/shard_map/ppermute | solution.py:820
  192.3 25.8 %collective-permute-done.27 = bf16[2,256,768]{2,1,0:T(8,128)(2,1)} collective-permute-done((bf16[2,256,768]{2,1,0:T(8,128)(2,1)}, bf16[2,256,768]{2,1,0:T(8,128)(2,1)}, u32[]{:S(2)}, u32[]{:S(2)}) %collective-permute-start.27) | collective-permute-done | bytes 786464 | tf_op jit(solution)/shard_map/ppermute | solution.py:817
  218.1 0.9 collective-permute-start.32
  219.1 1.2 collective-permute-start.30
  220.3 2.1 convert_add_fusion
  222.5 1.4 gradient_sum.1
  223.9 1.4 collective-permute-start.43
  225.9 1.6 collective-permute-start.41
  227.4 1.4 fusion
  229.5 1.1 collective-permute-done.42.refs_2_
  230.6 1.2 shared_sum.1
  231.9 2.0 input_gradient.1
  (169 shorter events, 27.0 us)
Async XLA Ops:
  0.6 42.3 %copy-start.43 = (s32[4,2]{1,0:T(4,128)S(1)}, s32[4,2]{1,0:T(4,128)}, u32[]{:S(2)}) copy-start(s32[4,2]{1,0:T(4,128)} %constant.112.clone) | copy-start | bytes 100
  0.7 43.6 %copy-start.42 = (s32[4,2]{1,0:T(4,128)S(1)}, s32[4,2]{1,0:T(4,128)}, u32[]{:S(2)}) copy-start(s32[4,2]{1,0:T(4,128)} %constant.111.clone) | copy-start | bytes 100
  0.7 41.6 %copy-start.44 = (s32[1,2048]{1,0:T(1,128)S(1)}, s32[1,2048]{1,0:T(1,128)}, u32[]{:S(2)}) copy-start(s32[1,2048]{1,0:T(1,128)} %param.20) | copy-start | bytes 24580
  0.7 17.5 %collective-permute-start.6 = (bf16[96,384]{1,0:T(8,128)(2,1)}, bf16[96,384]{1,0:T(8,128)(2,1)S(1)}, u32[]{:S(2)}, u32[]{:S(2)}) collective-permute-start(bf16[96,384]{1,0:T(8,128)(2,1)} %bitcast.40), channel_id=1, source_target_pairs={{0,4},{4,0},{8,12},{12,8},{16,20},{20,16},{24,28},{28,24},{1,5},{5... | collective-permute-start | bytes 221192 | tf_op jit(solution)/shard_map/ppermute | solution.py:823
  0.8 19.5 %collective-permute-start.5 = (bf16[96,384]{1,0:T(8,128)(2,1)}, bf16[96,384]{1,0:T(8,128)(2,1)S(1)}, u32[]{:S(2)}, u32[]{:S(2)}) collective-permute-start(bf16[96,384]{1,0:T(8,128)(2,1)} %bitcast.41), channel_id=1, source_target_pairs={{0,24},{4,28},{8,0},{12,4},{16,8},{20,12},{24,16},{28,20},{1,25},{... | collective-permute-start | bytes 221192 | tf_op jit(solution)/shard_map/ppermute | solution.py:820
  1.3 20.5 %collective-permute-start.4 = (bf16[96,384]{1,0:T(8,128)(2,1)}, bf16[96,384]{1,0:T(8,128)(2,1)S(1)}, u32[]{:S(2)}, u32[]{:S(2)}) collective-permute-start(bf16[96,384]{1,0:T(8,128)(2,1)} %bitcast.42), channel_id=1, source_target_pairs={{0,16},{4,20},{8,24},{12,28},{16,0},{20,4},{24,8},{28,12},{1,17},{... | collective-permute-start | bytes 221192 | tf_op jit(solution)/shard_map/ppermute | solution.py:820
  4.8 19.0 %collective-permute-start.3 = (bf16[96,384]{1,0:T(8,128)(2,1)}, bf16[96,384]{1,0:T(8,128)(2,1)S(1)}, u32[]{:S(2)}, u32[]{:S(2)}) collective-permute-start(bf16[96,384]{1,0:T(8,128)(2,1)} %bitcast.43), channel_id=1, source_target_pairs={{0,8},{4,12},{8,16},{12,20},{16,24},{20,28},{24,0},{28,4},{1,9},{5... | collective-permute-start | bytes 221192 | tf_op jit(solution)/shard_map/ppermute | solution.py:820
  6.5 11.7 %copy-start.16 = (bf16[96,1152]{1,0:T(8,128)(2,1)S(1)}, bf16[96,1152]{1,0:T(8,128)(2,1)}, u32[]{:S(2)}) copy-start(bf16[96,1152]{1,0:T(8,128)(2,1)} %pack_weights.1.refs_0_) | copy-start | bytes 663556
  6.5 21.0 %collective-permute-start.13 = (bf16[96,1152]{1,0:T(8,128)(2,1)}, bf16[96,1152]{1,0:T(8,128)(2,1)S(1)}, u32[]{:S(2)}, u32[]{:S(2)}) collective-permute-start(bf16[96,1152]{1,0:T(8,128)(2,1)} %pack_weights.1.refs_0_), channel_id=1, source_target_pairs={{0,4},{4,0},{8,12},{12,8},{16,20},{20,16},{24,28},{28,24},{1,5},{5... | collective-permute-start | bytes 663560 | tf_op jit(solution)/shard_map/ppermute | solution.py:823
  12.7 16.3 %copy-start.45 = (f32[6]{0:T(128)S(1)}, f32[6]{0:T(128)}, u32[]{:S(2)}) copy-start(f32[6]{0:T(128)} %param.30) | copy-start | bytes 76
  12.7 16.3 %copy-start.46 = (f32[6]{0:T(128)S(1)}, f32[6]{0:T(128)}, u32[]{:S(2)}) copy-start(f32[6]{0:T(128)} %exponential_negate_fusion) | copy-start | bytes 76
  16.3 39.4 %copy-start.4 = (bf16[512,768]{1,0:T(8,128)(2,1)S(1)}, bf16[512,768]{1,0:T(8,128)(2,1)}, u32[]{:S(2)}) copy-start(bf16[512,768]{1,0:T(8,128)(2,1)} %cot_ref.1) | copy-start | bytes 2359300
  17.6 38.1 %copy-start.19 = (bf16[256,768]{1,0:T(8,128)(2,1)}, bf16[256,768]{1,0:T(8,128)(2,1)S(1)}, u32[]{:S(2)}) copy-start(bf16[256,768]{1,0:T(8,128)(2,1)S(1)} %get-tuple-element.75.refs_9_) | copy-start | bytes 1179652
  18.2 9.8 %collective-permute-start.12 = (bf16[96,1152]{1,0:T(8,128)(2,1)S(1)}, bf16[96,1152]{1,0:T(8,128)(2,1)S(1)}, u32[]{:S(2)}, u32[]{:S(2)}) collective-permute-start(bf16[96,1152]{1,0:T(8,128)(2,1)S(1)} %copy-done.16), channel_id=1, source_target_pairs={{0,24},{4,28},{8,0},{12,4},{16,8},{20,12},{24,16},{28,20},{1,25},{... | collective-permute-start | bytes 663560 | tf_op jit(solution)/shard_map/ppermute | solution.py:820
  20.3 18.6 %collective-permute-start.17 = (bf16[256,768]{1,0:T(8,128)(2,1)S(1)}, bf16[256,768]{1,0:T(8,128)(2,1)}, u32[]{:S(2)}, u32[]{:S(2)}) collective-permute-start(bf16[256,768]{1,0:T(8,128)(2,1)S(1)} %get-tuple-element.74.refs_8_), channel_id=1, source_target_pairs={{0,1},{1,0},{2,3},{3,2},{4,5},{5,4},{6,7},{7,6},{8,9},{9,8},{10,11... | collective-permute-start | bytes 1179656 | tf_op jit(solution)/shard_map/ppermute | solution.py:817
  21.7 29.0 %copy-start.32 = (bf16[96,384]{1,0:T(8,128)(2,1)}, bf16[96,384]{1,0:T(8,128)(2,1)S(1)}, u32[]{:S(2)}) copy-start(bf16[96,384]{1,0:T(8,128)(2,1)S(1)} %collective-permute-done.4.refs_2_) | copy-start | bytes 221188
  21.8 18.6 %collective-permute-start.20 = (bf16[256,768]{1,0:T(8,128)(2,1)S(1)}, bf16[256,768]{1,0:T(8,128)(2,1)}, u32[]{:S(2)}, u32[]{:S(2)}) collective-permute-start(bf16[256,768]{1,0:T(8,128)(2,1)S(1)} %get-tuple-element.75.refs_9_), channel_id=1, source_target_pairs={{0,2},{1,3},{2,0},{3,1},{4,6},{5,7},{6,4},{7,5},{8,10},{9,11},{10,... | collective-permute-start | bytes 1179656 | tf_op jit(solution)/shard_map/ppermute | solution.py:817
  23.8 24.5 %copy-start.34 = (bf16[96,384]{1,0:T(8,128)(2,1)}, bf16[96,384]{1,0:T(8,128)(2,1)S(1)}, u32[]{:S(2)}) copy-start(bf16[96,384]{1,0:T(8,128)(2,1)S(1)} %collective-permute-done.3.refs_1_) | copy-start | bytes 221188
  23.8 1.3 collective-permute-start.9
  25.7 10.7 %collective-permute-start.11 = (bf16[96,1152]{1,0:T(8,128)(2,1)S(1)}, bf16[96,1152]{1,0:T(8,128)(2,1)S(1)}, u32[]{:S(2)}, u32[]{:S(2)}) collective-permute-start(bf16[96,1152]{1,0:T(8,128)(2,1)S(1)} %copy-done.16), channel_id=1, source_target_pairs={{0,16},{4,20},{8,24},{12,28},{16,0},{20,4},{24,8},{28,12},{1,17},{... | collective-permute-start | bytes 663560 | tf_op jit(solution)/shard_map/ppermute | solution.py:820
  27.5 20.8 %copy-start.25 = (bf16[96,1152]{1,0:T(8,128)(2,1)}, bf16[96,1152]{1,0:T(8,128)(2,1)S(1)}, u32[]{:S(2)}) copy-start(bf16[96,1152]{1,0:T(8,128)(2,1)S(1)} %collective-permute-done.13.refs_4_) | copy-start | bytes 663556
  27.5 24.9 %collective-permute-start.19 = (bf16[256,768]{1,0:T(8,128)(2,1)S(1)}, bf16[256,768]{1,0:T(8,128)(2,1)S(1)}, u32[]{:S(2)}, u32[]{:S(2)}) collective-permute-start(bf16[256,768]{1,0:T(8,128)(2,1)S(1)} %get-tuple-element.74.refs_8_), channel_id=1, source_target_pairs={{0,2},{1,3},{2,0},{3,1},{4,6},{5,7},{6,4},{7,5},{8,10},{9,11},{10,... | collective-permute-start | bytes 1179656 | tf_op jit(solution)/shard_map/ppermute | solution.py:817
  28.0 28.3 %copy-start.27 = (bf16[96,1152]{1,0:T(8,128)(2,1)}, bf16[96,1152]{1,0:T(8,128)(2,1)S(1)}, u32[]{:S(2)}) copy-start(bf16[96,1152]{1,0:T(8,128)(2,1)S(1)} %collective-permute-done.12.refs_3_) | copy-start | bytes 663556
  28.0 25.6 %collective-permute-start.18 = (bf16[256,768]{1,0:T(8,128)(2,1)S(1)}, bf16[256,768]{1,0:T(8,128)(2,1)S(1)}, u32[]{:S(2)}, u32[]{:S(2)}) collective-permute-start(bf16[256,768]{1,0:T(8,128)(2,1)S(1)} %get-tuple-element.75.refs_9_), channel_id=1, source_target_pairs={{0,1},{1,0},{2,3},{3,2},{4,5},{5,4},{6,7},{7,6},{8,9},{9,8},{10,11... | collective-permute-start | bytes 1179656 | tf_op jit(solution)/shard_map/ppermute | solution.py:817
  36.4 19.9 %copy-start.29 = (bf16[96,1152]{1,0:T(8,128)(2,1)}, bf16[96,1152]{1,0:T(8,128)(2,1)S(1)}, u32[]{:S(2)}) copy-start(bf16[96,1152]{1,0:T(8,128)(2,1)S(1)} %collective-permute-done.11.refs_2_) | copy-start | bytes 663556
  36.4 15.8 %collective-permute-start.10 = (bf16[96,1152]{1,0:T(8,128)(2,1)S(1)}, bf16[96,1152]{1,0:T(8,128)(2,1)}, u32[]{:S(2)}, u32[]{:S(2)}) collective-permute-start(bf16[96,1152]{1,0:T(8,128)(2,1)S(1)} %copy-done.16), channel_id=1, source_target_pairs={{0,8},{4,12},{8,16},{12,20},{16,24},{20,28},{24,0},{28,4},{1,9},{5... | collective-permute-start | bytes 663560 | tf_op jit(solution)/shard_map/ppermute | solution.py:820
  38.8 20.6 %collective-permute-start.21 = (bf16[256,768]{1,0:T(8,128)(2,1)}, bf16[256,768]{1,0:T(8,128)(2,1)}, u32[]{:S(2)}, u32[]{:S(2)}) collective-permute-start(bf16[256,768]{1,0:T(8,128)(2,1)} %collective-permute-done.17.refs_10_), channel_id=1, source_target_pairs={{0,2},{1,3},{2,0},{3,1},{4,6},{5,7},{6,4},{7,5},{8,10},{9,11},{10,... | collective-permute-start | bytes 1179656 | tf_op jit(solution)/shard_map/ppermute | solution.py:817
  40.3 19.1 %collective-permute-start.22 = (bf16[256,768]{1,0:T(8,128)(2,1)}, bf16[256,768]{1,0:T(8,128)(2,1)}, u32[]{:S(2)}, u32[]{:S(2)}) collective-permute-start(bf16[256,768]{1,0:T(8,128)(2,1)} %collective-permute-done.20.refs_13_), channel_id=1, source_target_pairs={{0,1},{1,0},{2,3},{3,2},{4,5},{5,4},{6,7},{7,6},{8,9},{9,8},{10,11... | collective-permute-start | bytes 1179656 | tf_op jit(solution)/shard_map/ppermute | solution.py:817
  52.3 3.5 %collective-permute-start.16 = (bf16[96,1152]{1,0:T(8,128)(2,1)S(1)}, bf16[96,1152]{1,0:T(8,128)(2,1)S(1)}, u32[]{:S(2)}, u32[]{:S(2)}) collective-permute-start(bf16[96,1152]{1,0:T(8,128)(2,1)S(1)} %collective-permute-done.12.refs_3_), channel_id=1, source_target_pairs={{0,4},{4,0},{8,12},{12,8},{16,20},{20,16},{24,28},{28,24},{1,5},{5... | collective-permute-start | bytes 663560 | tf_op jit(solution)/shard_map/ppermute | solution.py:823
  53.1 3.2 %collective-permute-start.15 = (bf16[96,1152]{1,0:T(8,128)(2,1)S(1)}, bf16[96,1152]{1,0:T(8,128)(2,1)S(1)}, u32[]{:S(2)}, u32[]{:S(2)}) collective-permute-start(bf16[96,1152]{1,0:T(8,128)(2,1)S(1)} %collective-permute-done.11.refs_2_), channel_id=1, source_target_pairs={{0,4},{4,0},{8,12},{12,8},{16,20},{20,16},{24,28},{28,24},{1,5},{5... | collective-permute-start | bytes 663560 | tf_op jit(solution)/shard_map/ppermute | solution.py:823
  54.4 3.5 %collective-permute-start.14 = (bf16[96,1152]{1,0:T(8,128)(2,1)}, bf16[96,1152]{1,0:T(8,128)(2,1)S(1)}, u32[]{:S(2)}, u32[]{:S(2)}) collective-permute-start(bf16[96,1152]{1,0:T(8,128)(2,1)} %collective-permute-done.10.refs_1_), channel_id=1, source_target_pairs={{0,4},{4,0},{8,12},{12,8},{16,20},{20,16},{24,28},{28,24},{1,5},{5... | collective-permute-start | bytes 663560 | tf_op jit(solution)/shard_map/ppermute | solution.py:823
  55.8 36.9 %collective-permute-start.2 = (bf16[512,768]{1,0:T(8,128)(2,1)S(1)}, bf16[512,768]{1,0:T(8,128)(2,1)S(1)}, u32[]{:S(2)}, u32[]{:S(2)}) collective-permute-start(bf16[512,768]{1,0:T(8,128)(2,1)S(1)} %copy-done.4), channel_id=1, source_target_pairs={{0,3},{1,2},{2,1},{3,0},{4,7},{5,6},{6,5},{7,4},{8,11},{9,10},{10,... | collective-permute-start | bytes 2359304 | tf_op jit(solution)/shard_map/ppermute | solution.py:817
  56.3 36.6 %collective-permute-start.1 = (bf16[512,768]{1,0:T(8,128)(2,1)S(1)}, bf16[512,768]{1,0:T(8,128)(2,1)S(1)}, u32[]{:S(2)}, u32[]{:S(2)}) collective-permute-start(bf16[512,768]{1,0:T(8,128)(2,1)S(1)} %copy-done.4), channel_id=1, source_target_pairs={{0,2},{1,3},{2,0},{3,1},{4,6},{5,7},{6,4},{7,5},{8,10},{9,11},{10,... | collective-permute-start | bytes 2359304 | tf_op jit(solution)/shard_map/ppermute | solution.py:817
  57.9 35.0 %collective-permute-start = (bf16[512,768]{1,0:T(8,128)(2,1)S(1)}, bf16[512,768]{1,0:T(8,128)(2,1)S(1)}, u32[]{:S(2)}, u32[]{:S(2)}) collective-permute-start(bf16[512,768]{1,0:T(8,128)(2,1)S(1)} %copy-done.4), channel_id=1, source_target_pairs={{0,1},{1,0},{2,3},{3,2},{4,5},{5,4},{6,7},{7,6},{8,9},{9,8},{10,11... | collective-permute-start | bytes 2359304 | tf_op jit(solution)/shard_map/ppermute | solution.py:817
  59.4 28.0 %collective-permute-start.8 = (bf16[96,384]{1,0:T(8,128)(2,1)}, bf16[96,384]{1,0:T(8,128)(2,1)S(1)}, u32[]{:S(2)}, u32[]{:S(2)}) collective-permute-start(bf16[96,384]{1,0:T(8,128)(2,1)} %copy-done.32), channel_id=1, source_target_pairs={{0,4},{4,0},{8,12},{12,8},{16,20},{20,16},{24,28},{28,24},{1,5},{5... | collective-permute-start | bytes 221192 | tf_op jit(solution)/shard_map/ppermute | solution.py:823
  59.4 28.0 %collective-permute-start.7 = (bf16[96,384]{1,0:T(8,128)(2,1)}, bf16[96,384]{1,0:T(8,128)(2,1)S(1)}, u32[]{:S(2)}, u32[]{:S(2)}) collective-permute-start(bf16[96,384]{1,0:T(8,128)(2,1)} %copy-done.34), channel_id=1, source_target_pairs={{0,4},{4,0},{8,12},{12,8},{16,20},{20,16},{24,28},{28,24},{1,5},{5... | collective-permute-start | bytes 221192 | tf_op jit(solution)/shard_map/ppermute | solution.py:823
  65.7 21.7 %copy-start.31 = (bf16[384,96]{0,1:T(8,128)(2,1)S(1)}, bf16[384,96]{0,1:T(8,128)(2,1)}, u32[]{:S(2)}) copy-start(bf16[384,96]{0,1:T(8,128)(2,1)} %param.34) | copy-start | bytes 221188
  65.7 21.7 %copy-start.33 = (bf16[96,384]{1,0:T(8,128)(2,1)S(1)}, bf16[96,384]{1,0:T(8,128)(2,1)}, u32[]{:S(2)}) copy-start(bf16[96,384]{1,0:T(8,128)(2,1)} %copy-done.32) | copy-start | bytes 221188
  65.7 21.8 %copy-start.35 = (bf16[96,384]{1,0:T(8,128)(2,1)S(1)}, bf16[96,384]{1,0:T(8,128)(2,1)}, u32[]{:S(2)}) copy-start(bf16[96,384]{1,0:T(8,128)(2,1)} %copy-done.34) | copy-start | bytes 221188
  65.7 21.8 %copy-start.37 = (bf16[96,384]{1,0:T(8,128)(2,1)S(1)}, bf16[96,384]{1,0:T(8,128)(2,1)}, u32[]{:S(2)}) copy-start(bf16[96,384]{1,0:T(8,128)(2,1)} %copy-done.36) | copy-start | bytes 221188
  95.5 4.7 %collective-permute-start.25 = (f32[8,2,256]{2,1,0:T(2,128)S(1)}, f32[8,2,256]{2,1,0:T(2,128)S(1)}, u32[]{:S(2)}, u32[]{:S(2)}) collective-permute-start(f32[8,2,256]{2,1,0:T(2,128)S(1)} %get-tuple-element.80), channel_id=1, source_target_pairs={{0,3},{1,2},{2,1},{3,0},{4,7},{5,6},{6,5},{7,4},{8,11},{9,10},{10,... | collective-permute-start | bytes 49160 | tf_op jit(solution)/shard_map/ppermute | solution.py:817
  96.7 3.7 %collective-permute-start.24 = (f32[8,2,256]{2,1,0:T(2,128)S(1)}, f32[8,2,256]{2,1,0:T(2,128)S(1)}, u32[]{:S(2)}, u32[]{:S(2)}) collective-permute-start(f32[8,2,256]{2,1,0:T(2,128)S(1)} %get-tuple-element.80), channel_id=1, source_target_pairs={{0,2},{1,3},{2,0},{3,1},{4,6},{5,7},{6,4},{7,5},{8,10},{9,11},{10,... | collective-permute-start | bytes 49160 | tf_op jit(solution)/shard_map/ppermute | solution.py:817
  98.1 3.7 %collective-permute-start.23 = (f32[8,2,256]{2,1,0:T(2,128)S(1)}, f32[8,2,256]{2,1,0:T(2,128)S(1)}, u32[]{:S(2)}, u32[]{:S(2)}) collective-permute-start(f32[8,2,256]{2,1,0:T(2,128)S(1)} %get-tuple-element.80), channel_id=1, source_target_pairs={{0,1},{1,0},{2,3},{3,2},{4,5},{5,4},{6,7},{7,6},{8,9},{9,8},{10,11... | collective-permute-start | bytes 49160 | tf_op jit(solution)/shard_map/ppermute | solution.py:817
  101.9 8.8 %copy-start.39 = (f32[2048,384]{1,0:T(8,128)S(1)}, f32[2048,384]{1,0:T(8,128)}, u32[]{:S(2)}) copy-start(f32[2048,384]{1,0:T(8,128)} %copy-done.38) | copy-start | bytes 9437188
  102.0 8.8 %copy-start.41 = (bf16[2048,640]{1,0:T(8,128)(2,1)S(1)}, bf16[2048,640]{1,0:T(8,128)(2,1)}, u32[]{:S(2)}) copy-start(bf16[2048,640]{1,0:T(8,128)(2,1)} %copy-done.40) | copy-start | bytes 7864324
  143.0 29.4 %collective-permute-start.33 = (bf16[400,768]{1,0:T(8,128)(2,1)S(1)}, bf16[400,768]{1,0:T(8,128)(2,1)S(1)}, u32[]{:S(2)}, u32[]{:S(2)}) collective-permute-start(bf16[400,768]{1,0:T(8,128)(2,1)S(1)} %get-tuple-element.105), channel_id=1, source_target_pairs={{0,4},{4,0},{8,12},{12,8},{16,20},{20,16},{24,28},{28,24},{1,5},{5... | collective-permute-start | bytes 1843208 | tf_op jit(solution)/shard_map/ppermute | solution.py:823
  143.0 22.5 %collective-permute-start.34 = (bf16[192,768]{1,0:T(8,128)(2,1)S(1)}, bf16[192,768]{1,0:T(8,128)(2,1)S(1)}, u32[]{:S(2)}, u32[]{:S(2)}) collective-permute-start(bf16[192,768]{1,0:T(8,128)(2,1)S(1)} %get-tuple-element.109), channel_id=1, source_target_pairs={{0,8},{4,12},{8,16},{12,20},{16,24},{20,28},{24,0},{28,4},{1,9},{5... | collective-permute-start | bytes 884744 | tf_op jit(solution)/shard_map/ppermute | solution.py:820
  144.5 21.6 %collective-permute-start.35 = (bf16[192,768]{1,0:T(8,128)(2,1)S(1)}, bf16[192,768]{1,0:T(8,128)(2,1)S(1)}, u32[]{:S(2)}, u32[]{:S(2)}) collective-permute-start(bf16[192,768]{1,0:T(8,128)(2,1)S(1)} %get-tuple-element.110), channel_id=1, source_target_pairs={{0,16},{4,20},{8,24},{12,28},{16,0},{20,4},{24,8},{28,12},{1,17},{... | collective-permute-start | bytes 884744 | tf_op jit(solution)/shard_map/ppermute | solution.py:820
  144.5 25.7 %collective-permute-start.36 = (bf16[192,768]{1,0:T(8,128)(2,1)S(1)}, bf16[192,768]{1,0:T(8,128)(2,1)S(1)}, u32[]{:S(2)}, u32[]{:S(2)}) collective-permute-start(bf16[192,768]{1,0:T(8,128)(2,1)S(1)} %get-tuple-element.111), channel_id=1, source_target_pairs={{0,24},{4,28},{8,0},{12,4},{16,8},{20,12},{24,16},{28,20},{1,25},{... | collective-permute-start | bytes 884744 | tf_op jit(solution)/shard_map/ppermute | solution.py:820
  146.0 34.0 %collective-permute-start.29 = (bf16[2,256,768]{2,1,0:T(8,128)(2,1)}, bf16[2,256,768]{2,1,0:T(8,128)(2,1)S(1)}, u32[]{:S(2)}, u32[]{:S(2)}) collective-permute-start(bf16[2,256,768]{2,1,0:T(8,128)(2,1)} %get-tuple-element.101), channel_id=1, source_target_pairs={{0,1},{1,0},{2,3},{3,2},{4,5},{5,4},{6,7},{7,6},{8,9},{9,8},{10,11... | collective-permute-start | bytes 2359304 | tf_op jit(solution)/shard_map/ppermute | solution.py:817
  165.5 22.5 %collective-permute-start.31 = (bf16[2,256,768]{2,1,0:T(8,128)(2,1)}, bf16[2,256,768]{2,1,0:T(8,128)(2,1)S(1)}, u32[]{:S(2)}, u32[]{:S(2)}) collective-permute-start(bf16[2,256,768]{2,1,0:T(8,128)(2,1)} %get-tuple-element.102), channel_id=1, source_target_pairs={{0,2},{1,3},{2,0},{3,1},{4,6},{5,7},{6,4},{7,5},{8,10},{9,11},{10,... | collective-permute-start | bytes 2359304 | tf_op jit(solution)/shard_map/ppermute | solution.py:817
  166.8 21.5 %collective-permute-start.26 = (bf16[2,256,768]{2,1,0:T(8,128)(2,1)}, bf16[2,256,768]{2,1,0:T(8,128)(2,1)}, u32[]{:S(2)}, u32[]{:S(2)}) collective-permute-start(bf16[2,256,768]{2,1,0:T(8,128)(2,1)} %get-tuple-element.82), channel_id=1, source_target_pairs={{0,1},{1,0},{2,3},{3,2},{4,5},{5,4},{6,7},{7,6},{8,9},{9,8},{10,11... | collective-permute-start | bytes 2359304 | tf_op jit(solution)/shard_map/ppermute | solution.py:817
  170.9 47.2 %collective-permute-start.27 = (bf16[2,256,768]{2,1,0:T(8,128)(2,1)}, bf16[2,256,768]{2,1,0:T(8,128)(2,1)}, u32[]{:S(2)}, u32[]{:S(2)}) collective-permute-start(bf16[2,256,768]{2,1,0:T(8,128)(2,1)} %get-tuple-element.83), channel_id=1, source_target_pairs={{0,2},{1,3},{2,0},{3,1},{4,6},{5,7},{6,4},{7,5},{8,10},{9,11},{10,... | collective-permute-start | bytes 2359304 | tf_op jit(solution)/shard_map/ppermute | solution.py:817
  173.2 45.9 %collective-permute-start.28 = (bf16[2,256,768]{2,1,0:T(8,128)(2,1)}, bf16[2,256,768]{2,1,0:T(8,128)(2,1)}, u32[]{:S(2)}, u32[]{:S(2)}) collective-permute-start(bf16[2,256,768]{2,1,0:T(8,128)(2,1)} %get-tuple-element.84), channel_id=1, source_target_pairs={{0,3},{1,2},{2,1},{3,0},{4,7},{5,6},{6,5},{7,4},{8,11},{9,10},{10,... | collective-permute-start | bytes 2359304 | tf_op jit(solution)/shard_map/ppermute | solution.py:817
  180.0 40.3 %copy-start.7 = (bf16[2,256,768]{2,1,0:T(8,128)(2,1)S(1)}, bf16[2,256,768]{2,1,0:T(8,128)(2,1)}, u32[]{:S(2)}) copy-start(bf16[2,256,768]{2,1,0:T(8,128)(2,1)} %copy-done.6) | copy-start | bytes 2359300
  180.0 8.2 %collective-permute-start.37 = (bf16[96,768]{1,0:T(8,128)(2,1)S(1)}, bf16[96,768]{1,0:T(8,128)(2,1)S(1)}, u32[]{:S(2)}, u32[]{:S(2)}) collective-permute-start(bf16[96,768]{1,0:T(8,128)(2,1)S(1)} %get-tuple-element.113), channel_id=1, source_target_pairs={{0,4},{4,0},{8,12},{12,8},{16,20},{20,16},{24,28},{28,24},{1,5},{5... | collective-permute-start | bytes 442376 | tf_op jit(solution)/shard_map/ppermute | solution.py:823
  188.0 34.4 %collective-permute-start.38 = (bf16[112,768]{1,0:T(8,128)(2,1)S(1)}, bf16[112,768]{1,0:T(8,128)(2,1)S(1)}, u32[]{:S(2)}, u32[]{:S(2)}) collective-permute-start(bf16[112,768]{1,0:T(8,128)(2,1)S(1)} %get-tuple-element.114), channel_id=1, source_target_pairs={{0,8},{4,12},{8,16},{12,20},{16,24},{20,28},{24,0},{28,4},{1,9},{5... | collective-permute-start | bytes 516104 | tf_op jit(solution)/shard_map/ppermute | solution.py:820
  188.2 34.2 %collective-permute-start.39 = (bf16[112,768]{1,0:T(8,128)(2,1)S(1)}, bf16[112,768]{1,0:T(8,128)(2,1)S(1)}, u32[]{:S(2)}, u32[]{:S(2)}) collective-permute-start(bf16[112,768]{1,0:T(8,128)(2,1)S(1)} %get-tuple-element.115), channel_id=1, source_target_pairs={{0,16},{4,20},{8,24},{12,28},{16,0},{20,4},{24,8},{28,12},{1,17},{... | collective-permute-start | bytes 516104 | tf_op jit(solution)/shard_map/ppermute | solution.py:820
  188.3 34.1 %collective-permute-start.40 = (bf16[112,768]{1,0:T(8,128)(2,1)S(1)}, bf16[112,768]{1,0:T(8,128)(2,1)S(1)}, u32[]{:S(2)}, u32[]{:S(2)}) collective-permute-start(bf16[112,768]{1,0:T(8,128)(2,1)S(1)} %get-tuple-element.116), channel_id=1, source_target_pairs={{0,24},{4,28},{8,0},{12,4},{16,8},{20,12},{24,16},{28,20},{1,25},{... | collective-permute-start | bytes 516104 | tf_op jit(solution)/shard_map/ppermute | solution.py:820
  218.1 13.7 %collective-permute-start.32 = (bf16[256,768]{1,0:T(8,128)(2,1)S(1)}, bf16[256,768]{1,0:T(8,128)(2,1)S(1)}, u32[]{:S(2)}, u32[]{:S(2)}) collective-permute-start(bf16[256,768]{1,0:T(8,128)(2,1)S(1)} %get-tuple-element.134), channel_id=1, source_target_pairs={{0,1},{1,0},{2,3},{3,2},{4,5},{5,4},{6,7},{7,6},{8,9},{9,8},{10,11... | collective-permute-start | bytes 1179656 | tf_op jit(solution)/shard_map/ppermute | solution.py:817
  219.1 12.8 %collective-permute-start.30 = (bf16[256,768]{1,0:T(8,128)(2,1)S(1)}, bf16[256,768]{1,0:T(8,128)(2,1)S(1)}, u32[]{:S(2)}, u32[]{:S(2)}) collective-permute-start(bf16[256,768]{1,0:T(8,128)(2,1)S(1)} %get-tuple-element.135), channel_id=1, source_target_pairs={{0,2},{1,3},{2,0},{3,1},{4,6},{5,7},{6,4},{7,5},{8,10},{9,11},{10,... | collective-permute-start | bytes 1179656 | tf_op jit(solution)/shard_map/ppermute | solution.py:817
  223.9 5.6 %collective-permute-start.43 = (bf16[112,256]{1,0:T(8,128)(2,1)S(1)}, bf16[112,256]{1,0:T(8,128)(2,1)S(1)}, u32[]{:S(2)}, u32[]{:S(2)}) collective-permute-start(bf16[112,256]{1,0:T(8,128)(2,1)S(1)} %get-tuple-element.117.refs_0_), channel_id=1, source_target_pairs={{0,3},{1,2},{2,1},{3,0},{4,7},{5,6},{6,5},{7,4},{8,11},{9,10},{10,... | collective-permute-start | bytes 172040 | tf_op jit(solution)/shard_map/ppermute | solution.py:817
  225.3 5.3 %collective-permute-start.42 = (bf16[112,256]{1,0:T(8,128)(2,1)S(1)}, bf16[112,256]{1,0:T(8,128)(2,1)S(1)}, u32[]{:S(2)}, u32[]{:S(2)}) collective-permute-start(bf16[112,256]{1,0:T(8,128)(2,1)S(1)} %get-tuple-element.117.refs_0_), channel_id=1, source_target_pairs={{0,2},{1,3},{2,0},{3,1},{4,6},{5,7},{6,4},{7,5},{8,10},{9,11},{10,... | collective-permute-start | bytes 172040 | tf_op jit(solution)/shard_map/ppermute | solution.py:817
  225.9 4.7 %collective-permute-start.41 = (bf16[112,256]{1,0:T(8,128)(2,1)S(1)}, bf16[112,256]{1,0:T(8,128)(2,1)S(1)}, u32[]{:S(2)}, u32[]{:S(2)}) collective-permute-start(bf16[112,256]{1,0:T(8,128)(2,1)S(1)} %get-tuple-element.117.refs_0_), channel_id=1, source_target_pairs={{0,1},{1,0},{2,3},{3,2},{4,5},{5,4},{6,7},{7,6},{8,9},{9,8},{10,11... | collective-permute-start | bytes 172040 | tf_op jit(solution)/shard_map/ppermute | solution.py:817
  (27 other events, 53.7 us)

commit v5 on v4

--- a/solution.py
+++ b/solution.py
@@ -139,21 +139,11 @@
     return [jnp.where(lane // dm.hd == j, 1.0, 0.0).astype(BF16) for j in range(dm.per)]
 
 
-def norm_kernel(part, x_hbm, gain_ref, *refs):
-    outs, (x_v, sem) = refs[:-2], refs[-2:]
-    count = x_v.shape[0] // part
-    copies = [
-        pltpu.make_async_copy(
-            x_hbm.at[pl.ds(k * part, part), :], x_v.at[pl.ds(k * part, part), :], sem.at[k]
-        )
-        for k in range(count)
-    ]
-    for copy in copies:
-        copy.start()
+def norm_kernel(x_ref, gain_ref, *outs):
     rows = outs[0].shape[0]
-    for k, copy in enumerate(copies):
-        copy.wait()
-        x = x_v[k * part : (k + 1) * part]
+    part = min(LANES, rows)
+    for k in range(x_ref.shape[0] // part):
+        x = x_ref[k * part : (k + 1) * part]
         root = lax.rsqrt(jnp.mean(x * x, axis=1, keepdims=True) + EPS)
         first = k * part % rows
         outs[k * part // rows][first : first + part] = (x * root * gain_ref[...][None]).astype(BF16)
@@ -393,7 +383,7 @@
     mine_out, theirs_out, kept_out = refs[15:18]
     nc_outs = refs[18 : 18 + len(groups)]
     (dh_ref, dbuf, tri_ref, dx_s, act_s, t1_s, t2_s) = refs[18 + len(groups) : 25 + len(groups)]
-    (pick_ref, skip_s, pj_s, full, acc, tap_out, head_out, nc_buf, nc_sem) = refs[25 + len(groups) :]
+    (pick_ref, skip_s, pj_s, full, acc, tap_out, head_out, nc_buf, nc_sem, own_sem) = refs[25 + len(groups) :]
     i = pl.program_id(0)
     blk = jnp.maximum(dm.blocks - 1 - i, 0)
     subs = q // SUB
@@ -582,9 +572,14 @@
     @pl.when(i == dm.blocks)
     def _():
         core, r = scalars[dm.at_core], dm.part_rows
+        owns = []
         for h in range(dm.n_hi):
             at = pl.multiple_of((2 * h + core) * r, 8)
-            mine_out[h * r : (h + 1) * r, :] = acc[pl.ds(at, r), :]
+            own = pltpu.make_async_copy(
+                acc.at[pl.ds(at, r), :], mine_out.at[h * r : (h + 1) * r, :], own_sem.at[h]
+            )
+            own.start()
+            owns.append(own)
             at = pl.multiple_of((2 * h + 1 - core) * r, 8)
             theirs_out[h * r : (h + 1) * r, :] = acc[pl.ds(at, r), :].astype(BF16)
         small = []
@@ -618,6 +613,8 @@
             parts = two_parts(jnp.concatenate(small[8 * c : 8 * c + 8], axis=0))
             theirs_out[dm.n_hi * r :, g] = parts
             kept_out[:, g] = parts
+        for own in owns:
+            own.wait()
         send(0, 1 - slot, 0).wait()
         send(0, slot, 0).wait()
 
@@ -828,19 +825,14 @@
     limit = 16 * 1024 * 1024
     params = pltpu.CompilerParams(dimension_semantics=("arbitrary",), vmem_limit_bytes=limit)
     hbm = pl.BlockSpec(memory_space=pl.ANY)
+    in_hbm = pl.BlockSpec(memory_space=pltpu.HBM)
 
     def out(*shape, dtype=F32):
         return jax.ShapeDtypeStruct(shape, dtype)
 
-    part = min(LANES, dm.piece_rows)
     normed = pl.pallas_call(
-        functools.partial(norm_kernel, part),
+        norm_kernel,
         out_shape=[out(dm.piece_rows, width, dtype=BF16)] * dm.halves,
-        in_specs=[hbm, pl.BlockSpec(memory_space=pltpu.VMEM)],
-        scratch_shapes=[
-            vmem((chunk_rows, width), F32),
-            pltpu.SemaphoreType.DMA((chunk_rows // part,)),
-        ],
         compiler_params=pltpu.CompilerParams(vmem_limit_bytes=limit),
         name="normalize",
     )(block_input, norm_gain)
@@ -960,7 +952,7 @@
         ],
         grid_spec=grid(
             nb,
-            [hbm] * (n_dp + dm.pieces)
+            [in_hbm] * (n_dp + dm.pieces)
             + [
                 pl.BlockSpec((16, q), lambda i, s: (0, i)),
                 const(8, vs),
@@ -1121,8 +1113,8 @@
                 bblock(LANES),
                 pl.BlockSpec((subs * state, ip), lambda i, s: (jnp.maximum(nb - 1 - i, 0), 0)),
             ],
-            [const(r_all, dm.late), const(r_all + 16, dm.late), const(16, dm.late)]
-            + [hbm] * len(dm.group_sizes),
+            [in_hbm, const(r_all + 16, dm.late), const(16, dm.late)]
+            + [in_hbm] * len(dm.group_sizes),
             [
                 vmem((state, ip), F32),
                 vmem((vs // LANES, q + 8, LANES), F32),
@@ -1140,6 +1132,7 @@
                 vmem((16, LANES), F32),
                 vmem((2, q, width), BF16),
                 pltpu.SemaphoreType.DMA((2,)),
+                pltpu.SemaphoreType.DMA((n_hi,)),
             ],
         ),
         compiler_params=params,

time: 235 us -> 234 us (level)
  no operation moved by 1% of the time
where the time goes in v5:
time: 234 us; the launch traced here: 233 us
  Pallas kernels  75.9 us (32%)
  waiting for transfers between devices  66.6 us (28%)
  starting transfers between devices  44.2 us (19%)
  local copies, waits for them, and re-layouts  30.3 us (13%)
  other arithmetic  14.9 us (6%)
    ppermute x22, waiting for transfers between devices, across(): return lax.ppermute(v, 'tensor', swap(n_t, k))  38.7 us
    pallas_call x1, Pallas kernels, body(): pl.pallas_call(functools.partial(backward_kernel, dm), out_shape=[out(r_a...  31.5 us
    ppermute x12, waiting for transfers between devices, along(): return lax.ppermute(v, 'dp', shift_hi(n_dp, k))  27.1 us
    ppermute x22, starting transfers between devices, across(): return lax.ppermute(v, 'tensor', swap(n_t, k))  25.6 us
    pallas_call x1, Pallas kernels, body(): pl.pallas_call(functools.partial(forward_kernel, dm), out_shape=[out(leng...  21.7 us
    unnamed x96, local copies, waits for them, and re-layouts  19.4 us
    ppermute x12, starting transfers between devices, along(): return lax.ppermute(v, 'dp', shift_hi(n_dp, k))  17.4 us
    pallas_call x1, Pallas kernels, body(): pl.pallas_call(functools.partial(gate_kernel, dm), out_shape=[out(length,...  7.94 us
  transfers between devices with their start and end apart: 44, of which 12 were waited for; matrix products, arithmetic and copies ran while one was open for 11% of the time, Pallas kernels for 14%

profile of v5, /device:TPU:16, one launch (start us, length us, event | category | flops | bytes accessed | tf_op | source)
XLA Modules:
  0.0 233.0 jit_solution(13432255947465652971)
XLA Ops:
  1.3 3.5 %collective-permute-start.4 = (bf16[96,384]{1,0:T(8,128)(2,1)}, bf16[96,384]{1,0:T(8,128)(2,1)S(1)}, u32[]{:S(2)}, u32[]{:S(2)}) collective-permute-start(bf16[96,384]{1,0:T(8,128)(2,1)} %bitcast.42), channel_id=1, source_target_pairs={{0,16},{4,20},{8,24},{12,28},{16,0},{20,4},{24,8},{28,12},{1,17},{... | collective-permute-start | bytes 221192 | tf_op jit(solution)/shard_map/ppermute | solution.py:817
  4.8 1.7 pack_weights.1.refs_0_
  8.6 1.2 exponential_negate_fusion
  11.1 1.6 fusion.13
  12.9 1.3 compare_convert_fusion
  14.2 1.4 copy-done
  17.2 2.0 collective-permute-start.12
  19.2 1.5 collective-permute-start.17
  20.7 1.5 collective-permute-start.20
  24.6 1.8 collective-permute-start.11
  28.5 6.8 %collective-permute-done.11.refs_2_ = bf16[96,1152]{1,0:T(8,128)(2,1)S(1)} collective-permute-done((bf16[96,1152]{1,0:T(8,128)(2,1)S(1)}, bf16[96,1152]{1,0:T(8,128)(2,1)S(1)}, u32[]{:S(2)}, u32[]{:S(2)}) %collective-permute-start.11) | collective-permute-done | bytes 221216 | tf_op jit(solution)/shard_map/ppermute | solution.py:817
  35.4 2.4 %collective-permute-start.10 = (bf16[96,1152]{1,0:T(8,128)(2,1)S(1)}, bf16[96,1152]{1,0:T(8,128)(2,1)}, u32[]{:S(2)}, u32[]{:S(2)}) collective-permute-start(bf16[96,1152]{1,0:T(8,128)(2,1)S(1)} %copy-done.16), channel_id=1, source_target_pairs={{0,8},{4,12},{8,16},{12,20},{16,24},{20,28},{24,0},{28,4},{1,9},{5... | collective-permute-start | bytes 663560 | tf_op jit(solution)/shard_map/ppermute | solution.py:817
  37.8 1.5 collective-permute-start.21
  39.3 1.5 collective-permute-start.22
  41.9 1.3 gather_fusion.1
  43.2 1.3 gather_fusion
  47.8 1.8 concatenate.38.refs_16_.refs_1_
  49.6 0.9 concatenate.35.scalars
  55.3 1.6 collective-permute-start.1
  56.8 1.5 collective-permute-start
  58.9 1.0 copy-done.20
  59.9 1.0 copy-done.22
  60.9 1.0 copy-done.24
  61.8 0.9 copy-done.26
  62.8 0.9 copy-done.28
  63.7 0.9 copy-done.30
  64.7 21.7 %block_forward.1 = (f32[2048,384]{1,0:T(8,128)S(1)}, bf16[2048,384]{1,0:T(8,128)(2,1)S(1)}, f32[2048,384]{1,0:T(8,128)S(1)}, bf16[2048,640]{1,0:T(8,128)(2,1)S(1...) custom-call(s32[73]{0:T(128)S(1)} %concatenate.35.scalars, ...), custom_call_target="tpu_custom_call" | custom-call | flops 30000001024 | bytes 30000000 | tf_op jit(solution)/shard_map/block_forward/pallas_call | solution.py:937
  86.4 4.3 %branch_output.1 = (bf16[768,384]{1,0:T(8,128)(2,1)S(1)}, bf16[2,256,768]{2,1,0:T(8,128)(2,1)S(1)}, bf16[2,256,768]{2,1,0:T(8,128)(2,1)}, bf16[2,256,768]{2,1,0:T(8,128)(2,1)}, bf16[2,256,768]{2,1,0:T(8,128)(2,1)}) custom-call(s32[73]{0:T(128)S(1)} %concatenate.35.scalars, bf16[96,384]{1,0:T(8,128)(2,1)S(1)} %bitcast.44, bf16[96,384]{1,0:T(8,128)(2,1)S(1)} %copy-done.35, ...), custom_call_target="tpu_custom_call" | custom-call | flops 3000000000 | bytes 10000000 | tf_op jit(solution)/shard_map/branch_output/pallas_call | solution.py:999
  90.7 0.9 copy-done.6
  91.9 2.6 %scaled_cotangent.1 = (bf16[2048,384]{1,0:T(8,128)(2,1)S(1)}, f32[8,2,256]{2,1,0:T(2,128)S(1)}, bf16[2048,768]{1,0:T(8,128)(2,1)S(1)}) custom-call(s32[73]{0:T(128)S(1)} %concatenate.35.scalars, bf16[512,768]{1,0:T(8,128)(2,1)S(1)} %copy-done.4, bf16[512,768]{1,0:T(8,128)(2,1)S(1)} %collective-permute-done.refs_1_, ...), custom_call_target="tpu_custom_call" | custom-call | flops 3000000000 | bytes 10000000 | tf_op jit(solution)/shard_map/scaled_cotangent/pallas_call | solution.py:1015
  94.4 1.2 collective-permute-start.25
  95.7 1.4 collective-permute-start.24
  97.1 0.9 collective-permute-start.23
  98.0 1.1 collective-permute-done.25
  99.4 1.4 collective-permute-done.23
  100.9 7.9 %gate_backward.1 = (bf16[2048,384]{1,0:T(8,128)(2,1)S(1)}, bf16[2048,384]{1,0:T(8,128)(2,1)S(1)}, f32[8,384]{1,0:T(8,128)S(1)}, f32[8,768]{1,0:T(8,128)S(1)}, f3...) custom-call(s32[73]{0:T(128)S(1)} %concatenate.35.scalars, ...), custom_call_target="tpu_custom_call" | custom-call | flops 6000000000 | bytes 20000000 | tf_op jit(solution)/shard_map/gate_backward/pallas_call | solution.py:1053
  109.7 31.5 %block_backward.1 = (f32[384,768]{1,0:T(8,128)S(1)}, bf16[400,768]{1,0:T(8,128)(2,1)S(1)}, bf16[16,768]{1,0:T(8,128)(2,1)S(1)}, bf16[2,256,768]{2,1,0:T(8,128)(2...) custom-call(s32[73]{0:T(128)S(1)} %concatenate.35.scalars, ...), custom_call_target="tpu_custom_call" | custom-call | flops 40000000000 | bytes 30000000 | tf_op jit(solution)/shard_map/block_backward/pallas_call | solution.py:1089
  141.2 1.0 copy-done.2
  142.2 1.5 collective-permute-start.34
  143.7 1.5 collective-permute-start.36
  145.2 1.1 collective-permute-start.29
  146.3 18.4 %collective-permute-done.34.refs_0_ = bf16[192,768]{1,0:T(8,128)(2,1)S(1)} collective-permute-done((bf16[192,768]{1,0:T(8,128)(2,1)S(1)}, bf16[192,768]{1,0:T(8,128)(2,1)S(1)}, u32[]{:S(2)}, u32[]{:S(2)}) %collective-permute-start.34) | collective-permute-done | bytes 294944 | tf_op jit(solution)/shard_map/ppermute | solution.py:817
  166.0 1.5 collective-permute-start.26
  167.5 1.9 collective-permute-done.36.refs_2_
  170.1 1.4 collective-permute-start.27
  171.5 0.8 copy-done.8
  172.4 1.1 collective-permute-start.28
  173.6 1.1 copy-done.11
  174.7 1.0 copy-done.13
  175.7 1.0 copy-done.15
  177.4 1.1 copy-done.9
  179.2 8.0 %collective-permute-done.31.refs_4_ = bf16[2,256,768]{2,1,0:T(8,128)(2,1)S(1)} collective-permute-done((bf16[2,256,768]{2,1,0:T(8,128)(2,1)}, bf16[2,256,768]{2,1,0:T(8,128)(2,1)S(1)}, u32[]{:S(2)}, u32[]{:S(2)}) %collective-permute-start.31) | collective-permute-done | bytes 786464 | tf_op jit(solution)/shard_map/ppermute | solution.py:814
  187.5 4.0 %collective-permute-start.40 = (bf16[112,768]{1,0:T(8,128)(2,1)S(1)}, bf16[112,768]{1,0:T(8,128)(2,1)S(1)}, u32[]{:S(2)}, u32[]{:S(2)}) collective-permute-start(bf16[112,768]{1,0:T(8,128)(2,1)S(1)} %get-tuple-element.116), channel_id=1, source_target_pairs={{0,24},{4,28},{8,0},{12,4},{16,8},{20,12},{24,16},{28,20},{1,25},{... | collective-permute-start | bytes 516104 | tf_op jit(solution)/shard_map/ppermute | solution.py:817
  191.6 25.8 %collective-permute-done.27 = bf16[2,256,768]{2,1,0:T(8,128)(2,1)} collective-permute-done((bf16[2,256,768]{2,1,0:T(8,128)(2,1)}, bf16[2,256,768]{2,1,0:T(8,128)(2,1)}, u32[]{:S(2)}, u32[]{:S(2)}) %collective-permute-start.27) | collective-permute-done | bytes 786464 | tf_op jit(solution)/shard_map/ppermute | solution.py:814
  217.4 0.9 collective-permute-start.32
  218.2 1.2 collective-permute-start.30
  219.5 2.1 convert_add_fusion
  221.6 1.4 gradient_sum.1
  223.0 1.5 collective-permute-start.43
  225.1 1.5 collective-permute-start.41
  226.6 1.4 fusion
  228.7 1.1 collective-permute-done.42.refs_2_
  229.8 1.2 shared_sum.1
  231.0 2.0 input_gradient.1
  (169 shorter events, 26.5 us)
Async XLA Ops:
  0.6 41.2 %copy-start.43 = (s32[4,2]{1,0:T(4,128)S(1)}, s32[4,2]{1,0:T(4,128)}, u32[]{:S(2)}) copy-start(s32[4,2]{1,0:T(4,128)} %constant.112.clone) | copy-start | bytes 100
  0.7 42.5 %copy-start.42 = (s32[4,2]{1,0:T(4,128)S(1)}, s32[4,2]{1,0:T(4,128)}, u32[]{:S(2)}) copy-start(s32[4,2]{1,0:T(4,128)} %constant.111.clone) | copy-start | bytes 100
  0.7 40.6 %copy-start.44 = (s32[1,2048]{1,0:T(1,128)S(1)}, s32[1,2048]{1,0:T(1,128)}, u32[]{:S(2)}) copy-start(s32[1,2048]{1,0:T(1,128)} %param.20) | copy-start | bytes 24580
  0.7 16.5 %collective-permute-start.6 = (bf16[96,384]{1,0:T(8,128)(2,1)}, bf16[96,384]{1,0:T(8,128)(2,1)S(1)}, u32[]{:S(2)}, u32[]{:S(2)}) collective-permute-start(bf16[96,384]{1,0:T(8,128)(2,1)} %bitcast.40), channel_id=1, source_target_pairs={{0,4},{4,0},{8,12},{12,8},{16,20},{20,16},{24,28},{28,24},{1,5},{5... | collective-permute-start | bytes 221192 | tf_op jit(solution)/shard_map/ppermute | solution.py:820
  0.8 18.4 %collective-permute-start.5 = (bf16[96,384]{1,0:T(8,128)(2,1)}, bf16[96,384]{1,0:T(8,128)(2,1)S(1)}, u32[]{:S(2)}, u32[]{:S(2)}) collective-permute-start(bf16[96,384]{1,0:T(8,128)(2,1)} %bitcast.41), channel_id=1, source_target_pairs={{0,24},{4,28},{8,0},{12,4},{16,8},{20,12},{24,16},{28,20},{1,25},{... | collective-permute-start | bytes 221192 | tf_op jit(solution)/shard_map/ppermute | solution.py:817
  1.3 19.4 %collective-permute-start.4 = (bf16[96,384]{1,0:T(8,128)(2,1)}, bf16[96,384]{1,0:T(8,128)(2,1)S(1)}, u32[]{:S(2)}, u32[]{:S(2)}) collective-permute-start(bf16[96,384]{1,0:T(8,128)(2,1)} %bitcast.42), channel_id=1, source_target_pairs={{0,16},{4,20},{8,24},{12,28},{16,0},{20,4},{24,8},{28,12},{1,17},{... | collective-permute-start | bytes 221192 | tf_op jit(solution)/shard_map/ppermute | solution.py:817
  4.8 18.0 %collective-permute-start.3 = (bf16[96,384]{1,0:T(8,128)(2,1)}, bf16[96,384]{1,0:T(8,128)(2,1)S(1)}, u32[]{:S(2)}, u32[]{:S(2)}) collective-permute-start(bf16[96,384]{1,0:T(8,128)(2,1)} %bitcast.43), channel_id=1, source_target_pairs={{0,8},{4,12},{8,16},{12,20},{16,24},{20,28},{24,0},{28,4},{1,9},{5... | collective-permute-start | bytes 221192 | tf_op jit(solution)/shard_map/ppermute | solution.py:817
  6.5 10.7 %copy-start.16 = (bf16[96,1152]{1,0:T(8,128)(2,1)S(1)}, bf16[96,1152]{1,0:T(8,128)(2,1)}, u32[]{:S(2)}) copy-start(bf16[96,1152]{1,0:T(8,128)(2,1)} %pack_weights.1.refs_0_) | copy-start | bytes 663556
  6.5 19.9 %collective-permute-start.13 = (bf16[96,1152]{1,0:T(8,128)(2,1)}, bf16[96,1152]{1,0:T(8,128)(2,1)S(1)}, u32[]{:S(2)}, u32[]{:S(2)}) collective-permute-start(bf16[96,1152]{1,0:T(8,128)(2,1)} %pack_weights.1.refs_0_), channel_id=1, source_target_pairs={{0,4},{4,0},{8,12},{12,8},{16,20},{20,16},{24,28},{28,24},{1,5},{5... | collective-permute-start | bytes 663560 | tf_op jit(solution)/shard_map/ppermute | solution.py:820
  12.7 15.3 %copy-start.45 = (f32[6]{0:T(128)S(1)}, f32[6]{0:T(128)}, u32[]{:S(2)}) copy-start(f32[6]{0:T(128)} %param.30) | copy-start | bytes 76
  12.7 15.3 %copy-start.46 = (f32[6]{0:T(128)S(1)}, f32[6]{0:T(128)}, u32[]{:S(2)}) copy-start(f32[6]{0:T(128)} %exponential_negate_fusion) | copy-start | bytes 76
  16.3 38.4 %copy-start.4 = (bf16[512,768]{1,0:T(8,128)(2,1)S(1)}, bf16[512,768]{1,0:T(8,128)(2,1)}, u32[]{:S(2)}) copy-start(bf16[512,768]{1,0:T(8,128)(2,1)} %cot_ref.1) | copy-start | bytes 2359300
  16.6 38.1 %copy-start.19 = (bf16[256,768]{1,0:T(8,128)(2,1)}, bf16[256,768]{1,0:T(8,128)(2,1)S(1)}, u32[]{:S(2)}) copy-start(bf16[256,768]{1,0:T(8,128)(2,1)S(1)} %get-tuple-element.75.refs_9_) | copy-start | bytes 1179652
  17.2 9.8 %collective-permute-start.12 = (bf16[96,1152]{1,0:T(8,128)(2,1)S(1)}, bf16[96,1152]{1,0:T(8,128)(2,1)S(1)}, u32[]{:S(2)}, u32[]{:S(2)}) collective-permute-start(bf16[96,1152]{1,0:T(8,128)(2,1)S(1)} %copy-done.16), channel_id=1, source_target_pairs={{0,24},{4,28},{8,0},{12,4},{16,8},{20,12},{24,16},{28,20},{1,25},{... | collective-permute-start | bytes 663560 | tf_op jit(solution)/shard_map/ppermute | solution.py:817
  19.2 18.6 %collective-permute-start.17 = (bf16[256,768]{1,0:T(8,128)(2,1)S(1)}, bf16[256,768]{1,0:T(8,128)(2,1)}, u32[]{:S(2)}, u32[]{:S(2)}) collective-permute-start(bf16[256,768]{1,0:T(8,128)(2,1)S(1)} %get-tuple-element.74.refs_8_), channel_id=1, source_target_pairs={{0,1},{1,0},{2,3},{3,2},{4,5},{5,4},{6,7},{7,6},{8,9},{9,8},{10,11... | collective-permute-start | bytes 1179656 | tf_op jit(solution)/shard_map/ppermute | solution.py:814
  20.7 29.0 %copy-start.32 = (bf16[96,384]{1,0:T(8,128)(2,1)}, bf16[96,384]{1,0:T(8,128)(2,1)S(1)}, u32[]{:S(2)}) copy-start(bf16[96,384]{1,0:T(8,128)(2,1)S(1)} %collective-permute-done.4.refs_2_) | copy-start | bytes 221188
  20.7 18.6 %collective-permute-start.20 = (bf16[256,768]{1,0:T(8,128)(2,1)S(1)}, bf16[256,768]{1,0:T(8,128)(2,1)}, u32[]{:S(2)}, u32[]{:S(2)}) collective-permute-start(bf16[256,768]{1,0:T(8,128)(2,1)S(1)} %get-tuple-element.75.refs_9_), channel_id=1, source_target_pairs={{0,2},{1,3},{2,0},{3,1},{4,6},{5,7},{6,4},{7,5},{8,10},{9,11},{10,... | collective-permute-start | bytes 1179656 | tf_op jit(solution)/shard_map/ppermute | solution.py:814
  22.7 24.5 %copy-start.34 = (bf16[96,384]{1,0:T(8,128)(2,1)}, bf16[96,384]{1,0:T(8,128)(2,1)S(1)}, u32[]{:S(2)}) copy-start(bf16[96,384]{1,0:T(8,128)(2,1)S(1)} %collective-permute-done.3.refs_1_) | copy-start | bytes 221188
  22.7 1.3 collective-permute-start.9
  24.6 10.7 %collective-permute-start.11 = (bf16[96,1152]{1,0:T(8,128)(2,1)S(1)}, bf16[96,1152]{1,0:T(8,128)(2,1)S(1)}, u32[]{:S(2)}, u32[]{:S(2)}) collective-permute-start(bf16[96,1152]{1,0:T(8,128)(2,1)S(1)} %copy-done.16), channel_id=1, source_target_pairs={{0,16},{4,20},{8,24},{12,28},{16,0},{20,4},{24,8},{28,12},{1,17},{... | collective-permute-start | bytes 663560 | tf_op jit(solution)/shard_map/ppermute | solution.py:817
  26.4 20.8 %copy-start.25 = (bf16[96,1152]{1,0:T(8,128)(2,1)}, bf16[96,1152]{1,0:T(8,128)(2,1)S(1)}, u32[]{:S(2)}) copy-start(bf16[96,1152]{1,0:T(8,128)(2,1)S(1)} %collective-permute-done.13.refs_4_) | copy-start | bytes 663556
  26.4 24.9 %collective-permute-start.19 = (bf16[256,768]{1,0:T(8,128)(2,1)S(1)}, bf16[256,768]{1,0:T(8,128)(2,1)S(1)}, u32[]{:S(2)}, u32[]{:S(2)}) collective-permute-start(bf16[256,768]{1,0:T(8,128)(2,1)S(1)} %get-tuple-element.74.refs_8_), channel_id=1, source_target_pairs={{0,2},{1,3},{2,0},{3,1},{4,6},{5,7},{6,4},{7,5},{8,10},{9,11},{10,... | collective-permute-start | bytes 1179656 | tf_op jit(solution)/shard_map/ppermute | solution.py:814
  27.0 28.3 %copy-start.27 = (bf16[96,1152]{1,0:T(8,128)(2,1)}, bf16[96,1152]{1,0:T(8,128)(2,1)S(1)}, u32[]{:S(2)}) copy-start(bf16[96,1152]{1,0:T(8,128)(2,1)S(1)} %collective-permute-done.12.refs_3_) | copy-start | bytes 663556
  27.0 25.6 %collective-permute-start.18 = (bf16[256,768]{1,0:T(8,128)(2,1)S(1)}, bf16[256,768]{1,0:T(8,128)(2,1)S(1)}, u32[]{:S(2)}, u32[]{:S(2)}) collective-permute-start(bf16[256,768]{1,0:T(8,128)(2,1)S(1)} %get-tuple-element.75.refs_9_), channel_id=1, source_target_pairs={{0,1},{1,0},{2,3},{3,2},{4,5},{5,4},{6,7},{7,6},{8,9},{9,8},{10,11... | collective-permute-start | bytes 1179656 | tf_op jit(solution)/shard_map/ppermute | solution.py:814
  35.4 19.9 %copy-start.29 = (bf16[96,1152]{1,0:T(8,128)(2,1)}, bf16[96,1152]{1,0:T(8,128)(2,1)S(1)}, u32[]{:S(2)}) copy-start(bf16[96,1152]{1,0:T(8,128)(2,1)S(1)} %collective-permute-done.11.refs_2_) | copy-start | bytes 663556
  35.4 15.8 %collective-permute-start.10 = (bf16[96,1152]{1,0:T(8,128)(2,1)S(1)}, bf16[96,1152]{1,0:T(8,128)(2,1)}, u32[]{:S(2)}, u32[]{:S(2)}) collective-permute-start(bf16[96,1152]{1,0:T(8,128)(2,1)S(1)} %copy-done.16), channel_id=1, source_target_pairs={{0,8},{4,12},{8,16},{12,20},{16,24},{20,28},{24,0},{28,4},{1,9},{5... | collective-permute-start | bytes 663560 | tf_op jit(solution)/shard_map/ppermute | solution.py:817
  37.8 20.6 %collective-permute-start.21 = (bf16[256,768]{1,0:T(8,128)(2,1)}, bf16[256,768]{1,0:T(8,128)(2,1)}, u32[]{:S(2)}, u32[]{:S(2)}) collective-permute-start(bf16[256,768]{1,0:T(8,128)(2,1)} %collective-permute-done.17.refs_10_), channel_id=1, source_target_pairs={{0,2},{1,3},{2,0},{3,1},{4,6},{5,7},{6,4},{7,5},{8,10},{9,11},{10,... | collective-permute-start | bytes 1179656 | tf_op jit(solution)/shard_map/ppermute | solution.py:814
  39.3 19.1 %collective-permute-start.22 = (bf16[256,768]{1,0:T(8,128)(2,1)}, bf16[256,768]{1,0:T(8,128)(2,1)}, u32[]{:S(2)}, u32[]{:S(2)}) collective-permute-start(bf16[256,768]{1,0:T(8,128)(2,1)} %collective-permute-done.20.refs_13_), channel_id=1, source_target_pairs={{0,1},{1,0},{2,3},{3,2},{4,5},{5,4},{6,7},{7,6},{8,9},{9,8},{10,11... | collective-permute-start | bytes 1179656 | tf_op jit(solution)/shard_map/ppermute | solution.py:814
  51.2 3.5 %collective-permute-start.16 = (bf16[96,1152]{1,0:T(8,128)(2,1)S(1)}, bf16[96,1152]{1,0:T(8,128)(2,1)S(1)}, u32[]{:S(2)}, u32[]{:S(2)}) collective-permute-start(bf16[96,1152]{1,0:T(8,128)(2,1)S(1)} %collective-permute-done.12.refs_3_), channel_id=1, source_target_pairs={{0,4},{4,0},{8,12},{12,8},{16,20},{20,16},{24,28},{28,24},{1,5},{5... | collective-permute-start | bytes 663560 | tf_op jit(solution)/shard_map/ppermute | solution.py:820
  52.1 3.2 %collective-permute-start.15 = (bf16[96,1152]{1,0:T(8,128)(2,1)S(1)}, bf16[96,1152]{1,0:T(8,128)(2,1)S(1)}, u32[]{:S(2)}, u32[]{:S(2)}) collective-permute-start(bf16[96,1152]{1,0:T(8,128)(2,1)S(1)} %collective-permute-done.11.refs_2_), channel_id=1, source_target_pairs={{0,4},{4,0},{8,12},{12,8},{16,20},{20,16},{24,28},{28,24},{1,5},{5... | collective-permute-start | bytes 663560 | tf_op jit(solution)/shard_map/ppermute | solution.py:820
  53.3 3.5 %collective-permute-start.14 = (bf16[96,1152]{1,0:T(8,128)(2,1)}, bf16[96,1152]{1,0:T(8,128)(2,1)S(1)}, u32[]{:S(2)}, u32[]{:S(2)}) collective-permute-start(bf16[96,1152]{1,0:T(8,128)(2,1)} %collective-permute-done.10.refs_1_), channel_id=1, source_target_pairs={{0,4},{4,0},{8,12},{12,8},{16,20},{20,16},{24,28},{28,24},{1,5},{5... | collective-permute-start | bytes 663560 | tf_op jit(solution)/shard_map/ppermute | solution.py:820
  54.7 36.9 %collective-permute-start.2 = (bf16[512,768]{1,0:T(8,128)(2,1)S(1)}, bf16[512,768]{1,0:T(8,128)(2,1)S(1)}, u32[]{:S(2)}, u32[]{:S(2)}) collective-permute-start(bf16[512,768]{1,0:T(8,128)(2,1)S(1)} %copy-done.4), channel_id=1, source_target_pairs={{0,3},{1,2},{2,1},{3,0},{4,7},{5,6},{6,5},{7,4},{8,11},{9,10},{10,... | collective-permute-start | bytes 2359304 | tf_op jit(solution)/shard_map/ppermute | solution.py:814
  55.3 36.6 %collective-permute-start.1 = (bf16[512,768]{1,0:T(8,128)(2,1)S(1)}, bf16[512,768]{1,0:T(8,128)(2,1)S(1)}, u32[]{:S(2)}, u32[]{:S(2)}) collective-permute-start(bf16[512,768]{1,0:T(8,128)(2,1)S(1)} %copy-done.4), channel_id=1, source_target_pairs={{0,2},{1,3},{2,0},{3,1},{4,6},{5,7},{6,4},{7,5},{8,10},{9,11},{10,... | collective-permute-start | bytes 2359304 | tf_op jit(solution)/shard_map/ppermute | solution.py:814
  56.8 35.0 %collective-permute-start = (bf16[512,768]{1,0:T(8,128)(2,1)S(1)}, bf16[512,768]{1,0:T(8,128)(2,1)S(1)}, u32[]{:S(2)}, u32[]{:S(2)}) collective-permute-start(bf16[512,768]{1,0:T(8,128)(2,1)S(1)} %copy-done.4), channel_id=1, source_target_pairs={{0,1},{1,0},{2,3},{3,2},{4,5},{5,4},{6,7},{7,6},{8,9},{9,8},{10,11... | collective-permute-start | bytes 2359304 | tf_op jit(solution)/shard_map/ppermute | solution.py:814
  58.3 28.0 %collective-permute-start.8 = (bf16[96,384]{1,0:T(8,128)(2,1)}, bf16[96,384]{1,0:T(8,128)(2,1)S(1)}, u32[]{:S(2)}, u32[]{:S(2)}) collective-permute-start(bf16[96,384]{1,0:T(8,128)(2,1)} %copy-done.32), channel_id=1, source_target_pairs={{0,4},{4,0},{8,12},{12,8},{16,20},{20,16},{24,28},{28,24},{1,5},{5... | collective-permute-start | bytes 221192 | tf_op jit(solution)/shard_map/ppermute | solution.py:820
  58.4 28.0 %collective-permute-start.7 = (bf16[96,384]{1,0:T(8,128)(2,1)}, bf16[96,384]{1,0:T(8,128)(2,1)S(1)}, u32[]{:S(2)}, u32[]{:S(2)}) collective-permute-start(bf16[96,384]{1,0:T(8,128)(2,1)} %copy-done.34), channel_id=1, source_target_pairs={{0,4},{4,0},{8,12},{12,8},{16,20},{20,16},{24,28},{28,24},{1,5},{5... | collective-permute-start | bytes 221192 | tf_op jit(solution)/shard_map/ppermute | solution.py:820
  64.7 21.7 %copy-start.31 = (bf16[384,96]{0,1:T(8,128)(2,1)S(1)}, bf16[384,96]{0,1:T(8,128)(2,1)}, u32[]{:S(2)}) copy-start(bf16[384,96]{0,1:T(8,128)(2,1)} %param.34) | copy-start | bytes 221188
  64.7 21.7 %copy-start.33 = (bf16[96,384]{1,0:T(8,128)(2,1)S(1)}, bf16[96,384]{1,0:T(8,128)(2,1)}, u32[]{:S(2)}) copy-start(bf16[96,384]{1,0:T(8,128)(2,1)} %copy-done.32) | copy-start | bytes 221188
  64.7 21.8 %copy-start.35 = (bf16[96,384]{1,0:T(8,128)(2,1)S(1)}, bf16[96,384]{1,0:T(8,128)(2,1)}, u32[]{:S(2)}) copy-start(bf16[96,384]{1,0:T(8,128)(2,1)} %copy-done.34) | copy-start | bytes 221188
  64.7 21.8 %copy-start.37 = (bf16[96,384]{1,0:T(8,128)(2,1)S(1)}, bf16[96,384]{1,0:T(8,128)(2,1)}, u32[]{:S(2)}) copy-start(bf16[96,384]{1,0:T(8,128)(2,1)} %copy-done.36) | copy-start | bytes 221188
  94.4 4.7 %collective-permute-start.25 = (f32[8,2,256]{2,1,0:T(2,128)S(1)}, f32[8,2,256]{2,1,0:T(2,128)S(1)}, u32[]{:S(2)}, u32[]{:S(2)}) collective-permute-start(f32[8,2,256]{2,1,0:T(2,128)S(1)} %get-tuple-element.80), channel_id=1, source_target_pairs={{0,3},{1,2},{2,1},{3,0},{4,7},{5,6},{6,5},{7,4},{8,11},{9,10},{10,... | collective-permute-start | bytes 49160 | tf_op jit(solution)/shard_map/ppermute | solution.py:814
  95.7 3.7 %collective-permute-start.24 = (f32[8,2,256]{2,1,0:T(2,128)S(1)}, f32[8,2,256]{2,1,0:T(2,128)S(1)}, u32[]{:S(2)}, u32[]{:S(2)}) collective-permute-start(f32[8,2,256]{2,1,0:T(2,128)S(1)} %get-tuple-element.80), channel_id=1, source_target_pairs={{0,2},{1,3},{2,0},{3,1},{4,6},{5,7},{6,4},{7,5},{8,10},{9,11},{10,... | collective-permute-start | bytes 49160 | tf_op jit(solution)/shard_map/ppermute | solution.py:814
  97.1 3.7 %collective-permute-start.23 = (f32[8,2,256]{2,1,0:T(2,128)S(1)}, f32[8,2,256]{2,1,0:T(2,128)S(1)}, u32[]{:S(2)}, u32[]{:S(2)}) collective-permute-start(f32[8,2,256]{2,1,0:T(2,128)S(1)} %get-tuple-element.80), channel_id=1, source_target_pairs={{0,1},{1,0},{2,3},{3,2},{4,5},{5,4},{6,7},{7,6},{8,9},{9,8},{10,11... | collective-permute-start | bytes 49160 | tf_op jit(solution)/shard_map/ppermute | solution.py:814
  100.9 8.8 %copy-start.39 = (f32[2048,384]{1,0:T(8,128)S(1)}, f32[2048,384]{1,0:T(8,128)}, u32[]{:S(2)}) copy-start(f32[2048,384]{1,0:T(8,128)} %copy-done.38) | copy-start | bytes 9437188
  100.9 8.8 %copy-start.41 = (bf16[2048,640]{1,0:T(8,128)(2,1)S(1)}, bf16[2048,640]{1,0:T(8,128)(2,1)}, u32[]{:S(2)}) copy-start(bf16[2048,640]{1,0:T(8,128)(2,1)} %copy-done.40) | copy-start | bytes 7864324
  142.2 29.4 %collective-permute-start.33 = (bf16[400,768]{1,0:T(8,128)(2,1)S(1)}, bf16[400,768]{1,0:T(8,128)(2,1)S(1)}, u32[]{:S(2)}, u32[]{:S(2)}) collective-permute-start(bf16[400,768]{1,0:T(8,128)(2,1)S(1)} %get-tuple-element.105), channel_id=1, source_target_pairs={{0,4},{4,0},{8,12},{12,8},{16,20},{20,16},{24,28},{28,24},{1,5},{5... | collective-permute-start | bytes 1843208 | tf_op jit(solution)/shard_map/ppermute | solution.py:820
  142.2 22.5 %collective-permute-start.34 = (bf16[192,768]{1,0:T(8,128)(2,1)S(1)}, bf16[192,768]{1,0:T(8,128)(2,1)S(1)}, u32[]{:S(2)}, u32[]{:S(2)}) collective-permute-start(bf16[192,768]{1,0:T(8,128)(2,1)S(1)} %get-tuple-element.109), channel_id=1, source_target_pairs={{0,8},{4,12},{8,16},{12,20},{16,24},{20,28},{24,0},{28,4},{1,9},{5... | collective-permute-start | bytes 884744 | tf_op jit(solution)/shard_map/ppermute | solution.py:817
  143.7 21.6 %collective-permute-start.35 = (bf16[192,768]{1,0:T(8,128)(2,1)S(1)}, bf16[192,768]{1,0:T(8,128)(2,1)S(1)}, u32[]{:S(2)}, u32[]{:S(2)}) collective-permute-start(bf16[192,768]{1,0:T(8,128)(2,1)S(1)} %get-tuple-element.110), channel_id=1, source_target_pairs={{0,16},{4,20},{8,24},{12,28},{16,0},{20,4},{24,8},{28,12},{1,17},{... | collective-permute-start | bytes 884744 | tf_op jit(solution)/shard_map/ppermute | solution.py:817
  143.7 25.7 %collective-permute-start.36 = (bf16[192,768]{1,0:T(8,128)(2,1)S(1)}, bf16[192,768]{1,0:T(8,128)(2,1)S(1)}, u32[]{:S(2)}, u32[]{:S(2)}) collective-permute-start(bf16[192,768]{1,0:T(8,128)(2,1)S(1)} %get-tuple-element.111), channel_id=1, source_target_pairs={{0,24},{4,28},{8,0},{12,4},{16,8},{20,12},{24,16},{28,20},{1,25},{... | collective-permute-start | bytes 884744 | tf_op jit(solution)/shard_map/ppermute | solution.py:817
  145.2 33.9 %collective-permute-start.29 = (bf16[2,256,768]{2,1,0:T(8,128)(2,1)}, bf16[2,256,768]{2,1,0:T(8,128)(2,1)S(1)}, u32[]{:S(2)}, u32[]{:S(2)}) collective-permute-start(bf16[2,256,768]{2,1,0:T(8,128)(2,1)} %get-tuple-element.101), channel_id=1, source_target_pairs={{0,1},{1,0},{2,3},{3,2},{4,5},{5,4},{6,7},{7,6},{8,9},{9,8},{10,11... | collective-permute-start | bytes 2359304 | tf_op jit(solution)/shard_map/ppermute | solution.py:814
  164.7 22.5 %collective-permute-start.31 = (bf16[2,256,768]{2,1,0:T(8,128)(2,1)}, bf16[2,256,768]{2,1,0:T(8,128)(2,1)S(1)}, u32[]{:S(2)}, u32[]{:S(2)}) collective-permute-start(bf16[2,256,768]{2,1,0:T(8,128)(2,1)} %get-tuple-element.102), channel_id=1, source_target_pairs={{0,2},{1,3},{2,0},{3,1},{4,6},{5,7},{6,4},{7,5},{8,10},{9,11},{10,... | collective-permute-start | bytes 2359304 | tf_op jit(solution)/shard_map/ppermute | solution.py:814
  166.0 21.5 %collective-permute-start.26 = (bf16[2,256,768]{2,1,0:T(8,128)(2,1)}, bf16[2,256,768]{2,1,0:T(8,128)(2,1)}, u32[]{:S(2)}, u32[]{:S(2)}) collective-permute-start(bf16[2,256,768]{2,1,0:T(8,128)(2,1)} %get-tuple-element.82), channel_id=1, source_target_pairs={{0,1},{1,0},{2,3},{3,2},{4,5},{5,4},{6,7},{7,6},{8,9},{9,8},{10,11... | collective-permute-start | bytes 2359304 | tf_op jit(solution)/shard_map/ppermute | solution.py:814
  170.1 47.2 %collective-permute-start.27 = (bf16[2,256,768]{2,1,0:T(8,128)(2,1)}, bf16[2,256,768]{2,1,0:T(8,128)(2,1)}, u32[]{:S(2)}, u32[]{:S(2)}) collective-permute-start(bf16[2,256,768]{2,1,0:T(8,128)(2,1)} %get-tuple-element.83), channel_id=1, source_target_pairs={{0,2},{1,3},{2,0},{3,1},{4,6},{5,7},{6,4},{7,5},{8,10},{9,11},{10,... | collective-permute-start | bytes 2359304 | tf_op jit(solution)/shard_map/ppermute | solution.py:814
  172.4 45.9 %collective-permute-start.28 = (bf16[2,256,768]{2,1,0:T(8,128)(2,1)}, bf16[2,256,768]{2,1,0:T(8,128)(2,1)}, u32[]{:S(2)}, u32[]{:S(2)}) collective-permute-start(bf16[2,256,768]{2,1,0:T(8,128)(2,1)} %get-tuple-element.84), channel_id=1, source_target_pairs={{0,3},{1,2},{2,1},{3,0},{4,7},{5,6},{6,5},{7,4},{8,11},{9,10},{10,... | collective-permute-start | bytes 2359304 | tf_op jit(solution)/shard_map/ppermute | solution.py:814
  179.1 40.3 %copy-start.7 = (bf16[2,256,768]{2,1,0:T(8,128)(2,1)S(1)}, bf16[2,256,768]{2,1,0:T(8,128)(2,1)}, u32[]{:S(2)}) copy-start(bf16[2,256,768]{2,1,0:T(8,128)(2,1)} %copy-done.6) | copy-start | bytes 2359300
  179.2 8.3 %collective-permute-start.37 = (bf16[96,768]{1,0:T(8,128)(2,1)S(1)}, bf16[96,768]{1,0:T(8,128)(2,1)S(1)}, u32[]{:S(2)}, u32[]{:S(2)}) collective-permute-start(bf16[96,768]{1,0:T(8,128)(2,1)S(1)} %get-tuple-element.113), channel_id=1, source_target_pairs={{0,4},{4,0},{8,12},{12,8},{16,20},{20,16},{24,28},{28,24},{1,5},{5... | collective-permute-start | bytes 442376 | tf_op jit(solution)/shard_map/ppermute | solution.py:820
  187.2 34.4 %collective-permute-start.38 = (bf16[112,768]{1,0:T(8,128)(2,1)S(1)}, bf16[112,768]{1,0:T(8,128)(2,1)S(1)}, u32[]{:S(2)}, u32[]{:S(2)}) collective-permute-start(bf16[112,768]{1,0:T(8,128)(2,1)S(1)} %get-tuple-element.114), channel_id=1, source_target_pairs={{0,8},{4,12},{8,16},{12,20},{16,24},{20,28},{24,0},{28,4},{1,9},{5... | collective-permute-start | bytes 516104 | tf_op jit(solution)/shard_map/ppermute | solution.py:817
  187.4 34.2 %collective-permute-start.39 = (bf16[112,768]{1,0:T(8,128)(2,1)S(1)}, bf16[112,768]{1,0:T(8,128)(2,1)S(1)}, u32[]{:S(2)}, u32[]{:S(2)}) collective-permute-start(bf16[112,768]{1,0:T(8,128)(2,1)S(1)} %get-tuple-element.115), channel_id=1, source_target_pairs={{0,16},{4,20},{8,24},{12,28},{16,0},{20,4},{24,8},{28,12},{1,17},{... | collective-permute-start | bytes 516104 | tf_op jit(solution)/shard_map/ppermute | solution.py:817
  187.5 34.1 %collective-permute-start.40 = (bf16[112,768]{1,0:T(8,128)(2,1)S(1)}, bf16[112,768]{1,0:T(8,128)(2,1)S(1)}, u32[]{:S(2)}, u32[]{:S(2)}) collective-permute-start(bf16[112,768]{1,0:T(8,128)(2,1)S(1)} %get-tuple-element.116), channel_id=1, source_target_pairs={{0,24},{4,28},{8,0},{12,4},{16,8},{20,12},{24,16},{28,20},{1,25},{... | collective-permute-start | bytes 516104 | tf_op jit(solution)/shard_map/ppermute | solution.py:817
  217.4 13.7 %collective-permute-start.32 = (bf16[256,768]{1,0:T(8,128)(2,1)S(1)}, bf16[256,768]{1,0:T(8,128)(2,1)S(1)}, u32[]{:S(2)}, u32[]{:S(2)}) collective-permute-start(bf16[256,768]{1,0:T(8,128)(2,1)S(1)} %get-tuple-element.134), channel_id=1, source_target_pairs={{0,1},{1,0},{2,3},{3,2},{4,5},{5,4},{6,7},{7,6},{8,9},{9,8},{10,11... | collective-permute-start | bytes 1179656 | tf_op jit(solution)/shard_map/ppermute | solution.py:814
  218.2 12.8 %collective-permute-start.30 = (bf16[256,768]{1,0:T(8,128)(2,1)S(1)}, bf16[256,768]{1,0:T(8,128)(2,1)S(1)}, u32[]{:S(2)}, u32[]{:S(2)}) collective-permute-start(bf16[256,768]{1,0:T(8,128)(2,1)S(1)} %get-tuple-element.135), channel_id=1, source_target_pairs={{0,2},{1,3},{2,0},{3,1},{4,6},{5,7},{6,4},{7,5},{8,10},{9,11},{10,... | collective-permute-start | bytes 1179656 | tf_op jit(solution)/shard_map/ppermute | solution.py:814
  223.0 5.6 %collective-permute-start.43 = (bf16[112,256]{1,0:T(8,128)(2,1)S(1)}, bf16[112,256]{1,0:T(8,128)(2,1)S(1)}, u32[]{:S(2)}, u32[]{:S(2)}) collective-permute-start(bf16[112,256]{1,0:T(8,128)(2,1)S(1)} %get-tuple-element.117.refs_0_), channel_id=1, source_target_pairs={{0,3},{1,2},{2,1},{3,0},{4,7},{5,6},{6,5},{7,4},{8,11},{9,10},{10,... | collective-permute-start | bytes 172040 | tf_op jit(solution)/shard_map/ppermute | solution.py:814
  224.5 5.3 %collective-permute-start.42 = (bf16[112,256]{1,0:T(8,128)(2,1)S(1)}, bf16[112,256]{1,0:T(8,128)(2,1)S(1)}, u32[]{:S(2)}, u32[]{:S(2)}) collective-permute-start(bf16[112,256]{1,0:T(8,128)(2,1)S(1)} %get-tuple-element.117.refs_0_), channel_id=1, source_target_pairs={{0,2},{1,3},{2,0},{3,1},{4,6},{5,7},{6,4},{7,5},{8,10},{9,11},{10,... | collective-permute-start | bytes 172040 | tf_op jit(solution)/shard_map/ppermute | solution.py:814
  225.1 4.7 %collective-permute-start.41 = (bf16[112,256]{1,0:T(8,128)(2,1)S(1)}, bf16[112,256]{1,0:T(8,128)(2,1)S(1)}, u32[]{:S(2)}, u32[]{:S(2)}) collective-permute-start(bf16[112,256]{1,0:T(8,128)(2,1)S(1)} %get-tuple-element.117.refs_0_), channel_id=1, source_target_pairs={{0,1},{1,0},{2,3},{3,2},{4,5},{5,4},{6,7},{7,6},{8,9},{9,8},{10,11... | collective-permute-start | bytes 172040 | tf_op jit(solution)/shard_map/ppermute | solution.py:814
  (27 other events, 53.7 us)

commit v6 on v5

--- a/solution.py
+++ b/solution.py
@@ -1032,9 +1032,10 @@
     root = lax.rsqrt(total[:, 0] / (inner * n_t) + EPS)
     pull = root * root * root * (total[:, 1] / (inner * n_t))
     rk = jnp.stack([root, pull], axis=1)
+    branch = branch[:1] + [across(branch[k], k) for k in range(1, n_t)]
     branch_sum = branch[0].astype(F32)
-    for k in range(1, n_t):
-        branch_sum = branch_sum + across(branch[k], k).astype(F32)
+    for piece in branch[1:]:
+        branch_sum = branch_sum + piece.astype(F32)
     own_root = lax.dynamic_slice_in_dim(root.reshape(length), me_t * chunk_rows, chunk_rows)
     block_output = block_input + own_root[:, None] * branch_sum.reshape(chunk_rows, width)
 

time: 234 us -> 234 us (level)
  no operation moved by 1% of the time
where the time goes in v6:
time: 234 us; the launch traced here: 233 us
  Pallas kernels  75.9 us (32%)
  waiting for transfers between devices  66.6 us (28%)
  starting transfers between devices  44.2 us (19%)
  local copies, waits for them, and re-layouts  30.3 us (13%)
  other arithmetic  14.9 us (6%)
    ppermute x22, waiting for transfers between devices, across(): return lax.ppermute(v, 'tensor', swap(n_t, k))  38.7 us
    pallas_call x1, Pallas kernels, body(): pl.pallas_call(functools.partial(backward_kernel, dm), out_shape=[out(r_a...  31.5 us
    ppermute x12, waiting for transfers between devices, along(): return lax.ppermute(v, 'dp', shift_hi(n_dp, k))  27.1 us
    ppermute x22, starting transfers between devices, across(): return lax.ppermute(v, 'tensor', swap(n_t, k))  25.6 us
    pallas_call x1, Pallas kernels, body(): pl.pallas_call(functools.partial(forward_kernel, dm), out_shape=[out(leng...  21.7 us
    unnamed x96, local copies, waits for them, and re-layouts  19.4 us
    ppermute x12, starting transfers between devices, along(): return lax.ppermute(v, 'dp', shift_hi(n_dp, k))  17.4 us
    pallas_call x1, Pallas kernels, body(): pl.pallas_call(functools.partial(gate_kernel, dm), out_shape=[out(length,...  7.94 us
  transfers between devices with their start and end apart: 44, of which 12 were waited for; matrix products, arithmetic and copies ran while one was open for 11% of the time, Pallas kernels for 14%

profile of v6, /device:TPU:16, one launch (start us, length us, event | category | flops | bytes accessed | tf_op | source)
XLA Modules:
  0.0 233.0 jit_solution(13432255947465652971)
XLA Ops:
  1.3 3.5 %collective-permute-start.4 = (bf16[96,384]{1,0:T(8,128)(2,1)}, bf16[96,384]{1,0:T(8,128)(2,1)S(1)}, u32[]{:S(2)}, u32[]{:S(2)}) collective-permute-start(bf16[96,384]{1,0:T(8,128)(2,1)} %bitcast.42), channel_id=1, source_target_pairs={{0,16},{4,20},{8,24},{12,28},{16,0},{20,4},{24,8},{28,12},{1,17},{... | collective-permute-start | bytes 221192 | tf_op jit(solution)/shard_map/ppermute | solution.py:817
  4.8 1.7 pack_weights.1.refs_0_
  8.6 1.2 exponential_negate_fusion
  11.1 1.6 fusion.13
  12.9 1.3 compare_convert_fusion
  14.2 1.4 copy-done
  17.2 2.0 collective-permute-start.12
  19.2 1.5 collective-permute-start.17
  20.7 1.5 collective-permute-start.20
  24.6 1.8 collective-permute-start.11
  28.5 6.8 %collective-permute-done.11.refs_2_ = bf16[96,1152]{1,0:T(8,128)(2,1)S(1)} collective-permute-done((bf16[96,1152]{1,0:T(8,128)(2,1)S(1)}, bf16[96,1152]{1,0:T(8,128)(2,1)S(1)}, u32[]{:S(2)}, u32[]{:S(2)}) %collective-permute-start.11) | collective-permute-done | bytes 221216 | tf_op jit(solution)/shard_map/ppermute | solution.py:817
  35.4 2.4 %collective-permute-start.10 = (bf16[96,1152]{1,0:T(8,128)(2,1)S(1)}, bf16[96,1152]{1,0:T(8,128)(2,1)}, u32[]{:S(2)}, u32[]{:S(2)}) collective-permute-start(bf16[96,1152]{1,0:T(8,128)(2,1)S(1)} %copy-done.16), channel_id=1, source_target_pairs={{0,8},{4,12},{8,16},{12,20},{16,24},{20,28},{24,0},{28,4},{1,9},{5... | collective-permute-start | bytes 663560 | tf_op jit(solution)/shard_map/ppermute | solution.py:817
  37.8 1.5 collective-permute-start.21
  39.3 1.5 collective-permute-start.22
  41.9 1.3 gather_fusion.1
  43.2 1.3 gather_fusion
  47.8 1.8 concatenate.38.refs_16_.refs_1_
  49.6 0.9 concatenate.35.scalars
  55.3 1.6 collective-permute-start.1
  56.8 1.5 collective-permute-start
  58.9 1.0 copy-done.20
  59.9 1.0 copy-done.22
  60.9 1.0 copy-done.24
  61.8 0.9 copy-done.26
  62.8 0.9 copy-done.28
  63.7 0.9 copy-done.30
  64.7 21.7 %block_forward.1 = (f32[2048,384]{1,0:T(8,128)S(1)}, bf16[2048,384]{1,0:T(8,128)(2,1)S(1)}, f32[2048,384]{1,0:T(8,128)S(1)}, bf16[2048,640]{1,0:T(8,128)(2,1)S(1...) custom-call(s32[73]{0:T(128)S(1)} %concatenate.35.scalars, ...), custom_call_target="tpu_custom_call" | custom-call | flops 30000001024 | bytes 30000000 | tf_op jit(solution)/shard_map/block_forward/pallas_call | solution.py:937
  86.4 4.3 %branch_output.1 = (bf16[768,384]{1,0:T(8,128)(2,1)S(1)}, bf16[2,256,768]{2,1,0:T(8,128)(2,1)S(1)}, bf16[2,256,768]{2,1,0:T(8,128)(2,1)}, bf16[2,256,768]{2,1,0:T(8,128)(2,1)}, bf16[2,256,768]{2,1,0:T(8,128)(2,1)}) custom-call(s32[73]{0:T(128)S(1)} %concatenate.35.scalars, bf16[96,384]{1,0:T(8,128)(2,1)S(1)} %bitcast.44, bf16[96,384]{1,0:T(8,128)(2,1)S(1)} %copy-done.35, ...), custom_call_target="tpu_custom_call" | custom-call | flops 3000000000 | bytes 10000000 | tf_op jit(solution)/shard_map/branch_output/pallas_call | solution.py:999
  90.7 0.9 copy-done.6
  91.9 2.6 %scaled_cotangent.1 = (bf16[2048,384]{1,0:T(8,128)(2,1)S(1)}, f32[8,2,256]{2,1,0:T(2,128)S(1)}, bf16[2048,768]{1,0:T(8,128)(2,1)S(1)}) custom-call(s32[73]{0:T(128)S(1)} %concatenate.35.scalars, bf16[512,768]{1,0:T(8,128)(2,1)S(1)} %copy-done.4, bf16[512,768]{1,0:T(8,128)(2,1)S(1)} %collective-permute-done.refs_1_, ...), custom_call_target="tpu_custom_call" | custom-call | flops 3000000000 | bytes 10000000 | tf_op jit(solution)/shard_map/scaled_cotangent/pallas_call | solution.py:1015
  94.4 1.2 collective-permute-start.25
  95.7 1.4 collective-permute-start.24
  97.1 0.9 collective-permute-start.23
  98.0 1.1 collective-permute-done.25
  99.4 1.4 collective-permute-done.23
  100.9 7.9 %gate_backward.1 = (bf16[2048,384]{1,0:T(8,128)(2,1)S(1)}, bf16[2048,384]{1,0:T(8,128)(2,1)S(1)}, f32[8,384]{1,0:T(8,128)S(1)}, f32[8,768]{1,0:T(8,128)S(1)}, f3...) custom-call(s32[73]{0:T(128)S(1)} %concatenate.35.scalars, ...), custom_call_target="tpu_custom_call" | custom-call | flops 6000000000 | bytes 20000000 | tf_op jit(solution)/shard_map/gate_backward/pallas_call | solution.py:1054
  109.7 31.5 %block_backward.1 = (f32[384,768]{1,0:T(8,128)S(1)}, bf16[400,768]{1,0:T(8,128)(2,1)S(1)}, bf16[16,768]{1,0:T(8,128)(2,1)S(1)}, bf16[2,256,768]{2,1,0:T(8,128)(2...) custom-call(s32[73]{0:T(128)S(1)} %concatenate.35.scalars, ...), custom_call_target="tpu_custom_call" | custom-call | flops 40000000000 | bytes 30000000 | tf_op jit(solution)/shard_map/block_backward/pallas_call | solution.py:1090
  141.2 1.0 copy-done.2
  142.2 1.5 collective-permute-start.34
  143.7 1.5 collective-permute-start.36
  145.2 1.1 collective-permute-start.29
  146.3 18.4 %collective-permute-done.34.refs_0_ = bf16[192,768]{1,0:T(8,128)(2,1)S(1)} collective-permute-done((bf16[192,768]{1,0:T(8,128)(2,1)S(1)}, bf16[192,768]{1,0:T(8,128)(2,1)S(1)}, u32[]{:S(2)}, u32[]{:S(2)}) %collective-permute-start.34) | collective-permute-done | bytes 294944 | tf_op jit(solution)/shard_map/ppermute | solution.py:817
  166.0 1.5 collective-permute-start.26
  167.5 1.9 collective-permute-done.36.refs_2_
  170.1 1.4 collective-permute-start.27
  171.5 0.8 copy-done.8
  172.4 1.1 collective-permute-start.28
  173.6 1.1 copy-done.11
  174.7 1.0 copy-done.13
  175.7 1.0 copy-done.15
  177.4 1.1 copy-done.9
  179.2 8.0 %collective-permute-done.31.refs_4_ = bf16[2,256,768]{2,1,0:T(8,128)(2,1)S(1)} collective-permute-done((bf16[2,256,768]{2,1,0:T(8,128)(2,1)}, bf16[2,256,768]{2,1,0:T(8,128)(2,1)S(1)}, u32[]{:S(2)}, u32[]{:S(2)}) %collective-permute-start.31) | collective-permute-done | bytes 786464 | tf_op jit(solution)/shard_map/ppermute | solution.py:814
  187.5 4.0 %collective-permute-start.40 = (bf16[112,768]{1,0:T(8,128)(2,1)S(1)}, bf16[112,768]{1,0:T(8,128)(2,1)S(1)}, u32[]{:S(2)}, u32[]{:S(2)}) collective-permute-start(bf16[112,768]{1,0:T(8,128)(2,1)S(1)} %get-tuple-element.116), channel_id=1, source_target_pairs={{0,24},{4,28},{8,0},{12,4},{16,8},{20,12},{24,16},{28,20},{1,25},{... | collective-permute-start | bytes 516104 | tf_op jit(solution)/shard_map/ppermute | solution.py:817
  191.6 25.8 %collective-permute-done.27 = bf16[2,256,768]{2,1,0:T(8,128)(2,1)} collective-permute-done((bf16[2,256,768]{2,1,0:T(8,128)(2,1)}, bf16[2,256,768]{2,1,0:T(8,128)(2,1)}, u32[]{:S(2)}, u32[]{:S(2)}) %collective-permute-start.27) | collective-permute-done | bytes 786464 | tf_op jit(solution)/shard_map/ppermute | solution.py:814
  217.4 0.9 collective-permute-start.32
  218.2 1.2 collective-permute-start.30
  219.5 2.1 convert_add_fusion
  221.6 1.4 gradient_sum.1
  223.0 1.5 collective-permute-start.43
  225.1 1.5 collective-permute-start.41
  226.6 1.4 fusion
  228.7 1.1 collective-permute-done.42.refs_2_
  229.8 1.2 shared_sum.1
  231.0 2.0 input_gradient.1
  (169 shorter events, 26.5 us)
Async XLA Ops:
  0.6 41.2 %copy-start.43 = (s32[4,2]{1,0:T(4,128)S(1)}, s32[4,2]{1,0:T(4,128)}, u32[]{:S(2)}) copy-start(s32[4,2]{1,0:T(4,128)} %constant.112.clone) | copy-start | bytes 100
  0.7 42.5 %copy-start.42 = (s32[4,2]{1,0:T(4,128)S(1)}, s32[4,2]{1,0:T(4,128)}, u32[]{:S(2)}) copy-start(s32[4,2]{1,0:T(4,128)} %constant.111.clone) | copy-start | bytes 100
  0.7 40.6 %copy-start.44 = (s32[1,2048]{1,0:T(1,128)S(1)}, s32[1,2048]{1,0:T(1,128)}, u32[]{:S(2)}) copy-start(s32[1,2048]{1,0:T(1,128)} %param.20) | copy-start | bytes 24580
  0.7 16.5 %collective-permute-start.6 = (bf16[96,384]{1,0:T(8,128)(2,1)}, bf16[96,384]{1,0:T(8,128)(2,1)S(1)}, u32[]{:S(2)}, u32[]{:S(2)}) collective-permute-start(bf16[96,384]{1,0:T(8,128)(2,1)} %bitcast.40), channel_id=1, source_target_pairs={{0,4},{4,0},{8,12},{12,8},{16,20},{20,16},{24,28},{28,24},{1,5},{5... | collective-permute-start | bytes 221192 | tf_op jit(solution)/shard_map/ppermute | solution.py:820
  0.8 18.4 %collective-permute-start.5 = (bf16[96,384]{1,0:T(8,128)(2,1)}, bf16[96,384]{1,0:T(8,128)(2,1)S(1)}, u32[]{:S(2)}, u32[]{:S(2)}) collective-permute-start(bf16[96,384]{1,0:T(8,128)(2,1)} %bitcast.41), channel_id=1, source_target_pairs={{0,24},{4,28},{8,0},{12,4},{16,8},{20,12},{24,16},{28,20},{1,25},{... | collective-permute-start | bytes 221192 | tf_op jit(solution)/shard_map/ppermute | solution.py:817
  1.3 19.4 %collective-permute-start.4 = (bf16[96,384]{1,0:T(8,128)(2,1)}, bf16[96,384]{1,0:T(8,128)(2,1)S(1)}, u32[]{:S(2)}, u32[]{:S(2)}) collective-permute-start(bf16[96,384]{1,0:T(8,128)(2,1)} %bitcast.42), channel_id=1, source_target_pairs={{0,16},{4,20},{8,24},{12,28},{16,0},{20,4},{24,8},{28,12},{1,17},{... | collective-permute-start | bytes 221192 | tf_op jit(solution)/shard_map/ppermute | solution.py:817
  4.8 18.0 %collective-permute-start.3 = (bf16[96,384]{1,0:T(8,128)(2,1)}, bf16[96,384]{1,0:T(8,128)(2,1)S(1)}, u32[]{:S(2)}, u32[]{:S(2)}) collective-permute-start(bf16[96,384]{1,0:T(8,128)(2,1)} %bitcast.43), channel_id=1, source_target_pairs={{0,8},{4,12},{8,16},{12,20},{16,24},{20,28},{24,0},{28,4},{1,9},{5... | collective-permute-start | bytes 221192 | tf_op jit(solution)/shard_map/ppermute | solution.py:817
  6.5 10.7 %copy-start.16 = (bf16[96,1152]{1,0:T(8,128)(2,1)S(1)}, bf16[96,1152]{1,0:T(8,128)(2,1)}, u32[]{:S(2)}) copy-start(bf16[96,1152]{1,0:T(8,128)(2,1)} %pack_weights.1.refs_0_) | copy-start | bytes 663556
  6.5 19.9 %collective-permute-start.13 = (bf16[96,1152]{1,0:T(8,128)(2,1)}, bf16[96,1152]{1,0:T(8,128)(2,1)S(1)}, u32[]{:S(2)}, u32[]{:S(2)}) collective-permute-start(bf16[96,1152]{1,0:T(8,128)(2,1)} %pack_weights.1.refs_0_), channel_id=1, source_target_pairs={{0,4},{4,0},{8,12},{12,8},{16,20},{20,16},{24,28},{28,24},{1,5},{5... | collective-permute-start | bytes 663560 | tf_op jit(solution)/shard_map/ppermute | solution.py:820
  12.7 15.3 %copy-start.45 = (f32[6]{0:T(128)S(1)}, f32[6]{0:T(128)}, u32[]{:S(2)}) copy-start(f32[6]{0:T(128)} %param.30) | copy-start | bytes 76
  12.7 15.3 %copy-start.46 = (f32[6]{0:T(128)S(1)}, f32[6]{0:T(128)}, u32[]{:S(2)}) copy-start(f32[6]{0:T(128)} %exponential_negate_fusion) | copy-start | bytes 76
  16.3 38.4 %copy-start.4 = (bf16[512,768]{1,0:T(8,128)(2,1)S(1)}, bf16[512,768]{1,0:T(8,128)(2,1)}, u32[]{:S(2)}) copy-start(bf16[512,768]{1,0:T(8,128)(2,1)} %cot_ref.1) | copy-start | bytes 2359300
  16.6 38.1 %copy-start.19 = (bf16[256,768]{1,0:T(8,128)(2,1)}, bf16[256,768]{1,0:T(8,128)(2,1)S(1)}, u32[]{:S(2)}) copy-start(bf16[256,768]{1,0:T(8,128)(2,1)S(1)} %get-tuple-element.75.refs_9_) | copy-start | bytes 1179652
  17.2 9.8 %collective-permute-start.12 = (bf16[96,1152]{1,0:T(8,128)(2,1)S(1)}, bf16[96,1152]{1,0:T(8,128)(2,1)S(1)}, u32[]{:S(2)}, u32[]{:S(2)}) collective-permute-start(bf16[96,1152]{1,0:T(8,128)(2,1)S(1)} %copy-done.16), channel_id=1, source_target_pairs={{0,24},{4,28},{8,0},{12,4},{16,8},{20,12},{24,16},{28,20},{1,25},{... | collective-permute-start | bytes 663560 | tf_op jit(solution)/shard_map/ppermute | solution.py:817
  19.2 18.6 %collective-permute-start.17 = (bf16[256,768]{1,0:T(8,128)(2,1)S(1)}, bf16[256,768]{1,0:T(8,128)(2,1)}, u32[]{:S(2)}, u32[]{:S(2)}) collective-permute-start(bf16[256,768]{1,0:T(8,128)(2,1)S(1)} %get-tuple-element.74.refs_8_), channel_id=1, source_target_pairs={{0,1},{1,0},{2,3},{3,2},{4,5},{5,4},{6,7},{7,6},{8,9},{9,8},{10,11... | collective-permute-start | bytes 1179656 | tf_op jit(solution)/shard_map/ppermute | solution.py:814
  20.7 29.0 %copy-start.32 = (bf16[96,384]{1,0:T(8,128)(2,1)}, bf16[96,384]{1,0:T(8,128)(2,1)S(1)}, u32[]{:S(2)}) copy-start(bf16[96,384]{1,0:T(8,128)(2,1)S(1)} %collective-permute-done.4.refs_2_) | copy-start | bytes 221188
  20.7 18.6 %collective-permute-start.20 = (bf16[256,768]{1,0:T(8,128)(2,1)S(1)}, bf16[256,768]{1,0:T(8,128)(2,1)}, u32[]{:S(2)}, u32[]{:S(2)}) collective-permute-start(bf16[256,768]{1,0:T(8,128)(2,1)S(1)} %get-tuple-element.75.refs_9_), channel_id=1, source_target_pairs={{0,2},{1,3},{2,0},{3,1},{4,6},{5,7},{6,4},{7,5},{8,10},{9,11},{10,... | collective-permute-start | bytes 1179656 | tf_op jit(solution)/shard_map/ppermute | solution.py:814
  22.7 24.5 %copy-start.34 = (bf16[96,384]{1,0:T(8,128)(2,1)}, bf16[96,384]{1,0:T(8,128)(2,1)S(1)}, u32[]{:S(2)}) copy-start(bf16[96,384]{1,0:T(8,128)(2,1)S(1)} %collective-permute-done.3.refs_1_) | copy-start | bytes 221188
  22.7 1.3 collective-permute-start.9
  24.6 10.7 %collective-permute-start.11 = (bf16[96,1152]{1,0:T(8,128)(2,1)S(1)}, bf16[96,1152]{1,0:T(8,128)(2,1)S(1)}, u32[]{:S(2)}, u32[]{:S(2)}) collective-permute-start(bf16[96,1152]{1,0:T(8,128)(2,1)S(1)} %copy-done.16), channel_id=1, source_target_pairs={{0,16},{4,20},{8,24},{12,28},{16,0},{20,4},{24,8},{28,12},{1,17},{... | collective-permute-start | bytes 663560 | tf_op jit(solution)/shard_map/ppermute | solution.py:817
  26.4 20.8 %copy-start.25 = (bf16[96,1152]{1,0:T(8,128)(2,1)}, bf16[96,1152]{1,0:T(8,128)(2,1)S(1)}, u32[]{:S(2)}) copy-start(bf16[96,1152]{1,0:T(8,128)(2,1)S(1)} %collective-permute-done.13.refs_4_) | copy-start | bytes 663556
  26.4 24.9 %collective-permute-start.19 = (bf16[256,768]{1,0:T(8,128)(2,1)S(1)}, bf16[256,768]{1,0:T(8,128)(2,1)S(1)}, u32[]{:S(2)}, u32[]{:S(2)}) collective-permute-start(bf16[256,768]{1,0:T(8,128)(2,1)S(1)} %get-tuple-element.74.refs_8_), channel_id=1, source_target_pairs={{0,2},{1,3},{2,0},{3,1},{4,6},{5,7},{6,4},{7,5},{8,10},{9,11},{10,... | collective-permute-start | bytes 1179656 | tf_op jit(solution)/shard_map/ppermute | solution.py:814
  27.0 28.3 %copy-start.27 = (bf16[96,1152]{1,0:T(8,128)(2,1)}, bf16[96,1152]{1,0:T(8,128)(2,1)S(1)}, u32[]{:S(2)}) copy-start(bf16[96,1152]{1,0:T(8,128)(2,1)S(1)} %collective-permute-done.12.refs_3_) | copy-start | bytes 663556
  27.0 25.6 %collective-permute-start.18 = (bf16[256,768]{1,0:T(8,128)(2,1)S(1)}, bf16[256,768]{1,0:T(8,128)(2,1)S(1)}, u32[]{:S(2)}, u32[]{:S(2)}) collective-permute-start(bf16[256,768]{1,0:T(8,128)(2,1)S(1)} %get-tuple-element.75.refs_9_), channel_id=1, source_target_pairs={{0,1},{1,0},{2,3},{3,2},{4,5},{5,4},{6,7},{7,6},{8,9},{9,8},{10,11... | collective-permute-start | bytes 1179656 | tf_op jit(solution)/shard_map/ppermute | solution.py:814
  35.4 19.9 %copy-start.29 = (bf16[96,1152]{1,0:T(8,128)(2,1)}, bf16[96,1152]{1,0:T(8,128)(2,1)S(1)}, u32[]{:S(2)}) copy-start(bf16[96,1152]{1,0:T(8,128)(2,1)S(1)} %collective-permute-done.11.refs_2_) | copy-start | bytes 663556
  35.4 15.8 %collective-permute-start.10 = (bf16[96,1152]{1,0:T(8,128)(2,1)S(1)}, bf16[96,1152]{1,0:T(8,128)(2,1)}, u32[]{:S(2)}, u32[]{:S(2)}) collective-permute-start(bf16[96,1152]{1,0:T(8,128)(2,1)S(1)} %copy-done.16), channel_id=1, source_target_pairs={{0,8},{4,12},{8,16},{12,20},{16,24},{20,28},{24,0},{28,4},{1,9},{5... | collective-permute-start | bytes 663560 | tf_op jit(solution)/shard_map/ppermute | solution.py:817
  37.8 20.6 %collective-permute-start.21 = (bf16[256,768]{1,0:T(8,128)(2,1)}, bf16[256,768]{1,0:T(8,128)(2,1)}, u32[]{:S(2)}, u32[]{:S(2)}) collective-permute-start(bf16[256,768]{1,0:T(8,128)(2,1)} %collective-permute-done.17.refs_10_), channel_id=1, source_target_pairs={{0,2},{1,3},{2,0},{3,1},{4,6},{5,7},{6,4},{7,5},{8,10},{9,11},{10,... | collective-permute-start | bytes 1179656 | tf_op jit(solution)/shard_map/ppermute | solution.py:814
  39.3 19.1 %collective-permute-start.22 = (bf16[256,768]{1,0:T(8,128)(2,1)}, bf16[256,768]{1,0:T(8,128)(2,1)}, u32[]{:S(2)}, u32[]{:S(2)}) collective-permute-start(bf16[256,768]{1,0:T(8,128)(2,1)} %collective-permute-done.20.refs_13_), channel_id=1, source_target_pairs={{0,1},{1,0},{2,3},{3,2},{4,5},{5,4},{6,7},{7,6},{8,9},{9,8},{10,11... | collective-permute-start | bytes 1179656 | tf_op jit(solution)/shard_map/ppermute | solution.py:814
  51.2 3.5 %collective-permute-start.16 = (bf16[96,1152]{1,0:T(8,128)(2,1)S(1)}, bf16[96,1152]{1,0:T(8,128)(2,1)S(1)}, u32[]{:S(2)}, u32[]{:S(2)}) collective-permute-start(bf16[96,1152]{1,0:T(8,128)(2,1)S(1)} %collective-permute-done.12.refs_3_), channel_id=1, source_target_pairs={{0,4},{4,0},{8,12},{12,8},{16,20},{20,16},{24,28},{28,24},{1,5},{5... | collective-permute-start | bytes 663560 | tf_op jit(solution)/shard_map/ppermute | solution.py:820
  52.1 3.2 %collective-permute-start.15 = (bf16[96,1152]{1,0:T(8,128)(2,1)S(1)}, bf16[96,1152]{1,0:T(8,128)(2,1)S(1)}, u32[]{:S(2)}, u32[]{:S(2)}) collective-permute-start(bf16[96,1152]{1,0:T(8,128)(2,1)S(1)} %collective-permute-done.11.refs_2_), channel_id=1, source_target_pairs={{0,4},{4,0},{8,12},{12,8},{16,20},{20,16},{24,28},{28,24},{1,5},{5... | collective-permute-start | bytes 663560 | tf_op jit(solution)/shard_map/ppermute | solution.py:820
  53.3 3.5 %collective-permute-start.14 = (bf16[96,1152]{1,0:T(8,128)(2,1)}, bf16[96,1152]{1,0:T(8,128)(2,1)S(1)}, u32[]{:S(2)}, u32[]{:S(2)}) collective-permute-start(bf16[96,1152]{1,0:T(8,128)(2,1)} %collective-permute-done.10.refs_1_), channel_id=1, source_target_pairs={{0,4},{4,0},{8,12},{12,8},{16,20},{20,16},{24,28},{28,24},{1,5},{5... | collective-permute-start | bytes 663560 | tf_op jit(solution)/shard_map/ppermute | solution.py:820
  54.7 36.9 %collective-permute-start.2 = (bf16[512,768]{1,0:T(8,128)(2,1)S(1)}, bf16[512,768]{1,0:T(8,128)(2,1)S(1)}, u32[]{:S(2)}, u32[]{:S(2)}) collective-permute-start(bf16[512,768]{1,0:T(8,128)(2,1)S(1)} %copy-done.4), channel_id=1, source_target_pairs={{0,3},{1,2},{2,1},{3,0},{4,7},{5,6},{6,5},{7,4},{8,11},{9,10},{10,... | collective-permute-start | bytes 2359304 | tf_op jit(solution)/shard_map/ppermute | solution.py:814
  55.3 36.6 %collective-permute-start.1 = (bf16[512,768]{1,0:T(8,128)(2,1)S(1)}, bf16[512,768]{1,0:T(8,128)(2,1)S(1)}, u32[]{:S(2)}, u32[]{:S(2)}) collective-permute-start(bf16[512,768]{1,0:T(8,128)(2,1)S(1)} %copy-done.4), channel_id=1, source_target_pairs={{0,2},{1,3},{2,0},{3,1},{4,6},{5,7},{6,4},{7,5},{8,10},{9,11},{10,... | collective-permute-start | bytes 2359304 | tf_op jit(solution)/shard_map/ppermute | solution.py:814
  56.8 35.0 %collective-permute-start = (bf16[512,768]{1,0:T(8,128)(2,1)S(1)}, bf16[512,768]{1,0:T(8,128)(2,1)S(1)}, u32[]{:S(2)}, u32[]{:S(2)}) collective-permute-start(bf16[512,768]{1,0:T(8,128)(2,1)S(1)} %copy-done.4), channel_id=1, source_target_pairs={{0,1},{1,0},{2,3},{3,2},{4,5},{5,4},{6,7},{7,6},{8,9},{9,8},{10,11... | collective-permute-start | bytes 2359304 | tf_op jit(solution)/shard_map/ppermute | solution.py:814
  58.3 28.0 %collective-permute-start.8 = (bf16[96,384]{1,0:T(8,128)(2,1)}, bf16[96,384]{1,0:T(8,128)(2,1)S(1)}, u32[]{:S(2)}, u32[]{:S(2)}) collective-permute-start(bf16[96,384]{1,0:T(8,128)(2,1)} %copy-done.32), channel_id=1, source_target_pairs={{0,4},{4,0},{8,12},{12,8},{16,20},{20,16},{24,28},{28,24},{1,5},{5... | collective-permute-start | bytes 221192 | tf_op jit(solution)/shard_map/ppermute | solution.py:820
  58.4 28.0 %collective-permute-start.7 = (bf16[96,384]{1,0:T(8,128)(2,1)}, bf16[96,384]{1,0:T(8,128)(2,1)S(1)}, u32[]{:S(2)}, u32[]{:S(2)}) collective-permute-start(bf16[96,384]{1,0:T(8,128)(2,1)} %copy-done.34), channel_id=1, source_target_pairs={{0,4},{4,0},{8,12},{12,8},{16,20},{20,16},{24,28},{28,24},{1,5},{5... | collective-permute-start | bytes 221192 | tf_op jit(solution)/shard_map/ppermute | solution.py:820
  64.7 21.7 %copy-start.31 = (bf16[384,96]{0,1:T(8,128)(2,1)S(1)}, bf16[384,96]{0,1:T(8,128)(2,1)}, u32[]{:S(2)}) copy-start(bf16[384,96]{0,1:T(8,128)(2,1)} %param.34) | copy-start | bytes 221188
  64.7 21.7 %copy-start.33 = (bf16[96,384]{1,0:T(8,128)(2,1)S(1)}, bf16[96,384]{1,0:T(8,128)(2,1)}, u32[]{:S(2)}) copy-start(bf16[96,384]{1,0:T(8,128)(2,1)} %copy-done.32) | copy-start | bytes 221188
  64.7 21.8 %copy-start.35 = (bf16[96,384]{1,0:T(8,128)(2,1)S(1)}, bf16[96,384]{1,0:T(8,128)(2,1)}, u32[]{:S(2)}) copy-start(bf16[96,384]{1,0:T(8,128)(2,1)} %copy-done.34) | copy-start | bytes 221188
  64.7 21.8 %copy-start.37 = (bf16[96,384]{1,0:T(8,128)(2,1)S(1)}, bf16[96,384]{1,0:T(8,128)(2,1)}, u32[]{:S(2)}) copy-start(bf16[96,384]{1,0:T(8,128)(2,1)} %copy-done.36) | copy-start | bytes 221188
  94.4 4.7 %collective-permute-start.25 = (f32[8,2,256]{2,1,0:T(2,128)S(1)}, f32[8,2,256]{2,1,0:T(2,128)S(1)}, u32[]{:S(2)}, u32[]{:S(2)}) collective-permute-start(f32[8,2,256]{2,1,0:T(2,128)S(1)} %get-tuple-element.80), channel_id=1, source_target_pairs={{0,3},{1,2},{2,1},{3,0},{4,7},{5,6},{6,5},{7,4},{8,11},{9,10},{10,... | collective-permute-start | bytes 49160 | tf_op jit(solution)/shard_map/ppermute | solution.py:814
  95.7 3.7 %collective-permute-start.24 = (f32[8,2,256]{2,1,0:T(2,128)S(1)}, f32[8,2,256]{2,1,0:T(2,128)S(1)}, u32[]{:S(2)}, u32[]{:S(2)}) collective-permute-start(f32[8,2,256]{2,1,0:T(2,128)S(1)} %get-tuple-element.80), channel_id=1, source_target_pairs={{0,2},{1,3},{2,0},{3,1},{4,6},{5,7},{6,4},{7,5},{8,10},{9,11},{10,... | collective-permute-start | bytes 49160 | tf_op jit(solution)/shard_map/ppermute | solution.py:814
  97.1 3.7 %collective-permute-start.23 = (f32[8,2,256]{2,1,0:T(2,128)S(1)}, f32[8,2,256]{2,1,0:T(2,128)S(1)}, u32[]{:S(2)}, u32[]{:S(2)}) collective-permute-start(f32[8,2,256]{2,1,0:T(2,128)S(1)} %get-tuple-element.80), channel_id=1, source_target_pairs={{0,1},{1,0},{2,3},{3,2},{4,5},{5,4},{6,7},{7,6},{8,9},{9,8},{10,11... | collective-permute-start | bytes 49160 | tf_op jit(solution)/shard_map/ppermute | solution.py:814
  100.9 8.8 %copy-start.39 = (f32[2048,384]{1,0:T(8,128)S(1)}, f32[2048,384]{1,0:T(8,128)}, u32[]{:S(2)}) copy-start(f32[2048,384]{1,0:T(8,128)} %copy-done.38) | copy-start | bytes 9437188
  100.9 8.8 %copy-start.41 = (bf16[2048,640]{1,0:T(8,128)(2,1)S(1)}, bf16[2048,640]{1,0:T(8,128)(2,1)}, u32[]{:S(2)}) copy-start(bf16[2048,640]{1,0:T(8,128)(2,1)} %copy-done.40) | copy-start | bytes 7864324
  142.2 29.4 %collective-permute-start.33 = (bf16[400,768]{1,0:T(8,128)(2,1)S(1)}, bf16[400,768]{1,0:T(8,128)(2,1)S(1)}, u32[]{:S(2)}, u32[]{:S(2)}) collective-permute-start(bf16[400,768]{1,0:T(8,128)(2,1)S(1)} %get-tuple-element.105), channel_id=1, source_target_pairs={{0,4},{4,0},{8,12},{12,8},{16,20},{20,16},{24,28},{28,24},{1,5},{5... | collective-permute-start | bytes 1843208 | tf_op jit(solution)/shard_map/ppermute | solution.py:820
  142.2 22.5 %collective-permute-start.34 = (bf16[192,768]{1,0:T(8,128)(2,1)S(1)}, bf16[192,768]{1,0:T(8,128)(2,1)S(1)}, u32[]{:S(2)}, u32[]{:S(2)}) collective-permute-start(bf16[192,768]{1,0:T(8,128)(2,1)S(1)} %get-tuple-element.109), channel_id=1, source_target_pairs={{0,8},{4,12},{8,16},{12,20},{16,24},{20,28},{24,0},{28,4},{1,9},{5... | collective-permute-start | bytes 884744 | tf_op jit(solution)/shard_map/ppermute | solution.py:817
  143.7 21.6 %collective-permute-start.35 = (bf16[192,768]{1,0:T(8,128)(2,1)S(1)}, bf16[192,768]{1,0:T(8,128)(2,1)S(1)}, u32[]{:S(2)}, u32[]{:S(2)}) collective-permute-start(bf16[192,768]{1,0:T(8,128)(2,1)S(1)} %get-tuple-element.110), channel_id=1, source_target_pairs={{0,16},{4,20},{8,24},{12,28},{16,0},{20,4},{24,8},{28,12},{1,17},{... | collective-permute-start | bytes 884744 | tf_op jit(solution)/shard_map/ppermute | solution.py:817
  143.7 25.7 %collective-permute-start.36 = (bf16[192,768]{1,0:T(8,128)(2,1)S(1)}, bf16[192,768]{1,0:T(8,128)(2,1)S(1)}, u32[]{:S(2)}, u32[]{:S(2)}) collective-permute-start(bf16[192,768]{1,0:T(8,128)(2,1)S(1)} %get-tuple-element.111), channel_id=1, source_target_pairs={{0,24},{4,28},{8,0},{12,4},{16,8},{20,12},{24,16},{28,20},{1,25},{... | collective-permute-start | bytes 884744 | tf_op jit(solution)/shard_map/ppermute | solution.py:817
  145.2 33.9 %collective-permute-start.29 = (bf16[2,256,768]{2,1,0:T(8,128)(2,1)}, bf16[2,256,768]{2,1,0:T(8,128)(2,1)S(1)}, u32[]{:S(2)}, u32[]{:S(2)}) collective-permute-start(bf16[2,256,768]{2,1,0:T(8,128)(2,1)} %get-tuple-element.101), channel_id=1, source_target_pairs={{0,1},{1,0},{2,3},{3,2},{4,5},{5,4},{6,7},{7,6},{8,9},{9,8},{10,11... | collective-permute-start | bytes 2359304 | tf_op jit(solution)/shard_map/ppermute | solution.py:814
  164.7 22.5 %collective-permute-start.31 = (bf16[2,256,768]{2,1,0:T(8,128)(2,1)}, bf16[2,256,768]{2,1,0:T(8,128)(2,1)S(1)}, u32[]{:S(2)}, u32[]{:S(2)}) collective-permute-start(bf16[2,256,768]{2,1,0:T(8,128)(2,1)} %get-tuple-element.102), channel_id=1, source_target_pairs={{0,2},{1,3},{2,0},{3,1},{4,6},{5,7},{6,4},{7,5},{8,10},{9,11},{10,... | collective-permute-start | bytes 2359304 | tf_op jit(solution)/shard_map/ppermute | solution.py:814
  166.0 21.5 %collective-permute-start.26 = (bf16[2,256,768]{2,1,0:T(8,128)(2,1)}, bf16[2,256,768]{2,1,0:T(8,128)(2,1)}, u32[]{:S(2)}, u32[]{:S(2)}) collective-permute-start(bf16[2,256,768]{2,1,0:T(8,128)(2,1)} %get-tuple-element.82), channel_id=1, source_target_pairs={{0,1},{1,0},{2,3},{3,2},{4,5},{5,4},{6,7},{7,6},{8,9},{9,8},{10,11... | collective-permute-start | bytes 2359304 | tf_op jit(solution)/shard_map/ppermute | solution.py:814
  170.1 47.2 %collective-permute-start.27 = (bf16[2,256,768]{2,1,0:T(8,128)(2,1)}, bf16[2,256,768]{2,1,0:T(8,128)(2,1)}, u32[]{:S(2)}, u32[]{:S(2)}) collective-permute-start(bf16[2,256,768]{2,1,0:T(8,128)(2,1)} %get-tuple-element.83), channel_id=1, source_target_pairs={{0,2},{1,3},{2,0},{3,1},{4,6},{5,7},{6,4},{7,5},{8,10},{9,11},{10,... | collective-permute-start | bytes 2359304 | tf_op jit(solution)/shard_map/ppermute | solution.py:814
  172.4 45.9 %collective-permute-start.28 = (bf16[2,256,768]{2,1,0:T(8,128)(2,1)}, bf16[2,256,768]{2,1,0:T(8,128)(2,1)}, u32[]{:S(2)}, u32[]{:S(2)}) collective-permute-start(bf16[2,256,768]{2,1,0:T(8,128)(2,1)} %get-tuple-element.84), channel_id=1, source_target_pairs={{0,3},{1,2},{2,1},{3,0},{4,7},{5,6},{6,5},{7,4},{8,11},{9,10},{10,... | collective-permute-start | bytes 2359304 | tf_op jit(solution)/shard_map/ppermute | solution.py:814
  179.1 40.3 %copy-start.7 = (bf16[2,256,768]{2,1,0:T(8,128)(2,1)S(1)}, bf16[2,256,768]{2,1,0:T(8,128)(2,1)}, u32[]{:S(2)}) copy-start(bf16[2,256,768]{2,1,0:T(8,128)(2,1)} %copy-done.6) | copy-start | bytes 2359300
  179.2 8.3 %collective-permute-start.37 = (bf16[96,768]{1,0:T(8,128)(2,1)S(1)}, bf16[96,768]{1,0:T(8,128)(2,1)S(1)}, u32[]{:S(2)}, u32[]{:S(2)}) collective-permute-start(bf16[96,768]{1,0:T(8,128)(2,1)S(1)} %get-tuple-element.113), channel_id=1, source_target_pairs={{0,4},{4,0},{8,12},{12,8},{16,20},{20,16},{24,28},{28,24},{1,5},{5... | collective-permute-start | bytes 442376 | tf_op jit(solution)/shard_map/ppermute | solution.py:820
  187.2 34.4 %collective-permute-start.38 = (bf16[112,768]{1,0:T(8,128)(2,1)S(1)}, bf16[112,768]{1,0:T(8,128)(2,1)S(1)}, u32[]{:S(2)}, u32[]{:S(2)}) collective-permute-start(bf16[112,768]{1,0:T(8,128)(2,1)S(1)} %get-tuple-element.114), channel_id=1, source_target_pairs={{0,8},{4,12},{8,16},{12,20},{16,24},{20,28},{24,0},{28,4},{1,9},{5... | collective-permute-start | bytes 516104 | tf_op jit(solution)/shard_map/ppermute | solution.py:817
  187.4 34.2 %collective-permute-start.39 = (bf16[112,768]{1,0:T(8,128)(2,1)S(1)}, bf16[112,768]{1,0:T(8,128)(2,1)S(1)}, u32[]{:S(2)}, u32[]{:S(2)}) collective-permute-start(bf16[112,768]{1,0:T(8,128)(2,1)S(1)} %get-tuple-element.115), channel_id=1, source_target_pairs={{0,16},{4,20},{8,24},{12,28},{16,0},{20,4},{24,8},{28,12},{1,17},{... | collective-permute-start | bytes 516104 | tf_op jit(solution)/shard_map/ppermute | solution.py:817
  187.5 34.1 %collective-permute-start.40 = (bf16[112,768]{1,0:T(8,128)(2,1)S(1)}, bf16[112,768]{1,0:T(8,128)(2,1)S(1)}, u32[]{:S(2)}, u32[]{:S(2)}) collective-permute-start(bf16[112,768]{1,0:T(8,128)(2,1)S(1)} %get-tuple-element.116), channel_id=1, source_target_pairs={{0,24},{4,28},{8,0},{12,4},{16,8},{20,12},{24,16},{28,20},{1,25},{... | collective-permute-start | bytes 516104 | tf_op jit(solution)/shard_map/ppermute | solution.py:817
  217.4 13.7 %collective-permute-start.32 = (bf16[256,768]{1,0:T(8,128)(2,1)S(1)}, bf16[256,768]{1,0:T(8,128)(2,1)S(1)}, u32[]{:S(2)}, u32[]{:S(2)}) collective-permute-start(bf16[256,768]{1,0:T(8,128)(2,1)S(1)} %get-tuple-element.134), channel_id=1, source_target_pairs={{0,1},{1,0},{2,3},{3,2},{4,5},{5,4},{6,7},{7,6},{8,9},{9,8},{10,11... | collective-permute-start | bytes 1179656 | tf_op jit(solution)/shard_map/ppermute | solution.py:814
  218.2 12.8 %collective-permute-start.30 = (bf16[256,768]{1,0:T(8,128)(2,1)S(1)}, bf16[256,768]{1,0:T(8,128)(2,1)S(1)}, u32[]{:S(2)}, u32[]{:S(2)}) collective-permute-start(bf16[256,768]{1,0:T(8,128)(2,1)S(1)} %get-tuple-element.135), channel_id=1, source_target_pairs={{0,2},{1,3},{2,0},{3,1},{4,6},{5,7},{6,4},{7,5},{8,10},{9,11},{10,... | collective-permute-start | bytes 1179656 | tf_op jit(solution)/shard_map/ppermute | solution.py:814
  223.0 5.6 %collective-permute-start.43 = (bf16[112,256]{1,0:T(8,128)(2,1)S(1)}, bf16[112,256]{1,0:T(8,128)(2,1)S(1)}, u32[]{:S(2)}, u32[]{:S(2)}) collective-permute-start(bf16[112,256]{1,0:T(8,128)(2,1)S(1)} %get-tuple-element.117.refs_0_), channel_id=1, source_target_pairs={{0,3},{1,2},{2,1},{3,0},{4,7},{5,6},{6,5},{7,4},{8,11},{9,10},{10,... | collective-permute-start | bytes 172040 | tf_op jit(solution)/shard_map/ppermute | solution.py:814
  224.5 5.3 %collective-permute-start.42 = (bf16[112,256]{1,0:T(8,128)(2,1)S(1)}, bf16[112,256]{1,0:T(8,128)(2,1)S(1)}, u32[]{:S(2)}, u32[]{:S(2)}) collective-permute-start(bf16[112,256]{1,0:T(8,128)(2,1)S(1)} %get-tuple-element.117.refs_0_), channel_id=1, source_target_pairs={{0,2},{1,3},{2,0},{3,1},{4,6},{5,7},{6,4},{7,5},{8,10},{9,11},{10,... | collective-permute-start | bytes 172040 | tf_op jit(solution)/shard_map/ppermute | solution.py:814
  225.1 4.7 %collective-permute-start.41 = (bf16[112,256]{1,0:T(8,128)(2,1)S(1)}, bf16[112,256]{1,0:T(8,128)(2,1)S(1)}, u32[]{:S(2)}, u32[]{:S(2)}) collective-permute-start(bf16[112,256]{1,0:T(8,128)(2,1)S(1)} %get-tuple-element.117.refs_0_), channel_id=1, source_target_pairs={{0,1},{1,0},{2,3},{3,2},{4,5},{5,4},{6,7},{7,6},{8,9},{9,8},{10,11... | collective-permute-start | bytes 172040 | tf_op jit(solution)/shard_map/ppermute | solution.py:814
  (27 other events, 53.7 us)
